TPU v7x, 128 devices: a whole 4x4x4 slice. The times are simulated.
128 devices in a mesh: cp: 32 (over z, y, x_lo), fsdp: 4 (over x_hi, core).
Axes of the slice: x: 4 (x_hi: 2, x_lo: 2; x = x_hi * 2 + x_lo), y: 4, z: 4, core: 2. Of those that a mesh axis runs over, the one named last changes fastest.
Arguments:
- query_states: bfloat16 [4, 4096, 1024], P('fsdp', 'cp'), may hold values from -32 to 32
- key_states: bfloat16 [4, 4096, 1024], P('fsdp', 'cp'), may hold values from -32 to 32
- value_states: bfloat16 [4, 4096, 1024], P('fsdp', 'cp'), may hold values from -6 to 6
- span_order: int32 [64], replicated, may hold values from 0 to 63, as said below
- block_mask: int32 [64, 64], replicated, may hold values from 0 to 1, as said below
- output_weight: bfloat16 [1024, 2048], P(('cp', 'fsdp')), may hold values from -0.1875 to 0.1875
- upstream: bfloat16 [4, 4096, 2048], P('fsdp', 'cp'), may hold values from -6 to 6
Outputs:
- projected: bfloat16 [4, 4096, 2048], P('fsdp', 'cp')
- query_gradient: bfloat16 [4, 4096, 1024], P('fsdp', 'cp')
- key_gradient: bfloat16 [4, 4096, 1024], P('fsdp', 'cp')
- value_gradient: bfloat16 [4, 4096, 1024], P('fsdp', 'cp')
- weight_gradient: float32 [1024, 2048], P(('cp', 'fsdp'))
Inputs may be any that keep to these rules, and one draw needn't show every extreme that they name: `span_order`: entries 2 d and 2 d + 1 hold positions p and 63 - p; every position appears once. `block_mask`: the diagonal is 1.
All inputs are finite; a program needn't handle non-finite values.
Results may differ from a plain program's by a relative error of at most 0.024.
Values may be sent and summed in bfloat16 or wider, within the bound.
No kernel may reach another device: no remote copies, remote signals or barrier semaphores. Data moves between devices by JAX's collectives and lax.ppermute only.
A program may use at most 128 MiB of HBM per device.

v0:
```python
import math

import jax
import jax.numpy as jnp
from jax import lax
from jax.sharding import PartitionSpec as P

HEADS = 8
HEAD = 128


lowest = -1e30


def side_by_side(arrays, axis, dim, along):
    widths = [a.shape[along] for a in arrays]
    both = jnp.concatenate(arrays, axis=along)
    filled = lax.all_gather(both, axis, axis=dim, tiled=True)
    return tuple(jnp.split(filled, [sum(widths[:k]) for k in range(1, len(widths))], axis=along))


def cut_along(array, dim, size):
    before, after = (array.shape[:dim], array.shape[dim + 1 :])
    return jnp.moveaxis(array.reshape(*before, size, -1, *after), dim, 0)


def summed_on_arrival(array, axis, dim):
    size = lax.axis_size(axis)
    tiles = lax.all_to_all(cut_along(array, dim, size), axis, 0, 0, tiled=True)
    return jnp.sum(tiles.astype(jnp.float32), axis=0)


def split_heads(row_block):
    return row_block.reshape(row_block.shape[0], HEADS, HEAD)


def pair_scores(query_rows, key_rows):
    return jnp.einsum(
        "qhd,khd->hqk",
        split_heads(query_rows),
        split_heads(key_rows),
        preferred_element_type=jnp.float32,
    ) * (1.0 / HEAD)


def storage_mask(span_order, block_mask):
    span_count = span_order.shape[0]
    onehot = (span_order[:, None] == jnp.arange(span_count, dtype=jnp.int32)[None, :]).astype(
        jnp.float32
    )
    permuted = jnp.dot(jnp.dot(onehot, block_mask.astype(jnp.float32)), onehot.T)
    return permuted > 0.5


def allowed_block(span_ok, positions, query_begin, query_total, key_begin, key_total, span_rows):
    span_sub = lax.dynamic_slice(
        span_ok,
        (query_begin // span_rows, key_begin // span_rows),
        (query_total // span_rows, key_total // span_rows),
    )
    spread = jnp.broadcast_to(
        span_sub[:, None, :, None],
        (query_total // span_rows, span_rows, key_total // span_rows, span_rows),
    )
    spread = spread.reshape(query_total, key_total)
    query_pos = lax.dynamic_slice_in_dim(positions, query_begin, query_total)
    key_pos = lax.dynamic_slice_in_dim(positions, key_begin, key_total)
    return spread & (key_pos[None, :] <= query_pos[:, None])


def local_terms(query_rows, grad_rows, log_rows, delta_rows, key_rows, value_rows, allowed):
    scores = pair_scores(query_rows, key_rows)
    probability = jnp.where(allowed[None], jnp.exp(scores - log_rows[..., None]), 0.0)
    dprob = jnp.einsum(
        "qhd,khd->hqk",
        split_heads(grad_rows),
        split_heads(value_rows),
        preferred_element_type=jnp.float32,
    )
    dscores = (probability * (dprob - delta_rows[..., None]) * (1.0 / HEAD)).astype(jnp.bfloat16)
    return (probability, dscores)


def local(query_states, key_states, value_states, span_order, block_mask, output_weight, upstream):
    query_rows = query_states[0]
    key_local = key_states[0]
    value_local = value_states[0]
    upstream_rows = upstream[0]
    tokens = query_rows.shape[0]
    span_rows = tokens // 2
    positions = (
        span_order[:, None] * span_rows + jnp.arange(span_rows, dtype=jnp.int32)[None, :]
    ).reshape(-1)
    span_ok = storage_mask(span_order, block_mask)
    own_start = lax.axis_index("cp") * tokens
    key_all, value_all = side_by_side((key_local, value_local), "cp", 0, 1)
    weight = lax.all_gather(output_weight, ("cp", "fsdp"), axis=0, tiled=True)
    length = key_all.shape[0]
    key_block = math.gcd(length, 512)
    block_count = length // key_block
    block_steps = jnp.arange(block_count, dtype=jnp.int32)

    def stats_step(running, step_index):
        key_begin = step_index * key_block
        key_rows = lax.dynamic_slice_in_dim(key_all, key_begin, key_block)
        allowed = allowed_block(
            span_ok, positions, own_start, tokens, key_begin, key_block, span_rows
        )
        maxima, totals = running
        scores = pair_scores(query_rows, key_rows)
        masked = jnp.where(allowed[None], scores, lowest)
        new_max = jnp.maximum(maxima, masked.max(-1))
        exp_terms = jnp.where(allowed[None], jnp.exp(scores - new_max[..., None]), 0.0)
        return ((new_max, totals * jnp.exp(maxima - new_max) + exp_terms.sum(-1)), None)

    stat_start = (
        jnp.full((HEADS, tokens), lowest, jnp.float32),
        jnp.zeros((HEADS, tokens), jnp.float32),
    )
    (maxima, totals), _ = lax.scan(stats_step, stat_start, block_steps)
    log_total = maxima + jnp.log(totals)

    def output_step(attn_sum, step_index):
        key_begin = step_index * key_block
        key_rows = lax.dynamic_slice_in_dim(key_all, key_begin, key_block)
        value_rows = lax.dynamic_slice_in_dim(value_all, key_begin, key_block)
        allowed = allowed_block(
            span_ok, positions, own_start, tokens, key_begin, key_block, span_rows
        )
        scores = pair_scores(query_rows, key_rows)
        probability = jnp.where(allowed[None], jnp.exp(scores - log_total[..., None]), 0.0)
        return (
            attn_sum
            + jnp.einsum(
                "hqk,khd->qhd",
                probability.astype(jnp.bfloat16),
                split_heads(value_rows),
                preferred_element_type=jnp.float32,
            ),
            None,
        )

    zero_heads = jnp.zeros((tokens, HEADS, HEAD), jnp.float32)
    attn_sum, _ = lax.scan(output_step, zero_heads, block_steps)
    attended = lax.optimization_barrier(attn_sum.reshape(tokens, -1).astype(jnp.bfloat16))
    projected = jnp.dot(attended, weight, preferred_element_type=jnp.float32).astype(jnp.bfloat16)
    grad_attended = lax.dot_general(
        upstream_rows, weight, (((1,), (1,)), ((), ())), preferred_element_type=jnp.float32
    ).astype(jnp.bfloat16)
    grad_attended = lax.optimization_barrier(grad_attended)
    weight_term = lax.dot_general(
        attended, upstream_rows, (((0,), (0,)), ((), ())), preferred_element_type=jnp.float32
    )
    row_delta = (
        (grad_attended.astype(jnp.float32) * attended.astype(jnp.float32))
        .reshape(tokens, HEADS, HEAD)
        .sum(-1)
    )
    delta_heads = row_delta.T

    def query_step(grad_sum, step_index):
        key_begin = step_index * key_block
        key_rows = lax.dynamic_slice_in_dim(key_all, key_begin, key_block)
        value_rows = lax.dynamic_slice_in_dim(value_all, key_begin, key_block)
        allowed = allowed_block(
            span_ok, positions, own_start, tokens, key_begin, key_block, span_rows
        )
        probability, dscores = local_terms(
            query_rows, grad_attended, log_total, delta_heads, key_rows, value_rows, allowed
        )
        return (
            grad_sum
            + jnp.einsum(
                "hqk,khd->qhd", dscores, split_heads(key_rows), preferred_element_type=jnp.float32
            ),
            None,
        )

    query_sum, _ = lax.scan(query_step, zero_heads, block_steps)
    query_gradient = query_sum.reshape(tokens, -1).astype(jnp.bfloat16)
    log_all, delta_all = side_by_side((log_total.T, row_delta), "cp", 0, 1)
    sums_now = (zero_heads, zero_heads)
    query_piece, grad_piece = side_by_side((query_rows, grad_attended), "cp", 0, 1)
    row_count = query_piece.shape[0]
    sources = row_count // tokens
    group_size = math.gcd(sources, max(1, 512 // tokens))
    group_rows = group_size * tokens

    def group_step(running, step_index):
        offset = step_index * group_rows
        query_group = lax.dynamic_slice_in_dim(query_piece, offset, group_rows)
        grad_group = lax.dynamic_slice_in_dim(grad_piece, offset, group_rows)
        log_group = lax.dynamic_slice_in_dim(log_all, offset, group_rows).T
        delta_group = lax.dynamic_slice_in_dim(delta_all, offset, group_rows).T
        allowed = allowed_block(
            span_ok, positions, offset, group_rows, own_start, tokens, span_rows
        )
        key_sum, value_sum = running
        probability, dscores = local_terms(
            query_group, grad_group, log_group, delta_group, key_local, value_local, allowed
        )
        probability_low = probability.astype(jnp.bfloat16).reshape(
            HEADS, group_size, tokens, tokens
        )
        dscores_group = dscores.reshape(HEADS, group_size, tokens, tokens)
        qsplit = query_group.reshape(group_size, tokens, HEADS, HEAD)
        gsplit = grad_group.reshape(group_size, tokens, HEADS, HEAD)
        key_part = jnp.einsum(
            "hgqk,gqhd->gkhd", dscores_group, qsplit, preferred_element_type=jnp.float32
        ).astype(jnp.bfloat16)
        value_part = jnp.einsum(
            "hgqk,gqhd->gkhd", probability_low, gsplit, preferred_element_type=jnp.float32
        ).astype(jnp.bfloat16)
        key_part, value_part = lax.optimization_barrier((key_part, value_part))
        return (
            (
                key_sum + key_part.astype(jnp.float32).sum(0),
                value_sum + value_part.astype(jnp.float32).sum(0),
            ),
            None,
        )

    sums_now, _ = lax.scan(group_step, sums_now, jnp.arange(sources // group_size, dtype=jnp.int32))
    key_sum, value_sum = sums_now
    key_gradient = key_sum.reshape(tokens, -1).astype(jnp.bfloat16)
    value_gradient = value_sum.reshape(tokens, -1).astype(jnp.bfloat16)
    cycle_count = lax.axis_size("cp")
    batch_count = lax.axis_size("fsdp")
    slab_rows = weight_term.shape[0] // (cycle_count * batch_count)
    reordered = weight_term.reshape(cycle_count, batch_count, slab_rows, -1).transpose(1, 0, 2, 3)
    reordered = reordered.reshape(weight_term.shape[0], -1)
    partial_batch = summed_on_arrival(reordered.astype(jnp.bfloat16), "fsdp", 0)
    weight_gradient = summed_on_arrival(partial_batch.astype(jnp.bfloat16), "cp", 0)
    return (
        projected[None],
        query_gradient[None],
        key_gradient[None],
        value_gradient[None],
        weight_gradient,
    )


def solution(mesh):
    return jax.shard_map(
        local,
        mesh=mesh,
        in_specs=(
            P("fsdp", "cp", None),
            P("fsdp", "cp", None),
            P("fsdp", "cp", None),
            P(),
            P(),
            P(("cp", "fsdp"), None),
            P("fsdp", "cp", None),
        ),
        out_specs=(
            P("fsdp", "cp", None),
            P("fsdp", "cp", None),
            P("fsdp", "cp", None),
            P("fsdp", "cp", None),
            P(("cp", "fsdp"), None),
        ),
        check_vma=False,
    )
```

profile of v0, /device:TPU:1, one launch (start us, length us, event | category | flops | bytes accessed | tf_op | source)
XLA Modules:
  0.0 1168.4 jit_solution(7732555768528166424)
XLA Ops:
  11.1 199.5 %all-gather.6.cloned.1.call-done = bf16[1024,2048]{1,0:T(8,128)(2,1)} async-done(((bf16[8,2048]{1,0:T(8,128)(2,1)}), bf16[1024,2048]{1,0:T(8,128)(2,1)}) %all-gather.6.cloned.1.call-update) | async-done | bytes 4194320 | tf_op jit(solution)/shard_map/all_gather | solution.py:97
  210.6 3.7 convolution_convert_fusion.3
  215.9 354.4 %all-gather.4.cloned.1.call-done = bf16[4096,2048]{0,1:T(8,128)(2,1)} async-done(((bf16[128,2048]{0,1:T(8,128)(2,1)}), bf16[4096,2048]{0,1:T(8,128)(2,1)}) %all-gather.4.cloned.1.call-update) | async-done | bytes 16777232 | tf_op jit(solution)/shard_map/all_gather | solution.py:18
  570.3 11.8 %fusion.61 = (bf16[4096,1024]{0,1:T(8,128)(2,1)}, bf16[4096,1024]{0,1:T(8,128)(2,1)}) fusion(bf16[4096,2048]{0,1:T(8,128)(2,1)} %all-gather.4.cloned.1.call-done), kind=kLoop, calls=%fused_computation.94 | loop fusion | bytes 33554432 | tf_op jit(solution)/shard_map/split | solution.py:19
  582.1 36.4 %while.60 = (s32[]{:T(128)}, f32[8,128]{1,0:T(8,128)S(1)}, f32[8,128]{1,0:T(8,128)S(1)}, s32[8]{0:T(128)S(1)}, pred[64,64]{1,0:T(8,128)(4,1)S(1)}, /*index=5*/s3...) while((s32[]{:T(128)}, f32[8,128]{1,0:T(8,128)S(1)}, ...), condition=%wide.region_3.4_spmd.clone, body=%wide.region_0.3_spmd.clone.sunk | while | flops 138023952 | bytes 8776669 | solution.py:120
  618.5 51.7 %while.61 = (s32[]{:T(128)}, f32[128,8,128]{0,2,1:T(8,128)}, s32[8]{0:T(128)S(1)}, bf16[4096,1024]{0,1:T(8,128)(2,1)}, pred[64,64]{1,0:T(8,128)(4,1)S(1)}, /*ind...) while((s32[]{:T(128)}, f32[128,8,128]{0,2,1:T(8,128)}, ...), condition=%wide.region_5.6_spmd.clone, body=%wide.region_4.5_spmd.clone.sunk | while | flops 270925856 | bytes 8661988 | solution.py:144
  627.9 2.8 fusion.109
  634.5 2.8 fusion.109
  641.1 2.8 fusion.109
  647.7 2.8 fusion.109
  654.3 2.8 fusion.109
  660.9 2.8 fusion.109
  667.5 2.8 fusion.109
  673.3 2.3 copy.258
  675.6 5.5 all-to-all-start
  681.2 75.2 %while.62 = (s32[]{:T(128)}, f32[128,8,128]{0,2,1:T(8,128)}, s32[8]{0:T(128)S(1)}, bf16[4096,1024]{0,1:T(8,128)(2,1)}, pred[64,64]{1,0:T(8,128)(4,1)S(1)}, /*ind...) while((s32[]{:T(128)}, f32[128,8,128]{0,2,1:T(8,128)}, ...), condition=%wide.region_8.9_spmd.clone, body=%wide.region_7.8_spmd.clone.sunk | while | flops 406716416 | bytes 14171124 | solution.py:179
  684.2 1.9 fusion.116
  686.9 3.6 fusion.117
  693.5 1.9 fusion.116
  696.2 3.7 fusion.117
  702.9 1.9 fusion.116
  705.6 3.7 fusion.117
  712.3 1.9 fusion.116
  715.0 3.7 fusion.117
  721.7 1.9 fusion.116
  724.4 3.7 fusion.117
  731.1 1.9 fusion.116
  733.8 3.7 fusion.117
  740.5 1.9 fusion.116
  743.2 3.7 fusion.117
  749.9 1.9 fusion.116
  752.6 3.7 fusion.117
  758.3 3.7 fusion.46
  762.0 13.3 %all-to-all-done = bf16[4,256,2048]{2,1,0:T(8,128)(2,1)} async-done(((bf16[4,256,2048]{2,1,0:T(8,128)(2,1)}), bf16[4,256,2048]{2,1,0:T(8,128)(2,1)}, u32[]{:S(2)}, u32[]{:S(2)}) %all-to-all-start) | async-done | bytes 4194336 | tf_op jit(solution)/shard_map/all_to_all | solution.py:29
  775.3 4.3 reduce_sum.70
  779.5 7.7 all-to-all-start.1
  787.3 94.1 %all_gather.15 = f32[4096,16]{0,1:T(8,128)S(1)} all-gather(f32[128,16]{0,1:T(8,128)S(1)} %pad_maximum_fusion.2), channel_id=1, replica_groups=mesh['cp'=32,'fsdp'=4] {'cp'}, dimensions={0}, use_global_device_ids=true | all-gather | bytes 270336 | tf_op jit(solution)/shard_map/all_gather | solution.py:18
  882.9 115.3 %all-gather.8.cloned.1.call-done = bf16[4096,2048]{1,0:T(8,128)(2,1)} async-done(((bf16[128,2048]{1,0:T(8,128)(2,1)}), bf16[4096,2048]{1,0:T(8,128)(2,1)}) %all-gather.8.cloned.1.call-update) | async-done | bytes 16777232 | tf_op jit(solution)/shard_map/all_gather | solution.py:18
  998.1 11.6 fusion.60
  1009.8 148.1 %while.63 = (s32[]{:T(128)}, f32[128,8,128]{0,2,1:T(8,128)}, f32[128,8,128]{0,2,1:T(8,128)}, s32[8]{0:T(128)S(1)}, bf16[4096,1024]{1,0:T(8,128)(2,1)}, /*index=5...) while((s32[]{:T(128)}, f32[128,8,128]{0,2,1:T(8,128)}, ...), condition=%wide.region_12.13_spmd.clone, body=%wide.region_9.12_spmd.clone.sunk | while | flops 544604160 | bytes 55680292 | solution.py:223
  1016.7 2.3 constant_dynamic-slice_fusion.16
  1035.2 2.3 constant_dynamic-slice_fusion.16
  1053.7 2.3 constant_dynamic-slice_fusion.16
  1072.3 2.3 constant_dynamic-slice_fusion.16
  1090.8 2.3 constant_dynamic-slice_fusion.16
  1109.3 2.3 constant_dynamic-slice_fusion.16
  1127.8 2.3 constant_dynamic-slice_fusion.16
  1146.3 2.3 constant_dynamic-slice_fusion.16
  (659 shorter events, 220.9 us)
Async XLA Ops:
  7.2 203.4 %copy-start = (bf16[1,128,2048]{2,1,0:T(8,128)(2,1)S(1)}, bf16[1,128,2048]{2,1,0:T(8,128)(2,1)}, u32[]{:S(2)}) copy-start(bf16[1,128,2048]{2,1,0:T(8,128)(2,1)} %param.21) | copy-start | bytes 1572868
  7.2 203.4 %all-gather.6.cloned.1.call-start = ((), (), s32[]{:S(2)}) async-start(), calls=%async_computation.3 | async-start | bytes 4227072 | tf_op jit(solution)/shard_map/all_gather | solution.py:97
  7.9 562.4 %all-gather.4.cloned.1.call-start = ((), (), s32[]{:S(2)}) async-start(), calls=%async_computation.2 | async-start | bytes 17301504 | tf_op jit(solution)/shard_map/all_gather | solution.py:18
  11.1 203.3 %copy-start.4 = (bf16[1,128,1024]{2,1,0:T(8,128)(2,1)S(1)}, bf16[1,128,1024]{2,1,0:T(8,128)(2,1)}, u32[]{:S(2)}) copy-start(bf16[1,128,1024]{2,1,0:T(8,128)(2,1)} %param.15) | copy-start | bytes 786436
  11.1 204.2 %copy-start.15 = (s32[64]{0:T(128)S(1)}, s32[64]{0:T(128)}, u32[]{:S(2)}) copy-start(s32[64]{0:T(128)} %param.18) | copy-start | bytes 772
  11.1 204.3 %copy-start.14 = (s32[64,64]{1,0:T(8,128)S(1)}, s32[64,64]{1,0:T(8,128)}, u32[]{:S(2)}) copy-start(s32[64,64]{1,0:T(8,128)} %param.19) | copy-start | bytes 49156
  11.1 987.0 %all-gather.8.cloned.1.call-start = ((), (), s32[]{:S(2)}) async-start(), calls=%async_computation.4 | async-start | bytes 17301504 | tf_op jit(solution)/shard_map/all_gather | solution.py:18
  675.6 99.6 %all-to-all-start = ((bf16[4,256,2048]{2,1,0:T(8,128)(2,1)}), bf16[4,256,2048]{2,1,0:T(8,128)(2,1)}, u32[]{:S(2)}, u32[]{:S(2)}) async-start(bf16[4,256,2048]{2,1,0:T(8,128)(2,1)} %bitcast.259), calls=%async_computation | async-start | bytes 8388608 | tf_op jit(solution)/shard_map/all_to_all | solution.py:29
  779.5 102.5 %all-to-all-start.1 = ((bf16[32,8,2048]{2,1,0:T(8,128)(2,1)}), bf16[32,8,2048]{2,1,0:T(8,128)(2,1)S(1)}, u32[]{:S(2)}, u32[]{:S(2)}) async-start(bf16[32,8,2048]{2,1,0:T(8,128)(2,1)} %bitcast.17), calls=%async_computation.1 | async-start | bytes 2097152 | tf_op jit(solution)/shard_map/all_to_all | solution.py:29
  882.9 126.9 %copy-start.10 = (bf16[1,128,1024]{2,1,0:T(8,128)(2,1)S(1)}, bf16[1,128,1024]{2,1,0:T(8,128)(2,1)}, u32[]{:S(2)}) copy-start(bf16[1,128,1024]{2,1,0:T(8,128)(2,1)} %param.16) | copy-start | bytes 786436
  1009.8 4.2 copy-start.12
  1016.7 4.5 copy-start.9
  1026.1 2.2 copy-start.11
  1026.1 2.2 copy-start.13
  1028.3 4.1 copy-start.12
  1035.2 4.5 copy-start.9
  1041.1 1.6 copy-start.2
  1044.6 2.2 copy-start.11
  1044.7 2.2 copy-start.13
  1046.8 4.1 copy-start.12
  1053.7 4.5 copy-start.9
  1063.1 2.2 copy-start.11
  1063.2 2.2 copy-start.13
  1065.4 4.1 copy-start.12
  1072.3 4.5 copy-start.9
  1081.7 2.2 copy-start.11
  1081.7 2.2 copy-start.13
  1083.9 4.1 copy-start.12
  1090.8 4.5 copy-start.9
  1096.6 1.6 copy-start.2
  1100.2 2.2 copy-start.11
  1100.2 2.2 copy-start.13
  1102.4 4.1 copy-start.12
  1109.3 4.5 copy-start.9
  1115.1 1.6 copy-start.2
  1118.7 2.2 copy-start.11
  1118.7 2.2 copy-start.13
  1120.9 4.1 copy-start.12
  1127.8 4.5 copy-start.9
  1133.6 1.6 copy-start.2
  1137.2 2.2 copy-start.11
  1137.2 2.2 copy-start.13
  1139.4 4.1 copy-start.12
  1146.3 4.5 copy-start.9
  1152.1 1.6 copy-start.2
  1155.7 2.2 copy-start.11
  1155.7 2.2 copy-start.13
  1157.9 3.9 copy-start.1
  (43 other events, 46.6 us)
Sparse Core Ops, SparseCore 0:
  9.7 200.8 all-gather.5
  212.2 358.1 all-gather.3
  572.0 426.1 all-gather.7
where the time goes:
time: 1170 us
  waiting for transfers between devices  683 us (58%)
  local copies, waits for them, and re-layouts  196 us (17%)
  matrix products  119 us (10%)
  blocking collectives  94.1 us (8%)
  other arithmetic  24.1 us (2%)
  loops' own time  23.7 us (2%)
  between operations  14 us (1%)
  starting transfers between devices  13.4 us (1%)
    all_gather x2, waiting for transfers between devices, side_by_side(): filled = lax.all_gather(both, axis, axis=dim, tiled=True)  470 us
    all_gather x1, waiting for transfers between devices, local(): weight = lax.all_gather(output_weight, ('cp', 'fsdp'), axis=0, tiled=True)  199 us
    all_gather x1, blocking collectives, side_by_side(): filled = lax.all_gather(both, axis, axis=dim, tiled=True)  94.1 us
    dot_general x24, matrix products, pair_scores(): jnp.einsum('qhd,khd->hqk', split_heads(query_rows), split_heads(key_rows)...  34.9 us
    dynamic_slice x16, local copies, waits for them, and re-layouts, group_step(): grad_group = lax.dynamic_slice_in_dim(grad_piece, offset, group_rows)  30.5 us
    dot_general x8, matrix products, query_step(): jnp.einsum('hqk,khd->qhd', dscores, split_heads(key_rows), preferred_elem...  29.7 us
    split x3, local copies, waits for them, and re-layouts, side_by_side(): jnp.split(filled, [sum(widths[:k]) for k in range(1, len(widths))], axis=...  24.1 us
  transfers between devices with their start and end apart: 5, of which 4 were waited for; matrix products, arithmetic and copies ran while one was open for 16% of the time, Pallas kernels for 0%

commit v1 on v0

v1 whole, which is shorter than its diff:
```python
import functools

import jax
import jax.numpy as jnp
from jax import lax
from jax.experimental import pallas as pl
from jax.experimental.pallas import tpu as pltpu
from jax.sharding import Mesh, PartitionSpec as P

HEADS = 8
HEAD = 128
SPAN = 64
UNITS = 16
ROWS = UNITS * SPAN
TILE = 256
LOW = -1e30
SCALE = 1.0 / HEAD
F32 = jnp.float32
BF16 = jnp.bfloat16
NT = (((1,), (1,)), ((), ()))
NN = (((1,), (0,)), ((), ()))
TN = (((0,), (0,)), ((), ()))


def dot(a, b, dims):
    return lax.dot_general(a, b, dims, preferred_element_type=F32)


def span_hot(first_span):
    span = lax.broadcasted_iota(jnp.int32, (TILE, HEAD), 0) // SPAN + first_span
    lane = lax.broadcasted_iota(jnp.int32, (TILE, HEAD), 1)
    return (span == lane).astype(F32).astype(BF16)


def query_wide(query, first_span):
    return jnp.concatenate([query * BF16(SCALE), span_hot(first_span)], axis=1)


def spread_bias(bias):
    return jnp.broadcast_to(bias[:, None, :], (UNITS, SPAN, HEAD)).reshape(ROWS, HEAD).astype(BF16)


def later_in_span():
    key = lax.broadcasted_iota(jnp.int32, (TILE, TILE), 0)
    query = lax.broadcasted_iota(jnp.int32, (TILE, TILE), 1)
    return (key // SPAN == query // SPAN) & (key > query)


def forward_body(first, *refs):
    if first:
        q_ref, kv0_ref, kv1_ref, bias_ref, o_ref, m_ref, l_ref, ka_ref, s_ref = refs
    else:
        (q_ref, kv0_ref, kv1_ref, bias_ref, o0_ref, m0_ref, l0_ref, att_ref, lse_ref, ka_ref, s_ref) = refs
    step = pl.program_id(0)

    @pl.when(step == 0)
    def _():
        for c, kv_ref in enumerate((kv0_ref, kv1_ref)):
            rows = pl.ds(c * ROWS, ROWS)
            ka_ref[rows, :HEAD] = kv_ref[:, :HEAD]
            ka_ref[rows, HEAD:] = spread_bias(bias_ref[c * UNITS : (c + 1) * UNITS, :])

    qa = query_wide(q_ref[...], step * (TILE // SPAN))
    for c in range(2):
        rows = pl.ds(c * ROWS, ROWS)
        s_ref[rows, :] = dot(ka_ref[rows, :], qa, NT)
    if first:
        rows = pl.ds(pl.multiple_of(step * TILE, TILE), TILE)
        s_ref[rows, :] = jnp.where(later_in_span(), LOW, s_ref[rows, :])
    top = jnp.max(s_ref[...], axis=0, keepdims=True)
    if not first:
        top = jnp.maximum(top, m0_ref[...])
    weights = jnp.exp(s_ref[...] - top)
    total = jnp.sum(weights, axis=0, keepdims=True)
    low = weights.astype(BF16)
    out = dot(kv0_ref[:, HEAD:], low[:ROWS], TN) + dot(kv1_ref[:, HEAD:], low[ROWS:], TN)
    if first:
        o_ref[...] = out
        m_ref[...] = top
        l_ref[...] = total
    else:
        fade = jnp.exp(m0_ref[...] - top)
        total = total + l0_ref[...] * fade
        out = (out + o0_ref[...] * fade) / total
        att_ref[...] = out.T.astype(BF16)
        lse_ref[...] = top + jnp.log(total)


def tile_spec(cols):
    return pl.BlockSpec((TILE, cols), lambda i: (i, 0))


def row_spec(rows):
    return pl.BlockSpec((rows, TILE), lambda i: (0, i))


def whole(rows, cols):
    return pl.BlockSpec((rows, cols), lambda i: (0, 0))


def cost(matmuls, pairs):
    return pl.CostEstimate(
        flops=matmuls * 2 * pairs * 2 * HEAD, bytes_accessed=4 << 20, transcendentals=pairs
    )


def forward(first, q, kv0, kv1, bias, *carry):
    stat = jax.ShapeDtypeStruct((1, ROWS), F32)
    if first:
        outs = [jax.ShapeDtypeStruct((HEAD, ROWS), F32), stat, stat]
        out_specs = [row_spec(HEAD), row_spec(1), row_spec(1)]
        carry_specs = []
    else:
        outs = [jax.ShapeDtypeStruct((ROWS, HEAD), BF16), stat]
        out_specs = [tile_spec(HEAD), row_spec(1)]
        carry_specs = [row_spec(HEAD), row_spec(1), row_spec(1)]
    return pl.pallas_call(
        functools.partial(forward_body, first),
        out_shape=outs,
        grid=(ROWS // TILE,),
        in_specs=[
            tile_spec(HEAD),
            whole(ROWS, 2 * HEAD),
            whole(ROWS, 2 * HEAD),
            whole(2 * UNITS, HEAD),
            *carry_specs,
        ],
        out_specs=out_specs,
        scratch_shapes=[
            pltpu.VMEM((2 * ROWS, 2 * HEAD), BF16),
            pltpu.VMEM((2 * ROWS, TILE), F32),
        ],
        cost_estimate=cost(2, 2 * ROWS * ROWS),
        compiler_params=pltpu.CompilerParams(vmem_limit_bytes=40 << 20),
        name="forward_a" if first else "forward_b",
    )(q, kv0, kv1, bias, *carry)


def delta_body(g_ref, att_ref, d_ref):
    product = g_ref[...].astype(F32) * att_ref[...].astype(F32)
    d_ref[...] = jnp.sum(product.T, axis=0, keepdims=True)


def row_delta(g, att):
    return pl.pallas_call(
        delta_body,
        out_shape=jax.ShapeDtypeStruct((1, ROWS), F32),
        in_specs=[pl.BlockSpec(memory_space=pltpu.VMEM)] * 2,
        out_specs=pl.BlockSpec(memory_space=pltpu.VMEM),
        name="delta",
    )(g, att)


def query_body(q_ref, g_ref, lse_ref, delta_ref, kv0, kv1, kv2, kv3, bias_ref, dq_ref, ka_ref, s_ref):
    step = pl.program_id(0)
    chunks = (kv0, kv1, kv2, kv3)

    @pl.when(step == 0)
    def _():
        for c, kv_ref in enumerate(chunks):
            rows = pl.ds(c * ROWS, ROWS)
            ka_ref[rows, :HEAD] = kv_ref[:, :HEAD]
            ka_ref[rows, HEAD:] = spread_bias(bias_ref[c * UNITS : (c + 1) * UNITS, :])

    qa = query_wide(q_ref[...], step * (TILE // SPAN))
    g = g_ref[...]
    lse = lse_ref[...]
    delta = delta_ref[...]
    total = jnp.zeros((HEAD, TILE), F32)
    for c, kv_ref in enumerate(chunks):
        s_ref[...] = dot(ka_ref[pl.ds(c * ROWS, ROWS), :], qa, NT)
        if c == 0:
            rows = pl.ds(pl.multiple_of(step * TILE, TILE), TILE)
            s_ref[rows, :] = jnp.where(later_in_span(), LOW, s_ref[rows, :])
        prob = jnp.exp(s_ref[...] - lse)
        dprob = dot(kv_ref[:, HEAD:], g, NT)
        ds = (prob * (dprob - delta)).astype(BF16)
        total += dot(kv_ref[:, :HEAD], ds, TN)
    dq_ref[...] = (total * SCALE).T.astype(BF16)


def query_grad(q, g, lse, delta, kvs, bias):
    return pl.pallas_call(
        query_body,
        out_shape=jax.ShapeDtypeStruct((ROWS, HEAD), BF16),
        grid=(ROWS // TILE,),
        in_specs=[
            tile_spec(HEAD),
            tile_spec(HEAD),
            row_spec(1),
            row_spec(1),
            *[whole(ROWS, 2 * HEAD)] * 4,
            whole(4 * UNITS, HEAD),
        ],
        out_specs=tile_spec(HEAD),
        scratch_shapes=[
            pltpu.VMEM((4 * ROWS, 2 * HEAD), BF16),
            pltpu.VMEM((ROWS, TILE), F32),
        ],
        cost_estimate=cost(3, 4 * ROWS * ROWS),
        compiler_params=pltpu.CompilerParams(vmem_limit_bytes=40 << 20),
        name="query_grad",
    )(q, g, lse, delta, *kvs, bias)


def key_body(*refs):
    kv_ref, bias_ref = refs[:2]
    qs, gs, stats = refs[2:6], refs[6:10], refs[10:14]
    dk_ref, dv_ref, ka_ref, s_ref, dk_acc, dv_acc = refs[14:]
    ka_ref[:, :HEAD] = kv_ref[:, :HEAD]
    ka_ref[:, HEAD:] = spread_bias(bias_ref[:UNITS, :])
    dk_acc[...] = jnp.zeros_like(dk_acc)
    dv_acc[...] = jnp.zeros_like(dv_acc)
    for c in range(4):

        def tile(i, _, c=c):
            rows = pl.ds(pl.multiple_of(i * TILE, TILE), TILE)
            q = qs[c][rows, :]
            g = gs[c][rows, :]
            lse = stats[c][0:1, rows]
            delta = stats[c][1:2, rows]
            qa = query_wide(q, i * (TILE // SPAN) + c * UNITS)
            s_ref[...] = dot(ka_ref[...], qa, NT)
            if c == 0:
                s_ref[rows, :] = jnp.where(later_in_span(), LOW, s_ref[rows, :])
            prob = jnp.exp(s_ref[...] - lse)
            dprob = dot(kv_ref[:, HEAD:], g, NT)
            ds = (prob * (dprob - delta)).astype(BF16)
            dv_acc[...] += dot(prob.astype(BF16), g, NN)
            dk_acc[...] += dot(ds, q, NN)
            return 0

        lax.fori_loop(0, ROWS // TILE, tile, 0)
    dk_ref[...] = (dk_acc[...] * SCALE).astype(BF16)
    dv_ref[...] = dv_acc[...].astype(BF16)


def key_grad(kv, bias, qs, gs, stats):
    in_vmem = pl.BlockSpec(memory_space=pltpu.VMEM)
    return pl.pallas_call(
        key_body,
        out_shape=[jax.ShapeDtypeStruct((ROWS, HEAD), BF16)] * 2,
        in_specs=[in_vmem] * 14,
        out_specs=[in_vmem] * 2,
        scratch_shapes=[
            pltpu.VMEM((ROWS, 2 * HEAD), BF16),
            pltpu.VMEM((ROWS, TILE), F32),
            pltpu.VMEM((ROWS, HEAD), F32),
            pltpu.VMEM((ROWS, HEAD), F32),
        ],
        cost_estimate=cost(4, 4 * ROWS * ROWS),
        compiler_params=pltpu.CompilerParams(vmem_limit_bytes=40 << 20),
        name="key_grad",
    )(kv, bias, *qs, *gs, *stats)


ZY = ("z", "y")
CHIPS = ("z", "y", "xl", "xh")
SWAP = [(0, 1), (1, 0)]


def other_core(x):
    return lax.ppermute(x, "core", SWAP)


def other_chip(x):
    return lax.ppermute(x, "xl", SWAP)


def everyone(x):
    far = other_chip(x)
    return x, other_core(x), far, other_core(far)


def exchange(x, axes):
    return lax.all_to_all(x, axes, 0, 0, tiled=True)


def in_order(first, own, peer):
    return jnp.stack([jnp.where(first, own, peer), jnp.where(first, peer, own)])


def span_bias(span_order, block_mask, xl, core):
    count = span_order.shape[0]
    row = jnp.arange(count, dtype=jnp.int32)
    owner, unit = row // UNITS, row % UNITS
    row_xl = xl ^ (owner // 2)
    half = core ^ (owner % 2) ^ ((unit // 4 + unit % 4) % 2)
    storage = 2 * (2 * unit + row_xl) + half
    held = (storage[:, None] == jnp.arange(count, dtype=jnp.int32)[None, :]).astype(jnp.int32)
    position = jnp.sum(held * span_order[None, :], axis=1)
    hot = (position[:, None] == jnp.arange(count, dtype=jnp.int32)[None, :]).astype(F32)
    pairs = jnp.dot(hot, jnp.dot(block_mask.astype(F32).T, hot.T))
    allowed = (pairs > 0.5) & (position[:, None] <= position[None, :])
    bias = jnp.where(allowed, 0.0, LOW).astype(F32)
    return jnp.pad(bias, ((0, 0), (0, HEAD - count)))


def by_unit(rows, kinds):
    split = rows.reshape(2, SPAN, kinds, HEADS, HEAD)
    return split.transpose(0, 3, 1, 2, 4).reshape(UNITS, SPAN, kinds * HEAD)


def by_row(blocks, kinds):
    split = blocks.reshape(2, HEADS, SPAN, kinds, HEAD)
    return split.transpose(0, 2, 3, 1, 4).reshape(2, SPAN, kinds * HEADS * HEAD)


def local(query_states, key_states, value_states, span_order, block_mask, output_weight, upstream):
    z, y, xl, core = (lax.axis_index(a) for a in ("z", "y", "xl", "core"))
    first_core = core == 0
    half = core ^ ((z + y) % 2)

    def share(rows):
        halves = rows.reshape(2, SPAN, -1)
        own = lax.dynamic_index_in_dim(halves, half, 0, False)
        peer = other_core(lax.dynamic_index_in_dim(halves, 1 - half, 0, False))
        return in_order(first_core, own, peer)

    def unshare(both):
        own = lax.dynamic_index_in_dim(both, core, 0, False)
        peer = other_core(lax.dynamic_index_in_dim(both, 1 - core, 0, False))
        return in_order(half == 0, own, peer).reshape(2 * SPAN, -1)

    states = share(jnp.concatenate([query_states[0], key_states[0], value_states[0]], axis=1))
    up = share(upstream[0]).reshape(2 * SPAN, -1)
    bias = span_bias(span_order, block_mask, xl, core)

    blocks = exchange(by_unit(states, 3), ZY).reshape(ROWS, 3 * HEAD)
    q = blocks[:, :HEAD]
    kvs = everyone(blocks[:, HEAD:])

    copies = jnp.broadcast_to(output_weight[None], (64, *output_weight.shape))
    weight_own = exchange(copies, CHIPS)
    weight_peer = other_core(weight_own)
    weight = in_order(first_core, weight_own, weight_peer).transpose(1, 0, 2, 3)
    weight = weight.reshape(HEADS * HEAD, -1)

    partial = forward(True, q, kvs[0], kvs[1], bias[: 2 * UNITS])
    attended, lse = forward(False, q, kvs[2], kvs[3], bias[2 * UNITS :], *partial)

    grad_rows = dot(up, weight, NT).astype(BF16).reshape(2, SPAN, -1)
    g = exchange(by_unit(grad_rows, 1), ZY).reshape(ROWS, HEAD)
    gs = everyone(g)
    qs = everyone(q)
    attended_rows = by_row(exchange(attended.reshape(UNITS, SPAN, HEAD), ZY), 1)
    attended_rows = attended_rows.reshape(2 * SPAN, -1)
    delta = row_delta(g, attended)
    stats = everyone(jnp.concatenate([lse, delta], axis=0))

    query_out = query_grad(q, g, lse, delta, kvs, bias)

    projected = dot(attended_rows, weight, NN).astype(BF16).reshape(2, SPAN, -1)
    projected = unshare(projected)
    term = dot(attended_rows, up, TN).astype(BF16).reshape(64, 2, 8, -1)
    term_own = lax.dynamic_index_in_dim(term, core, 1, False)
    term_peer = other_core(lax.dynamic_index_in_dim(term, 1 - core, 1, False))
    pair = (term_own.astype(F32) + term_peer.astype(F32)).astype(BF16)
    weight_gradient = jnp.sum(exchange(pair, CHIPS).astype(F32), axis=0)

    key_out, value_out = key_grad(kvs[0], bias, qs, gs, stats)
    grads = jnp.concatenate([query_out, key_out, value_out], axis=1).reshape(UNITS, SPAN, -1)
    grads = unshare(by_row(exchange(grads, ZY), 3))
    query_gradient, key_gradient, value_gradient = jnp.split(grads, 3, axis=1)
    return (
        projected[None],
        query_gradient[None],
        key_gradient[None],
        value_gradient[None],
        weight_gradient,
    )


def solution(mesh):
    axes = ("z", "y", "xl", "xh", "core")
    fine = Mesh(mesh.devices.reshape(4, 4, 2, 2, 2), axes)
    rows = P(("xh", "core"), ("z", "y", "xl"), None)
    return jax.shard_map(
        local,
        mesh=fine,
        in_specs=(rows, rows, rows, P(), P(), P(axes, None), rows),
        out_specs=(rows, rows, rows, rows, P(axes, None)),
        check_vma=False,
    )
```

time: 1170 us -> 215 us (0.18)
  waiting for transfers between devices: 683 us -> 66.4 us
  local copies, waits for them, and re-layouts: 196 us -> 16.9 us
  matrix products: 119 us -> 10 us
  blocking collectives: 94.1 us -> 21.5 us
  Pallas kernels: 0 us -> 37.7 us
  starting transfers between devices: 13.4 us -> 44.9 us
  loops' own time: 23.7 us -> 0 us
  between operations: 14 us -> 1.05 us
    all_gather x3 -> x0, waiting for transfers between devices: 669 us -> none  [the longest x2 470 us: side_by_side(): filled = lax.all_gather(both, axis, axis=dim, tiled=True)]
    dot_general x68 -> x4, matrix products: 119 us -> 10 us  [the longest x3 9.69 us: dot(): return lax.dot_general(a, b, dims, preferred_element_type=F32)]
    dynamic_slice x153 -> x0, local copies, waits for them, and re-layouts: 107 us -> none  [the longest x16 30.5 us: group_step(): grad_group = lax.dynamic_slice_in_dim(grad_piece, offset, group_rows)]
    all_gather x1 -> x0, blocking collectives: 94.1 us -> none  [side_by_side(): filled = lax.all_gather(both, axis, axis=dim, tiled=True)]
    all_to_all x2 -> x5, waiting for transfers between devices: 13.3 us -> 64.1 us  [exchange(): return lax.all_to_all(x, axes, 0, 0, tiled=True)]
    pallas_call x0 -> x5, Pallas kernels: none -> 37.7 us  [the longest x1 15.7 us: key_grad(): pl.pallas_call(key_body, out_shape=[jax.ShapeDtypeStruct((ROWS, HEAD), BF...]
    split x3 -> x0, local copies, waits for them, and re-layouts: 24.1 us -> none  [side_by_side(): jnp.split(filled, [sum(widths[:k]) for k in range(1, len(widths))], axis=...]
    another operation x4 -> x0, loops' own time: 23.7 us -> none  [the longest x1 6.16 us: local(): (maxima, totals), _ = lax.scan(stats_step, stat_start, block_steps)]
  transfers between devices with their start and end apart: 5 -> 23, of which waited for: 4 -> 7; matrix products, arithmetic and copies ran while one was open for 16% -> 17% of each run, Pallas kernels for 0% -> 18%
where the time goes in v1:
time: 215 us; the launch traced here: 214 us
  waiting for transfers between devices  66.4 us (31%)
  starting transfers between devices  44.9 us (21%)
  Pallas kernels  37.7 us (18%)
  blocking collectives  21.5 us (10%)
  local copies, waits for them, and re-layouts  16.9 us (8%)
  other arithmetic  15.4 us (7%)
  matrix products  10 us (5%)
    all_to_all x5, waiting for transfers between devices, exchange(): return lax.all_to_all(x, axes, 0, 0, tiled=True)  64.1 us
    all_to_all x5, starting transfers between devices, exchange(): return lax.all_to_all(x, axes, 0, 0, tiled=True)  27 us
    all_to_all x1, blocking collectives, exchange(): return lax.all_to_all(x, axes, 0, 0, tiled=True)  21.5 us
    pallas_call x1, Pallas kernels, key_grad(): pl.pallas_call(key_body, out_shape=[jax.ShapeDtypeStruct((ROWS, HEAD), BF...  15.7 us
    ppermute x14, starting transfers between devices, other_core(): return lax.ppermute(x, 'core', SWAP)  14.6 us
    pallas_call x2, Pallas kernels, forward(): pl.pallas_call(functools.partial(forward_body, first), out_shape=outs, gr...  11.6 us
    dot_general x3, matrix products, dot(): return lax.dot_general(a, b, dims, preferred_element_type=F32)  9.69 us
    pallas_call x1, Pallas kernels, query_grad(): pl.pallas_call(query_body, out_shape=jax.ShapeDtypeStruct((ROWS, HEAD), B...  8.66 us
  transfers between devices with their start and end apart: 23, of which 7 were waited for; matrix products, arithmetic and copies ran while one was open for 17% of the time, Pallas kernels for 18%

profile of v1, /device:TPU:1, one launch (start us, length us, event | category | flops | bytes accessed | tf_op | source)
XLA Modules:
  0.0 213.8 jit_solution(5501748126574328068)
XLA Ops:
  0.7 1.2 pad_maximum_fusion.1
  1.9 1.5 collective-permute-start
  3.4 1.3 collective-permute-done
  6.2 21.5 %all_to_all.30 = bf16[16,64,384]{2,1,0:T(8,128)(2,1)S(1)} all-to-all(bf16[16,64,384]{2,1,0:T(8,128)(2,1)S(1)} %reshape.161), channel_id=1, replica_groups=mesh['z'=4,'y'=4,'xl'=2,'xh'=2,'core'=2] {'z','y'}, dimensions={0} | all-to-all | bytes 1572864 | tf_op jit(solution)/shard_map/all_to_all | solution.py:276
  27.7 1.6 broadcast_in_dim.32
  29.3 7.1 %all-to-all-start.2 = ((bf16[64,8,2048]{2,1,0:T(8,128)(2,1)}), bf16[64,8,2048]{2,1,0:T(8,128)(2,1)}, u32[]{:S(2)}, u32[]{:S(2)}) async-start(bf16[64,8,2048]{2,1,0:T(8,128)(2,1)} %broadcast_in_dim.32), calls=%async_computation.2 | async-start | bytes 4194304 | tf_op jit(solution)/shard_map/all_to_all | solution.py:276
  36.4 1.0 collective-permute-start.1
  37.5 27.8 %all-to-all-done.2 = bf16[64,8,2048]{2,1,0:T(8,128)(2,1)} async-done(((bf16[64,8,2048]{2,1,0:T(8,128)(2,1)}), bf16[64,8,2048]{2,1,0:T(8,128)(2,1)}, u32[]{:S(2)}, u32[]{:S(2)}) %all-to-all-start.2) | async-done | bytes 2097184 | tf_op jit(solution)/shard_map/all_to_all | solution.py:276
  65.3 3.9 %collective-permute-start.4 = (bf16[64,8,2048]{2,1,0:T(8,128)(2,1)}, bf16[64,8,2048]{2,1,0:T(8,128)(2,1)}, u32[]{:S(2)}, u32[]{:S(2)}) collective-permute-start(bf16[64,8,2048]{2,1,0:T(8,128)(2,1)} %all-to-all-done.2), channel_id=1, source_target_pairs={{0,1},{1,0},{2,3},{3,2},{4,5},{5,4},{6,7},{7,6},{8,9},{9,8},{10,11... | collective-permute-start | bytes 6291464 | tf_op jit(solution)/shard_map/ppermute | solution.py:263
  70.6 1.7 collective-permute-start.2
  73.1 1.0 collective-permute-done.3.refs_2_.kv1
  74.1 5.5 %forward_a.1 = (f32[128,1024]{1,0:T(8,128)S(1)}, f32[1,1024]{1,0:T(1,128)S(1)}, f32[1,1024]{1,0:T(1,128)S(1)}) custom-call(bf16[1024,128]{1,0:T(8,128)(2,1)S(1)} %slice.16.refs_0_.q_ref.refs_2_, bf16[1024,256]{1,0:T(8,128)(2,1)S(1)} %slice.17.refs_1_.kv0.refs_0_, bf16[1024,256]{1,0:T(8,128)(2,1)S(1)} %collective-permute-done.3.refs_2_.kv1, ...), custom_call_target="tpu_custom_call" | custom-call | flops 2147483648 | bytes 4194304 | tf_op jit(solution)/shard_map/forward_a/pallas_call | solution.py:117
  79.6 6.1 %forward_b.1 = (bf16[1024,128]{1,0:T(8,128)(2,1)}, f32[1,1024]{1,0:T(1,128)S(1)}) custom-call(bf16[1024,128]{1,0:T(8,128)(2,1)S(1)} %slice.16.refs_0_.q_ref.refs_2_, bf16[1024,256]{1,0:T(8,128)(2,1)S(1)} %collective-permute-done.1.refs_1_.kv2, bf16[1024,256]{1,0:T(8,128)(2,1)S(1)} %collective-permute-done.2.refs_2_.kv3, ...), custom_call_target="tpu_custom_call" | custom-call | flops 2147483648 | bytes 4194304 | tf_op jit(solution)/shard_map/forward_b/pallas_call | solution.py:117
  85.7 5.6 %all-to-all-start.1 = ((bf16[16,64,128]{2,1,0:T(8,128)(2,1)}), bf16[16,64,128]{2,1,0:T(8,128)(2,1)S(1)}, u32[]{:S(2)}, u32[]{:S(2)}) async-start(bf16[16,64,128]{2,1,0:T(8,128)(2,1)} %bitcast.7), calls=%async_computation.1 | async-start | bytes 524288 | tf_op jit(solution)/shard_map/all_to_all | solution.py:276
  91.3 1.1 fusion.20
  92.4 0.8 pad_maximum_fusion.5
  93.8 5.7 %all-to-all-done.1 = bf16[16,64,128]{2,1,0:T(8,128)(2,1)S(1)} async-done(((bf16[16,64,128]{2,1,0:T(8,128)(2,1)}), bf16[16,64,128]{2,1,0:T(8,128)(2,1)S(1)}, u32[]{:S(2)}, u32[]{:S(2)}) %all-to-all-start.1) | async-done | bytes 262176 | tf_op jit(solution)/shard_map/all_to_all | solution.py:276
  99.7 4.4 %convolution_convert_fusion = bf16[1024,2048]{1,0:T(8,128)(2,1)} fusion(bf16[128,2048]{1,0:T(8,128)(2,1)} %bitcast.126, bf16[16,8,8,128]{3,2,1,0:T(8,128)(2,1)S(1)} %bitcast.129), kind=kOutput, calls=%fused_computation.4 | convolution fusion | flops 538968064 | bytes 4980736 | tf_op jit(solution)/shard_map/dot_general | solution.py:26
  104.1 2.5 %select_bitcast_fusion.1 = (bf16[1,64,8,2048]{3,2,0,1:T(8,128)(2,1)S(1)}, bf16[1,64,8,2048]{3,2,0,1:T(8,128)(2,1)S(1)}) fusion(bf16[64,8,2048]{2,1,0:T(8,128)(2,1)} %all-to-all-done.2, bf16[64,8,2048]{2,1,0:T(8,128)(2,1)} %collective-permute-done.4, pred[]{:T(512)S(6)} %eq.41), kind=kLoop, calls=%fused_computation.8 | loop fusion | flops 2097152 | bytes 8388609 | tf_op jit(solution)/shard_map/stack | solution.py:280
  107.7 1.5 fusion.1
  109.3 0.8 copy.25
  110.0 3.5 %all-to-all-start.3 = ((bf16[16,64,128]{2,1,0:T(8,128)(2,1)}), bf16[16,64,128]{2,1,0:T(8,128)(2,1)S(1)}, u32[]{:S(2)}, u32[]{:S(2)}) async-start(bf16[16,64,128]{2,1,0:T(8,128)(2,1)} %bitcast.139), calls=%async_computation.3 | async-start | bytes 524288 | tf_op jit(solution)/shard_map/all_to_all | solution.py:276
  113.6 3.2 %dynamic-slice_bitcast_fusion = bf16[64,8,2048]{2,1,0:T(8,128)(2,1)} fusion(bf16[64,2,8,2048]{3,2,1,0:T(8,128)(2,1)} %bitcast.124, s32[]{:T(128)S(6)} %select_n.168), kind=kLoop, calls=%fused_computation.6 | loop fusion | bytes 4194308 | tf_op jit(solution)/shard_map/jit(dynamic_index_in_dim)/squeeze | solution.py:357
  116.8 1.4 collective-permute-start.17
  118.2 2.9 %all-to-all-done.3 = bf16[16,64,128]{2,1,0:T(8,128)(2,1)S(1)} async-done(((bf16[16,64,128]{2,1,0:T(8,128)(2,1)}), bf16[16,64,128]{2,1,0:T(8,128)(2,1)S(1)}, u32[]{:S(2)}, u32[]{:S(2)}) %all-to-all-start.3) | async-done | bytes 262176 | tf_op jit(solution)/shard_map/all_to_all | solution.py:276
  121.1 1.2 collective-permute-start.11
  122.3 1.8 delta.1.delta_ref
  124.8 0.8 collective-permute-start.14
  125.6 3.8 %convolution_convert_fusion.1 = bf16[128,2048]{1,0:T(8,128)(2,1)} fusion(bf16[1024,2048]{1,0:T(8,128)(2,1)} %bitcast.123, bf16[16,8,8,128]{3,2,1,0:T(8,128)(2,1)} %bitcast.130), kind=kOutput, calls=%fused_computation.5 | convolution fusion | flops 537133056 | bytes 4980736 | tf_op jit(solution)/shard_map/dot_general | solution.py:26
  129.4 2.8 %collective-permute-start.10 = (bf16[1024,128]{1,0:T(8,128)(2,1)S(1)}, bf16[1024,128]{1,0:T(8,128)(2,1)S(1)}, u32[]{:S(2)}, u32[]{:S(2)}) collective-permute-start(bf16[1024,128]{1,0:T(8,128)(2,1)S(1)} %bitcast.119), channel_id=1, source_target_pairs={{0,1},{1,0},{2,3},{3,2},{4,5},{5,4},{6,7},{7,6},{8,9},{9,8},{10,11... | collective-permute-start | bytes 786440 | tf_op jit(solution)/shard_map/ppermute | solution.py:263
  132.9 8.7 %query_grad.1 = bf16[1024,128]{1,0:T(8,128)(2,1)S(1)} custom-call(bf16[1024,128]{1,0:T(8,128)(2,1)S(1)} %slice.16.refs_0_.q_ref.refs_2_, bf16[1024,128]{1,0:T(8,128)(2,1)S(1)} %bitcast.120, f32[1,1024]{1,0:T(1,128)S(1)} %get-tuple-element.16.lse_ref, f32[1,1024]{1,0:T(1,128)S(1)} %copy-done.2, bf16[1024,256]{1,0:T(8,128)(2,1)S(1)} %slice.17.refs_1_.kv0.refs_0_, ...), custom_call_target="tpu_custom_call" | custom-call | flops 6442450944 | bytes 4194304 | tf_op jit(solution)/shard_map/query_grad/pallas_call | solution.py:183
  141.6 15.7 %key_grad.1 = (bf16[1024,128]{1,0:T(8,128)(2,1)S(1)}, bf16[1024,128]{1,0:T(8,128)(2,1)S(1)}) custom-call(bf16[1024,256]{1,0:T(8,128)(2,1)S(1)} %slice.17.refs_1_.kv0.refs_0_, f32[64,128]{1,0:T(8,128)S(1)} %pad.4.bias_ref.refs_1_, bf16[1024,128]{1,0:T(8,128)(2,1)S(1)} %slice.16.refs_0_.q_ref.refs_2_, bf16[1024,128]{1,0:T(8,128)(2,1)S(1)} %collective-permute-done.7.refs_3_, ...), custom_call_target="tpu_custom_call" | custom-call | flops 8589934592 | bytes 4194304 | tf_op jit(solution)/shard_map/key_grad/pallas_call | solution.py:240
  157.2 1.0 pad_maximum_fusion.2
  158.2 3.6 %all-to-all-start.4 = ((bf16[16,64,384]{2,1,0:T(8,128)(2,1)}), bf16[16,64,384]{2,1,0:T(8,128)(2,1)S(1)}, u32[]{:S(2)}, u32[]{:S(2)}) async-start(bf16[16,64,384]{2,1,0:T(8,128)(2,1)} %bitcast.31), calls=%async_computation.4 | async-start | bytes 1572864 | tf_op jit(solution)/shard_map/all_to_all | solution.py:276
  161.9 0.7 dynamic-slice_bitcast_fusion.4
  163.0 4.5 %fusion = bf16[64,8,2048]{2,1,0:T(8,128)(2,1)} fusion(bf16[64,8,2048]{2,1,0:T(8,128)(2,1)} %collective-permute-done.17, bf16[64,2,8,2048]{3,2,1,0:T(8,128)(2,1)} %bitcast.125, s32[]{:T(128)S(6)} %select_n.167), kind=kLoop, calls=%fused_computation.2 | loop fusion | flops 4194304 | bytes 6291460 | tf_op jit(solution)/shard_map/convert_element_type | solution.py:358
  167.5 8.1 %all-to-all-done.4 = bf16[16,64,384]{2,1,0:T(8,128)(2,1)S(1)} async-done(((bf16[16,64,384]{2,1,0:T(8,128)(2,1)}), bf16[16,64,384]{2,1,0:T(8,128)(2,1)S(1)}, u32[]{:S(2)}, u32[]{:S(2)}) %all-to-all-start.4) | async-done | bytes 786464 | tf_op jit(solution)/shard_map/all_to_all | solution.py:276
  175.6 0.9 copy-done.6
  176.5 7.1 %all-to-all-start.5 = ((bf16[64,8,2048]{2,1,0:T(8,128)(2,1)}), bf16[64,8,2048]{2,1,0:T(8,128)(2,1)S(1)}, u32[]{:S(2)}, u32[]{:S(2)}) async-start(bf16[64,8,2048]{2,1,0:T(8,128)(2,1)} %fusion), calls=%async_computation.5 | async-start | bytes 4194304 | tf_op jit(solution)/shard_map/all_to_all | solution.py:276
  183.6 2.4 %reshape.171 = bf16[2,8,64,3,128]{4,3,2,1,0:T(4,128)(2,1)S(1)} reshape(bf16[16,64,384]{2,1,0:T(8,128)(2,1)} %copy-done.6) | data formatting | bytes 1572864 | tf_op jit(solution)/shard_map/reshape | solution.py:305
  186.0 1.8 copy.26
  187.8 1.5 reshape.172
  189.3 1.1 collective-permute-start.16
  190.5 1.0 fusion.22
  191.5 0.8 pad_maximum_fusion.4
  192.4 0.9 slice_bitcast_fusion
  193.3 19.6 %all-to-all-done.5 = bf16[64,8,2048]{2,1,0:T(8,128)(2,1)S(1)} async-done(((bf16[64,8,2048]{2,1,0:T(8,128)(2,1)}), bf16[64,8,2048]{2,1,0:T(8,128)(2,1)S(1)}, u32[]{:S(2)}, u32[]{:S(2)}) %all-to-all-start.5) | async-done | bytes 2097184 | tf_op jit(solution)/shard_map/all_to_all | solution.py:276
  212.9 0.9 convert_reduce_fusion
  (72 shorter events, 7.5 us)
Async XLA Ops:
  1.9 2.9 %collective-permute-start = (bf16[64,3072]{1,0:T(8,128)(2,1)S(1)}, bf16[64,3072]{1,0:T(8,128)(2,1)S(1)}, u32[]{:S(2)}, u32[]{:S(2)}) collective-permute-start(bf16[64,3072]{1,0:T(8,128)(2,1)S(1)} %dynamic-slice_bitcast_fusion.2), channel_id=1, source_target_pairs={{0,1},{1,0},{2,3},{3,2},{4,5},{5,4},{6,7},{7,6},{8,9},{9,8},{10,11... | collective-permute-start | bytes 1179656 | tf_op jit(solution)/shard_map/ppermute | solution.py:263
  5.5 22.2 %copy-start.10 = (bf16[8,2048]{1,0:T(8,128)(2,1)S(1)}, bf16[8,2048]{1,0:T(8,128)(2,1)}, u32[]{:S(2)}) copy-start(bf16[8,2048]{1,0:T(8,128)(2,1)} %param.12) | copy-start | bytes 98308
  29.3 39.9 %copy-start.9 = (bf16[1,128,2048]{2,1,0:T(8,128)(2,1)S(1)}, bf16[1,128,2048]{2,1,0:T(8,128)(2,1)}, u32[]{:S(2)}) copy-start(bf16[1,128,2048]{2,1,0:T(8,128)(2,1)} %param.13) | copy-start | bytes 1572868
  29.3 41.1 %copy-start.12 = (s32[64]{0:T(128)S(1)}, s32[64]{0:T(128)}, u32[]{:S(2)}) copy-start(s32[64]{0:T(128)} %param.10) | copy-start | bytes 772
  29.3 43.0 %copy-start.11 = (s32[64,64]{1,0:T(8,128)S(1)}, s32[64,64]{1,0:T(8,128)}, u32[]{:S(2)}) copy-start(s32[64,64]{1,0:T(8,128)} %param.11) | copy-start | bytes 49156
  29.3 36.0 %all-to-all-start.2 = ((bf16[64,8,2048]{2,1,0:T(8,128)(2,1)}), bf16[64,8,2048]{2,1,0:T(8,128)(2,1)}, u32[]{:S(2)}, u32[]{:S(2)}) async-start(bf16[64,8,2048]{2,1,0:T(8,128)(2,1)} %broadcast_in_dim.32), calls=%async_computation.2 | async-start | bytes 4194304 | tf_op jit(solution)/shard_map/all_to_all | solution.py:276
  36.4 34.2 %collective-permute-start.1 = (bf16[1024,256]{1,0:T(8,128)(2,1)S(1)}, bf16[1024,256]{1,0:T(8,128)(2,1)S(1)}, u32[]{:S(2)}, u32[]{:S(2)}) collective-permute-start(bf16[1024,256]{1,0:T(8,128)(2,1)S(1)} %slice.17.refs_1_.kv0.refs_0_), channel_id=1, source_target_pairs={{0,4},{4,0},{1,5},{5,1},{2,6},{6,2},{3,7},{7,3},{8,12},{12,8},{9,1... | collective-permute-start | bytes 1572872 | tf_op jit(solution)/shard_map/ppermute | solution.py:267
  65.3 38.8 %collective-permute-start.4 = (bf16[64,8,2048]{2,1,0:T(8,128)(2,1)}, bf16[64,8,2048]{2,1,0:T(8,128)(2,1)}, u32[]{:S(2)}, u32[]{:S(2)}) collective-permute-start(bf16[64,8,2048]{2,1,0:T(8,128)(2,1)} %all-to-all-done.2), channel_id=1, source_target_pairs={{0,1},{1,0},{2,3},{3,2},{4,5},{5,4},{6,7},{7,6},{8,9},{9,8},{10,11... | collective-permute-start | bytes 6291464 | tf_op jit(solution)/shard_map/ppermute | solution.py:263
  69.9 21.4 %collective-permute-start.6 = (bf16[64,2048]{1,0:T(8,128)(2,1)}, bf16[64,2048]{1,0:T(8,128)(2,1)}, u32[]{:S(2)}, u32[]{:S(2)}) collective-permute-start(bf16[64,2048]{1,0:T(8,128)(2,1)} %dynamic-slice_bitcast_fusion.3), channel_id=1, source_target_pairs={{0,1},{1,0},{2,3},{3,2},{4,5},{5,4},{6,7},{7,6},{8,9},{9,8},{10,11... | collective-permute-start | bytes 786440 | tf_op jit(solution)/shard_map/ppermute | solution.py:263
  69.9 4.2 %collective-permute-start.3 = (bf16[1024,256]{1,0:T(8,128)(2,1)S(1)}, bf16[1024,256]{1,0:T(8,128)(2,1)S(1)}, u32[]{:S(2)}, u32[]{:S(2)}) collective-permute-start(bf16[1024,256]{1,0:T(8,128)(2,1)S(1)} %slice.17.refs_1_.kv0.refs_0_), channel_id=1, source_target_pairs={{0,1},{1,0},{2,3},{3,2},{4,5},{5,4},{6,7},{7,6},{8,9},{9,8},{10,11... | collective-permute-start | bytes 1572872 | tf_op jit(solution)/shard_map/ppermute | solution.py:263
  70.6 9.0 %collective-permute-start.2 = (bf16[1024,256]{1,0:T(8,128)(2,1)S(1)}, bf16[1024,256]{1,0:T(8,128)(2,1)S(1)}, u32[]{:S(2)}, u32[]{:S(2)}) collective-permute-start(bf16[1024,256]{1,0:T(8,128)(2,1)S(1)} %collective-permute-done.1.refs_1_.kv2), channel_id=1, source_target_pairs={{0,1},{1,0},{2,3},{3,2},{4,5},{5,4},{6,7},{7,6},{8,9},{9,8},{10,11... | collective-permute-start | bytes 1572872 | tf_op jit(solution)/shard_map/ppermute | solution.py:263
  72.7 21.1 %collective-permute-start.8 = (bf16[1024,128]{1,0:T(8,128)(2,1)S(1)}, bf16[1024,128]{1,0:T(8,128)(2,1)S(1)}, u32[]{:S(2)}, u32[]{:S(2)}) collective-permute-start(bf16[1024,128]{1,0:T(8,128)(2,1)S(1)} %slice.16.refs_0_.q_ref.refs_2_), channel_id=1, source_target_pairs={{0,4},{4,0},{1,5},{5,1},{2,6},{6,2},{3,7},{7,3},{8,12},{12,8},{9,1... | collective-permute-start | bytes 786440 | tf_op jit(solution)/shard_map/ppermute | solution.py:267
  85.7 13.9 %all-to-all-start.1 = ((bf16[16,64,128]{2,1,0:T(8,128)(2,1)}), bf16[16,64,128]{2,1,0:T(8,128)(2,1)S(1)}, u32[]{:S(2)}, u32[]{:S(2)}) async-start(bf16[16,64,128]{2,1,0:T(8,128)(2,1)} %bitcast.7), calls=%async_computation.1 | async-start | bytes 524288 | tf_op jit(solution)/shard_map/all_to_all | solution.py:276
  93.3 36.2 %collective-permute-start.7 = (bf16[1024,128]{1,0:T(8,128)(2,1)S(1)}, bf16[1024,128]{1,0:T(8,128)(2,1)S(1)}, u32[]{:S(2)}, u32[]{:S(2)}) collective-permute-start(bf16[1024,128]{1,0:T(8,128)(2,1)S(1)} %slice.16.refs_0_.q_ref.refs_2_), channel_id=1, source_target_pairs={{0,1},{1,0},{2,3},{3,2},{4,5},{5,4},{6,7},{7,6},{8,9},{9,8},{10,11... | collective-permute-start | bytes 786440 | tf_op jit(solution)/shard_map/ppermute | solution.py:263
  93.8 38.4 %collective-permute-start.9 = (bf16[1024,128]{1,0:T(8,128)(2,1)S(1)}, bf16[1024,128]{1,0:T(8,128)(2,1)S(1)}, u32[]{:S(2)}, u32[]{:S(2)}) collective-permute-start(bf16[1024,128]{1,0:T(8,128)(2,1)S(1)} %collective-permute-done.8.refs_4_), channel_id=1, source_target_pairs={{0,1},{1,0},{2,3},{3,2},{4,5},{5,4},{6,7},{7,6},{8,9},{9,8},{10,11... | collective-permute-start | bytes 786440 | tf_op jit(solution)/shard_map/ppermute | solution.py:263
  99.7 4.4 %copy-start.5 = (bf16[2,64,1,8,128]{4,3,1,0,2:T(8,128)(2,1)}, bf16[2,64,1,8,128]{4,3,1,0,2:T(8,128)(2,1)S(1)}, u32[]{:S(2)}) copy-start(bf16[2,64,1,8,128]{4,3,1,0,2:T(8,128)(2,1)S(1)} %copy.23) | copy-start | bytes 786436
  106.6 1.0 copy-start.4
  107.0 2.1 %copy-start.3 = (bf16[2,64,8,2048]{3,2,0,1:T(8,128)(2,1)}, bf16[2,64,8,2048]{3,2,0,1:T(8,128)(2,1)S(1)}, u32[]{:S(2)}) copy-start(bf16[2,64,8,2048]{3,2,0,1:T(8,128)(2,1)S(1)} %pad_maximum_fusion) | copy-start | bytes 12582916
  110.0 11.1 %all-to-all-start.3 = ((bf16[16,64,128]{2,1,0:T(8,128)(2,1)}), bf16[16,64,128]{2,1,0:T(8,128)(2,1)S(1)}, u32[]{:S(2)}, u32[]{:S(2)}) async-start(bf16[16,64,128]{2,1,0:T(8,128)(2,1)} %bitcast.139), calls=%async_computation.3 | async-start | bytes 524288 | tf_op jit(solution)/shard_map/all_to_all | solution.py:276
  116.8 46.2 %collective-permute-start.17 = (bf16[64,8,2048]{2,1,0:T(8,128)(2,1)}, bf16[64,8,2048]{2,1,0:T(8,128)(2,1)}, u32[]{:S(2)}, u32[]{:S(2)}) collective-permute-start(bf16[64,8,2048]{2,1,0:T(8,128)(2,1)} %dynamic-slice_bitcast_fusion), channel_id=1, source_target_pairs={{0,1},{1,0},{2,3},{3,2},{4,5},{5,4},{6,7},{7,6},{8,9},{9,8},{10,11... | collective-permute-start | bytes 6291464 | tf_op jit(solution)/shard_map/ppermute | solution.py:263
  121.1 1.2 copy-start
  121.1 11.6 %collective-permute-start.11 = (bf16[1024,128]{1,0:T(8,128)(2,1)S(1)}, bf16[1024,128]{1,0:T(8,128)(2,1)}, u32[]{:S(2)}, u32[]{:S(2)}) collective-permute-start(bf16[1024,128]{1,0:T(8,128)(2,1)S(1)} %bitcast.117), channel_id=1, source_target_pairs={{0,4},{4,0},{1,5},{5,1},{2,6},{6,2},{3,7},{7,3},{8,12},{12,8},{9,1... | collective-permute-start | bytes 786440 | tf_op jit(solution)/shard_map/ppermute | solution.py:267
  124.8 4.6 %copy-start.1 = (bf16[16,64,128]{2,1,0:T(8,128)(2,1)S(1)}, bf16[16,64,128]{2,1,0:T(8,128)(2,1)}, u32[]{:S(2)}) copy-start(bf16[16,64,128]{2,1,0:T(8,128)(2,1)} %copy-done) | copy-start | bytes 786436
  124.8 8.0 %copy-start.2 = (f32[1,1024]{1,0:T(1,128)S(1)}, f32[1,1024]{1,0:T(1,128)}, u32[]{:S(2)}) copy-start(f32[1,1024]{1,0:T(1,128)} %delta.1.delta_ref) | copy-start | bytes 12292
  124.8 7.5 %collective-permute-start.14 = (f32[2,1024]{1,0:T(2,128)S(1)}, f32[2,1024]{1,0:T(2,128)S(1)}, u32[]{:S(2)}, u32[]{:S(2)}) collective-permute-start(f32[2,1024]{1,0:T(2,128)S(1)} %pad_maximum_fusion.6.refs_10_), channel_id=1, source_target_pairs={{0,4},{4,0},{1,5},{5,1},{2,6},{6,2},{3,7},{7,3},{8,12},{12,8},{9,1... | collective-permute-start | bytes 24584 | tf_op jit(solution)/shard_map/ppermute | solution.py:267
  129.4 12.1 %collective-permute-start.10 = (bf16[1024,128]{1,0:T(8,128)(2,1)S(1)}, bf16[1024,128]{1,0:T(8,128)(2,1)S(1)}, u32[]{:S(2)}, u32[]{:S(2)}) collective-permute-start(bf16[1024,128]{1,0:T(8,128)(2,1)S(1)} %bitcast.119), channel_id=1, source_target_pairs={{0,1},{1,0},{2,3},{3,2},{4,5},{5,4},{6,7},{7,6},{8,9},{9,8},{10,11... | collective-permute-start | bytes 786440 | tf_op jit(solution)/shard_map/ppermute | solution.py:263
  132.2 9.3 %collective-permute-start.13 = (f32[2,1024]{1,0:T(2,128)S(1)}, f32[2,1024]{1,0:T(2,128)S(1)}, u32[]{:S(2)}, u32[]{:S(2)}) collective-permute-start(f32[2,1024]{1,0:T(2,128)S(1)} %pad_maximum_fusion.6.refs_10_), channel_id=1, source_target_pairs={{0,1},{1,0},{2,3},{3,2},{4,5},{5,4},{6,7},{7,6},{8,9},{9,8},{10,11... | collective-permute-start | bytes 24584 | tf_op jit(solution)/shard_map/ppermute | solution.py:263
  132.3 9.2 %collective-permute-start.15 = (f32[2,1024]{1,0:T(2,128)S(1)}, f32[2,1024]{1,0:T(2,128)S(1)}, u32[]{:S(2)}, u32[]{:S(2)}) collective-permute-start(f32[2,1024]{1,0:T(2,128)S(1)} %collective-permute-done.14.refs_12_), channel_id=1, source_target_pairs={{0,1},{1,0},{2,3},{3,2},{4,5},{5,4},{6,7},{7,6},{8,9},{9,8},{10,11... | collective-permute-start | bytes 24584 | tf_op jit(solution)/shard_map/ppermute | solution.py:263
  132.8 8.8 %collective-permute-start.12 = (bf16[1024,128]{1,0:T(8,128)(2,1)}, bf16[1024,128]{1,0:T(8,128)(2,1)S(1)}, u32[]{:S(2)}, u32[]{:S(2)}) collective-permute-start(bf16[1024,128]{1,0:T(8,128)(2,1)} %collective-permute-done.11.refs_8_), channel_id=1, source_target_pairs={{0,1},{1,0},{2,3},{3,2},{4,5},{5,4},{6,7},{7,6},{8,9},{9,8},{10,11... | collective-permute-start | bytes 786440 | tf_op jit(solution)/shard_map/ppermute | solution.py:263
  157.2 4.6 %copy-start.7 = (bf16[128,2048]{1,0:T(8,128)(2,1)S(1)}, bf16[128,2048]{1,0:T(8,128)(2,1)}, u32[]{:S(2)}) copy-start(bf16[128,2048]{1,0:T(8,128)(2,1)} %convolution_convert_fusion.1) | copy-start | bytes 1572868
  158.2 17.3 %all-to-all-start.4 = ((bf16[16,64,384]{2,1,0:T(8,128)(2,1)}), bf16[16,64,384]{2,1,0:T(8,128)(2,1)S(1)}, u32[]{:S(2)}, u32[]{:S(2)}) async-start(bf16[16,64,384]{2,1,0:T(8,128)(2,1)} %bitcast.31), calls=%async_computation.4 | async-start | bytes 1572864 | tf_op jit(solution)/shard_map/all_to_all | solution.py:276
  162.6 27.9 %collective-permute-start.5 = (bf16[64,2048]{1,0:T(8,128)(2,1)}, bf16[64,2048]{1,0:T(8,128)(2,1)}, u32[]{:S(2)}, u32[]{:S(2)}) collective-permute-start(bf16[64,2048]{1,0:T(8,128)(2,1)} %dynamic-slice_bitcast_fusion.4), channel_id=1, source_target_pairs={{0,1},{1,0},{2,3},{3,2},{4,5},{5,4},{6,7},{7,6},{8,9},{9,8},{10,11... | collective-permute-start | bytes 786440 | tf_op jit(solution)/shard_map/ppermute | solution.py:263
  175.6 0.9 copy-start.6
  176.5 36.4 %all-to-all-start.5 = ((bf16[64,8,2048]{2,1,0:T(8,128)(2,1)}), bf16[64,8,2048]{2,1,0:T(8,128)(2,1)S(1)}, u32[]{:S(2)}, u32[]{:S(2)}) async-start(bf16[64,8,2048]{2,1,0:T(8,128)(2,1)} %fusion), calls=%async_computation.5 | async-start | bytes 4194304 | tf_op jit(solution)/shard_map/all_to_all | solution.py:276
  187.8 2.7 %copy-start.8 = (bf16[128,2048]{1,0:T(8,128)(2,1)S(1)}, bf16[128,2048]{1,0:T(8,128)(2,1)}, u32[]{:S(2)}) copy-start(bf16[128,2048]{1,0:T(8,128)(2,1)} %convolution_convert_fusion.1) | copy-start | bytes 1572868
  189.3 3.0 %collective-permute-start.16 = (bf16[64,3072]{1,0:T(8,128)(2,1)S(1)}, bf16[64,3072]{1,0:T(8,128)(2,1)S(1)}, u32[]{:S(2)}, u32[]{:S(2)}) collective-permute-start(bf16[64,3072]{1,0:T(8,128)(2,1)S(1)} %dynamic-slice_bitcast_fusion.1), channel_id=1, source_target_pairs={{0,1},{1,0},{2,3},{3,2},{4,5},{5,4},{6,7},{7,6},{8,9},{9,8},{10,11... | collective-permute-start | bytes 1179656 | tf_op jit(solution)/shard_map/ppermute | solution.py:263

commit v2 on v1

--- a/solution.py
+++ b/solution.py
@@ -306,10 +306,45 @@
     return split.transpose(0, 2, 3, 1, 4).reshape(2, SPAN, kinds * HEADS * HEAD)
 
 
+def side_by_side(first, own, peer):
+    return jnp.concatenate([jnp.where(first, own, peer), jnp.where(first, peer, own)], axis=-1)
+
+
+def from_chips(x):
+    place = 2 * lax.axis_index("xl") + lax.axis_index("xh")
+    held = [x] + [
+        lax.ppermute(x, ("xl", "xh"), [(k, k ^ step) for k in range(4)]) for step in (1, 2, 3)
+    ]
+    low, high = place % 2 == 1, place >= 2
+    pairs = [
+        (jnp.where(low, held[k + 1], held[k]), jnp.where(low, held[k], held[k + 1])) for k in (0, 2)
+    ]
+    front = [jnp.where(high, pairs[1][k], pairs[0][k]) for k in (0, 1)]
+    back = [jnp.where(high, pairs[0][k], pairs[1][k]) for k in (0, 1)]
+    return jnp.stack(front + back, axis=1)
+
+
+def sum_to_chips(x):
+    place = 2 * lax.axis_index("xl") + lax.axis_index("xh")
+    total = lax.dynamic_index_in_dim(x, place, 1, False).astype(F32)
+    for step in (1, 2, 3):
+        part = lax.dynamic_index_in_dim(x, place ^ step, 1, False)
+        sent = lax.ppermute(part, ("xl", "xh"), [(k, k ^ step) for k in range(4)])
+        total = total + sent.astype(F32)
+    return total.astype(x.dtype)
+
+
 def local(query_states, key_states, value_states, span_order, block_mask, output_weight, upstream):
     z, y, xl, core = (lax.axis_index(a) for a in ("z", "y", "xl", "core"))
     first_core = core == 0
     half = core ^ ((z + y) % 2)
+    cols = output_weight.shape[1] // 2
+
+    def mine(x, axis):
+        return lax.dynamic_index_in_dim(x, core, axis, False)
+
+    def theirs(x, axis):
+        return lax.dynamic_index_in_dim(x, 1 - core, axis, False)
 
     def share(rows):
         halves = rows.reshape(2, SPAN, -1)
@@ -318,49 +353,61 @@
         return in_order(first_core, own, peer)
 
     def unshare(both):
-        own = lax.dynamic_index_in_dim(both, core, 0, False)
-        peer = other_core(lax.dynamic_index_in_dim(both, 1 - core, 0, False))
+        own = mine(both, 0)
+        peer = other_core(theirs(both, 0))
         return in_order(half == 0, own, peer).reshape(2 * SPAN, -1)
 
+    weight_cols = output_weight.reshape(-1, 2, cols)
+    weight_rows = in_order(first_core, mine(weight_cols, 1), other_core(theirs(weight_cols, 1)))
+    weight_rows = weight_rows.reshape(-1, cols)
+    copies = jnp.broadcast_to(weight_rows[None], (UNITS, *weight_rows.shape))
     states = share(jnp.concatenate([query_states[0], key_states[0], value_states[0]], axis=1))
-    up = share(upstream[0]).reshape(2 * SPAN, -1)
+    weight_rows = exchange(copies, ZY)
+    sent, weight_rows = lax.optimization_barrier((by_unit(states, 3), weight_rows))
+    weight = from_chips(weight_rows)
+    blocks = exchange(sent, ZY).reshape(ROWS, 3 * HEAD)
     bias = span_bias(span_order, block_mask, xl, core)
 
-    blocks = exchange(by_unit(states, 3), ZY).reshape(ROWS, 3 * HEAD)
+    up_cols = upstream[0].reshape(2 * SPAN, 2, cols)
+    up = in_order(first_core, mine(up_cols, 1), other_core(theirs(up_cols, 1)))
+    up = up.reshape(2, 2, SPAN, cols)
+    up = in_order(half == 0, up[:, 0], up[:, 1]).reshape(4 * SPAN, cols)
+
     q = blocks[:, :HEAD]
     kvs = everyone(blocks[:, HEAD:])
-
-    copies = jnp.broadcast_to(output_weight[None], (64, *output_weight.shape))
-    weight_own = exchange(copies, CHIPS)
-    weight_peer = other_core(weight_own)
-    weight = in_order(first_core, weight_own, weight_peer).transpose(1, 0, 2, 3)
-    weight = weight.reshape(HEADS * HEAD, -1)
-
     partial = forward(True, q, kvs[0], kvs[1], bias[: 2 * UNITS])
-    attended, lse = forward(False, q, kvs[2], kvs[3], bias[2 * UNITS :], *partial)
-
-    grad_rows = dot(up, weight, NT).astype(BF16).reshape(2, SPAN, -1)
+
+    weight = weight.reshape(HEADS * HEAD, cols)
+    grad_rows = dot(up, weight, NT)
+    grad_rows = grad_rows[: 2 * SPAN] + other_core(grad_rows[2 * SPAN :])
+    grad_rows = grad_rows.astype(BF16).reshape(2, SPAN, -1)
     g = exchange(by_unit(grad_rows, 1), ZY).reshape(ROWS, HEAD)
     gs = everyone(g)
     qs = everyone(q)
-    attended_rows = by_row(exchange(attended.reshape(UNITS, SPAN, HEAD), ZY), 1)
-    attended_rows = attended_rows.reshape(2 * SPAN, -1)
+
+    attended, lse = forward(False, q, kvs[2], kvs[3], bias[2 * UNITS :], *partial)
+    attended, g = lax.optimization_barrier((attended, g))
     delta = row_delta(g, attended)
     stats = everyone(jnp.concatenate([lse, delta], axis=0))
-
     query_out = query_grad(q, g, lse, delta, kvs, bias)
 
-    projected = dot(attended_rows, weight, NN).astype(BF16).reshape(2, SPAN, -1)
-    projected = unshare(projected)
-    term = dot(attended_rows, up, TN).astype(BF16).reshape(64, 2, 8, -1)
-    term_own = lax.dynamic_index_in_dim(term, core, 1, False)
-    term_peer = other_core(lax.dynamic_index_in_dim(term, 1 - core, 1, False))
-    pair = (term_own.astype(F32) + term_peer.astype(F32)).astype(BF16)
-    weight_gradient = jnp.sum(exchange(pair, CHIPS).astype(F32), axis=0)
-
-    key_out, value_out = key_grad(kvs[0], bias, qs, gs, stats)
+    attended_rows = by_row(exchange(attended.reshape(UNITS, SPAN, HEAD), ZY), 1)
+    attended_rows = jnp.stack([attended_rows, other_core(attended_rows)]).reshape(4 * SPAN, -1)
+    term = dot(attended_rows, up, TN).astype(BF16).reshape(UNITS, 4, 16, cols)
+    term, key_side = lax.optimization_barrier((term, kvs[0]))
+    term = sum_to_chips(term)
+    projected = dot(attended_rows, weight, NN).astype(BF16).reshape(2, 2, SPAN, cols)
+    own, peer = mine(projected, 1), other_core(theirs(projected, 1))
+    own = in_order(half == 0, own[0], own[1]).reshape(2 * SPAN, cols)
+    peer = in_order(half == 0, peer[1], peer[0]).reshape(2 * SPAN, cols)
+    projected = side_by_side(first_core, own, peer)
+
+    key_out, value_out = key_grad(key_side, bias, qs, gs, stats)
     grads = jnp.concatenate([query_out, key_out, value_out], axis=1).reshape(UNITS, SPAN, -1)
-    grads = unshare(by_row(exchange(grads, ZY), 3))
+    grads, term = lax.optimization_barrier((exchange(grads, ZY), term))
+    summed = jnp.sum(exchange(term, ZY).astype(F32), axis=0).reshape(2, -1, cols)
+    weight_gradient = side_by_side(first_core, mine(summed, 0), other_core(theirs(summed, 0)))
+    grads = unshare(by_row(grads, 3))
     query_gradient, key_gradient, value_gradient = jnp.split(grads, 3, axis=1)
     return (
         projected[None],

time: 215 us -> 203 us (0.944)
  blocking collectives: 21.5 us -> 0 us
  starting transfers between devices: 44.9 us -> 60.4 us
  matrix products: 10 us -> 5.01 us
  local copies, waits for them, and re-layouts: 16.9 us -> 20.4 us
  other arithmetic: 15.4 us -> 12 us
  waiting for transfers between devices: 66.4 us -> 64.2 us
    all_to_all x5 -> x6, waiting for transfers between devices: 64.1 us -> 22.2 us  [exchange(): return lax.all_to_all(x, axes, 0, 0, tiled=True)]
    ppermute x0 -> x6, waiting for transfers between devices: none -> 36.7 us  [the longest x3 20.5 us: sum_to_chips(): sent = lax.ppermute(part, ('xl', 'xh'), [(k, k ^ step) for k in range(4)])]
    all_to_all x1 -> x0, blocking collectives: 21.5 us -> none  [exchange(): return lax.all_to_all(x, axes, 0, 0, tiled=True)]
    ppermute x0 -> x6, starting transfers between devices: none -> 7.8 us  [the longest x3 3.94 us: sum_to_chips(): sent = lax.ppermute(part, ('xl', 'xh'), [(k, k ^ step) for k in range(4)])]
    another operation x8 -> x4, other arithmetic: 6.78 us -> 0.2 us  [in_order(): return jnp.stack([jnp.where(first, own, peer), jnp.where(first, peer, own)])]
    all_to_all x5 -> x6, starting transfers between devices: 27 us -> 32.7 us  [exchange(): return lax.all_to_all(x, axes, 0, 0, tiled=True)]
    ppermute x4, waiting for transfers between devices: 0.01 us -> 5.33 us  [other_chip(): return lax.ppermute(x, 'xl', SWAP)]
    dot_general x3, matrix products: 9.69 us -> 4.7 us  [dot(): return lax.dot_general(a, b, dims, preferred_element_type=F32)]
  transfers between devices with their start and end apart: 23 -> 32, of which waited for: 7 -> 11; matrix products, arithmetic and copies ran while one was open for 17% -> 15% of each run, Pallas kernels for 18% -> 11%
where the time goes in v2:
time: 203 us; the launch traced here: 201 us
  waiting for transfers between devices  64.2 us (32%)
  starting transfers between devices  60.4 us (30%)
  Pallas kernels  38 us (19%)
  local copies, waits for them, and re-layouts  20.4 us (10%)
  other arithmetic  12 us (6%)
  matrix products  5.01 us (2%)
    all_to_all x6, starting transfers between devices, exchange(): return lax.all_to_all(x, axes, 0, 0, tiled=True)  32.7 us
    all_to_all x6, waiting for transfers between devices, exchange(): return lax.all_to_all(x, axes, 0, 0, tiled=True)  22.2 us
    ppermute x3, waiting for transfers between devices, sum_to_chips(): sent = lax.ppermute(part, ('xl', 'xh'), [(k, k ^ step) for k in range(4)])  20.5 us
    ppermute x16, starting transfers between devices, other_core(): return lax.ppermute(x, 'core', SWAP)  19.3 us
    ppermute x3, waiting for transfers between devices, from_chips(): lax.ppermute(x, ('xl', 'xh'), [(k, k ^ step) for k in range(4)])  16.2 us
    pallas_call x1, Pallas kernels, key_grad(): pl.pallas_call(key_body, out_shape=[jax.ShapeDtypeStruct((ROWS, HEAD), BF...  15.9 us
    pallas_call x2, Pallas kernels, forward(): pl.pallas_call(functools.partial(forward_body, first), out_shape=outs, gr...  11.6 us
    pallas_call x1, Pallas kernels, query_grad(): pl.pallas_call(query_body, out_shape=jax.ShapeDtypeStruct((ROWS, HEAD), B...  8.63 us
  transfers between devices with their start and end apart: 32, of which 11 were waited for; matrix products, arithmetic and copies ran while one was open for 15% of the time, Pallas kernels for 11%

profile of v2, /device:TPU:1, one launch (start us, length us, event | category | flops | bytes accessed | tf_op | source)
XLA Modules:
  0.0 201.3 jit_solution(14516574421126463702)
XLA Ops:
  1.4 1.4 collective-permute-start.1
  2.9 1.2 pad_maximum_fusion.1
  5.4 7.9 %all-to-all-start = ((bf16[16,16,1024]{2,1,0:T(8,128)(2,1)}), bf16[16,16,1024]{2,1,0:T(8,128)(2,1)S(1)}, u32[]{:S(2)}, u32[]{:S(2)}) async-start(bf16[16,16,1024]{2,1,0:T(8,128)(2,1)} %broadcast_in_dim.35), calls=%async_computation | async-start | bytes 1048576 | tf_op jit(solution)/shard_map/all_to_all | solution.py:276
  15.7 1.5 reshape.264
  17.1 6.7 %all-to-all-done = bf16[16,16,1024]{2,1,0:T(8,128)(2,1)S(1)} async-done(((bf16[16,16,1024]{2,1,0:T(8,128)(2,1)}), bf16[16,16,1024]{2,1,0:T(8,128)(2,1)S(1)}, u32[]{:S(2)}, u32[]{:S(2)}) %all-to-all-start) | async-done | bytes 524320 | tf_op jit(solution)/shard_map/all_to_all | solution.py:276
  23.8 2.5 %collective-permute-start.6 = (bf16[16,16,1024]{2,1,0:T(8,128)(2,1)S(1)}, bf16[16,16,1024]{2,1,0:T(8,128)(2,1)S(1)}, u32[]{:S(2)}, u32[]{:S(2)}) collective-permute-start(bf16[16,16,1024]{2,1,0:T(8,128)(2,1)S(1)} %all-to-all-done), channel_id=1, source_target_pairs={{0,6},{2,4},{4,2},{6,0},{1,7},{3,5},{5,3},{7,1},{8,14},{10,12},{12... | collective-permute-start | bytes 1572872 | tf_op jit(solution)/shard_map/ppermute | solution.py:316
  26.3 1.4 collective-permute-start.8
  27.8 1.0 bitcast_select_fusion.5
  29.0 3.6 %all-to-all-start.1 = ((bf16[16,64,384]{2,1,0:T(8,128)(2,1)}), bf16[16,64,384]{2,1,0:T(8,128)(2,1)S(1)}, u32[]{:S(2)}, u32[]{:S(2)}) async-start(bf16[16,64,384]{2,1,0:T(8,128)(2,1)} %reshape.264), calls=%async_computation.1 | async-start | bytes 1572864 | tf_op jit(solution)/shard_map/all_to_all | solution.py:276
  32.6 3.9 %collective-permute-done.6 = bf16[16,16,1024]{2,1,0:T(8,128)(2,1)S(1)} collective-permute-done((bf16[16,16,1024]{2,1,0:T(8,128)(2,1)S(1)}, bf16[16,16,1024]{2,1,0:T(8,128)(2,1)S(1)}, u32[]{:S(2)}, u32[]{:S(2)}) %collective-permute-start.6) | collective-permute-done | bytes 524320 | tf_op jit(solution)/shard_map/ppermute | solution.py:316
  36.5 1.0 collective-permute-done.7
  37.5 11.2 %collective-permute-done.8 = bf16[16,16,1024]{2,1,0:T(8,128)(2,1)} collective-permute-done((bf16[16,16,1024]{2,1,0:T(8,128)(2,1)S(1)}, bf16[16,16,1024]{2,1,0:T(8,128)(2,1)}, u32[]{:S(2)}, u32[]{:S(2)}) %collective-permute-start.8) | collective-permute-done | bytes 524320 | tf_op jit(solution)/shard_map/ppermute | solution.py:316
  48.8 1.2 select_bitcast_fusion.3
  50.3 1.3 copy-done.6
  52.5 1.0 slice.55
  53.5 3.3 %collective-permute-start.9 = (f32[128,1024]{1,0:T(8,128)}, f32[128,1024]{1,0:T(8,128)S(1)}, u32[]{:S(2)}, u32[]{:S(2)}) collective-permute-start(f32[128,1024]{1,0:T(8,128)} %slice.55), channel_id=1, source_target_pairs={{0,1},{1,0},{2,3},{3,2},{4,5},{5,4},{6,7},{7,6},{8,9},{9,8},{10,11... | collective-permute-start | bytes 1572872 | tf_op jit(solution)/shard_map/ppermute | solution.py:263
  57.5 5.3 %collective-permute-done.2.refs_1_.kv2 = bf16[1024,256]{1,0:T(8,128)(2,1)S(1)} collective-permute-done((bf16[1024,256]{1,0:T(8,128)(2,1)S(1)}, bf16[1024,256]{1,0:T(8,128)(2,1)S(1)}, u32[]{:S(2)}, u32[]{:S(2)}) %collective-permute-start.2) | collective-permute-done | bytes 524320 | tf_op jit(solution)/shard_map/ppermute | solution.py:267
  62.8 4.0 %collective-permute-start.3 = (bf16[1024,256]{1,0:T(8,128)(2,1)S(1)}, bf16[1024,256]{1,0:T(8,128)(2,1)S(1)}, u32[]{:S(2)}, u32[]{:S(2)}) collective-permute-start(bf16[1024,256]{1,0:T(8,128)(2,1)S(1)} %collective-permute-done.2.refs_1_.kv2), channel_id=1, source_target_pairs={{0,1},{1,0},{2,3},{3,2},{4,5},{5,4},{6,7},{7,6},{8,9},{9,8},{10,11... | collective-permute-start | bytes 1572872 | tf_op jit(solution)/shard_map/ppermute | solution.py:263
  66.8 1.1 fusion.21
  68.8 4.1 %all-to-all-start.2 = ((bf16[16,64,128]{2,1,0:T(8,128)(2,1)}), bf16[16,64,128]{2,1,0:T(8,128)(2,1)S(1)}, u32[]{:S(2)}, u32[]{:S(2)}) async-start(bf16[16,64,128]{2,1,0:T(8,128)(2,1)} %bitcast.30), calls=%async_computation.2 | async-start | bytes 524288 | tf_op jit(solution)/shard_map/all_to_all | solution.py:276
  72.9 1.0 slice.50.refs_0_.q_ref.refs_2_
  74.0 5.5 %forward_a.1 = (f32[128,1024]{1,0:T(8,128)S(1)}, f32[1,1024]{1,0:T(1,128)S(1)}, f32[1,1024]{1,0:T(1,128)S(1)}) custom-call(bf16[1024,128]{1,0:T(8,128)(2,1)S(1)} %slice.50.refs_0_.q_ref.refs_2_, bf16[1024,256]{1,0:T(8,128)(2,1)S(1)} %slice.51.refs_1_.kv0.refs_0_, bf16[1024,256]{1,0:T(8,128)(2,1)S(1)} %collective-permute-done.4.refs_2_.kv1, ...), custom_call_target="tpu_custom_call" | custom-call | flops 2147483648 | bytes 4194304 | tf_op jit(solution)/shard_map/forward_a/pallas_call | solution.py:117
  80.3 1.1 all-to-all-done.2
  81.7 1.0 copy-done.5
  82.8 6.1 %forward_b.1 = (bf16[1024,128]{1,0:T(8,128)(2,1)}, f32[1,1024]{1,0:T(1,128)S(1)}) custom-call(bf16[1024,128]{1,0:T(8,128)(2,1)S(1)} %slice.50.refs_0_.q_ref.refs_2_, bf16[1024,256]{1,0:T(8,128)(2,1)S(1)} %collective-permute-done.2.refs_1_.kv2, bf16[1024,256]{1,0:T(8,128)(2,1)S(1)} %collective-permute-done.3.refs_2_.kv3, ...), custom_call_target="tpu_custom_call" | custom-call | flops 2147483648 | bytes 4194304 | tf_op jit(solution)/shard_map/forward_b/pallas_call | solution.py:117
  88.9 6.7 %all-to-all-start.3 = ((bf16[16,64,128]{2,1,0:T(8,128)(2,1)}), bf16[16,64,128]{2,1,0:T(8,128)(2,1)S(1)}, u32[]{:S(2)}, u32[]{:S(2)}) async-start(bf16[16,64,128]{2,1,0:T(8,128)(2,1)} %bitcast.32), calls=%async_computation.3 | async-start | bytes 524288 | tf_op jit(solution)/shard_map/all_to_all | solution.py:276
  95.6 1.5 collective-permute-start.12
  97.8 1.8 delta.1.delta_ref
  99.7 3.5 %all-to-all-done.3 = bf16[16,64,128]{2,1,0:T(8,128)(2,1)S(1)} async-done(((bf16[16,64,128]{2,1,0:T(8,128)(2,1)}), bf16[16,64,128]{2,1,0:T(8,128)(2,1)S(1)}, u32[]{:S(2)}, u32[]{:S(2)}) %all-to-all-start.3) | async-done | bytes 262176 | tf_op jit(solution)/shard_map/all_to_all | solution.py:276
  103.8 1.1 copy.46
  105.8 2.5 %collective-permute-start.10 = (bf16[2,64,1024]{2,1,0:T(8,128)(2,1)}, bf16[2,64,1024]{2,1,0:T(8,128)(2,1)}, u32[]{:S(2)}, u32[]{:S(2)}) collective-permute-start(bf16[2,64,1024]{2,1,0:T(8,128)(2,1)} %reshape.273), channel_id=1, source_target_pairs={{0,1},{1,0},{2,3},{3,2},{4,5},{5,4},{6,7},{7,6},{8,9},{9,8},{10,11... | collective-permute-start | bytes 786440 | tf_op jit(solution)/shard_map/ppermute | solution.py:263
  109.9 8.6 %query_grad.1 = bf16[1024,128]{1,0:T(8,128)(2,1)S(1)} custom-call(bf16[1024,128]{1,0:T(8,128)(2,1)S(1)} %slice.50.refs_0_.q_ref.refs_2_, bf16[1024,128]{1,0:T(8,128)(2,1)S(1)} %bitcast.152, f32[1,1024]{1,0:T(1,128)S(1)} %get-tuple-element.28.lse_ref, f32[1,1024]{1,0:T(1,128)S(1)} %copy-done.3, bf16[1024,256]{1,0:T(8,128)(2,1)S(1)} %slice.51.refs_1_.kv0.refs_0_, ...), custom_call_target="tpu_custom_call" | custom-call | flops 6442450944 | bytes 4194304 | tf_op jit(solution)/shard_map/query_grad/pallas_call | solution.py:183
  118.6 1.1 stack_reshape.3
  119.7 3.2 %bitcast_convert_fusion = bf16[1024,1024]{1,0:T(8,128)(2,1)} fusion(bf16[1,2,64,1024]{3,2,1,0:T(8,128)(2,1)} %bitcast.35, bf16[1,2,64,1024]{3,2,1,0:T(8,128)(2,1)S(1)} %stack_reshape.3, bf16[1,2,64,1024]{3,2,1,0:T(8,128)(2,1)} %copy-done.13, bf16[1,2,64,1024]{3,2,1,0:T(8,128)(2,1)} %copy-done.12), kind=kOutput, calls=%fused_computation | convolution fusion | flops 538443776 | bytes 3145728 | tf_op jit(solution)/shard_map/dot_general | solution.py:26
  123.5 1.8 pad_maximum_fusion.5
  125.3 15.9 %key_grad.1 = (bf16[1024,128]{1,0:T(8,128)(2,1)S(1)}, bf16[1024,128]{1,0:T(8,128)(2,1)S(1)}) custom-call(bf16[1024,256]{1,0:T(8,128)(2,1)S(1)} %slice.51.refs_1_.kv0.refs_0_, f32[64,128]{1,0:T(8,128)S(1)} %pad.4.bias_ref.refs_1_, bf16[1024,128]{1,0:T(8,128)(2,1)S(1)} %slice.50.refs_0_.q_ref.refs_2_, bf16[1024,128]{1,0:T(8,128)(2,1)} %collective-permute-done.12.refs_3_, ...), custom_call_target="tpu_custom_call" | custom-call | flops 8589934592 | bytes 4194304 | tf_op jit(solution)/shard_map/key_grad/pallas_call | solution.py:240
  141.2 1.0 pad_maximum_fusion.2
  142.3 3.9 %all-to-all-start.4 = ((bf16[16,64,384]{2,1,0:T(8,128)(2,1)}), bf16[16,64,384]{2,1,0:T(8,128)(2,1)S(1)}, u32[]{:S(2)}, u32[]{:S(2)}) async-start(bf16[16,64,384]{2,1,0:T(8,128)(2,1)} %bitcast.159), calls=%async_computation.4 | async-start | bytes 1572864 | tf_op jit(solution)/shard_map/all_to_all | solution.py:276
  146.1 1.5 dynamic-slice_bitcast_fusion.2
  147.7 2.6 %collective-permute-start.23 = (bf16[16,16,1024]{2,1,0:T(8,128)(2,1)S(1)}, bf16[16,16,1024]{2,1,0:T(8,128)(2,1)S(1)}, u32[]{:S(2)}, u32[]{:S(2)}) collective-permute-start(bf16[16,16,1024]{2,1,0:T(8,128)(2,1)S(1)} %get-tuple-element.36), channel_id=1, source_target_pairs={{0,6},{2,4},{4,2},{6,0},{1,7},{3,5},{5,3},{7,1},{8,14},{10,12},{12... | collective-permute-start | bytes 1572872 | tf_op jit(solution)/shard_map/ppermute | solution.py:332
  152.4 1.4 collective-permute-start.11
  153.8 8.4 %collective-permute-done.23 = bf16[16,16,1024]{2,1,0:T(8,128)(2,1)S(1)} collective-permute-done((bf16[16,16,1024]{2,1,0:T(8,128)(2,1)S(1)}, bf16[16,16,1024]{2,1,0:T(8,128)(2,1)S(1)}, u32[]{:S(2)}, u32[]{:S(2)}) %collective-permute-start.23) | collective-permute-done | bytes 524320 | tf_op jit(solution)/shard_map/ppermute | solution.py:332
  163.2 11.1 %collective-permute-done.21 = bf16[16,16,1024]{2,1,0:T(8,128)(2,1)S(1)} collective-permute-done((bf16[16,16,1024]{2,1,0:T(8,128)(2,1)S(1)}, bf16[16,16,1024]{2,1,0:T(8,128)(2,1)S(1)}, u32[]{:S(2)}, u32[]{:S(2)}) %collective-permute-start.21) | collective-permute-done | bytes 524320 | tf_op jit(solution)/shard_map/ppermute | solution.py:332
  174.3 2.2 %fusion.14 = bf16[16,16,1024]{2,1,0:T(8,128)(2,1)} fusion(bf16[16,16,1024]{2,1,0:T(8,128)(2,1)S(1)} %collective-permute-done.23, bf16[16,16,1024]{2,1,0:T(8,128)(2,1)S(1)} %collective-permute-done.22, bf16[16,16,1024]{2,1,0:T(8,128)(2,1)S(1)} %collective-permute-done.21, bf16[16,4,16,1024]{3,2,1,0:T(8,128)(2,1)} %bitcast.166, s32[]{:T(128)S(6)} %select_n.352), kind=kLoop, calls=%fused_computation.11 | loop fusion | flops 2097152 | bytes 2621444 | tf_op jit(solution)/shard_map/convert_element_type | solution.py:334
  178.1 1.5 collective-permute-start.24
  180.5 6.6 %all-to-all-start.5 = ((bf16[16,16,1024]{2,1,0:T(8,128)(2,1)}), bf16[16,16,1024]{2,1,0:T(8,128)(2,1)S(1)}, u32[]{:S(2)}, u32[]{:S(2)}) async-start(bf16[16,16,1024]{2,1,0:T(8,128)(2,1)} %fusion.14), calls=%async_computation.5 | async-start | bytes 1048576 | tf_op jit(solution)/shard_map/all_to_all | solution.py:276
  187.2 10.9 %all-to-all-done.5 = bf16[16,16,1024]{2,1,0:T(8,128)(2,1)S(1)} async-done(((bf16[16,16,1024]{2,1,0:T(8,128)(2,1)}), bf16[16,16,1024]{2,1,0:T(8,128)(2,1)S(1)}, u32[]{:S(2)}, u32[]{:S(2)}) %all-to-all-start.5) | async-done | bytes 524320 | tf_op jit(solution)/shard_map/all_to_all | solution.py:276
  198.2 1.5 collective-permute-start.25
  (118 shorter events, 20.3 us)
Async XLA Ops:
  0.6 3.8 %copy-start.16 = (bf16[8,2048]{1,0:T(8,128)(2,1)S(1)}, bf16[8,2048]{1,0:T(8,128)(2,1)}, u32[]{:S(2)}) copy-start(bf16[8,2048]{1,0:T(8,128)(2,1)} %param.12) | copy-start | bytes 98308
  0.6 3.5 %copy-start.14 = (bf16[1,128,2048]{2,1,0:T(8,128)(2,1)S(1)}, bf16[1,128,2048]{2,1,0:T(8,128)(2,1)}, u32[]{:S(2)}) copy-start(bf16[1,128,2048]{2,1,0:T(8,128)(2,1)} %param.13) | copy-start | bytes 1572868
  1.4 3.0 %collective-permute-start.1 = (bf16[8,1024]{1,0:T(8,128)(2,1)S(1)}, bf16[8,1024]{1,0:T(8,128)(2,1)S(1)}, u32[]{:S(2)}, u32[]{:S(2)}) collective-permute-start(bf16[8,1024]{1,0:T(8,128)(2,1)S(1)} %dynamic-slice_bitcast_fusion.7), channel_id=1, source_target_pairs={{0,1},{1,0},{2,3},{3,2},{4,5},{5,4},{6,7},{7,6},{8,9},{9,8},{10,11... | collective-permute-start | bytes 49160 | tf_op jit(solution)/shard_map/ppermute | solution.py:263
  4.1 10.8 %collective-permute-start = (bf16[64,3072]{1,0:T(8,128)(2,1)S(1)}, bf16[64,3072]{1,0:T(8,128)(2,1)S(1)}, u32[]{:S(2)}, u32[]{:S(2)}) collective-permute-start(bf16[64,3072]{1,0:T(8,128)(2,1)S(1)} %dynamic-slice_bitcast_fusion.4), channel_id=1, source_target_pairs={{0,1},{1,0},{2,3},{3,2},{4,5},{5,4},{6,7},{7,6},{8,9},{9,8},{10,11... | collective-permute-start | bytes 1179656 | tf_op jit(solution)/shard_map/ppermute | solution.py:263
  5.4 18.4 %all-to-all-start = ((bf16[16,16,1024]{2,1,0:T(8,128)(2,1)}), bf16[16,16,1024]{2,1,0:T(8,128)(2,1)S(1)}, u32[]{:S(2)}, u32[]{:S(2)}) async-start(bf16[16,16,1024]{2,1,0:T(8,128)(2,1)} %broadcast_in_dim.35), calls=%async_computation | async-start | bytes 1048576 | tf_op jit(solution)/shard_map/all_to_all | solution.py:276
  14.1 13.7 %collective-permute-start.5 = (bf16[128,1024]{1,0:T(8,128)(2,1)}, bf16[128,1024]{1,0:T(8,128)(2,1)}, u32[]{:S(2)}, u32[]{:S(2)}) collective-permute-start(bf16[128,1024]{1,0:T(8,128)(2,1)} %bitcast.15), channel_id=1, source_target_pairs={{0,1},{1,0},{2,3},{3,2},{4,5},{5,4},{6,7},{7,6},{8,9},{9,8},{10,11... | collective-permute-start | bytes 786440 | tf_op jit(solution)/shard_map/ppermute | solution.py:263
  23.8 12.7 %collective-permute-start.6 = (bf16[16,16,1024]{2,1,0:T(8,128)(2,1)S(1)}, bf16[16,16,1024]{2,1,0:T(8,128)(2,1)S(1)}, u32[]{:S(2)}, u32[]{:S(2)}) collective-permute-start(bf16[16,16,1024]{2,1,0:T(8,128)(2,1)S(1)} %all-to-all-done), channel_id=1, source_target_pairs={{0,6},{2,4},{4,2},{6,0},{1,7},{3,5},{5,3},{7,1},{8,14},{10,12},{12... | collective-permute-start | bytes 1572872 | tf_op jit(solution)/shard_map/ppermute | solution.py:316
  26.3 11.2 %collective-permute-start.7 = (bf16[16,16,1024]{2,1,0:T(8,128)(2,1)S(1)}, bf16[16,16,1024]{2,1,0:T(8,128)(2,1)S(1)}, u32[]{:S(2)}, u32[]{:S(2)}) collective-permute-start(bf16[16,16,1024]{2,1,0:T(8,128)(2,1)S(1)} %all-to-all-done), channel_id=1, source_target_pairs={{0,4},{2,6},{4,0},{6,2},{1,5},{3,7},{5,1},{7,3},{8,12},{10,14},{12... | collective-permute-start | bytes 1572872 | tf_op jit(solution)/shard_map/ppermute | solution.py:316
  26.3 22.5 %collective-permute-start.8 = (bf16[16,16,1024]{2,1,0:T(8,128)(2,1)S(1)}, bf16[16,16,1024]{2,1,0:T(8,128)(2,1)}, u32[]{:S(2)}, u32[]{:S(2)}) collective-permute-start(bf16[16,16,1024]{2,1,0:T(8,128)(2,1)S(1)} %all-to-all-done), channel_id=1, source_target_pairs={{0,2},{2,0},{4,6},{6,4},{1,3},{3,1},{5,7},{7,5},{8,10},{10,8},{12,... | collective-permute-start | bytes 1572872 | tf_op jit(solution)/shard_map/ppermute | solution.py:316
  28.9 8.6 %copy-start.12 = (bf16[1,2,64,1024]{3,2,1,0:T(8,128)(2,1)}, bf16[1,2,64,1024]{3,2,1,0:T(8,128)(2,1)S(1)}, u32[]{:S(2)}) copy-start(bf16[1,2,64,1024]{3,2,1,0:T(8,128)(2,1)S(1)} %get-tuple-element.53) | copy-start | bytes 786436
  28.9 8.6 %copy-start.13 = (bf16[1,2,64,1024]{3,2,1,0:T(8,128)(2,1)}, bf16[1,2,64,1024]{3,2,1,0:T(8,128)(2,1)S(1)}, u32[]{:S(2)}) copy-start(bf16[1,2,64,1024]{3,2,1,0:T(8,128)(2,1)S(1)} %get-tuple-element.54) | copy-start | bytes 786436
  29.0 23.4 %all-to-all-start.1 = ((bf16[16,64,384]{2,1,0:T(8,128)(2,1)}), bf16[16,64,384]{2,1,0:T(8,128)(2,1)S(1)}, u32[]{:S(2)}, u32[]{:S(2)}) async-start(bf16[16,64,384]{2,1,0:T(8,128)(2,1)} %reshape.264), calls=%async_computation.1 | async-start | bytes 1572864 | tf_op jit(solution)/shard_map/all_to_all | solution.py:276
  50.3 1.3 copy-start.6
  51.6 5.3 %copy-start.18 = (s32[64]{0:T(128)S(1)}, s32[64]{0:T(128)}, u32[]{:S(2)}) copy-start(s32[64]{0:T(128)} %param.10) | copy-start | bytes 772
  51.6 5.6 %copy-start.17 = (s32[64,64]{1,0:T(8,128)S(1)}, s32[64,64]{1,0:T(8,128)}, u32[]{:S(2)}) copy-start(s32[64,64]{1,0:T(8,128)} %param.11) | copy-start | bytes 49156
  52.3 4.5 %copy-start.8 = (f32[256,1024]{1,0:T(8,128)}, f32[256,1024]{1,0:T(8,128)S(1)}, u32[]{:S(2)}) copy-start(f32[256,1024]{1,0:T(8,128)S(1)} %fusion.33) | copy-start | bytes 3145732
  52.4 4.5 %copy-start.9 = (bf16[16,64,384]{2,1,0:T(8,128)(2,1)}, bf16[16,64,384]{2,1,0:T(8,128)(2,1)S(1)}, u32[]{:S(2)}) copy-start(bf16[16,64,384]{2,1,0:T(8,128)(2,1)S(1)} %all-to-all-done.1) | copy-start | bytes 2359300
  52.4 10.4 %collective-permute-start.2 = (bf16[1024,256]{1,0:T(8,128)(2,1)S(1)}, bf16[1024,256]{1,0:T(8,128)(2,1)S(1)}, u32[]{:S(2)}, u32[]{:S(2)}) collective-permute-start(bf16[1024,256]{1,0:T(8,128)(2,1)S(1)} %slice.51.refs_1_.kv0.refs_0_), channel_id=1, source_target_pairs={{0,4},{4,0},{1,5},{5,1},{2,6},{6,2},{3,7},{7,3},{8,12},{12,8},{9,1... | collective-permute-start | bytes 1572872 | tf_op jit(solution)/shard_map/ppermute | solution.py:267
  53.5 13.3 %collective-permute-start.9 = (f32[128,1024]{1,0:T(8,128)}, f32[128,1024]{1,0:T(8,128)S(1)}, u32[]{:S(2)}, u32[]{:S(2)}) collective-permute-start(f32[128,1024]{1,0:T(8,128)} %slice.55), channel_id=1, source_target_pairs={{0,1},{1,0},{2,3},{3,2},{4,5},{5,4},{6,7},{7,6},{8,9},{9,8},{10,11... | collective-permute-start | bytes 1572872 | tf_op jit(solution)/shard_map/ppermute | solution.py:263
  57.1 16.9 %collective-permute-start.4 = (bf16[1024,256]{1,0:T(8,128)(2,1)S(1)}, bf16[1024,256]{1,0:T(8,128)(2,1)S(1)}, u32[]{:S(2)}, u32[]{:S(2)}) collective-permute-start(bf16[1024,256]{1,0:T(8,128)(2,1)S(1)} %slice.51.refs_1_.kv0.refs_0_), channel_id=1, source_target_pairs={{0,1},{1,0},{2,3},{3,2},{4,5},{5,4},{6,7},{7,6},{8,9},{9,8},{10,11... | collective-permute-start | bytes 1572872 | tf_op jit(solution)/shard_map/ppermute | solution.py:263
  62.8 18.9 %collective-permute-start.3 = (bf16[1024,256]{1,0:T(8,128)(2,1)S(1)}, bf16[1024,256]{1,0:T(8,128)(2,1)S(1)}, u32[]{:S(2)}, u32[]{:S(2)}) collective-permute-start(bf16[1024,256]{1,0:T(8,128)(2,1)S(1)} %collective-permute-done.2.refs_1_.kv2), channel_id=1, source_target_pairs={{0,1},{1,0},{2,3},{3,2},{4,5},{5,4},{6,7},{7,6},{8,9},{9,8},{10,11... | collective-permute-start | bytes 1572872 | tf_op jit(solution)/shard_map/ppermute | solution.py:263
  68.8 12.7 %all-to-all-start.2 = ((bf16[16,64,128]{2,1,0:T(8,128)(2,1)}), bf16[16,64,128]{2,1,0:T(8,128)(2,1)S(1)}, u32[]{:S(2)}, u32[]{:S(2)}) async-start(bf16[16,64,128]{2,1,0:T(8,128)(2,1)} %bitcast.30), calls=%async_computation.2 | async-start | bytes 524288 | tf_op jit(solution)/shard_map/all_to_all | solution.py:276
  73.9 23.2 %collective-permute-start.13 = (bf16[1024,128]{1,0:T(8,128)(2,1)S(1)}, bf16[1024,128]{1,0:T(8,128)(2,1)S(1)}, u32[]{:S(2)}, u32[]{:S(2)}) collective-permute-start(bf16[1024,128]{1,0:T(8,128)(2,1)S(1)} %slice.50.refs_0_.q_ref.refs_2_), channel_id=1, source_target_pairs={{0,4},{4,0},{1,5},{5,1},{2,6},{6,2},{3,7},{7,3},{8,12},{12,8},{9,1... | collective-permute-start | bytes 786440 | tf_op jit(solution)/shard_map/ppermute | solution.py:267
  81.4 15.7 %copy-start = (bf16[16,64,128]{2,1,0:T(8,128)(2,1)}, bf16[16,64,128]{2,1,0:T(8,128)(2,1)S(1)}, u32[]{:S(2)}) copy-start(bf16[16,64,128]{2,1,0:T(8,128)(2,1)S(1)} %all-to-all-done.2) | copy-start | bytes 786436
  81.4 16.1 %collective-permute-start.16 = (bf16[1024,128]{1,0:T(8,128)(2,1)S(1)}, bf16[1024,128]{1,0:T(8,128)(2,1)S(1)}, u32[]{:S(2)}, u32[]{:S(2)}) collective-permute-start(bf16[1024,128]{1,0:T(8,128)(2,1)S(1)} %bitcast.149), channel_id=1, source_target_pairs={{0,4},{4,0},{1,5},{5,1},{2,6},{6,2},{3,7},{7,3},{8,12},{12,8},{9,1... | collective-permute-start | bytes 786440 | tf_op jit(solution)/shard_map/ppermute | solution.py:267
  81.7 1.0 copy-start.5
  88.9 14.3 %all-to-all-start.3 = ((bf16[16,64,128]{2,1,0:T(8,128)(2,1)}), bf16[16,64,128]{2,1,0:T(8,128)(2,1)S(1)}, u32[]{:S(2)}, u32[]{:S(2)}) async-start(bf16[16,64,128]{2,1,0:T(8,128)(2,1)} %bitcast.32), calls=%async_computation.3 | async-start | bytes 524288 | tf_op jit(solution)/shard_map/all_to_all | solution.py:276
  95.6 27.4 %collective-permute-start.12 = (bf16[1024,128]{1,0:T(8,128)(2,1)S(1)}, bf16[1024,128]{1,0:T(8,128)(2,1)}, u32[]{:S(2)}, u32[]{:S(2)}) collective-permute-start(bf16[1024,128]{1,0:T(8,128)(2,1)S(1)} %slice.50.refs_0_.q_ref.refs_2_), channel_id=1, source_target_pairs={{0,1},{1,0},{2,3},{3,2},{4,5},{5,4},{6,7},{7,6},{8,9},{9,8},{10,11... | collective-permute-start | bytes 786440 | tf_op jit(solution)/shard_map/ppermute | solution.py:263
  97.0 28.3 %collective-permute-start.14 = (bf16[1024,128]{1,0:T(8,128)(2,1)S(1)}, bf16[1024,128]{1,0:T(8,128)(2,1)}, u32[]{:S(2)}, u32[]{:S(2)}) collective-permute-start(bf16[1024,128]{1,0:T(8,128)(2,1)S(1)} %collective-permute-done.13.refs_4_), channel_id=1, source_target_pairs={{0,1},{1,0},{2,3},{3,2},{4,5},{5,4},{6,7},{7,6},{8,9},{9,8},{10,11... | collective-permute-start | bytes 786440 | tf_op jit(solution)/shard_map/ppermute | solution.py:263
  97.1 28.2 %collective-permute-start.15 = (bf16[1024,128]{1,0:T(8,128)(2,1)S(1)}, bf16[1024,128]{1,0:T(8,128)(2,1)}, u32[]{:S(2)}, u32[]{:S(2)}) collective-permute-start(bf16[1024,128]{1,0:T(8,128)(2,1)S(1)} %bitcast.150), channel_id=1, source_target_pairs={{0,1},{1,0},{2,3},{3,2},{4,5},{5,4},{6,7},{7,6},{8,9},{9,8},{10,11... | collective-permute-start | bytes 786440 | tf_op jit(solution)/shard_map/ppermute | solution.py:263
  97.6 27.8 %collective-permute-start.17 = (bf16[1024,128]{1,0:T(8,128)(2,1)S(1)}, bf16[1024,128]{1,0:T(8,128)(2,1)}, u32[]{:S(2)}, u32[]{:S(2)}) collective-permute-start(bf16[1024,128]{1,0:T(8,128)(2,1)S(1)} %collective-permute-done.16.refs_8_), channel_id=1, source_target_pairs={{0,1},{1,0},{2,3},{3,2},{4,5},{5,4},{6,7},{7,6},{8,9},{9,8},{10,11... | collective-permute-start | bytes 786440 | tf_op jit(solution)/shard_map/ppermute | solution.py:263
  104.9 3.3 %copy-start.10 = (bf16[2,8,64,1,128]{4,1,2,0,3:T(8,128)(2,1)}, bf16[2,8,64,1,128]{4,1,2,0,3:T(8,128)(2,1)S(1)}, u32[]{:S(2)}) copy-start(bf16[2,8,64,1,128]{4,1,2,0,3:T(8,128)(2,1)S(1)} %copy.46) | copy-start | bytes 786436
  105.8 13.9 %collective-permute-start.10 = (bf16[2,64,1024]{2,1,0:T(8,128)(2,1)}, bf16[2,64,1024]{2,1,0:T(8,128)(2,1)}, u32[]{:S(2)}, u32[]{:S(2)}) collective-permute-start(bf16[2,64,1024]{2,1,0:T(8,128)(2,1)} %reshape.273), channel_id=1, source_target_pairs={{0,1},{1,0},{2,3},{3,2},{4,5},{5,4},{6,7},{7,6},{8,9},{9,8},{10,11... | collective-permute-start | bytes 786440 | tf_op jit(solution)/shard_map/ppermute | solution.py:263
  108.3 1.0 copy-start.1
  119.6 3.6 %collective-permute-start.19 = (f32[2,1024]{1,0:T(2,128)S(1)}, f32[2,1024]{1,0:T(2,128)S(1)}, u32[]{:S(2)}, u32[]{:S(2)}) collective-permute-start(f32[2,1024]{1,0:T(2,128)S(1)} %pad_maximum_fusion.10.refs_10_), channel_id=1, source_target_pairs={{0,4},{4,0},{1,5},{5,1},{2,6},{6,2},{3,7},{7,3},{8,12},{12,8},{9,1... | collective-permute-start | bytes 24584 | tf_op jit(solution)/shard_map/ppermute | solution.py:267
  119.7 5.6 %copy-start.2 = (bf16[16,64,128]{2,1,0:T(8,128)(2,1)S(1)}, bf16[16,64,128]{2,1,0:T(8,128)(2,1)}, u32[]{:S(2)}) copy-start(bf16[16,64,128]{2,1,0:T(8,128)(2,1)} %copy-done) | copy-start | bytes 786436
  123.0 2.3 %collective-permute-start.18 = (f32[2,1024]{1,0:T(2,128)S(1)}, f32[2,1024]{1,0:T(2,128)S(1)}, u32[]{:S(2)}, u32[]{:S(2)}) collective-permute-start(f32[2,1024]{1,0:T(2,128)S(1)} %pad_maximum_fusion.10.refs_10_), channel_id=1, source_target_pairs={{0,1},{1,0},{2,3},{3,2},{4,5},{5,4},{6,7},{7,6},{8,9},{9,8},{10,11... | collective-permute-start | bytes 24584 | tf_op jit(solution)/shard_map/ppermute | solution.py:263
  123.3 2.0 %collective-permute-start.20 = (f32[2,1024]{1,0:T(2,128)S(1)}, f32[2,1024]{1,0:T(2,128)S(1)}, u32[]{:S(2)}, u32[]{:S(2)}) collective-permute-start(f32[2,1024]{1,0:T(2,128)S(1)} %collective-permute-done.19.refs_12_), channel_id=1, source_target_pairs={{0,1},{1,0},{2,3},{3,2},{4,5},{5,4},{6,7},{7,6},{8,9},{9,8},{10,11... | collective-permute-start | bytes 24584 | tf_op jit(solution)/shard_map/ppermute | solution.py:263
  142.3 9.3 %copy-start.7 = (bf16[16,4,16,1024]{3,2,1,0:T(8,128)(2,1)S(1)}, bf16[16,4,16,1024]{3,2,1,0:T(8,128)(2,1)}, u32[]{:S(2)}) copy-start(bf16[16,4,16,1024]{3,2,1,0:T(8,128)(2,1)} %copy-done.6) | copy-start | bytes 6291460
  142.3 9.3 %copy-start.15 = (bf16[2,2,64,1024]{3,2,1,0:T(8,128)(2,1)S(1)}, bf16[2,2,64,1024]{3,2,1,0:T(8,128)(2,1)}, u32[]{:S(2)}) copy-start(bf16[2,2,64,1024]{3,2,1,0:T(8,128)(2,1)} %pad_maximum_fusion.5) | copy-start | bytes 1572868
  142.3 34.3 %all-to-all-start.4 = ((bf16[16,64,384]{2,1,0:T(8,128)(2,1)}), bf16[16,64,384]{2,1,0:T(8,128)(2,1)S(1)}, u32[]{:S(2)}, u32[]{:S(2)}) async-start(bf16[16,64,384]{2,1,0:T(8,128)(2,1)} %bitcast.159), calls=%async_computation.4 | async-start | bytes 1572864 | tf_op jit(solution)/shard_map/all_to_all | solution.py:276
  147.7 14.5 %collective-permute-start.23 = (bf16[16,16,1024]{2,1,0:T(8,128)(2,1)S(1)}, bf16[16,16,1024]{2,1,0:T(8,128)(2,1)S(1)}, u32[]{:S(2)}, u32[]{:S(2)}) collective-permute-start(bf16[16,16,1024]{2,1,0:T(8,128)(2,1)S(1)} %get-tuple-element.36), channel_id=1, source_target_pairs={{0,6},{2,4},{4,2},{6,0},{1,7},{3,5},{5,3},{7,1},{8,14},{10,12},{12... | collective-permute-start | bytes 1572872 | tf_op jit(solution)/shard_map/ppermute | solution.py:332
  150.2 12.9 %collective-permute-start.22 = (bf16[16,16,1024]{2,1,0:T(8,128)(2,1)S(1)}, bf16[16,16,1024]{2,1,0:T(8,128)(2,1)S(1)}, u32[]{:S(2)}, u32[]{:S(2)}) collective-permute-start(bf16[16,16,1024]{2,1,0:T(8,128)(2,1)S(1)} %get-tuple-element.37), channel_id=1, source_target_pairs={{0,4},{2,6},{4,0},{6,2},{1,5},{3,7},{5,1},{7,3},{8,12},{10,14},{12... | collective-permute-start | bytes 1572872 | tf_op jit(solution)/shard_map/ppermute | solution.py:332
  151.1 23.2 %collective-permute-start.21 = (bf16[16,16,1024]{2,1,0:T(8,128)(2,1)S(1)}, bf16[16,16,1024]{2,1,0:T(8,128)(2,1)S(1)}, u32[]{:S(2)}, u32[]{:S(2)}) collective-permute-start(bf16[16,16,1024]{2,1,0:T(8,128)(2,1)S(1)} %get-tuple-element.35), channel_id=1, source_target_pairs={{0,2},{2,0},{4,6},{6,4},{1,3},{3,1},{5,7},{7,5},{8,10},{10,8},{12,... | collective-permute-start | bytes 1572872 | tf_op jit(solution)/shard_map/ppermute | solution.py:332
  152.4 27.2 %collective-permute-start.11 = (bf16[2,64,1024]{2,1,0:T(8,128)(2,1)S(1)}, bf16[2,64,1024]{2,1,0:T(8,128)(2,1)S(1)}, u32[]{:S(2)}, u32[]{:S(2)}) collective-permute-start(bf16[2,64,1024]{2,1,0:T(8,128)(2,1)S(1)} %dynamic-slice_bitcast_fusion.5), channel_id=1, source_target_pairs={{0,1},{1,0},{2,3},{3,2},{4,5},{5,4},{6,7},{7,6},{8,9},{9,8},{10,11... | collective-permute-start | bytes 786440 | tf_op jit(solution)/shard_map/ppermute | solution.py:263
  178.1 9.0 %collective-permute-start.24 = (bf16[64,3072]{1,0:T(8,128)(2,1)S(1)}, bf16[64,3072]{1,0:T(8,128)(2,1)S(1)}, u32[]{:S(2)}, u32[]{:S(2)}) collective-permute-start(bf16[64,3072]{1,0:T(8,128)(2,1)S(1)} %dynamic-slice_bitcast_fusion.3), channel_id=1, source_target_pairs={{0,1},{1,0},{2,3},{3,2},{4,5},{5,4},{6,7},{7,6},{8,9},{9,8},{10,11... | collective-permute-start | bytes 1179656 | tf_op jit(solution)/shard_map/ppermute | solution.py:263
  180.5 17.7 %all-to-all-start.5 = ((bf16[16,16,1024]{2,1,0:T(8,128)(2,1)}), bf16[16,16,1024]{2,1,0:T(8,128)(2,1)S(1)}, u32[]{:S(2)}, u32[]{:S(2)}) async-start(bf16[16,16,1024]{2,1,0:T(8,128)(2,1)} %fusion.14), calls=%async_computation.5 | async-start | bytes 1048576 | tf_op jit(solution)/shard_map/all_to_all | solution.py:276
  198.2 2.4 %collective-permute-start.25 = (f32[8,1024]{1,0:T(8,128)S(1)}, f32[8,1024]{1,0:T(8,128)S(1)}, u32[]{:S(2)}, u32[]{:S(2)}) collective-permute-start(f32[8,1024]{1,0:T(8,128)S(1)} %dynamic-slice_bitcast_fusion.6), channel_id=1, source_target_pairs={{0,1},{1,0},{2,3},{3,2},{4,5},{5,4},{6,7},{7,6},{8,9},{9,8},{10,11... | collective-permute-start | bytes 98312 | tf_op jit(solution)/shard_map/ppermute | solution.py:263
  (3 other events, 2.2 us)

commit v3 on v2

--- a/solution.py
+++ b/solution.py
@@ -205,8 +205,8 @@
 
 def key_body(*refs):
     kv_ref, bias_ref = refs[:2]
-    qs, gs, stats = refs[2:6], refs[6:10], refs[10:14]
-    dk_ref, dv_ref, ka_ref, s_ref, dk_acc, dv_acc = refs[14:]
+    pairs, stats = refs[2:6], refs[6]
+    dk_ref, dv_ref, ka_ref, s_ref, dk_acc, dv_acc = refs[7:]
     ka_ref[:, :HEAD] = kv_ref[:, :HEAD]
     ka_ref[:, HEAD:] = spread_bias(bias_ref[:UNITS, :])
     dk_acc[...] = jnp.zeros_like(dk_acc)
@@ -215,10 +215,10 @@
 
         def tile(i, _, c=c):
             rows = pl.ds(pl.multiple_of(i * TILE, TILE), TILE)
-            q = qs[c][rows, :]
-            g = gs[c][rows, :]
-            lse = stats[c][0:1, rows]
-            delta = stats[c][1:2, rows]
+            q = pairs[c][rows, :HEAD]
+            g = pairs[c][rows, HEAD:]
+            lse = stats[2 * c : 2 * c + 1, rows]
+            delta = stats[2 * c + 1 : 2 * c + 2, rows]
             qa = query_wide(q, i * (TILE // SPAN) + c * UNITS)
             s_ref[...] = dot(ka_ref[...], qa, NT)
             if c == 0:
@@ -235,12 +235,12 @@
     dv_ref[...] = dv_acc[...].astype(BF16)
 
 
-def key_grad(kv, bias, qs, gs, stats):
+def key_grad(kv, bias, pairs, stats):
     in_vmem = pl.BlockSpec(memory_space=pltpu.VMEM)
     return pl.pallas_call(
         key_body,
         out_shape=[jax.ShapeDtypeStruct((ROWS, HEAD), BF16)] * 2,
-        in_specs=[in_vmem] * 14,
+        in_specs=[in_vmem] * 7,
         out_specs=[in_vmem] * 2,
         scratch_shapes=[
             pltpu.VMEM((ROWS, 2 * HEAD), BF16),
@@ -251,7 +251,7 @@
         cost_estimate=cost(4, 4 * ROWS * ROWS),
         compiler_params=pltpu.CompilerParams(vmem_limit_bytes=40 << 20),
         name="key_grad",
-    )(kv, bias, *qs, *gs, *stats)
+    )(kv, bias, *pairs, stats)
 
 
 ZY = ("z", "y")
@@ -310,28 +310,70 @@
     return jnp.concatenate([jnp.where(first, own, peer), jnp.where(first, peer, own)], axis=-1)
 
 
-def from_chips(x):
-    place = 2 * lax.axis_index("xl") + lax.axis_index("xh")
-    held = [x] + [
-        lax.ppermute(x, ("xl", "xh"), [(k, k ^ step) for k in range(4)]) for step in (1, 2, 3)
+def to_narrow(x):
+    return jnp.concatenate(jnp.split(x, 4, axis=-1), axis=-2)
+
+
+def from_narrow(x):
+    return jnp.concatenate(jnp.split(x, 4, axis=-2), axis=-1)
+
+
+def chip_place():
+    return 2 * lax.axis_index("xl") + lax.axis_index("xh")
+
+
+def chip_copies(parts):
+    return [
+        lax.ppermute(part, ("xl", "xh"), [(k, k ^ step) for k in range(4)])
+        for step, part in zip((1, 2, 3), parts)
     ]
-    low, high = place % 2 == 1, place >= 2
-    pairs = [
-        (jnp.where(low, held[k + 1], held[k]), jnp.where(low, held[k], held[k + 1])) for k in (0, 2)
-    ]
-    front = [jnp.where(high, pairs[1][k], pairs[0][k]) for k in (0, 1)]
-    back = [jnp.where(high, pairs[0][k], pairs[1][k]) for k in (0, 1)]
-    return jnp.stack(front + back, axis=1)
-
-
-def sum_to_chips(x):
-    place = 2 * lax.axis_index("xl") + lax.axis_index("xh")
-    total = lax.dynamic_index_in_dim(x, place, 1, False).astype(F32)
-    for step in (1, 2, 3):
-        part = lax.dynamic_index_in_dim(x, place ^ step, 1, False)
-        sent = lax.ppermute(part, ("xl", "xh"), [(k, k ^ step) for k in range(4)])
-        total = total + sent.astype(F32)
-    return total.astype(x.dtype)
+
+
+def weight_body(place_ref, *refs):
+    parts, out_ref = refs[:4], refs[4]
+    for step in range(4):
+        chip = place_ref[0] ^ step
+        for c in range(4):
+            rows = parts[step][:, c * 16 : (c + 1) * 16, :]
+            out_ref[:, chip, :, c * 256 : (c + 1) * 256] = rows
+
+
+def weight_whole(place, parts):
+    in_vmem = pl.BlockSpec(memory_space=pltpu.VMEM)
+    return pl.pallas_call(
+        weight_body,
+        out_shape=jax.ShapeDtypeStruct((UNITS, 4, 16, 1024), BF16),
+        in_specs=[pl.BlockSpec(memory_space=pltpu.SMEM)] + [in_vmem] * 4,
+        out_specs=in_vmem,
+        cost_estimate=pl.CostEstimate(flops=0, bytes_accessed=4 << 20, transcendentals=0),
+        compiler_params=pltpu.CompilerParams(vmem_limit_bytes=24 << 20),
+        name="weight_whole",
+    )(place, *parts)
+
+
+def term_body(place_ref, att_ref, up_ref, *refs):
+    outs, sum_ref = refs[:4], refs[4]
+    for c in range(4):
+        cols = slice(c * 256, (c + 1) * 256)
+        sum_ref[...] = dot(att_ref[...], up_ref[:, cols], TN).astype(BF16).reshape(sum_ref.shape)
+        for step in range(4):
+            outs[step][:, c * 16 : (c + 1) * 16, :] = sum_ref[:, place_ref[0] ^ step]
+
+
+def weight_terms(place, att, up):
+    in_vmem = pl.BlockSpec(memory_space=pltpu.VMEM)
+    return pl.pallas_call(
+        term_body,
+        out_shape=[jax.ShapeDtypeStruct((UNITS, SPAN, 256), BF16)] * 4,
+        in_specs=[pl.BlockSpec(memory_space=pltpu.SMEM)] + [in_vmem] * 2,
+        out_specs=[in_vmem] * 4,
+        scratch_shapes=[pltpu.VMEM((UNITS, 4, 16, 256), BF16)],
+        cost_estimate=pl.CostEstimate(
+            flops=2 * 256 * 1024 * 1024, bytes_accessed=4 << 20, transcendentals=0
+        ),
+        compiler_params=pltpu.CompilerParams(vmem_limit_bytes=24 << 20),
+        name="weight_terms",
+    )(place, att, up)
 
 
 def local(query_states, key_states, value_states, span_order, block_mask, output_weight, upstream):
@@ -359,13 +401,17 @@
 
     weight_cols = output_weight.reshape(-1, 2, cols)
     weight_rows = in_order(first_core, mine(weight_cols, 1), other_core(theirs(weight_cols, 1)))
-    weight_rows = weight_rows.reshape(-1, cols)
+    weight_rows = to_narrow(weight_rows.reshape(-1, cols))
     copies = jnp.broadcast_to(weight_rows[None], (UNITS, *weight_rows.shape))
     states = share(jnp.concatenate([query_states[0], key_states[0], value_states[0]], axis=1))
-    weight_rows = exchange(copies, ZY)
-    sent, weight_rows = lax.optimization_barrier((by_unit(states, 3), weight_rows))
-    weight = from_chips(weight_rows)
-    blocks = exchange(sent, ZY).reshape(ROWS, 3 * HEAD)
+    blocks = exchange(jnp.concatenate([by_unit(states, 3), copies], axis=2), ZY)
+    q = blocks[:, :, :HEAD].reshape(ROWS, HEAD)
+    own_kv = blocks[:, :, HEAD : 3 * HEAD].reshape(ROWS, 2 * HEAD)
+    far_kv = other_chip(own_kv)
+    near_kv = other_core(own_kv)
+    weight_own = blocks[:, :, 3 * HEAD :]
+    weight_others = chip_copies([weight_own] * 3)
+    place = chip_place().reshape(1)
     bias = span_bias(span_order, block_mask, xl, core)
 
     up_cols = upstream[0].reshape(2 * SPAN, 2, cols)
@@ -373,39 +419,44 @@
     up = up.reshape(2, 2, SPAN, cols)
     up = in_order(half == 0, up[:, 0], up[:, 1]).reshape(4 * SPAN, cols)
 
-    q = blocks[:, :HEAD]
-    kvs = everyone(blocks[:, HEAD:])
-    partial = forward(True, q, kvs[0], kvs[1], bias[: 2 * UNITS])
-
-    weight = weight.reshape(HEADS * HEAD, cols)
+    partial = forward(True, q, own_kv, near_kv, bias[: 2 * UNITS])
+    far_kv, *partial = lax.optimization_barrier((far_kv, *partial))
+    kvs = (own_kv, near_kv, far_kv, other_core(far_kv))
+
+    attended, lse = forward(False, q, kvs[2], kvs[3], bias[2 * UNITS :], *partial)
+    attended_units = exchange(attended.reshape(UNITS, SPAN, HEAD), ZY)
+    attended_units, *weight_others = lax.optimization_barrier((attended_units, *weight_others))
+    weight = weight_whole(place, [weight_own, *weight_others]).reshape(HEADS * HEAD, cols)
     grad_rows = dot(up, weight, NT)
     grad_rows = grad_rows[: 2 * SPAN] + other_core(grad_rows[2 * SPAN :])
     grad_rows = grad_rows.astype(BF16).reshape(2, SPAN, -1)
     g = exchange(by_unit(grad_rows, 1), ZY).reshape(ROWS, HEAD)
-    gs = everyone(g)
-    qs = everyone(q)
-
-    attended, lse = forward(False, q, kvs[2], kvs[3], bias[2 * UNITS :], *partial)
-    attended, g = lax.optimization_barrier((attended, g))
-    delta = row_delta(g, attended)
-    stats = everyone(jnp.concatenate([lse, delta], axis=0))
-    query_out = query_grad(q, g, lse, delta, kvs, bias)
-
-    attended_rows = by_row(exchange(attended.reshape(UNITS, SPAN, HEAD), ZY), 1)
+
+    attended_rows = by_row(attended_units, 1)
     attended_rows = jnp.stack([attended_rows, other_core(attended_rows)]).reshape(4 * SPAN, -1)
-    term = dot(attended_rows, up, TN).astype(BF16).reshape(UNITS, 4, 16, cols)
-    term, key_side = lax.optimization_barrier((term, kvs[0]))
-    term = sum_to_chips(term)
+    terms = weight_terms(place, attended_rows, up)
+    *terms, g = lax.optimization_barrier((*terms, g))
+    pairs = everyone(jnp.concatenate([q, g], axis=1))
+    others = chip_copies(terms[1:])
     projected = dot(attended_rows, weight, NN).astype(BF16).reshape(2, 2, SPAN, cols)
     own, peer = mine(projected, 1), other_core(theirs(projected, 1))
     own = in_order(half == 0, own[0], own[1]).reshape(2 * SPAN, cols)
     peer = in_order(half == 0, peer[1], peer[0]).reshape(2 * SPAN, cols)
     projected = side_by_side(first_core, own, peer)
 
-    key_out, value_out = key_grad(key_side, bias, qs, gs, stats)
-    grads = jnp.concatenate([query_out, key_out, value_out], axis=1).reshape(UNITS, SPAN, -1)
-    grads, term = lax.optimization_barrier((exchange(grads, ZY), term))
-    summed = jnp.sum(exchange(term, ZY).astype(F32), axis=0).reshape(2, -1, cols)
+    delta = row_delta(g, attended)
+    stats = jnp.concatenate([lse, delta], axis=0)
+    stats = jnp.concatenate([stats, other_core(stats)], axis=0)
+    stats = jnp.concatenate([stats, other_chip(stats)], axis=0)
+    query_out = query_grad(q, g, lse, delta, kvs, bias)
+    key_out, value_out = key_grad(own_kv, bias, pairs, stats)
+    key_out, *others = lax.optimization_barrier((key_out, *others))
+    term = sum((x.astype(F32) for x in others), terms[0].astype(F32)).astype(BF16)
+    grads = [x.reshape(UNITS, SPAN, HEAD) for x in (query_out, key_out, value_out)]
+    grads = exchange(jnp.concatenate([*grads, term], axis=2), ZY)
+    summed = jnp.sum(grads[:, :, 3 * HEAD :].astype(F32), axis=0)
+    summed = from_narrow(summed).reshape(2, -1, cols)
+    grads = grads[:, :, : 3 * HEAD]
     weight_gradient = side_by_side(first_core, mine(summed, 0), other_core(theirs(summed, 0)))
     grads = unshare(by_row(grads, 3))
     query_gradient, key_gradient, value_gradient = jnp.split(grads, 3, axis=1)

time: 203 us -> 198 us (0.975)
  local copies, waits for them, and re-layouts: 20.4 us -> 31.2 us
  starting transfers between devices: 60.4 us -> 50.2 us
  waiting for transfers between devices: 64.2 us -> 56.7 us
  Pallas kernels: 38 us -> 41.3 us
  matrix products: 5.01 us -> 1.76 us
    ppermute x6, waiting for transfers between devices: 36.7 us -> 5.98 us  [chip_copies(): lax.ppermute(part, ('xl', 'xh'), [(k, k ^ step) for k in range(4)])]
    unnamed x42 -> x72, local copies, waits for them, and re-layouts: 5.97 us -> 19.9 us
    all_to_all x6 -> x4, waiting for transfers between devices: 22.2 us -> 34.7 us  [exchange(): return lax.all_to_all(x, axes, 0, 0, tiled=True)]
    all_to_all x6 -> x4, starting transfers between devices: 32.7 us -> 20.3 us  [exchange(): return lax.all_to_all(x, axes, 0, 0, tiled=True)]
    ppermute x4 -> x3, waiting for transfers between devices: 5.33 us -> 11.3 us  [other_chip(): return lax.ppermute(x, 'xl', SWAP)]
    ppermute x16 -> x13, waiting for transfers between devices: 0.04 us -> 4.7 us  [other_core(): return lax.ppermute(x, 'core', SWAP)]
    dot_general x3 -> x2, matrix products: 4.7 us -> 1.45 us  [dot(): return lax.dot_general(a, b, dims, preferred_element_type=F32)]
    concatenate x2 -> x7, other arithmetic: 1.04 us -> 4 us  [the longest x1 1.28 us: local(): grads = exchange(jnp.concatenate([*grads, term], axis=2), ZY)]
  transfers between devices with their start and end apart: 32 -> 26, of which waited for: 11 -> 11; matrix products, arithmetic and copies ran while one was open for 15% -> 10% of each run, Pallas kernels for 11% -> 21%
where the time goes in v3:
time: 198 us; the launch traced here: 196 us
  waiting for transfers between devices  56.7 us (29%)
  starting transfers between devices  50.2 us (25%)
  Pallas kernels  41.3 us (21%)
  local copies, waits for them, and re-layouts  31.2 us (16%)
  other arithmetic  13.9 us (7%)
    all_to_all x4, waiting for transfers between devices, exchange(): return lax.all_to_all(x, axes, 0, 0, tiled=True)  34.7 us
    all_to_all x4, starting transfers between devices, exchange(): return lax.all_to_all(x, axes, 0, 0, tiled=True)  20.3 us
    unnamed x72, local copies, waits for them, and re-layouts  19.9 us
    ppermute x13, starting transfers between devices, other_core(): return lax.ppermute(x, 'core', SWAP)  16.9 us
    pallas_call x1, Pallas kernels, key_grad(): pl.pallas_call(key_body, out_shape=[jax.ShapeDtypeStruct((ROWS, HEAD), BF...  15.8 us
    pallas_call x2, Pallas kernels, forward(): pl.pallas_call(functools.partial(forward_body, first), out_shape=outs, gr...  12.6 us
    ppermute x3, waiting for transfers between devices, other_chip(): return lax.ppermute(x, 'xl', SWAP)  11.3 us
    ppermute x6, starting transfers between devices, chip_copies(): lax.ppermute(part, ('xl', 'xh'), [(k, k ^ step) for k in range(4)])  9.9 us
  transfers between devices with their start and end apart: 26, of which 11 were waited for; matrix products, arithmetic and copies ran while one was open for 10% of the time, Pallas kernels for 21%

profile of v3, /device:TPU:1, one launch (start us, length us, event | category | flops | bytes accessed | tf_op | source)
XLA Modules:
  0.0 196.3 jit_solution(6429301864791396751)
XLA Ops:
  1.4 1.4 collective-permute-start.1
  2.8 1.2 pad_maximum_fusion.2
  4.2 1.6 collective-permute-done
  7.4 1.2 pad_maximum_fusion
  8.6 8.0 %all-to-all-start = ((bf16[16,64,640]{2,1,0:T(8,128)(2,1)}), bf16[16,64,640]{2,1,0:T(8,128)(2,1)S(1)}, u32[]{:S(2)}, u32[]{:S(2)}) async-start(bf16[16,64,640]{2,1,0:T(8,128)(2,1)} %pad_maximum_fusion), calls=%async_computation | async-start | bytes 2621440 | tf_op jit(solution)/shard_map/all_to_all | solution.py:276
  17.7 19.8 %all-to-all-done = bf16[16,64,640]{2,1,0:T(8,128)(2,1)S(1)} async-done(((bf16[16,64,640]{2,1,0:T(8,128)(2,1)}), bf16[16,64,640]{2,1,0:T(8,128)(2,1)S(1)}, u32[]{:S(2)}, u32[]{:S(2)}) %all-to-all-start) | async-done | bytes 1310752 | tf_op jit(solution)/shard_map/all_to_all | solution.py:276
  38.6 1.6 collective-permute-start.3
  40.4 1.3 collective-permute-start.2
  43.0 5.5 %forward_a.1 = (f32[128,1024]{1,0:T(8,128)S(1)}, f32[1,1024]{1,0:T(1,128)S(1)}, f32[1,1024]{1,0:T(1,128)S(1)}) custom-call(bf16[1024,128]{1,0:T(8,128)(2,1)S(1)} %bitcast.137, bf16[1024,256]{1,0:T(8,128)(2,1)S(1)} %bitcast.145, bf16[1024,256]{1,0:T(8,128)(2,1)S(1)} %collective-permute-done.3.refs_2_.kv1, f32[32,128]{1,0:T(8,128)S(1)} %get-tuple-element.91.refs_3_), custom_call_target="tpu_custom_call" | custom-call | flops 2147483648 | bytes 4194304 | tf_op jit(solution)/shard_map/forward_a/pallas_call | solution.py:117
  49.4 4.7 %collective-permute-done.2.refs_1_.kv2 = bf16[1024,256]{1,0:T(8,128)(2,1)} collective-permute-done((bf16[1024,256]{1,0:T(8,128)(2,1)S(1)}, bf16[1024,256]{1,0:T(8,128)(2,1)}, u32[]{:S(2)}, u32[]{:S(2)}) %collective-permute-start.2) | collective-permute-done | bytes 524320 | tf_op jit(solution)/shard_map/ppermute | solution.py:267
  56.6 2.5 %collective-permute-start.7 = (bf16[16,64,256]{2,1,0:T(8,128)(2,1)S(1)}, bf16[16,64,256]{2,1,0:T(8,128)(2,1)S(1)}, u32[]{:S(2)}, u32[]{:S(2)}) collective-permute-start(bf16[16,64,256]{2,1,0:T(8,128)(2,1)S(1)} %get-tuple-element.61.refs_0_), channel_id=1, source_target_pairs={{0,6},{2,4},{4,2},{6,0},{1,7},{3,5},{5,3},{7,1},{8,14},{10,12},{12... | collective-permute-start | bytes 1572872 | tf_op jit(solution)/shard_map/ppermute | solution.py:327
  59.1 1.4 collective-permute-start.5
  60.5 1.8 bitcast_select_fusion.5
  62.3 1.2 copy-done.26
  63.5 7.1 %forward_b.1 = (bf16[1024,128]{1,0:T(8,128)(2,1)}, f32[1,1024]{1,0:T(1,128)S(1)}) custom-call(bf16[1024,128]{1,0:T(8,128)(2,1)S(1)} %bitcast.138, bf16[1024,256]{1,0:T(8,128)(2,1)} %collective-permute-done.2.refs_1_.kv2, bf16[1024,256]{1,0:T(8,128)(2,1)S(1)} %collective-permute-done.4.refs_2_.kv3, f32[32,128]{1,0:T(8,128)S(1)} %get-tuple-element.90.refs_3_, ...), custom_call_target="tpu_custom_call" | custom-call | flops 2147483648 | bytes 4194304 | tf_op jit(solution)/shard_map/forward_b/pallas_call | solution.py:117
  70.6 3.5 %all-to-all-start.1 = ((bf16[16,64,128]{2,1,0:T(8,128)(2,1)}), bf16[16,64,128]{2,1,0:T(8,128)(2,1)S(1)}, u32[]{:S(2)}, u32[]{:S(2)}) async-start(bf16[16,64,128]{2,1,0:T(8,128)(2,1)} %bitcast.14), calls=%async_computation.1 | async-start | bytes 524288 | tf_op jit(solution)/shard_map/all_to_all | solution.py:276
  74.2 1.1 select_bitcast_fusion.1
  77.0 6.0 %collective-permute-done.5.refs_1_ = bf16[16,64,256]{2,1,0:T(8,128)(2,1)S(1)} collective-permute-done((bf16[16,64,256]{2,1,0:T(8,128)(2,1)S(1)}, bf16[16,64,256]{2,1,0:T(8,128)(2,1)S(1)}, u32[]{:S(2)}, u32[]{:S(2)}) %collective-permute-start.5) | collective-permute-done | bytes 524320 | tf_op jit(solution)/shard_map/ppermute | solution.py:327
  83.7 1.0 copy-done.7
  84.8 1.0 copy-done.9
  85.8 1.0 copy-done.11
  89.7 1.7 collective-permute-start.11
  93.2 1.3 fusion.18
  95.3 3.5 %all-to-all-start.2 = ((bf16[16,64,128]{2,1,0:T(8,128)(2,1)}), bf16[16,64,128]{2,1,0:T(8,128)(2,1)S(1)}, u32[]{:S(2)}, u32[]{:S(2)}) async-start(bf16[16,64,128]{2,1,0:T(8,128)(2,1)} %bitcast.39), calls=%async_computation.2 | async-start | bytes 524288 | tf_op jit(solution)/shard_map/all_to_all | solution.py:276
  99.0 1.0 pad_maximum_fusion.4
  105.1 2.1 %all-to-all-done.2 = bf16[16,64,128]{2,1,0:T(8,128)(2,1)S(1)} async-done(((bf16[16,64,128]{2,1,0:T(8,128)(2,1)}), bf16[16,64,128]{2,1,0:T(8,128)(2,1)S(1)}, u32[]{:S(2)}, u32[]{:S(2)}) %all-to-all-start.2) | async-done | bytes 262176 | tf_op jit(solution)/shard_map/all_to_all | solution.py:276
  108.0 1.8 delta.1.delta_ref
  110.5 1.3 collective-permute-start.15
  111.9 3.6 %collective-permute-start.17 = (bf16[16,64,256]{2,1,0:T(8,128)(2,1)}, bf16[16,64,256]{2,1,0:T(8,128)(2,1)S(1)}, u32[]{:S(2)}, u32[]{:S(2)}) collective-permute-start(bf16[16,64,256]{2,1,0:T(8,128)(2,1)} %copy-done.24), channel_id=1, source_target_pairs={{0,2},{2,0},{4,6},{6,4},{1,3},{3,1},{5,7},{7,5},{8,10},{10,8},{12,... | collective-permute-start | bytes 1572872 | tf_op jit(solution)/shard_map/ppermute | solution.py:327
  116.2 1.5 collective-permute-start.16
  117.7 2.2 %collective-permute-done.13.refs_4_ = bf16[1024,256]{1,0:T(8,128)(2,1)} collective-permute-done((bf16[1024,256]{1,0:T(8,128)(2,1)S(1)}, bf16[1024,256]{1,0:T(8,128)(2,1)}, u32[]{:S(2)}, u32[]{:S(2)}) %collective-permute-start.13) | collective-permute-done | bytes 524320 | tf_op jit(solution)/shard_map/ppermute | solution.py:267
  119.9 3.8 %collective-permute-start.14 = (bf16[1024,256]{1,0:T(8,128)(2,1)}, bf16[1024,256]{1,0:T(8,128)(2,1)S(1)}, u32[]{:S(2)}, u32[]{:S(2)}) collective-permute-start(bf16[1024,256]{1,0:T(8,128)(2,1)} %collective-permute-done.13.refs_4_), channel_id=1, source_target_pairs={{0,1},{1,0},{2,3},{3,2},{4,5},{5,4},{6,7},{7,6},{8,9},{9,8},{10,11... | collective-permute-start | bytes 1572872 | tf_op jit(solution)/shard_map/ppermute | solution.py:263
  124.7 1.0 copy-done.15
  126.4 1.0 copy-done.18
  127.5 1.0 copy-done.20
  128.5 9.7 %query_grad.1 = bf16[1024,128]{1,0:T(8,128)(2,1)S(1)} custom-call(bf16[1024,128]{1,0:T(8,128)(2,1)S(1)} %bitcast.140, bf16[1024,128]{1,0:T(8,128)(2,1)S(1)} %bitcast.134, f32[1,1024]{1,0:T(1,128)S(1)} %get-tuple-element.50.lse_ref, f32[1,1024]{1,0:T(1,128)S(1)} %copy-done.16, bf16[1024,256]{1,0:T(8,128)(2,1)S(1)} %bitcast.146, ...), custom_call_target="tpu_custom_call" | custom-call | flops 6442450944 | bytes 4194304 | tf_op jit(solution)/shard_map/query_grad/pallas_call | solution.py:183
  138.3 4.3 %collective-permute-done.16 = f32[4,1024]{1,0:T(4,128)S(1)} collective-permute-done((f32[4,1024]{1,0:T(4,128)S(1)}, f32[4,1024]{1,0:T(4,128)S(1)}, u32[]{:S(2)}, u32[]{:S(2)}) %collective-permute-start.16) | collective-permute-done | bytes 16416 | tf_op jit(solution)/shard_map/ppermute | solution.py:267
  142.6 2.5 %collective-permute-start.19 = (bf16[16,64,256]{2,1,0:T(8,128)(2,1)S(1)}, bf16[16,64,256]{2,1,0:T(8,128)(2,1)S(1)}, u32[]{:S(2)}, u32[]{:S(2)}) collective-permute-start(bf16[16,64,256]{2,1,0:T(8,128)(2,1)S(1)} %copy-done.22), channel_id=1, source_target_pairs={{0,6},{2,4},{4,2},{6,0},{1,7},{3,5},{5,3},{7,1},{8,14},{10,12},{12... | collective-permute-start | bytes 1572872 | tf_op jit(solution)/shard_map/ppermute | solution.py:327
  145.2 15.8 %key_grad.1 = (bf16[1024,128]{1,0:T(8,128)(2,1)S(1)}, bf16[1024,128]{1,0:T(8,128)(2,1)S(1)}) custom-call(bf16[1024,256]{1,0:T(8,128)(2,1)S(1)} %bitcast.147, f32[64,128]{1,0:T(8,128)S(1)} %pad.4.bias_ref.refs_1_, bf16[1024,256]{1,0:T(8,128)(2,1)S(1)} %pad_maximum_fusion.6.refs_2_, bf16[1024,256]{1,0:T(8,128)(2,1)S(1)} %collective-permute-done.12.refs_3_, ...), custom_call_target="tpu_custom_call" | custom-call | flops 8589934592 | bytes 4194304 | tf_op jit(solution)/shard_map/key_grad/pallas_call | solution.py:240
  161.3 1.3 pad_maximum_fusion.1
  162.6 5.3 %all-to-all-start.3 = ((bf16[16,64,640]{2,1,0:T(8,128)(2,1)}), bf16[16,64,640]{2,1,0:T(8,128)(2,1)}, u32[]{:S(2)}, u32[]{:S(2)}) async-start(bf16[16,64,640]{2,1,0:T(8,128)(2,1)} %pad_maximum_fusion.1), calls=%async_computation.3 | async-start | bytes 2621440 | tf_op jit(solution)/shard_map/all_to_all | solution.py:276
  168.7 2.2 %collective-permute-start.9 = (bf16[2,64,1024]{2,1,0:T(8,128)(2,1)S(1)}, bf16[2,64,1024]{2,1,0:T(8,128)(2,1)S(1)}, u32[]{:S(2)}, u32[]{:S(2)}) collective-permute-start(bf16[2,64,1024]{2,1,0:T(8,128)(2,1)S(1)} %dynamic-slice_bitcast_fusion.2), channel_id=1, source_target_pairs={{0,1},{1,0},{2,3},{3,2},{4,5},{5,4},{6,7},{7,6},{8,9},{9,8},{10,11... | collective-permute-start | bytes 786440 | tf_op jit(solution)/shard_map/ppermute | solution.py:263
  170.8 1.1 collective-permute-done.9
  172.9 12.7 %all-to-all-done.3 = bf16[16,64,640]{2,1,0:T(8,128)(2,1)} async-done(((bf16[16,64,640]{2,1,0:T(8,128)(2,1)}), bf16[16,64,640]{2,1,0:T(8,128)(2,1)}, u32[]{:S(2)}, u32[]{:S(2)}) %all-to-all-start.3) | async-done | bytes 1310752 | tf_op jit(solution)/shard_map/all_to_all | solution.py:276
  185.6 1.1 convert_reduce_fusion
  186.8 3.8 %collective-permute-start.21 = (f32[8,1024]{1,0:T(8,128)S(1)}, f32[8,1024]{1,0:T(8,128)S(1)}, u32[]{:S(2)}, u32[]{:S(2)}) collective-permute-start(f32[8,1024]{1,0:T(8,128)S(1)} %dynamic-slice_bitcast_fusion.3), channel_id=1, source_target_pairs={{0,1},{1,0},{2,3},{3,2},{4,5},{5,4},{6,7},{7,6},{8,9},{9,8},{10,11... | collective-permute-start | bytes 98312 | tf_op jit(solution)/shard_map/ppermute | solution.py:263
  190.6 1.2 slice.71
  194.2 1.0 collective-permute-done.20
  (143 shorter events, 31.7 us)
Async XLA Ops:
  0.6 3.5 %copy-start.31 = (bf16[8,2048]{1,0:T(8,128)(2,1)S(1)}, bf16[8,2048]{1,0:T(8,128)(2,1)}, u32[]{:S(2)}) copy-start(bf16[8,2048]{1,0:T(8,128)(2,1)} %param.12) | copy-start | bytes 98308
  1.4 2.7 %collective-permute-start.1 = (bf16[8,1024]{1,0:T(8,128)(2,1)S(1)}, bf16[8,1024]{1,0:T(8,128)(2,1)S(1)}, u32[]{:S(2)}, u32[]{:S(2)}) collective-permute-start(bf16[8,1024]{1,0:T(8,128)(2,1)S(1)} %dynamic-slice_bitcast_fusion.4), channel_id=1, source_target_pairs={{0,1},{1,0},{2,3},{3,2},{4,5},{5,4},{6,7},{7,6},{8,9},{9,8},{10,11... | collective-permute-start | bytes 49160 | tf_op jit(solution)/shard_map/ppermute | solution.py:263
  4.1 1.8 collective-permute-start
  8.6 8.0 %copy-start.30 = (bf16[1,128,2048]{2,1,0:T(8,128)(2,1)S(1)}, bf16[1,128,2048]{2,1,0:T(8,128)(2,1)}, u32[]{:S(2)}) copy-start(bf16[1,128,2048]{2,1,0:T(8,128)(2,1)} %param.13) | copy-start | bytes 1572868
  8.6 28.9 %all-to-all-start = ((bf16[16,64,640]{2,1,0:T(8,128)(2,1)}), bf16[16,64,640]{2,1,0:T(8,128)(2,1)S(1)}, u32[]{:S(2)}, u32[]{:S(2)}) async-start(bf16[16,64,640]{2,1,0:T(8,128)(2,1)} %pad_maximum_fusion), calls=%async_computation | async-start | bytes 2621440 | tf_op jit(solution)/shard_map/all_to_all | solution.py:276
  16.7 23.5 %copy-start.33 = (s32[64]{0:T(128)S(1)}, s32[64]{0:T(128)}, u32[]{:S(2)}) copy-start(s32[64]{0:T(128)} %param.10) | copy-start | bytes 772
  16.7 25.0 %copy-start.32 = (s32[64,64]{1,0:T(8,128)S(1)}, s32[64,64]{1,0:T(8,128)}, u32[]{:S(2)}) copy-start(s32[64,64]{1,0:T(8,128)} %param.11) | copy-start | bytes 49156
  37.5 1.1 copy-start.27
  37.6 10.9 %copy-start.14 = (bf16[16,64,256]{2,1,0:T(8,128)(2,1)}, bf16[16,64,256]{2,1,0:T(8,128)(2,1)S(1)}, u32[]{:S(2)}) copy-start(bf16[16,64,256]{2,1,0:T(8,128)(2,1)S(1)} %get-tuple-element.62) | copy-start | bytes 1572868
  38.6 4.4 %collective-permute-start.3 = (bf16[1024,256]{1,0:T(8,128)(2,1)S(1)}, bf16[1024,256]{1,0:T(8,128)(2,1)S(1)}, u32[]{:S(2)}, u32[]{:S(2)}) collective-permute-start(bf16[1024,256]{1,0:T(8,128)(2,1)S(1)} %bitcast.143), channel_id=1, source_target_pairs={{0,1},{1,0},{2,3},{3,2},{4,5},{5,4},{6,7},{7,6},{8,9},{9,8},{10,11... | collective-permute-start | bytes 1572872 | tf_op jit(solution)/shard_map/ppermute | solution.py:263
  40.4 13.7 %collective-permute-start.2 = (bf16[1024,256]{1,0:T(8,128)(2,1)S(1)}, bf16[1024,256]{1,0:T(8,128)(2,1)}, u32[]{:S(2)}, u32[]{:S(2)}) collective-permute-start(bf16[1024,256]{1,0:T(8,128)(2,1)S(1)} %bitcast.144), channel_id=1, source_target_pairs={{0,4},{4,0},{1,5},{5,1},{2,6},{6,2},{3,7},{7,3},{8,12},{12,8},{9,1... | collective-permute-start | bytes 1572872 | tf_op jit(solution)/shard_map/ppermute | solution.py:267
  43.0 19.3 %copy-start.2 = (bf16[16,64,128]{2,1,0:T(8,128)(2,1)}, bf16[16,64,128]{2,1,0:T(8,128)(2,1)S(1)}, u32[]{:S(2)}) copy-start(bf16[16,64,128]{2,1,0:T(8,128)(2,1)S(1)} %slice.62) | copy-start | bytes 786436
  43.0 5.6 %copy-start.17 = (bf16[1024,256]{1,0:T(8,128)(2,1)}, bf16[1024,256]{1,0:T(8,128)(2,1)S(1)}, u32[]{:S(2)}) copy-start(bf16[1024,256]{1,0:T(8,128)(2,1)S(1)} %collective-permute-done.3.refs_2_.kv1) | copy-start | bytes 1572868
  43.0 11.9 %copy-start.29 = (bf16[1,128,2048]{1,2,0:T(8,128)(2,1)S(1)}, bf16[1,128,2048]{1,2,0:T(8,128)(2,1)}, u32[]{:S(2)}) copy-start(bf16[1,128,2048]{1,2,0:T(8,128)(2,1)} %copy.31) | copy-start | bytes 1572868
  54.1 8.2 %collective-permute-start.4 = (bf16[1024,256]{1,0:T(8,128)(2,1)}, bf16[1024,256]{1,0:T(8,128)(2,1)S(1)}, u32[]{:S(2)}, u32[]{:S(2)}) collective-permute-start(bf16[1024,256]{1,0:T(8,128)(2,1)} %collective-permute-done.2.refs_1_.kv2), channel_id=1, source_target_pairs={{0,1},{1,0},{2,3},{3,2},{4,5},{5,4},{6,7},{7,6},{8,9},{9,8},{10,11... | collective-permute-start | bytes 1572872 | tf_op jit(solution)/shard_map/ppermute | solution.py:263
  55.8 4.7 %collective-permute-start.10 = (bf16[128,1024]{1,0:T(8,128)(2,1)}, bf16[128,1024]{1,0:T(8,128)(2,1)}, u32[]{:S(2)}, u32[]{:S(2)}) collective-permute-start(bf16[128,1024]{1,0:T(8,128)(2,1)} %bitcast.30), channel_id=1, source_target_pairs={{0,1},{1,0},{2,3},{3,2},{4,5},{5,4},{6,7},{7,6},{8,9},{9,8},{10,11... | collective-permute-start | bytes 786440 | tf_op jit(solution)/shard_map/ppermute | solution.py:263
  56.6 18.7 %collective-permute-start.7 = (bf16[16,64,256]{2,1,0:T(8,128)(2,1)S(1)}, bf16[16,64,256]{2,1,0:T(8,128)(2,1)S(1)}, u32[]{:S(2)}, u32[]{:S(2)}) collective-permute-start(bf16[16,64,256]{2,1,0:T(8,128)(2,1)S(1)} %get-tuple-element.61.refs_0_), channel_id=1, source_target_pairs={{0,6},{2,4},{4,2},{6,0},{1,7},{3,5},{5,3},{7,1},{8,14},{10,12},{12... | collective-permute-start | bytes 1572872 | tf_op jit(solution)/shard_map/ppermute | solution.py:327
  59.1 17.0 %collective-permute-start.6 = (bf16[16,64,256]{2,1,0:T(8,128)(2,1)S(1)}, bf16[16,64,256]{2,1,0:T(8,128)(2,1)S(1)}, u32[]{:S(2)}, u32[]{:S(2)}) collective-permute-start(bf16[16,64,256]{2,1,0:T(8,128)(2,1)S(1)} %get-tuple-element.61.refs_0_), channel_id=1, source_target_pairs={{0,4},{2,6},{4,0},{6,2},{1,5},{3,7},{5,1},{7,3},{8,12},{10,14},{12... | collective-permute-start | bytes 1572872 | tf_op jit(solution)/shard_map/ppermute | solution.py:327
  59.1 23.8 %collective-permute-start.5 = (bf16[16,64,256]{2,1,0:T(8,128)(2,1)S(1)}, bf16[16,64,256]{2,1,0:T(8,128)(2,1)S(1)}, u32[]{:S(2)}, u32[]{:S(2)}) collective-permute-start(bf16[16,64,256]{2,1,0:T(8,128)(2,1)S(1)} %get-tuple-element.61.refs_0_), channel_id=1, source_target_pairs={{0,2},{2,0},{4,6},{6,4},{1,3},{3,1},{5,7},{7,5},{8,10},{10,8},{12,... | collective-permute-start | bytes 1572872 | tf_op jit(solution)/shard_map/ppermute | solution.py:327
  62.3 8.3 %copy-start.19 = (bf16[1024,256]{1,0:T(8,128)(2,1)}, bf16[1024,256]{1,0:T(8,128)(2,1)S(1)}, u32[]{:S(2)}) copy-start(bf16[1024,256]{1,0:T(8,128)(2,1)S(1)} %collective-permute-done.4.refs_2_.kv3) | copy-start | bytes 1572868
  62.3 1.2 copy-start.26
  70.6 13.1 %all-to-all-start.1 = ((bf16[16,64,128]{2,1,0:T(8,128)(2,1)}), bf16[16,64,128]{2,1,0:T(8,128)(2,1)S(1)}, u32[]{:S(2)}, u32[]{:S(2)}) async-start(bf16[16,64,128]{2,1,0:T(8,128)(2,1)} %bitcast.14), calls=%async_computation.1 | async-start | bytes 524288 | tf_op jit(solution)/shard_map/all_to_all | solution.py:276
  83.7 1.0 copy-start.7
  84.8 1.0 copy-start.9
  85.8 1.0 copy-start.11
  87.9 1.0 copy-start.28
  89.7 3.6 %collective-permute-start.11 = (f32[128,1024]{1,0:T(8,128)}, f32[128,1024]{1,0:T(8,128)}, u32[]{:S(2)}, u32[]{:S(2)}) collective-permute-start(f32[128,1024]{1,0:T(8,128)} %slice.70), channel_id=1, source_target_pairs={{0,1},{1,0},{2,3},{3,2},{4,5},{5,4},{6,7},{7,6},{8,9},{9,8},{10,11... | collective-permute-start | bytes 1572872 | tf_op jit(solution)/shard_map/ppermute | solution.py:263
  92.4 6.6 %collective-permute-start.8 = (bf16[2,64,1024]{2,1,0:T(8,128)(2,1)}, bf16[2,64,1024]{2,1,0:T(8,128)(2,1)}, u32[]{:S(2)}, u32[]{:S(2)}) collective-permute-start(bf16[2,64,1024]{2,1,0:T(8,128)(2,1)} %reshape.281), channel_id=1, source_target_pairs={{0,1},{1,0},{2,3},{3,2},{4,5},{5,4},{6,7},{7,6},{8,9},{9,8},{10,11... | collective-permute-start | bytes 786440 | tf_op jit(solution)/shard_map/ppermute | solution.py:263
  95.3 11.9 %all-to-all-start.2 = ((bf16[16,64,128]{2,1,0:T(8,128)(2,1)}), bf16[16,64,128]{2,1,0:T(8,128)(2,1)S(1)}, u32[]{:S(2)}, u32[]{:S(2)}) async-start(bf16[16,64,128]{2,1,0:T(8,128)(2,1)} %bitcast.39), calls=%async_computation.2 | async-start | bytes 524288 | tf_op jit(solution)/shard_map/all_to_all | solution.py:276
  99.0 8.3 %copy-start.3 = (bf16[16,64,128]{2,1,0:T(8,128)(2,1)S(1)}, bf16[16,64,128]{2,1,0:T(8,128)(2,1)}, u32[]{:S(2)}) copy-start(bf16[16,64,128]{2,1,0:T(8,128)(2,1)} %copy-done.2) | copy-start | bytes 786436
  107.3 12.6 %collective-permute-start.13 = (bf16[1024,256]{1,0:T(8,128)(2,1)S(1)}, bf16[1024,256]{1,0:T(8,128)(2,1)}, u32[]{:S(2)}, u32[]{:S(2)}) collective-permute-start(bf16[1024,256]{1,0:T(8,128)(2,1)S(1)} %pad_maximum_fusion.6.refs_2_), channel_id=1, source_target_pairs={{0,4},{4,0},{1,5},{5,1},{2,6},{6,2},{3,7},{7,3},{8,12},{12,8},{9,1... | collective-permute-start | bytes 1572872 | tf_op jit(solution)/shard_map/ppermute | solution.py:267
  110.5 5.0 %collective-permute-start.15 = (f32[2,1024]{1,0:T(2,128)S(1)}, f32[2,1024]{1,0:T(2,128)S(1)}, u32[]{:S(2)}, u32[]{:S(2)}) collective-permute-start(f32[2,1024]{1,0:T(2,128)S(1)} %pad_maximum_fusion.14), channel_id=1, source_target_pairs={{0,1},{1,0},{2,3},{3,2},{4,5},{5,4},{6,7},{7,6},{8,9},{9,8},{10,11... | collective-permute-start | bytes 24584 | tf_op jit(solution)/shard_map/ppermute | solution.py:263
  111.8 33.3 %collective-permute-start.12 = (bf16[1024,256]{1,0:T(8,128)(2,1)S(1)}, bf16[1024,256]{1,0:T(8,128)(2,1)S(1)}, u32[]{:S(2)}, u32[]{:S(2)}) collective-permute-start(bf16[1024,256]{1,0:T(8,128)(2,1)S(1)} %pad_maximum_fusion.6.refs_2_), channel_id=1, source_target_pairs={{0,1},{1,0},{2,3},{3,2},{4,5},{5,4},{6,7},{7,6},{8,9},{9,8},{10,11... | collective-permute-start | bytes 1572872 | tf_op jit(solution)/shard_map/ppermute | solution.py:263
  111.9 49.1 %collective-permute-start.17 = (bf16[16,64,256]{2,1,0:T(8,128)(2,1)}, bf16[16,64,256]{2,1,0:T(8,128)(2,1)S(1)}, u32[]{:S(2)}, u32[]{:S(2)}) collective-permute-start(bf16[16,64,256]{2,1,0:T(8,128)(2,1)} %copy-done.24), channel_id=1, source_target_pairs={{0,2},{2,0},{4,6},{6,4},{1,3},{3,1},{5,7},{7,5},{8,10},{10,8},{12,... | collective-permute-start | bytes 1572872 | tf_op jit(solution)/shard_map/ppermute | solution.py:327
  115.5 45.5 %collective-permute-start.18 = (bf16[16,64,256]{2,1,0:T(8,128)(2,1)}, bf16[16,64,256]{2,1,0:T(8,128)(2,1)S(1)}, u32[]{:S(2)}, u32[]{:S(2)}) collective-permute-start(bf16[16,64,256]{2,1,0:T(8,128)(2,1)} %copy-done.23), channel_id=1, source_target_pairs={{0,4},{2,6},{4,0},{6,2},{1,5},{3,7},{5,1},{7,3},{8,12},{10,14},{12... | collective-permute-start | bytes 1572872 | tf_op jit(solution)/shard_map/ppermute | solution.py:327
  116.2 26.5 %collective-permute-start.16 = (f32[4,1024]{1,0:T(4,128)S(1)}, f32[4,1024]{1,0:T(4,128)S(1)}, u32[]{:S(2)}, u32[]{:S(2)}) collective-permute-start(f32[4,1024]{1,0:T(4,128)S(1)} %pad_maximum_fusion.13), channel_id=1, source_target_pairs={{0,4},{4,0},{1,5},{5,1},{2,6},{6,2},{3,7},{7,3},{8,12},{12,8},{9,1... | collective-permute-start | bytes 49160 | tf_op jit(solution)/shard_map/ppermute | solution.py:267
  119.9 25.2 %collective-permute-start.14 = (bf16[1024,256]{1,0:T(8,128)(2,1)}, bf16[1024,256]{1,0:T(8,128)(2,1)S(1)}, u32[]{:S(2)}, u32[]{:S(2)}) collective-permute-start(bf16[1024,256]{1,0:T(8,128)(2,1)} %collective-permute-done.13.refs_4_), channel_id=1, source_target_pairs={{0,1},{1,0},{2,3},{3,2},{4,5},{5,4},{6,7},{7,6},{8,9},{9,8},{10,11... | collective-permute-start | bytes 1572872 | tf_op jit(solution)/shard_map/ppermute | solution.py:263
  124.7 1.0 copy-start.15
  126.4 1.0 copy-start.18
  127.5 1.0 copy-start.20
  128.5 14.1 %copy-start.22 = (bf16[16,64,256]{2,1,0:T(8,128)(2,1)S(1)}, bf16[16,64,256]{2,1,0:T(8,128)(2,1)}, u32[]{:S(2)}) copy-start(bf16[16,64,256]{2,1,0:T(8,128)(2,1)} %copy-done.21) | copy-start | bytes 1572868
  142.6 18.3 %collective-permute-start.19 = (bf16[16,64,256]{2,1,0:T(8,128)(2,1)S(1)}, bf16[16,64,256]{2,1,0:T(8,128)(2,1)S(1)}, u32[]{:S(2)}, u32[]{:S(2)}) collective-permute-start(bf16[16,64,256]{2,1,0:T(8,128)(2,1)S(1)} %copy-done.22), channel_id=1, source_target_pairs={{0,6},{2,4},{4,2},{6,0},{1,7},{3,5},{5,3},{7,1},{8,14},{10,12},{12... | collective-permute-start | bytes 1572872 | tf_op jit(solution)/shard_map/ppermute | solution.py:327
  145.1 15.9 %copy-start.5 = (bf16[16,64,256]{2,1,0:T(8,128)(2,1)S(1)}, bf16[16,64,256]{2,1,0:T(8,128)(2,1)}, u32[]{:S(2)}) copy-start(bf16[16,64,256]{2,1,0:T(8,128)(2,1)} %copy-done.4) | copy-start | bytes 1572868
  162.6 5.3 %copy-start.13 = (bf16[2,2,64,1024]{3,2,1,0:T(8,128)(2,1)S(1)}, bf16[2,2,64,1024]{3,2,1,0:T(8,128)(2,1)}, u32[]{:S(2)}) copy-start(bf16[2,2,64,1024]{3,2,1,0:T(8,128)(2,1)} %copy-done.12) | copy-start | bytes 1572868
  162.6 23.0 %all-to-all-start.3 = ((bf16[16,64,640]{2,1,0:T(8,128)(2,1)}), bf16[16,64,640]{2,1,0:T(8,128)(2,1)}, u32[]{:S(2)}, u32[]{:S(2)}) async-start(bf16[16,64,640]{2,1,0:T(8,128)(2,1)} %pad_maximum_fusion.1), calls=%async_computation.3 | async-start | bytes 2621440 | tf_op jit(solution)/shard_map/all_to_all | solution.py:276
  168.7 3.3 %collective-permute-start.9 = (bf16[2,64,1024]{2,1,0:T(8,128)(2,1)S(1)}, bf16[2,64,1024]{2,1,0:T(8,128)(2,1)S(1)}, u32[]{:S(2)}, u32[]{:S(2)}) collective-permute-start(bf16[2,64,1024]{2,1,0:T(8,128)(2,1)S(1)} %dynamic-slice_bitcast_fusion.2), channel_id=1, source_target_pairs={{0,1},{1,0},{2,3},{3,2},{4,5},{5,4},{6,7},{7,6},{8,9},{9,8},{10,11... | collective-permute-start | bytes 786440 | tf_op jit(solution)/shard_map/ppermute | solution.py:263
  186.8 6.7 %collective-permute-start.21 = (f32[8,1024]{1,0:T(8,128)S(1)}, f32[8,1024]{1,0:T(8,128)S(1)}, u32[]{:S(2)}, u32[]{:S(2)}) collective-permute-start(f32[8,1024]{1,0:T(8,128)S(1)} %dynamic-slice_bitcast_fusion.3), channel_id=1, source_target_pairs={{0,1},{1,0},{2,3},{3,2},{4,5},{5,4},{6,7},{7,6},{8,9},{9,8},{10,11... | collective-permute-start | bytes 98312 | tf_op jit(solution)/shard_map/ppermute | solution.py:263
  193.4 1.8 collective-permute-start.20
  (12 other events, 9.6 us)

commit v4 on v2

v4 whole, which is shorter than its diff:
```python
import functools

import jax
import jax.numpy as jnp
from jax import lax
from jax.experimental import pallas as pl
from jax.experimental.pallas import tpu as pltpu
from jax.sharding import Mesh, PartitionSpec as P

HEADS = 8
HEAD = 128
SPAN = 64
UNITS = 16
ROWS = UNITS * SPAN
TILE = 256
LOW = -1e30
SCALE = 1.0 / HEAD
F32 = jnp.float32
BF16 = jnp.bfloat16
NT = (((1,), (1,)), ((), ()))
NN = (((1,), (0,)), ((), ()))
TN = (((0,), (0,)), ((), ()))


def dot(a, b, dims):
    return lax.dot_general(a, b, dims, preferred_element_type=F32)


def span_hot(first_span):
    span = lax.broadcasted_iota(jnp.int32, (TILE, HEAD), 0) // SPAN + first_span
    lane = lax.broadcasted_iota(jnp.int32, (TILE, HEAD), 1)
    return (span == lane).astype(F32).astype(BF16)


def query_wide(query, first_span):
    return jnp.concatenate([query * BF16(SCALE), span_hot(first_span)], axis=1)


def spread_bias(bias):
    return jnp.broadcast_to(bias[:, None, :], (UNITS, SPAN, HEAD)).reshape(ROWS, HEAD).astype(BF16)


def fill_keys(chunks, bias_ref, ka_ref):
    for c, kv_ref in enumerate(chunks):
        rows = pl.ds(c * ROWS, ROWS)
        ka_ref[rows, :HEAD] = kv_ref[:, :HEAD]
        ka_ref[rows, HEAD:] = spread_bias(bias_ref[c * UNITS : (c + 1) * UNITS, :])


def later_in_span():
    key = lax.broadcasted_iota(jnp.int32, (TILE, TILE), 0)
    query = lax.broadcasted_iota(jnp.int32, (TILE, TILE), 1)
    return (key // SPAN == query // SPAN) & (key > query)


def forward_body(q_ref, kv0, kv1, kv2, kv3, bias_ref, att_ref, lse_ref, ka_ref, s_ref):
    step = pl.program_id(0)
    chunks = (kv0, kv1, kv2, kv3)

    @pl.when(step == 0)
    def _():
        fill_keys(chunks, bias_ref, ka_ref)

    qa = query_wide(q_ref[...], step * (TILE // SPAN))
    top = None
    for c in range(4):
        rows = pl.ds(c * ROWS, ROWS)
        s_ref[rows, :] = dot(ka_ref[rows, :], qa, NT)
        if c == 0:
            own = pl.ds(pl.multiple_of(step * TILE, TILE), TILE)
            s_ref[own, :] = jnp.where(later_in_span(), LOW, s_ref[own, :])
        chunk_top = jnp.max(s_ref[rows, :], axis=0, keepdims=True)
        top = chunk_top if c == 0 else jnp.maximum(top, chunk_top)
    total = jnp.zeros((1, TILE), F32)
    out = jnp.zeros((HEAD, TILE), F32)
    for c, kv_ref in enumerate(chunks):
        weights = jnp.exp(s_ref[pl.ds(c * ROWS, ROWS), :] - top)
        total += jnp.sum(weights, axis=0, keepdims=True)
        out += dot(kv_ref[:, HEAD:], weights.astype(BF16), TN)
    att_ref[...] = (out / total).T.astype(BF16)
    lse_ref[...] = top + jnp.log(total)


def tile_spec(cols):
    return pl.BlockSpec((TILE, cols), lambda i: (i, 0))


def row_spec(rows):
    return pl.BlockSpec((rows, TILE), lambda i: (0, i))


def cost(matmuls, pairs):
    return pl.CostEstimate(
        flops=matmuls * 2 * pairs * 2 * HEAD, bytes_accessed=4 << 20, transcendentals=pairs
    )


def once(*shape):
    return pl.BlockSpec(shape, lambda i: (0,) * len(shape), pipeline_mode=pl.Buffered(1))


def forward(q, kvs, bias):
    return pl.pallas_call(
        forward_body,
        out_shape=[
            jax.ShapeDtypeStruct((ROWS, HEAD), BF16),
            jax.ShapeDtypeStruct((1, ROWS), F32),
        ],
        grid=(ROWS // TILE,),
        in_specs=[tile_spec(HEAD), *[once(ROWS, 2 * HEAD)] * 4, once(4 * UNITS, HEAD)],
        out_specs=[tile_spec(HEAD), row_spec(1)],
        scratch_shapes=[
            pltpu.VMEM((4 * ROWS, 2 * HEAD), BF16),
            pltpu.VMEM((4 * ROWS, TILE), F32),
        ],
        cost_estimate=cost(2, 4 * ROWS * ROWS),
        compiler_params=pltpu.CompilerParams(vmem_limit_bytes=24 << 20),
        name="forward",
    )(q, *kvs, bias)


def delta_body(g_ref, att_ref, d_ref):
    product = g_ref[...].astype(F32) * att_ref[...].astype(F32)
    d_ref[...] = jnp.sum(product.T, axis=0, keepdims=True)


def row_delta(g, att):
    return pl.pallas_call(
        delta_body,
        out_shape=jax.ShapeDtypeStruct((1, ROWS), F32),
        grid=(ROWS // TILE,),
        in_specs=[tile_spec(HEAD)] * 2,
        out_specs=row_spec(1),
        cost_estimate=pl.CostEstimate(flops=0, bytes_accessed=1 << 20, transcendentals=0),
        name="delta",
    )(g, att)


def query_body(q_ref, g_ref, lse_ref, delta_ref, kv0, kv1, kv2, kv3, bias_ref, dq_ref, ka_ref, s_ref):
    step = pl.program_id(0)
    chunks = (kv0, kv1, kv2, kv3)

    @pl.when(step == 0)
    def _():
        fill_keys(chunks, bias_ref, ka_ref)

    qa = query_wide(q_ref[...], step * (TILE // SPAN))
    g = g_ref[...]
    lse = lse_ref[...]
    delta = delta_ref[...]
    total = jnp.zeros((HEAD, TILE), F32)
    for c, kv_ref in enumerate(chunks):
        s_ref[...] = dot(ka_ref[pl.ds(c * ROWS, ROWS), :], qa, NT)
        if c == 0:
            rows = pl.ds(pl.multiple_of(step * TILE, TILE), TILE)
            s_ref[rows, :] = jnp.where(later_in_span(), LOW, s_ref[rows, :])
        prob = jnp.exp(s_ref[...] - lse)
        dprob = dot(kv_ref[:, HEAD:], g, NT)
        ds = (prob * (dprob - delta)).astype(BF16)
        total += dot(kv_ref[:, :HEAD], ds, TN)
    dq_ref[...] = (total * SCALE).T.astype(BF16)


def query_grad(q, g, lse, delta, kvs, bias):
    return pl.pallas_call(
        query_body,
        out_shape=jax.ShapeDtypeStruct((ROWS, HEAD), BF16),
        grid=(ROWS // TILE,),
        in_specs=[
            tile_spec(HEAD),
            tile_spec(HEAD),
            row_spec(1),
            row_spec(1),
            *[once(ROWS, 2 * HEAD)] * 4,
            once(4 * UNITS, HEAD),
        ],
        out_specs=tile_spec(HEAD),
        scratch_shapes=[
            pltpu.VMEM((4 * ROWS, 2 * HEAD), BF16),
            pltpu.VMEM((ROWS, TILE), F32),
        ],
        cost_estimate=cost(3, 4 * ROWS * ROWS),
        compiler_params=pltpu.CompilerParams(vmem_limit_bytes=16 << 20),
        name="query_grad",
    )(q, g, lse, delta, *kvs, bias)


def key_body(*refs):
    kv_ref, bias_ref = refs[:2]
    qs, gs, stats = refs[2:6], refs[6:10], refs[10]
    dk_ref, dv_ref, ka_ref, s_ref, dk_acc, dv_acc = refs[11:]
    ka_ref[:, :HEAD] = kv_ref[:, :HEAD]
    ka_ref[:, HEAD:] = spread_bias(bias_ref[:UNITS, :])
    dk_acc[...] = jnp.zeros_like(dk_acc)
    dv_acc[...] = jnp.zeros_like(dv_acc)
    for c in range(4):

        def tile(i, _, c=c):
            rows = pl.ds(pl.multiple_of(i * TILE, TILE), TILE)
            q = qs[c][rows, :]
            g = gs[c][rows, :]
            lse = stats[2 * c : 2 * c + 1, rows]
            delta = stats[2 * c + 1 : 2 * c + 2, rows]
            qa = query_wide(q, i * (TILE // SPAN) + c * UNITS)
            s_ref[...] = dot(ka_ref[...], qa, NT)
            if c == 0:
                s_ref[rows, :] = jnp.where(later_in_span(), LOW, s_ref[rows, :])
            prob = jnp.exp(s_ref[...] - lse)
            dprob = dot(kv_ref[:, HEAD:], g, NT)
            ds = (prob * (dprob - delta)).astype(BF16)
            dv_acc[...] += dot(prob.astype(BF16), g, NN)
            dk_acc[...] += dot(ds, q, NN)
            return 0

        lax.fori_loop(0, ROWS // TILE, tile, 0)
    dk_ref[...] = (dk_acc[...] * SCALE).astype(BF16)
    dv_ref[...] = dv_acc[...].astype(BF16)


def key_grad(kv, bias, qs, gs, stats):
    return pl.pallas_call(
        key_body,
        out_shape=[jax.ShapeDtypeStruct((ROWS, HEAD), BF16)] * 2,
        grid=(1,),
        in_specs=[
            once(ROWS, 2 * HEAD),
            once(4 * UNITS, HEAD),
            *[once(ROWS, HEAD)] * 8,
            once(8, ROWS),
        ],
        out_specs=[once(ROWS, HEAD)] * 2,
        scratch_shapes=[
            pltpu.VMEM((ROWS, 2 * HEAD), BF16),
            pltpu.VMEM((ROWS, TILE), F32),
            pltpu.VMEM((ROWS, HEAD), F32),
            pltpu.VMEM((ROWS, HEAD), F32),
        ],
        cost_estimate=cost(4, 4 * ROWS * ROWS),
        compiler_params=pltpu.CompilerParams(vmem_limit_bytes=16 << 20),
        name="key_grad",
    )(kv, bias, *qs, *gs, stats)


ZY = ("z", "y")
CHIPS = ("z", "y", "xl", "xh")
SWAP = [(0, 1), (1, 0)]


def other_core(x):
    return lax.ppermute(x, "core", SWAP)


def other_chip(x):
    return lax.ppermute(x, "xl", SWAP)


def everyone(x):
    far = other_chip(x)
    return x, other_core(x), far, other_core(far)


def exchange(x, axes):
    return lax.all_to_all(x, axes, 0, 0, tiled=True)


def in_order(first, own, peer):
    return jnp.stack([jnp.where(first, own, peer), jnp.where(first, peer, own)])


def span_bias(span_order, block_mask, xl, core):
    count = span_order.shape[0]
    row = jnp.arange(count, dtype=jnp.int32)
    owner, unit = row // UNITS, row % UNITS
    row_xl = xl ^ (owner // 2)
    half = core ^ (owner % 2) ^ ((unit // 4 + unit % 4) % 2)
    storage = 2 * (2 * unit + row_xl) + half
    held = (storage[:, None] == jnp.arange(count, dtype=jnp.int32)[None, :]).astype(jnp.int32)
    position = jnp.sum(held * span_order[None, :], axis=1)
    hot = (position[:, None] == jnp.arange(count, dtype=jnp.int32)[None, :]).astype(F32)
    pairs = jnp.dot(hot, jnp.dot(block_mask.astype(F32).T, hot.T))
    allowed = (pairs > 0.5) & (position[:, None] <= position[None, :])
    bias = jnp.where(allowed, 0.0, LOW).astype(F32)
    return jnp.pad(bias, ((0, 0), (0, HEAD - count)))


def by_unit(rows, kinds):
    split = rows.reshape(2, SPAN, kinds, HEADS, HEAD)
    return split.transpose(0, 3, 1, 2, 4).reshape(UNITS, SPAN, kinds * HEAD)


def by_row(blocks, kinds):
    split = blocks.reshape(2, HEADS, SPAN, kinds, HEAD)
    return split.transpose(0, 2, 3, 1, 4).reshape(2, SPAN, kinds * HEADS * HEAD)


def side_by_side(first, own, peer):
    return jnp.concatenate([jnp.where(first, own, peer), jnp.where(first, peer, own)], axis=-1)


def to_narrow(x):
    return jnp.concatenate(jnp.split(x, 2, axis=-1), axis=-2)


def from_narrow(x):
    return jnp.concatenate(jnp.split(x, 2, axis=-2), axis=-1)


def across(x):
    return lax.ppermute(x, ("xl", "xh"), [(k, k ^ 3) for k in range(4)])


def weight_body(xl_ref, own_ref, other_ref, out_ref):
    for flip, part in enumerate((own_ref, other_ref)):
        for c in range(2):
            rows = part[:, c * 32 : (c + 1) * 32, :]
            out_ref[:, xl_ref[0] ^ flip, :, c * 512 : (c + 1) * 512] = rows


def weight_whole(xl, own, other):
    return pl.pallas_call(
        weight_body,
        out_shape=jax.ShapeDtypeStruct((UNITS, 2, 32, 1024), BF16),
        grid=(1,),
        in_specs=[pl.BlockSpec(memory_space=pltpu.SMEM)] + [once(UNITS, SPAN, 512)] * 2,
        out_specs=once(UNITS, 2, 32, 1024),
        cost_estimate=pl.CostEstimate(flops=0, bytes_accessed=4 << 20, transcendentals=0),
        compiler_params=pltpu.CompilerParams(vmem_limit_bytes=12 << 20),
        name="weight_whole",
    )(xl, own, other)


def term_body(xl_ref, att_ref, up_ref, own_ref, other_ref, sum_ref):
    for c in range(2):
        cols = slice(c * 512, (c + 1) * 512)
        sum_ref[...] = dot(att_ref[...], up_ref[:, cols], TN).astype(BF16).reshape(sum_ref.shape)
        for flip, part in enumerate((own_ref, other_ref)):
            part[:, c * 32 : (c + 1) * 32, :] = sum_ref[:, xl_ref[0] ^ flip]


def weight_terms(xl, att, up):
    return pl.pallas_call(
        term_body,
        out_shape=[jax.ShapeDtypeStruct((UNITS, SPAN, 512), BF16)] * 2,
        grid=(1,),
        in_specs=[pl.BlockSpec(memory_space=pltpu.SMEM), once(256, 1024), once(256, 1024)],
        out_specs=[once(UNITS, SPAN, 512)] * 2,
        scratch_shapes=[pltpu.VMEM((UNITS, 2, 32, 512), BF16)],
        cost_estimate=pl.CostEstimate(
            flops=2 * 256 * 1024 * 1024, bytes_accessed=4 << 20, transcendentals=0
        ),
        compiler_params=pltpu.CompilerParams(vmem_limit_bytes=16 << 20),
        name="weight_terms",
    )(xl, att, up)


def local(query_states, key_states, value_states, span_order, block_mask, output_weight, upstream):
    z, y, xl, xh, core = (lax.axis_index(a) for a in ("z", "y", "xl", "xh", "core"))
    first_core = core == 0
    half = core ^ ((z + y) % 2)
    cols = output_weight.shape[1] // 2

    def mine(x, axis):
        return lax.dynamic_index_in_dim(x, core, axis, False)

    def theirs(x, axis):
        return lax.dynamic_index_in_dim(x, 1 - core, axis, False)

    def share(rows):
        halves = rows.reshape(2, SPAN, -1)
        own = lax.dynamic_index_in_dim(halves, half, 0, False)
        peer = other_core(lax.dynamic_index_in_dim(halves, 1 - half, 0, False))
        return in_order(first_core, own, peer)

    def unshare(both):
        own = mine(both, 0)
        peer = other_core(theirs(both, 0))
        return in_order(half == 0, own, peer).reshape(2 * SPAN, -1)

    weight_cols = output_weight.reshape(-1, 2, cols)
    weight_rows = in_order(first_core, mine(weight_cols, 1), other_core(theirs(weight_cols, 1)))
    weight_rows = weight_rows.reshape(-1, cols)
    weight_rows = in_order(xh == 0, weight_rows, lax.ppermute(weight_rows, "xh", SWAP))
    weight_rows = to_narrow(weight_rows.reshape(-1, cols))
    copies = jnp.broadcast_to(weight_rows[None], (UNITS, *weight_rows.shape))
    states = share(jnp.concatenate([query_states[0], key_states[0], value_states[0]], axis=1))
    blocks = exchange(jnp.concatenate([by_unit(states, 3), copies], axis=2), ZY)
    q = blocks[:, :, :HEAD].reshape(ROWS, HEAD)
    own_kv = blocks[:, :, HEAD : 3 * HEAD].reshape(ROWS, 2 * HEAD)
    far_kv = other_chip(own_kv)
    weight_own = blocks[:, :, 3 * HEAD :]
    weight_other = across(weight_own)
    kvs = (own_kv, other_core(own_kv), far_kv, other_core(far_kv))
    bias = span_bias(span_order, block_mask, xl, core)

    up_cols = upstream[0].reshape(2 * SPAN, 2, cols)
    up = in_order(first_core, mine(up_cols, 1), other_core(theirs(up_cols, 1)))
    up = up.reshape(2, 2, SPAN, cols)
    up = in_order(half == 0, up[:, 0], up[:, 1]).reshape(4 * SPAN, cols)

    attended, lse = forward(q, kvs, bias)

    place, lse = lax.optimization_barrier((xl.reshape(1), lse))
    weight = weight_whole(place, weight_own, weight_other).reshape(HEADS * HEAD, cols)
    grad_rows = dot(up, weight, NT)
    grad_rows = grad_rows[: 2 * SPAN] + other_core(grad_rows[2 * SPAN :])
    grad_rows = grad_rows.astype(BF16).reshape(2, SPAN, -1)
    crossing = jnp.concatenate(
        [attended.reshape(UNITS, SPAN, HEAD), by_unit(grad_rows, 1)], axis=2
    )
    crossed = exchange(crossing, ZY)
    qs = everyone(q)
    g = crossed[:, :, HEAD:].reshape(ROWS, HEAD)
    delta = row_delta(g, attended)
    stats = jnp.concatenate([lse, delta], axis=0)
    stats = jnp.concatenate([stats, other_core(stats)], axis=0)
    stats_far = other_chip(stats)
    gs = everyone(g)

    attended_rows = by_row(crossed[:, :, :HEAD], 1)
    attended_rows = jnp.stack([attended_rows, other_core(attended_rows)]).reshape(4 * SPAN, -1)
    place, stats_far = lax.optimization_barrier((xl.reshape(1), stats_far))
    stats = jnp.concatenate([stats, stats_far], axis=0)
    term_own, term_sent = weight_terms(place, attended_rows, up)
    term_other = across(term_sent)
    projected = dot(attended_rows, weight, NN).astype(BF16).reshape(2, 2, SPAN, cols)
    own, peer = mine(projected, 1), other_core(theirs(projected, 1))
    own = in_order(half == 0, own[0], own[1]).reshape(2 * SPAN, cols)
    peer = in_order(half == 0, peer[1], peer[0]).reshape(2 * SPAN, cols)
    projected = side_by_side(first_core, own, peer)

    query_out = query_grad(q, g, lse, delta, kvs, bias)
    key_out, value_out = key_grad(own_kv, bias, qs, gs, stats)
    term = (term_own.astype(F32) + term_other.astype(F32)).astype(BF16)
    grads = [x.reshape(UNITS, SPAN, HEAD) for x in (query_out, key_out, value_out)]
    grads = exchange(jnp.concatenate([*grads, term], axis=2), ZY)
    summed = jnp.sum(grads[:, :, 3 * HEAD :].astype(F32), axis=0)
    summed = from_narrow(summed).reshape(2, 16, cols)
    partner = lax.ppermute(lax.dynamic_index_in_dim(summed, 1 - xh, 0, False), "xh", SWAP)
    summed = (lax.dynamic_index_in_dim(summed, xh, 0, False) + partner).reshape(2, -1, cols)
    grads = grads[:, :, : 3 * HEAD]
    weight_gradient = side_by_side(first_core, mine(summed, 0), other_core(theirs(summed, 0)))
    grads = unshare(by_row(grads, 3))
    query_gradient, key_gradient, value_gradient = jnp.split(grads, 3, axis=1)
    return (
        projected[None],
        query_gradient[None],
        key_gradient[None],
        value_gradient[None],
        weight_gradient,
    )


def solution(mesh):
    axes = ("z", "y", "xl", "xh", "core")
    fine = Mesh(mesh.devices.reshape(4, 4, 2, 2, 2), axes)
    rows = P(("xh", "core"), ("z", "y", "xl"), None)
    return jax.shard_map(
        local,
        mesh=fine,
        in_specs=(rows, rows, rows, P(), P(), P(axes, None), rows),
        out_specs=(rows, rows, rows, rows, P(axes, None)),
        check_vma=False,
    )
```

time: 203 us -> 194 us (0.956)
  blocking collectives: 0 us -> 32.1 us
  starting transfers between devices: 60.4 us -> 31.8 us
  waiting for transfers between devices: 64.2 us -> 54.7 us
  matrix products: 5.01 us -> 1.76 us
    all_to_all x0 -> x1, blocking collectives: none -> 32.1 us  [exchange(): return lax.all_to_all(x, axes, 0, 0, tiled=True)]
    ppermute x6 -> x4, waiting for transfers between devices: 36.7 us -> 4.65 us  [the longest x2 2.57 us: across(): return lax.ppermute(x, ('xl', 'xh'), [(k, k ^ 3) for k in range(4)])]
    all_to_all x6 -> x2, starting transfers between devices: 32.7 us -> 8.13 us  [exchange(): return lax.all_to_all(x, axes, 0, 0, tiled=True)]
    all_to_all x6 -> x2, waiting for transfers between devices: 22.2 us -> 38.4 us  [exchange(): return lax.all_to_all(x, axes, 0, 0, tiled=True)]
    ppermute x16 -> x15, waiting for transfers between devices: 0.04 us -> 5.3 us  [other_core(): return lax.ppermute(x, 'core', SWAP)]
    slice x3 -> x5, local copies, waits for them, and re-layouts: 1.01 us -> 5.2 us  [the longest x1 1.86 us: local(): q = blocks[:, :, :HEAD].reshape(ROWS, HEAD)]
    ppermute x16 -> x15, starting transfers between devices: 19.3 us -> 15.8 us  [other_core(): return lax.ppermute(x, 'core', SWAP)]
    dot_general x3 -> x2, matrix products: 4.7 us -> 1.45 us  [dot(): return lax.dot_general(a, b, dims, preferred_element_type=F32)]
  transfers between devices with their start and end apart: 32 -> 25, of which waited for: 11 -> 13; matrix products, arithmetic and copies ran while one was open for 15% -> 10% of each run, Pallas kernels for 11% -> 20%
where the time goes in v4:
time: 194 us; the launch traced here: 193 us
  waiting for transfers between devices  54.7 us (28%)
  Pallas kernels  39.5 us (20%)
  blocking collectives  32.1 us (17%)
  starting transfers between devices  31.8 us (16%)
  local copies, waits for them, and re-layouts  20.1 us (10%)
  other arithmetic  12.1 us (6%)
    all_to_all x2, waiting for transfers between devices, exchange(): return lax.all_to_all(x, axes, 0, 0, tiled=True)  38.4 us
    all_to_all x1, blocking collectives, exchange(): return lax.all_to_all(x, axes, 0, 0, tiled=True)  32.1 us
    pallas_call x1, Pallas kernels, key_grad(): pl.pallas_call(key_body, out_shape=[jax.ShapeDtypeStruct((ROWS, HEAD), BF...  16 us
    ppermute x15, starting transfers between devices, other_core(): return lax.ppermute(x, 'core', SWAP)  15.8 us
    pallas_call x1, Pallas kernels, query_grad(): pl.pallas_call(query_body, out_shape=jax.ShapeDtypeStruct((ROWS, HEAD), B...  9.93 us
    pallas_call x1, Pallas kernels, forward(): pl.pallas_call(forward_body, out_shape=[jax.ShapeDtypeStruct((ROWS, HEAD)...  9.41 us
    all_to_all x2, starting transfers between devices, exchange(): return lax.all_to_all(x, axes, 0, 0, tiled=True)  8.13 us
    ppermute x4, waiting for transfers between devices, other_chip(): return lax.ppermute(x, 'xl', SWAP)  6.42 us
  transfers between devices with their start and end apart: 25, of which 13 were waited for; matrix products, arithmetic and copies ran while one was open for 10% of the time, Pallas kernels for 20%

profile of v4, /device:TPU:1, one launch (start us, length us, event | category | flops | bytes accessed | tf_op | source)
XLA Modules:
  0.0 193.4 jit_solution(965070461787548291)
XLA Ops:
  1.4 1.4 collective-permute-start.1
  2.8 1.2 pad_maximum_fusion.2
  4.7 2.9 %collective-permute-start.2 = (bf16[16,1024]{1,0:T(8,128)(2,1)S(1)}, bf16[16,1024]{1,0:T(8,128)(2,1)S(1)}, u32[]{:S(2)}, u32[]{:S(2)}) collective-permute-start(bf16[16,1024]{1,0:T(8,128)(2,1)S(1)} %maximum_bitcast_fusion.2), channel_id=1, source_target_pairs={{0,2},{2,0},{1,3},{3,1},{4,6},{6,4},{5,7},{7,5},{8,10},{10,8},{9,1... | collective-permute-start | bytes 98312 | tf_op jit(solution)/shard_map/ppermute | solution.py:382
  8.0 1.0 collective-permute-done.2
  11.3 32.1 %all_to_all.15 = bf16[16,64,896]{2,1,0:T(8,128)(2,1)S(1)} all-to-all(bf16[16,64,896]{2,1,0:T(8,128)(2,1)S(1)} %pad_maximum_fusion), channel_id=1, replica_groups=mesh['z'=4,'y'=4,'xl'=2,'xh'=2,'core'=2] {'z','y'}, dimensions={0} | all-to-all | bytes 3670016 | tf_op jit(solution)/shard_map/all_to_all | solution.py:263
  43.5 1.2 copy-done.14
  45.6 0.9 copy.32
  46.5 2.8 %collective-permute-start.6 = (bf16[128,1024]{1,0:T(8,128)(2,1)}, bf16[128,1024]{1,0:T(8,128)(2,1)}, u32[]{:S(2)}, u32[]{:S(2)}) collective-permute-start(bf16[128,1024]{1,0:T(8,128)(2,1)} %bitcast.20), channel_id=1, source_target_pairs={{0,1},{1,0},{2,3},{3,2},{4,5},{5,4},{6,7},{7,6},{8,9},{9,8},{10,11... | collective-permute-start | bytes 786440 | tf_op jit(solution)/shard_map/ppermute | solution.py:250
  49.6 1.3 slice.66.own_ref
  50.9 1.9 collective-permute-start.7
  52.8 3.3 %collective-permute-done.4.kv2 = bf16[1024,256]{1,0:T(8,128)(2,1)S(1)} collective-permute-done((bf16[1024,256]{1,0:T(8,128)(2,1)S(1)}, bf16[1024,256]{1,0:T(8,128)(2,1)S(1)}, u32[]{:S(2)}, u32[]{:S(2)}) %collective-permute-start.4) | collective-permute-done | bytes 524320 | tf_op jit(solution)/shard_map/ppermute | solution.py:254
  56.1 3.0 %collective-permute-start.5 = (bf16[1024,256]{1,0:T(8,128)(2,1)S(1)}, bf16[1024,256]{1,0:T(8,128)(2,1)}, u32[]{:S(2)}, u32[]{:S(2)}) collective-permute-start(bf16[1024,256]{1,0:T(8,128)(2,1)S(1)} %collective-permute-done.4.kv2), channel_id=1, source_target_pairs={{0,1},{1,0},{2,3},{3,2},{4,5},{5,4},{6,7},{7,6},{8,9},{9,8},{10,11... | collective-permute-start | bytes 1572872 | tf_op jit(solution)/shard_map/ppermute | solution.py:250
  59.4 0.9 copy.31
  60.3 1.1 bitcast_select_fusion.5
  61.5 1.9 slice.62
  63.4 1.0 copy-done.12
  64.4 9.4 %forward.1 = (bf16[1024,128]{1,0:T(8,128)(2,1)S(1)}, f32[1,1024]{1,0:T(1,128)S(1)}) custom-call(bf16[1024,128]{1,0:T(8,128)(2,1)} %bitcast.15.q_ref.refs_2_, bf16[1024,256]{1,0:T(8,128)(2,1)S(1)} %bitcast.158, bf16[1024,256]{1,0:T(8,128)(2,1)} %collective-permute-done.3.kv1, bf16[1024,256]{1,0:T(8,128)(2,1)S(1)} %copy-done.12, ...), custom_call_target="tpu_custom_call" | custom-call | flops 4294967296 | bytes 4194304 | tf_op jit(solution)/shard_map/forward/pallas_call | solution.py:103
  73.9 2.6 %collective-permute-done.7.other_ref = bf16[16,64,512]{2,1,0:T(8,128)(2,1)S(1)} collective-permute-done((bf16[16,64,512]{2,1,0:T(8,128)(2,1)S(1)}, bf16[16,64,512]{2,1,0:T(8,128)(2,1)S(1)}, u32[]{:S(2)}, u32[]{:S(2)}) %collective-permute-start.7) | collective-permute-done | bytes 1048608 | tf_op jit(solution)/shard_map/ppermute | solution.py:309
  76.4 1.0 copy-done.2
  77.5 1.2 copy-done.3
  79.7 1.4 collective-permute-start.8
  81.1 1.5 collective-permute-done.8
  82.8 0.9 pad_maximum_fusion.5
  83.7 3.6 %all-to-all-start.1 = ((bf16[16,64,256]{2,1,0:T(8,128)(2,1)}), bf16[16,64,256]{2,1,0:T(8,128)(2,1)S(1)}, u32[]{:S(2)}, u32[]{:S(2)}) async-start(bf16[16,64,256]{2,1,0:T(8,128)(2,1)} %pad_maximum_fusion.5), calls=%async_computation.1 | async-start | bytes 1048576 | tf_op jit(solution)/shard_map/all_to_all | solution.py:263
  87.4 10.9 %all-to-all-done.1 = bf16[16,64,256]{2,1,0:T(8,128)(2,1)S(1)} async-done(((bf16[16,64,256]{2,1,0:T(8,128)(2,1)}), bf16[16,64,256]{2,1,0:T(8,128)(2,1)S(1)}, u32[]{:S(2)}, u32[]{:S(2)}) %all-to-all-start.1) | async-done | bytes 524320 | tf_op jit(solution)/shard_map/all_to_all | solution.py:263
  100.7 1.5 collective-permute-start.9
  102.2 3.1 %delta.1.delta_ref = f32[1,1024]{1,0:T(1,128)} custom-call(bf16[1024,128]{1,0:T(8,128)(2,1)} %bitcast.150, bf16[1024,128]{1,0:T(8,128)(2,1)} %copy-done.5), custom_call_target="tpu_custom_call" | custom-call | bytes 1048576 | tf_op jit(solution)/shard_map/delta/pallas_call | solution.py:128
  106.3 1.1 collective-permute-done.17
  108.5 1.0 collective-permute-start.11
  109.5 1.8 stack_reshape.3
  111.3 3.1 %collective-permute-done.18 = f32[4,1024]{1,0:T(4,128)S(1)} collective-permute-done((f32[4,1024]{1,0:T(4,128)S(1)}, f32[4,1024]{1,0:T(4,128)S(1)}, u32[]{:S(2)}, u32[]{:S(2)}) %collective-permute-start.18) | collective-permute-done | bytes 16416 | tf_op jit(solution)/shard_map/ppermute | solution.py:254
  114.4 1.1 collective-permute-start.14
  115.5 1.1 pad_maximum_fusion.6
  116.6 0.9 weight_terms.1
  117.6 1.9 collective-permute-start.19
  119.8 9.9 %query_grad.1 = bf16[1024,128]{1,0:T(8,128)(2,1)S(1)} custom-call(bf16[1024,128]{1,0:T(8,128)(2,1)} %bitcast.15.q_ref.refs_2_, bf16[1024,128]{1,0:T(8,128)(2,1)S(1)} %bitcast.153, f32[1,1024]{1,0:T(1,128)S(1)} %get-tuple-element.18.lse_ref, f32[1,1024]{1,0:T(1,128)S(1)} %copy-done.10, bf16[1024,256]{1,0:T(8,128)(2,1)S(1)} %bitcast.159, ...), custom_call_target="tpu_custom_call" | custom-call | flops 6442450944 | bytes 4194304 | tf_op jit(solution)/shard_map/query_grad/pallas_call | solution.py:165
  129.8 16.0 %key_grad.1 = (bf16[1024,128]{1,0:T(8,128)(2,1)S(1)}, bf16[1024,128]{1,0:T(8,128)(2,1)S(1)}) custom-call(bf16[1024,256]{1,0:T(8,128)(2,1)S(1)} %bitcast.160, f32[64,128]{1,0:T(8,128)S(1)} %pad.4.bias_ref.refs_1_, bf16[1024,128]{1,0:T(8,128)(2,1)} %bitcast.15.q_ref.refs_2_, bf16[1024,128]{1,0:T(8,128)(2,1)} %collective-permute-done.11.refs_3_, ...), custom_call_target="tpu_custom_call" | custom-call | flops 8589934592 | bytes 4194304 | tf_op jit(solution)/shard_map/key_grad/pallas_call | solution.py:221
  146.1 1.5 pad_maximum_fusion.1
  147.6 4.6 %all-to-all-start.2 = ((bf16[16,64,896]{2,1,0:T(8,128)(2,1)}), bf16[16,64,896]{2,1,0:T(8,128)(2,1)}, u32[]{:S(2)}, u32[]{:S(2)}) async-start(bf16[16,64,896]{2,1,0:T(8,128)(2,1)} %pad_maximum_fusion.1), calls=%async_computation.2 | async-start | bytes 3670016 | tf_op jit(solution)/shard_map/all_to_all | solution.py:263
  153.2 1.3 collective-permute-done.10
  154.6 27.5 %all-to-all-done.2 = bf16[16,64,896]{2,1,0:T(8,128)(2,1)} async-done(((bf16[16,64,896]{2,1,0:T(8,128)(2,1)}), bf16[16,64,896]{2,1,0:T(8,128)(2,1)}, u32[]{:S(2)}, u32[]{:S(2)}) %all-to-all-start.2) | async-done | bytes 1835040 | tf_op jit(solution)/shard_map/all_to_all | solution.py:263
  182.1 1.4 convert_reduce_fusion
  183.7 0.8 maximum_bitcast_fusion.1
  184.5 1.2 slice.73
  186.0 0.9 copy.37
  187.2 1.0 collective-permute-done.21
  188.3 2.2 %collective-permute-start.22 = (f32[8,1024]{1,0:T(8,128)S(1)}, f32[8,1024]{1,0:T(8,128)S(1)}, u32[]{:S(2)}, u32[]{:S(2)}) collective-permute-start(f32[8,1024]{1,0:T(8,128)S(1)} %dynamic-slice_bitcast_fusion.4), channel_id=1, source_target_pairs={{0,1},{1,0},{2,3},{3,2},{4,5},{5,4},{6,7},{7,6},{8,9},{9,8},{10,11... | collective-permute-start | bytes 98312 | tf_op jit(solution)/shard_map/ppermute | solution.py:250
  192.5 0.9 slice_bitcast_fusion
  (116 shorter events, 16.0 us)
Async XLA Ops:
  1.4 2.6 %collective-permute-start.1 = (bf16[8,1024]{1,0:T(8,128)(2,1)S(1)}, bf16[8,1024]{1,0:T(8,128)(2,1)S(1)}, u32[]{:S(2)}, u32[]{:S(2)}) collective-permute-start(bf16[8,1024]{1,0:T(8,128)(2,1)S(1)} %dynamic-slice_bitcast_fusion.5), channel_id=1, source_target_pairs={{0,1},{1,0},{2,3},{3,2},{4,5},{5,4},{6,7},{7,6},{8,9},{9,8},{10,11... | collective-permute-start | bytes 49160 | tf_op jit(solution)/shard_map/ppermute | solution.py:250
  4.7 4.3 %collective-permute-start.2 = (bf16[16,1024]{1,0:T(8,128)(2,1)S(1)}, bf16[16,1024]{1,0:T(8,128)(2,1)S(1)}, u32[]{:S(2)}, u32[]{:S(2)}) collective-permute-start(bf16[16,1024]{1,0:T(8,128)(2,1)S(1)} %maximum_bitcast_fusion.2), channel_id=1, source_target_pairs={{0,2},{2,0},{1,3},{3,1},{4,6},{6,4},{5,7},{7,5},{8,10},{10,8},{9,1... | collective-permute-start | bytes 98312 | tf_op jit(solution)/shard_map/ppermute | solution.py:382
  7.7 1.8 collective-permute-start
  11.3 34.0 %copy-start.16 = (bf16[1,128,2048]{2,1,0:T(8,128)(2,1)S(1)}, bf16[1,128,2048]{2,1,0:T(8,128)(2,1)}, u32[]{:S(2)}) copy-start(bf16[1,128,2048]{2,1,0:T(8,128)(2,1)} %param.13) | copy-start | bytes 1572868
  43.5 1.3 copy-start.14
  43.5 5.9 %copy-start.18 = (s32[64]{0:T(128)S(1)}, s32[64]{0:T(128)}, u32[]{:S(2)}) copy-start(s32[64]{0:T(128)} %param.10) | copy-start | bytes 772
  44.8 18.6 %copy-start.6 = (bf16[16,64,256]{2,1,0:T(8,128)(2,1)}, bf16[16,64,256]{2,1,0:T(8,128)(2,1)S(1)}, u32[]{:S(2)}) copy-start(bf16[16,64,256]{2,1,0:T(8,128)(2,1)S(1)} %slice.63) | copy-start | bytes 1572868
  44.8 11.3 %collective-permute-start.4 = (bf16[1024,256]{1,0:T(8,128)(2,1)S(1)}, bf16[1024,256]{1,0:T(8,128)(2,1)S(1)}, u32[]{:S(2)}, u32[]{:S(2)}) collective-permute-start(bf16[1024,256]{1,0:T(8,128)(2,1)S(1)} %bitcast.156), channel_id=1, source_target_pairs={{0,4},{4,0},{1,5},{5,1},{2,6},{6,2},{3,7},{7,3},{8,12},{12,8},{9,1... | collective-permute-start | bytes 1572872 | tf_op jit(solution)/shard_map/ppermute | solution.py:254
  45.6 13.5 %copy-start.17 = (s32[64,64]{1,0:T(8,128)S(1)}, s32[64,64]{1,0:T(8,128)}, u32[]{:S(2)}) copy-start(s32[64,64]{1,0:T(8,128)} %param.11) | copy-start | bytes 49156
  46.5 13.8 %collective-permute-start.6 = (bf16[128,1024]{1,0:T(8,128)(2,1)}, bf16[128,1024]{1,0:T(8,128)(2,1)}, u32[]{:S(2)}, u32[]{:S(2)}) collective-permute-start(bf16[128,1024]{1,0:T(8,128)(2,1)} %bitcast.20), channel_id=1, source_target_pairs={{0,1},{1,0},{2,3},{3,2},{4,5},{5,4},{6,7},{7,6},{8,9},{9,8},{10,11... | collective-permute-start | bytes 786440 | tf_op jit(solution)/shard_map/ppermute | solution.py:250
  49.5 13.9 %collective-permute-start.3 = (bf16[1024,256]{1,0:T(8,128)(2,1)S(1)}, bf16[1024,256]{1,0:T(8,128)(2,1)}, u32[]{:S(2)}, u32[]{:S(2)}) collective-permute-start(bf16[1024,256]{1,0:T(8,128)(2,1)S(1)} %bitcast.157), channel_id=1, source_target_pairs={{0,1},{1,0},{2,3},{3,2},{4,5},{5,4},{6,7},{7,6},{8,9},{9,8},{10,11... | collective-permute-start | bytes 1572872 | tf_op jit(solution)/shard_map/ppermute | solution.py:250
  50.9 25.5 %collective-permute-start.7 = (bf16[16,64,512]{2,1,0:T(8,128)(2,1)S(1)}, bf16[16,64,512]{2,1,0:T(8,128)(2,1)S(1)}, u32[]{:S(2)}, u32[]{:S(2)}) collective-permute-start(bf16[16,64,512]{2,1,0:T(8,128)(2,1)S(1)} %slice.66.own_ref), channel_id=1, source_target_pairs={{0,6},{2,4},{4,2},{6,0},{1,7},{3,5},{5,3},{7,1},{8,14},{10,12},{12... | collective-permute-start | bytes 3145736 | tf_op jit(solution)/shard_map/ppermute | solution.py:309
  56.1 7.3 %copy-start.11 = (bf16[1024,256]{1,0:T(8,128)(2,1)}, bf16[1024,256]{1,0:T(8,128)(2,1)S(1)}, u32[]{:S(2)}) copy-start(bf16[1024,256]{1,0:T(8,128)(2,1)S(1)} %collective-permute-done.4.kv2) | copy-start | bytes 1572868
  56.1 7.3 %collective-permute-start.5 = (bf16[1024,256]{1,0:T(8,128)(2,1)S(1)}, bf16[1024,256]{1,0:T(8,128)(2,1)}, u32[]{:S(2)}, u32[]{:S(2)}) collective-permute-start(bf16[1024,256]{1,0:T(8,128)(2,1)S(1)} %collective-permute-done.4.kv2), channel_id=1, source_target_pairs={{0,1},{1,0},{2,3},{3,2},{4,5},{5,4},{6,7},{7,6},{8,9},{9,8},{10,11... | collective-permute-start | bytes 1572872 | tf_op jit(solution)/shard_map/ppermute | solution.py:250
  61.5 17.4 %copy-start = (bf16[2,2,64,1024]{3,2,1,0:T(8,128)(2,1)}, bf16[2,2,64,1024]{3,2,1,0:T(8,128)(2,1)S(1)}, u32[]{:S(2)}) copy-start(bf16[2,2,64,1024]{3,2,1,0:T(8,128)(2,1)S(1)} %pad_maximum_fusion.4) | copy-start | bytes 1572868
  63.4 1.0 copy-start.12
  73.9 9.8 %copy-start.5 = (bf16[1024,128]{1,0:T(8,128)(2,1)}, bf16[1024,128]{1,0:T(8,128)(2,1)S(1)}, u32[]{:S(2)}) copy-start(bf16[1024,128]{1,0:T(8,128)(2,1)S(1)} %get-tuple-element.15.att_ref) | copy-start | bytes 786436
  76.4 1.0 copy-start.2
  77.5 1.2 copy-start.3
  79.7 3.0 %collective-permute-start.8 = (f32[128,1024]{1,0:T(8,128)S(1)}, f32[128,1024]{1,0:T(8,128)S(1)}, u32[]{:S(2)}, u32[]{:S(2)}) collective-permute-start(f32[128,1024]{1,0:T(8,128)S(1)} %slice.68), channel_id=1, source_target_pairs={{0,1},{1,0},{2,3},{3,2},{4,5},{5,4},{6,7},{7,6},{8,9},{9,8},{10,11... | collective-permute-start | bytes 1572872 | tf_op jit(solution)/shard_map/ppermute | solution.py:250
  83.7 14.5 %all-to-all-start.1 = ((bf16[16,64,256]{2,1,0:T(8,128)(2,1)}), bf16[16,64,256]{2,1,0:T(8,128)(2,1)S(1)}, u32[]{:S(2)}, u32[]{:S(2)}) async-start(bf16[16,64,256]{2,1,0:T(8,128)(2,1)} %pad_maximum_fusion.5), calls=%async_computation.1 | async-start | bytes 1048576 | tf_op jit(solution)/shard_map/all_to_all | solution.py:263
  87.2 29.4 %copy-start.1 = (bf16[2,2,64,1024]{3,2,1,0:T(8,128)(2,1)S(1)}, bf16[2,2,64,1024]{3,2,1,0:T(8,128)(2,1)}, u32[]{:S(2)}) copy-start(bf16[2,2,64,1024]{3,2,1,0:T(8,128)(2,1)} %copy-done) | copy-start | bytes 1572868
  87.3 22.2 %collective-permute-start.12 = (bf16[1024,128]{1,0:T(8,128)(2,1)}, bf16[1024,128]{1,0:T(8,128)(2,1)}, u32[]{:S(2)}, u32[]{:S(2)}) collective-permute-start(bf16[1024,128]{1,0:T(8,128)(2,1)} %bitcast.15.q_ref.refs_2_), channel_id=1, source_target_pairs={{0,4},{4,0},{1,5},{5,1},{2,6},{6,2},{3,7},{7,3},{8,12},{12,8},{9,1... | collective-permute-start | bytes 786440 | tf_op jit(solution)/shard_map/ppermute | solution.py:254
  99.0 15.4 %copy-start.4 = (bf16[16,64,128]{2,1,0:T(8,128)(2,1)S(1)}, bf16[16,64,128]{2,1,0:T(8,128)(2,1)}, u32[]{:S(2)}) copy-start(bf16[16,64,128]{2,1,0:T(8,128)(2,1)} %get-tuple-element.32) | copy-start | bytes 786436
  99.2 0.7 copy-start.15
  100.7 19.1 %copy-start.7 = (bf16[16,64,256]{2,1,0:T(8,128)(2,1)S(1)}, bf16[16,64,256]{2,1,0:T(8,128)(2,1)}, u32[]{:S(2)}) copy-start(bf16[16,64,256]{2,1,0:T(8,128)(2,1)} %copy-done.6) | copy-start | bytes 1572868
  100.7 14.8 %collective-permute-start.9 = (bf16[2,64,1024]{2,1,0:T(8,128)(2,1)}, bf16[2,64,1024]{2,1,0:T(8,128)(2,1)}, u32[]{:S(2)}, u32[]{:S(2)}) collective-permute-start(bf16[2,64,1024]{2,1,0:T(8,128)(2,1)} %reshape.293), channel_id=1, source_target_pairs={{0,1},{1,0},{2,3},{3,2},{4,5},{5,4},{6,7},{7,6},{8,9},{9,8},{10,11... | collective-permute-start | bytes 786440 | tf_op jit(solution)/shard_map/ppermute | solution.py:250
  105.3 14.4 %copy-start.10 = (f32[1,1024]{1,0:T(1,128)S(1)}, f32[1,1024]{1,0:T(1,128)}, u32[]{:S(2)}) copy-start(f32[1,1024]{1,0:T(1,128)} %delta.1.delta_ref) | copy-start | bytes 12292
  106.1 1.3 collective-permute-start.17
  106.2 13.2 %collective-permute-start.15 = (bf16[1024,128]{1,0:T(8,128)(2,1)}, bf16[1024,128]{1,0:T(8,128)(2,1)}, u32[]{:S(2)}, u32[]{:S(2)}) collective-permute-start(bf16[1024,128]{1,0:T(8,128)(2,1)} %bitcast.151), channel_id=1, source_target_pairs={{0,4},{4,0},{1,5},{5,1},{2,6},{6,2},{3,7},{7,3},{8,12},{12,8},{9,1... | collective-permute-start | bytes 786440 | tf_op jit(solution)/shard_map/ppermute | solution.py:254
  108.0 6.4 %collective-permute-start.18 = (f32[4,1024]{1,0:T(4,128)S(1)}, f32[4,1024]{1,0:T(4,128)S(1)}, u32[]{:S(2)}, u32[]{:S(2)}) collective-permute-start(f32[4,1024]{1,0:T(4,128)S(1)} %pad_maximum_fusion.15), channel_id=1, source_target_pairs={{0,4},{4,0},{1,5},{5,1},{2,6},{6,2},{3,7},{7,3},{8,12},{12,8},{9,1... | collective-permute-start | bytes 49160 | tf_op jit(solution)/shard_map/ppermute | solution.py:254
  108.5 21.2 %collective-permute-start.11 = (bf16[1024,128]{1,0:T(8,128)(2,1)}, bf16[1024,128]{1,0:T(8,128)(2,1)}, u32[]{:S(2)}, u32[]{:S(2)}) collective-permute-start(bf16[1024,128]{1,0:T(8,128)(2,1)} %bitcast.15.q_ref.refs_2_), channel_id=1, source_target_pairs={{0,1},{1,0},{2,3},{3,2},{4,5},{5,4},{6,7},{7,6},{8,9},{9,8},{10,11... | collective-permute-start | bytes 786440 | tf_op jit(solution)/shard_map/ppermute | solution.py:250
  109.5 20.2 %collective-permute-start.13 = (bf16[1024,128]{1,0:T(8,128)(2,1)}, bf16[1024,128]{1,0:T(8,128)(2,1)}, u32[]{:S(2)}, u32[]{:S(2)}) collective-permute-start(bf16[1024,128]{1,0:T(8,128)(2,1)} %collective-permute-done.12.refs_4_), channel_id=1, source_target_pairs={{0,1},{1,0},{2,3},{3,2},{4,5},{5,4},{6,7},{7,6},{8,9},{9,8},{10,11... | collective-permute-start | bytes 786440 | tf_op jit(solution)/shard_map/ppermute | solution.py:250
  111.3 8.5 %copy-start.13 = (bf16[1024,256]{1,0:T(8,128)(2,1)S(1)}, bf16[1024,256]{1,0:T(8,128)(2,1)}, u32[]{:S(2)}) copy-start(bf16[1024,256]{1,0:T(8,128)(2,1)} %copy-done.11) | copy-start | bytes 1572868
  114.4 15.4 %collective-permute-start.14 = (bf16[1024,128]{1,0:T(8,128)(2,1)S(1)}, bf16[1024,128]{1,0:T(8,128)(2,1)S(1)}, u32[]{:S(2)}, u32[]{:S(2)}) collective-permute-start(bf16[1024,128]{1,0:T(8,128)(2,1)S(1)} %bitcast.152), channel_id=1, source_target_pairs={{0,1},{1,0},{2,3},{3,2},{4,5},{5,4},{6,7},{7,6},{8,9},{9,8},{10,11... | collective-permute-start | bytes 786440 | tf_op jit(solution)/shard_map/ppermute | solution.py:250
  116.6 0.9 copy-start.8
  117.6 28.2 %collective-permute-start.19 = (bf16[16,64,512]{2,1,0:T(8,128)(2,1)S(1)}, bf16[16,64,512]{2,1,0:T(8,128)(2,1)S(1)}, u32[]{:S(2)}, u32[]{:S(2)}) collective-permute-start(bf16[16,64,512]{2,1,0:T(8,128)(2,1)S(1)} %get-tuple-element.24), channel_id=1, source_target_pairs={{0,6},{2,4},{4,2},{6,0},{1,7},{3,5},{5,3},{7,1},{8,14},{10,12},{12... | collective-permute-start | bytes 3145736 | tf_op jit(solution)/shard_map/ppermute | solution.py:309
  119.4 10.3 %collective-permute-start.16 = (bf16[1024,128]{1,0:T(8,128)(2,1)}, bf16[1024,128]{1,0:T(8,128)(2,1)S(1)}, u32[]{:S(2)}, u32[]{:S(2)}) collective-permute-start(bf16[1024,128]{1,0:T(8,128)(2,1)} %collective-permute-done.15.refs_8_), channel_id=1, source_target_pairs={{0,1},{1,0},{2,3},{3,2},{4,5},{5,4},{6,7},{7,6},{8,9},{9,8},{10,11... | collective-permute-start | bytes 786440 | tf_op jit(solution)/shard_map/ppermute | solution.py:250
  147.6 4.6 %copy-start.9 = (bf16[2,2,64,1024]{3,2,1,0:T(8,128)(2,1)S(1)}, bf16[2,2,64,1024]{3,2,1,0:T(8,128)(2,1)}, u32[]{:S(2)}) copy-start(bf16[2,2,64,1024]{3,2,1,0:T(8,128)(2,1)} %copy-done.8) | copy-start | bytes 1572868
  147.6 34.5 %all-to-all-start.2 = ((bf16[16,64,896]{2,1,0:T(8,128)(2,1)}), bf16[16,64,896]{2,1,0:T(8,128)(2,1)}, u32[]{:S(2)}, u32[]{:S(2)}) async-start(bf16[16,64,896]{2,1,0:T(8,128)(2,1)} %pad_maximum_fusion.1), calls=%async_computation.2 | async-start | bytes 3670016 | tf_op jit(solution)/shard_map/all_to_all | solution.py:263
  152.9 1.6 collective-permute-start.10
  183.6 4.7 %collective-permute-start.21 = (f32[16,1024]{1,0:T(8,128)S(1)}, f32[16,1024]{1,0:T(8,128)S(1)}, u32[]{:S(2)}, u32[]{:S(2)}) collective-permute-start(f32[16,1024]{1,0:T(8,128)S(1)} %dynamic-slice_bitcast_fusion.3), channel_id=1, source_target_pairs={{0,2},{2,0},{1,3},{3,1},{4,6},{6,4},{5,7},{7,5},{8,10},{10,8},{9,1... | collective-permute-start | bytes 196616 | tf_op jit(solution)/shard_map/ppermute | solution.py:438
  188.3 3.1 %collective-permute-start.22 = (f32[8,1024]{1,0:T(8,128)S(1)}, f32[8,1024]{1,0:T(8,128)S(1)}, u32[]{:S(2)}, u32[]{:S(2)}) collective-permute-start(f32[8,1024]{1,0:T(8,128)S(1)} %dynamic-slice_bitcast_fusion.4), channel_id=1, source_target_pairs={{0,1},{1,0},{2,3},{3,2},{4,5},{5,4},{6,7},{7,6},{8,9},{9,8},{10,11... | collective-permute-start | bytes 98312 | tf_op jit(solution)/shard_map/ppermute | solution.py:250
  190.6 1.8 collective-permute-start.20

commit v5 on v4

--- a/solution.py
+++ b/solution.py
@@ -119,24 +119,11 @@
     )(q, *kvs, bias)
 
 
-def delta_body(g_ref, att_ref, d_ref):
-    product = g_ref[...].astype(F32) * att_ref[...].astype(F32)
-    d_ref[...] = jnp.sum(product.T, axis=0, keepdims=True)
-
-
 def row_delta(g, att):
-    return pl.pallas_call(
-        delta_body,
-        out_shape=jax.ShapeDtypeStruct((1, ROWS), F32),
-        grid=(ROWS // TILE,),
-        in_specs=[tile_spec(HEAD)] * 2,
-        out_specs=row_spec(1),
-        cost_estimate=pl.CostEstimate(flops=0, bytes_accessed=1 << 20, transcendentals=0),
-        name="delta",
-    )(g, att)
-
-
-def query_body(q_ref, g_ref, lse_ref, delta_ref, kv0, kv1, kv2, kv3, bias_ref, dq_ref, ka_ref, s_ref):
+    return jnp.sum((g.astype(F32) * att.astype(F32)).T, axis=0, keepdims=True)
+
+
+def query_body(q_ref, g_ref, att_ref, lse_ref, kv0, kv1, kv2, kv3, bias_ref, dq_ref, ka_ref, s_ref):
     step = pl.program_id(0)
     chunks = (kv0, kv1, kv2, kv3)
 
@@ -147,7 +134,7 @@
     qa = query_wide(q_ref[...], step * (TILE // SPAN))
     g = g_ref[...]
     lse = lse_ref[...]
-    delta = delta_ref[...]
+    delta = row_delta(g, att_ref[...])
     total = jnp.zeros((HEAD, TILE), F32)
     for c, kv_ref in enumerate(chunks):
         s_ref[...] = dot(ka_ref[pl.ds(c * ROWS, ROWS), :], qa, NT)
@@ -161,7 +148,7 @@
     dq_ref[...] = (total * SCALE).T.astype(BF16)
 
 
-def query_grad(q, g, lse, delta, kvs, bias):
+def query_grad(q, g, att, lse, kvs, bias):
     return pl.pallas_call(
         query_body,
         out_shape=jax.ShapeDtypeStruct((ROWS, HEAD), BF16),
@@ -169,7 +156,7 @@
         in_specs=[
             tile_spec(HEAD),
             tile_spec(HEAD),
-            row_spec(1),
+            tile_spec(HEAD),
             row_spec(1),
             *[once(ROWS, 2 * HEAD)] * 4,
             once(4 * UNITS, HEAD),
@@ -182,12 +169,12 @@
         cost_estimate=cost(3, 4 * ROWS * ROWS),
         compiler_params=pltpu.CompilerParams(vmem_limit_bytes=16 << 20),
         name="query_grad",
-    )(q, g, lse, delta, *kvs, bias)
+    )(q, g, att, lse, *kvs, bias)
 
 
 def key_body(*refs):
     kv_ref, bias_ref = refs[:2]
-    qs, gs, stats = refs[2:6], refs[6:10], refs[10]
+    pairs, gs, lses = refs[2:6], refs[6:10], refs[10]
     dk_ref, dv_ref, ka_ref, s_ref, dk_acc, dv_acc = refs[11:]
     ka_ref[:, :HEAD] = kv_ref[:, :HEAD]
     ka_ref[:, HEAD:] = spread_bias(bias_ref[:UNITS, :])
@@ -197,10 +184,10 @@
 
         def tile(i, _, c=c):
             rows = pl.ds(pl.multiple_of(i * TILE, TILE), TILE)
-            q = qs[c][rows, :]
+            q = pairs[c][rows, :HEAD]
             g = gs[c][rows, :]
-            lse = stats[2 * c : 2 * c + 1, rows]
-            delta = stats[2 * c + 1 : 2 * c + 2, rows]
+            lse = lses[c : c + 1, rows]
+            delta = row_delta(g, pairs[c][rows, HEAD:])
             qa = query_wide(q, i * (TILE // SPAN) + c * UNITS)
             s_ref[...] = dot(ka_ref[...], qa, NT)
             if c == 0:
@@ -217,7 +204,7 @@
     dv_ref[...] = dv_acc[...].astype(BF16)
 
 
-def key_grad(kv, bias, qs, gs, stats):
+def key_grad(kv, bias, pairs, gs, lses):
     return pl.pallas_call(
         key_body,
         out_shape=[jax.ShapeDtypeStruct((ROWS, HEAD), BF16)] * 2,
@@ -225,8 +212,9 @@
         in_specs=[
             once(ROWS, 2 * HEAD),
             once(4 * UNITS, HEAD),
-            *[once(ROWS, HEAD)] * 8,
-            once(8, ROWS),
+            *[once(ROWS, 2 * HEAD)] * 4,
+            *[once(ROWS, HEAD)] * 4,
+            once(4, ROWS),
         ],
         out_specs=[once(ROWS, HEAD)] * 2,
         scratch_shapes=[
@@ -238,7 +226,7 @@
         cost_estimate=cost(4, 4 * ROWS * ROWS),
         compiler_params=pltpu.CompilerParams(vmem_limit_bytes=16 << 20),
         name="key_grad",
-    )(kv, bias, *qs, *gs, stats)
+    )(kv, bias, *pairs, *gs, lses)
 
 
 ZY = ("z", "y")
@@ -283,26 +271,8 @@
     return jnp.pad(bias, ((0, 0), (0, HEAD - count)))
 
 
-def by_unit(rows, kinds):
-    split = rows.reshape(2, SPAN, kinds, HEADS, HEAD)
-    return split.transpose(0, 3, 1, 2, 4).reshape(UNITS, SPAN, kinds * HEAD)
-
-
-def by_row(blocks, kinds):
-    split = blocks.reshape(2, HEADS, SPAN, kinds, HEAD)
-    return split.transpose(0, 2, 3, 1, 4).reshape(2, SPAN, kinds * HEADS * HEAD)
-
-
 def side_by_side(first, own, peer):
     return jnp.concatenate([jnp.where(first, own, peer), jnp.where(first, peer, own)], axis=-1)
-
-
-def to_narrow(x):
-    return jnp.concatenate(jnp.split(x, 2, axis=-1), axis=-2)
-
-
-def from_narrow(x):
-    return jnp.concatenate(jnp.split(x, 2, axis=-2), axis=-1)
 
 
 def across(x):
@@ -329,118 +299,214 @@
     )(xl, own, other)
 
 
-def term_body(xl_ref, att_ref, up_ref, own_ref, other_ref, sum_ref):
+def term_body(own_ref, peer_ref, up_ref, out_ref):
+    att = jnp.concatenate([own_ref[...], peer_ref[...]], axis=0)
     for c in range(2):
         cols = slice(c * 512, (c + 1) * 512)
-        sum_ref[...] = dot(att_ref[...], up_ref[:, cols], TN).astype(BF16).reshape(sum_ref.shape)
-        for flip, part in enumerate((own_ref, other_ref)):
-            part[:, c * 32 : (c + 1) * 32, :] = sum_ref[:, xl_ref[0] ^ flip]
-
-
-def weight_terms(xl, att, up):
+        out_ref[:, cols] = dot(att, up_ref[:, cols], TN).astype(BF16)
+
+
+def weight_terms(own, peer, up):
     return pl.pallas_call(
         term_body,
-        out_shape=[jax.ShapeDtypeStruct((UNITS, SPAN, 512), BF16)] * 2,
+        out_shape=jax.ShapeDtypeStruct((1024, 1024), BF16),
         grid=(1,),
-        in_specs=[pl.BlockSpec(memory_space=pltpu.SMEM), once(256, 1024), once(256, 1024)],
-        out_specs=[once(UNITS, SPAN, 512)] * 2,
-        scratch_shapes=[pltpu.VMEM((UNITS, 2, 32, 512), BF16)],
+        in_specs=[once(128, 1024), once(128, 1024), once(256, 1024)],
+        out_specs=once(1024, 1024),
         cost_estimate=pl.CostEstimate(
             flops=2 * 256 * 1024 * 1024, bytes_accessed=4 << 20, transcendentals=0
         ),
         compiler_params=pltpu.CompilerParams(vmem_limit_bytes=16 << 20),
         name="weight_terms",
-    )(xl, att, up)
+    )(own, peer, up)
+
+
+IN_SMEM = pl.BlockSpec(memory_space=pltpu.SMEM)
+
+
+def move(body, name, outs, scalars, *arrays):
+    return pl.pallas_call(
+        body,
+        out_shape=[jax.ShapeDtypeStruct(shape, BF16) for shape in outs],
+        grid=(1,),
+        in_specs=[IN_SMEM] * len(scalars) + [once(*x.shape) for x in arrays],
+        out_specs=[once(*shape) for shape in outs],
+        cost_estimate=pl.CostEstimate(flops=0, bytes_accessed=4 << 20, transcendentals=0),
+        compiler_params=pltpu.CompilerParams(vmem_limit_bytes=12 << 20),
+        name=name,
+    )(*scalars, *arrays)
+
+
+def head_cols(h):
+    return slice(h * HEAD, (h + 1) * HEAD)
+
+
+def span_rows(half):
+    return pl.ds(pl.multiple_of(half * SPAN, SPAN), SPAN)
+
+
+def cut_body(half_ref, q_ref, k_ref, v_ref, own_ref, sent_ref):
+    for side, out in enumerate((own_ref, sent_ref)):
+        rows = span_rows(half_ref[0] ^ side)
+        for t, x in enumerate((q_ref, k_ref, v_ref)):
+            for h in range(HEADS):
+                out[h, :, head_cols(t)] = x[rows, head_cols(h)]
+
+
+def fill_body(core_ref, xh_ref, own_ref, peer_ref, w0, w1, w2, w3, out_ref):
+    core, xh = core_ref[0], xh_ref[0]
+    out_ref[pl.ds(core * HEADS, HEADS), :, : 3 * HEAD] = own_ref[...]
+    out_ref[pl.ds((1 - core) * HEADS, HEADS), :, : 3 * HEAD] = peer_ref[...]
+    first, mine_first = core == 0, xh == 0
+    w = [x[...].astype(F32) for x in (w0, w1, w2, w3)]
+    near = [jnp.where(first, w[0], w[1]), jnp.where(first, w[1], w[0])]
+    far = [jnp.where(first, w[2], w[3]), jnp.where(first, w[3], w[2])]
+    front = [jnp.where(mine_first, a, b) for a, b in zip(near, far)]
+    back = [jnp.where(mine_first, b, a) for a, b in zip(near, far)]
+    rows = jnp.concatenate(front + back, axis=0).astype(BF16)
+    for c in range(2):
+        part = rows[:, c * 512 : (c + 1) * 512]
+        for unit in range(UNITS):
+            out_ref[unit, c * 32 : (c + 1) * 32, 3 * HEAD :] = part
+
+
+def split_body(x_ref, q_ref, kv_ref, w_ref):
+    x = x_ref[...]
+    q_ref[...] = x[:, :, :HEAD].reshape(ROWS, HEAD)
+    kv_ref[...] = x[:, :, HEAD : 3 * HEAD].reshape(ROWS, 2 * HEAD)
+    w_ref[...] = x[:, :, 3 * HEAD :]
+
+
+def cross_body(att_ref, own_ref, peer_ref, out_ref):
+    for s in range(2):
+        for h in range(HEADS):
+            unit, rows = s * HEADS + h, slice(s * SPAN, (s + 1) * SPAN)
+            out_ref[unit, :, :HEAD] = att_ref[unit * SPAN : (unit + 1) * SPAN, :]
+            total = own_ref[rows, head_cols(h)] + peer_ref[rows, head_cols(h)]
+            out_ref[unit, :, HEAD:] = total.astype(BF16)
+
+
+def land_body(x_ref, att_ref, g_ref):
+    g_ref[...] = x_ref[:, :, HEAD:].reshape(ROWS, HEAD)
+    for s in range(2):
+        for h in range(HEADS):
+            att_ref[s * SPAN : (s + 1) * SPAN, head_cols(h)] = x_ref[s * HEADS + h, :, :HEAD]
+
+
+def final_body(core_ref, half_ref, own_ref, peer_ref, dq_ref, dk_ref, dv_ref):
+    core, half = core_ref[0], half_ref[0]
+    for t, out in enumerate((dq_ref, dk_ref, dv_ref)):
+        for h in range(HEADS):
+            out[span_rows(half), head_cols(h)] = own_ref[core * HEADS + h, :, head_cols(t)]
+            out[span_rows(1 - half), head_cols(h)] = peer_ref[h, :, head_cols(t)]
 
 
 def local(query_states, key_states, value_states, span_order, block_mask, output_weight, upstream):
     z, y, xl, xh, core = (lax.axis_index(a) for a in ("z", "y", "xl", "xh", "core"))
     first_core = core == 0
     half = core ^ ((z + y) % 2)
+    core_1, xl_1, xh_1, half_1 = (x.reshape(1) for x in (core, xl, xh, half))
     cols = output_weight.shape[1] // 2
 
-    def mine(x, axis):
-        return lax.dynamic_index_in_dim(x, core, axis, False)
-
-    def theirs(x, axis):
-        return lax.dynamic_index_in_dim(x, 1 - core, axis, False)
-
-    def share(rows):
-        halves = rows.reshape(2, SPAN, -1)
-        own = lax.dynamic_index_in_dim(halves, half, 0, False)
-        peer = other_core(lax.dynamic_index_in_dim(halves, 1 - half, 0, False))
-        return in_order(first_core, own, peer)
-
-    def unshare(both):
-        own = mine(both, 0)
-        peer = other_core(theirs(both, 0))
-        return in_order(half == 0, own, peer).reshape(2 * SPAN, -1)
-
-    weight_cols = output_weight.reshape(-1, 2, cols)
-    weight_rows = in_order(first_core, mine(weight_cols, 1), other_core(theirs(weight_cols, 1)))
-    weight_rows = weight_rows.reshape(-1, cols)
-    weight_rows = in_order(xh == 0, weight_rows, lax.ppermute(weight_rows, "xh", SWAP))
-    weight_rows = to_narrow(weight_rows.reshape(-1, cols))
-    copies = jnp.broadcast_to(weight_rows[None], (UNITS, *weight_rows.shape))
-    states = share(jnp.concatenate([query_states[0], key_states[0], value_states[0]], axis=1))
-    blocks = exchange(jnp.concatenate([by_unit(states, 3), copies], axis=2), ZY)
-    q = blocks[:, :, :HEAD].reshape(ROWS, HEAD)
-    own_kv = blocks[:, :, HEAD : 3 * HEAD].reshape(ROWS, 2 * HEAD)
+    def by_core(x):
+        left, right = x[..., :cols], x[..., cols:]
+        return jnp.where(first_core, left, right), jnp.where(first_core, right, left)
+
+    weight_mine, weight_theirs = by_core(output_weight)
+    weight_rows = [
+        weight_mine,
+        other_core(weight_theirs),
+        lax.ppermute(weight_mine, "xh", SWAP),
+        lax.ppermute(weight_theirs, ("xh", "core"), [(k, 3 - k) for k in range(4)]),
+    ]
+    unit_rows = (HEADS, SPAN, 3 * HEAD)
+    own, sent = move(
+        cut_body,
+        "cut",
+        [unit_rows] * 2,
+        [half_1],
+        query_states[0],
+        key_states[0],
+        value_states[0],
+    )
+    (blocks,) = move(
+        fill_body,
+        "fill",
+        [(UNITS, SPAN, 3 * HEAD + 512)],
+        [core_1, xh_1],
+        own,
+        other_core(sent),
+        *weight_rows,
+    )
+    blocks = exchange(blocks, ZY)
+    q, own_kv, weight_own = move(
+        split_body,
+        "split",
+        [(ROWS, HEAD), (ROWS, 2 * HEAD), (UNITS, SPAN, 512)],
+        [],
+        blocks,
+    )
     far_kv = other_chip(own_kv)
-    weight_own = blocks[:, :, 3 * HEAD :]
     weight_other = across(weight_own)
     kvs = (own_kv, other_core(own_kv), far_kv, other_core(far_kv))
     bias = span_bias(span_order, block_mask, xl, core)
 
-    up_cols = upstream[0].reshape(2 * SPAN, 2, cols)
-    up = in_order(first_core, mine(up_cols, 1), other_core(theirs(up_cols, 1)))
-    up = up.reshape(2, 2, SPAN, cols)
+    up_mine, up_theirs = by_core(upstream[0])
+    up = in_order(first_core, up_mine, other_core(up_theirs)).reshape(2, 2, SPAN, cols)
     up = in_order(half == 0, up[:, 0], up[:, 1]).reshape(4 * SPAN, cols)
 
     attended, lse = forward(q, kvs, bias)
 
-    place, lse = lax.optimization_barrier((xl.reshape(1), lse))
+    place, lse = lax.optimization_barrier((xl_1, lse))
     weight = weight_whole(place, weight_own, weight_other).reshape(HEADS * HEAD, cols)
     grad_rows = dot(up, weight, NT)
-    grad_rows = grad_rows[: 2 * SPAN] + other_core(grad_rows[2 * SPAN :])
-    grad_rows = grad_rows.astype(BF16).reshape(2, SPAN, -1)
-    crossing = jnp.concatenate(
-        [attended.reshape(UNITS, SPAN, HEAD), by_unit(grad_rows, 1)], axis=2
+    grad_own, grad_sent = grad_rows[: 2 * SPAN], grad_rows[2 * SPAN :]
+    (crossing,) = move(
+        cross_body, "cross", [(UNITS, SPAN, 2 * HEAD)], [], attended, grad_own, other_core(grad_sent)
     )
     crossed = exchange(crossing, ZY)
-    qs = everyone(q)
-    g = crossed[:, :, HEAD:].reshape(ROWS, HEAD)
-    delta = row_delta(g, attended)
-    stats = jnp.concatenate([lse, delta], axis=0)
-    stats = jnp.concatenate([stats, other_core(stats)], axis=0)
-    stats_far = other_chip(stats)
+    pairs = everyone(jnp.concatenate([q, attended], axis=1))
+    lses = jnp.concatenate([lse, other_core(lse)], axis=0)
+    lses = jnp.concatenate([lses, other_chip(lses)], axis=0)
+
+    att_own, g = move(land_body, "land", [(2 * SPAN, HEADS * HEAD), (ROWS, HEAD)], [], crossed)
     gs = everyone(g)
-
-    attended_rows = by_row(crossed[:, :, :HEAD], 1)
-    attended_rows = jnp.stack([attended_rows, other_core(attended_rows)]).reshape(4 * SPAN, -1)
-    place, stats_far = lax.optimization_barrier((xl.reshape(1), stats_far))
-    stats = jnp.concatenate([stats, stats_far], axis=0)
-    term_own, term_sent = weight_terms(place, attended_rows, up)
-    term_other = across(term_sent)
-    projected = dot(attended_rows, weight, NN).astype(BF16).reshape(2, 2, SPAN, cols)
-    own, peer = mine(projected, 1), other_core(theirs(projected, 1))
-    own = in_order(half == 0, own[0], own[1]).reshape(2 * SPAN, cols)
-    peer = in_order(half == 0, peer[1], peer[0]).reshape(2 * SPAN, cols)
+    att_peer = other_core(att_own)
+    term = weight_terms(att_own, att_peer, up).reshape(UNITS, SPAN, cols)
+    term = exchange(term, ZY)
+
+    query_out = query_grad(q, g, attended, lse, kvs, bias)
+    key_out, value_out = key_grad(own_kv, bias, pairs, gs, lses)
+    grads = [x.reshape(UNITS, SPAN, HEAD) for x in (query_out, key_out, value_out)]
+    grads = exchange(jnp.concatenate(grads, axis=2), ZY)
+
+    def project(att):
+        return dot(att, weight, NN).astype(BF16).reshape(2, SPAN, cols)
+
+    own, peer = project(att_own), project(att_peer)
+    kept = [lax.dynamic_index_in_dim(x, core, 0, False) for x in (own, peer)]
+    gone = jnp.stack([lax.dynamic_index_in_dim(x, 1 - core, 0, False) for x in (own, peer)])
+    gone = other_core(gone)
+    own = in_order(half == 0, kept[0], kept[1]).reshape(2 * SPAN, cols)
+    peer = in_order(half == 0, gone[1], gone[0]).reshape(2 * SPAN, cols)
     projected = side_by_side(first_core, own, peer)
 
-    query_out = query_grad(q, g, lse, delta, kvs, bias)
-    key_out, value_out = key_grad(own_kv, bias, qs, gs, stats)
-    term = (term_own.astype(F32) + term_other.astype(F32)).astype(BF16)
-    grads = [x.reshape(UNITS, SPAN, HEAD) for x in (query_out, key_out, value_out)]
-    grads = exchange(jnp.concatenate([*grads, term], axis=2), ZY)
-    summed = jnp.sum(grads[:, :, 3 * HEAD :].astype(F32), axis=0)
-    summed = from_narrow(summed).reshape(2, 16, cols)
-    partner = lax.ppermute(lax.dynamic_index_in_dim(summed, 1 - xh, 0, False), "xh", SWAP)
-    summed = (lax.dynamic_index_in_dim(summed, xh, 0, False) + partner).reshape(2, -1, cols)
-    grads = grads[:, :, : 3 * HEAD]
-    weight_gradient = side_by_side(first_core, mine(summed, 0), other_core(theirs(summed, 0)))
-    grads = unshare(by_row(grads, 3))
-    query_gradient, key_gradient, value_gradient = jnp.split(grads, 3, axis=1)
+    summed = jnp.sum(term.astype(F32), axis=0).reshape(4, 16, cols)
+    chip = 2 * xl + xh
+    total = lax.dynamic_index_in_dim(summed, chip, 0, False)
+    for step in (1, 2, 3):
+        part = lax.dynamic_index_in_dim(summed, chip ^ step, 0, False)
+        total = total + lax.ppermute(part, ("xl", "xh"), [(k, k ^ step) for k in range(4)])
+    total = total.reshape(2, -1, cols)
+    own = lax.dynamic_index_in_dim(total, core, 0, False)
+    peer = other_core(lax.dynamic_index_in_dim(total, 1 - core, 0, False))
+    weight_gradient = side_by_side(first_core, own, peer)
+
+    peer = other_core(lax.dynamic_slice_in_dim(grads, (1 - core) * HEADS, HEADS, 0))
+    own_rows = (2 * SPAN, HEADS * HEAD)
+    query_gradient, key_gradient, value_gradient = move(
+        final_body, "final", [own_rows] * 3, [core_1, half_1], grads, peer
+    )
     return (
         projected[None],
         query_gradient[None],

time: 194 us -> 172 us (0.89)
  waiting for transfers between devices: 54.7 us -> 36.2 us
  starting transfers between devices: 31.8 us -> 38.6 us
  local copies, waits for them, and re-layouts: 20.1 us -> 13.6 us
  other arithmetic: 12.1 us -> 7.62 us
    all_to_all x2 -> x3, waiting for transfers between devices: 38.4 us -> 15.2 us  [exchange(): return lax.all_to_all(x, axes, 0, 0, tiled=True)]
    all_to_all x2 -> x3, starting transfers between devices: 8.13 us -> 16.6 us  [exchange(): return lax.all_to_all(x, axes, 0, 0, tiled=True)]
    unnamed x42 -> x43, local copies, waits for them, and re-layouts: 5.72 us -> 12.6 us
    slice x6 -> x1, local copies, waits for them, and re-layouts: 5.24 us -> 0.09 us  [local(): grad_own, grad_sent = (grad_rows[:2 * SPAN], grad_rows[2 * SPAN:])]
    ppermute x2 -> x5, starting transfers between devices: 2.99 us -> 7.56 us  [the longest x3 3.94 us: local(): lax.ppermute(part, ('xl', 'xh'), [(k, k ^ step) for k in range(4)])]
    ppermute x4, waiting for transfers between devices: 6.42 us -> 10.7 us  [other_chip(): return lax.ppermute(x, 'xl', SWAP)]
    concatenate x9 -> x3, other arithmetic: 5.3 us -> 1.05 us  [the longest x1 1.02 us: local(): grads = exchange(jnp.concatenate(grads, axis=2), ZY)]
    ppermute x2 -> x1, starting transfers between devices: 3.78 us -> 0.52 us  [across(): return lax.ppermute(x, ('xl', 'xh'), [(k, k ^ 3) for k in range(4)])]
  transfers between devices with their start and end apart: 25 -> 28, of which waited for: 13 -> 12; matrix products, arithmetic and copies ran while one was open for 10% -> 6% of each run, Pallas kernels for 20% -> 22%
where the time goes in v5:
time: 172 us; the launch traced here: 171 us
  Pallas kernels  39.5 us (23%)
  starting transfers between devices  38.6 us (22%)
  waiting for transfers between devices  36.2 us (21%)
  blocking collectives  32.7 us (19%)
  local copies, waits for them, and re-layouts  13.6 us (8%)
  other arithmetic  7.62 us (4%)
  matrix products  1.94 us (1%)
    all_to_all x1, blocking collectives, exchange(): return lax.all_to_all(x, axes, 0, 0, tiled=True)  32.7 us
    all_to_all x3, starting transfers between devices, exchange(): return lax.all_to_all(x, axes, 0, 0, tiled=True)  16.6 us
    pallas_call x1, Pallas kernels, key_grad(): pl.pallas_call(key_body, out_shape=[jax.ShapeDtypeStruct((ROWS, HEAD), BF...  16.4 us
    all_to_all x3, waiting for transfers between devices, exchange(): return lax.all_to_all(x, axes, 0, 0, tiled=True)  15.2 us
    ppermute x15, starting transfers between devices, other_core(): return lax.ppermute(x, 'core', SWAP)  13.5 us
    unnamed x43, local copies, waits for them, and re-layouts  12.6 us
    ppermute x4, waiting for transfers between devices, other_chip(): return lax.ppermute(x, 'xl', SWAP)  10.7 us
    pallas_call x1, Pallas kernels, query_grad(): pl.pallas_call(query_body, out_shape=jax.ShapeDtypeStruct((ROWS, HEAD), B...  9.97 us
  transfers between devices with their start and end apart: 28, of which 12 were waited for; matrix products, arithmetic and copies ran while one was open for 6% of the time, Pallas kernels for 22%

profile of v5, /device:TPU:1, one launch (start us, length us, event | category | flops | bytes accessed | tf_op | source)
XLA Modules:
  0.0 171.3 jit_solution(14821409946069409591)
XLA Ops:
  0.7 0.9 copy-done.9
  1.6 0.9 copy-done.10
  2.6 0.9 copy-done.11
  3.6 1.5 collective-permute-start
  5.1 0.7 broadcast_select_fusion.10
  5.9 2.9 %collective-permute-start.2 = (bf16[8,1024]{1,0:T(8,128)(2,1)S(1)}, bf16[8,1024]{1,0:T(8,128)(2,1)S(1)}, u32[]{:S(2)}, u32[]{:S(2)}) collective-permute-start(bf16[8,1024]{1,0:T(8,128)(2,1)S(1)} %get-tuple-element.57.w0), channel_id=1, source_target_pairs={{0,2},{2,0},{1,3},{3,1},{4,6},{6,4},{5,7},{7,5},{8,10},{10,8},{9,1... | collective-permute-start | bytes 49160 | tf_op jit(solution)/shard_map/ppermute | solution.py:419
  10.1 3.9 %collective-permute-done.3.w3 = bf16[8,1024]{1,0:T(8,128)(2,1)S(1)} collective-permute-done((bf16[8,1024]{1,0:T(8,128)(2,1)S(1)}, bf16[8,1024]{1,0:T(8,128)(2,1)S(1)}, u32[]{:S(2)}, u32[]{:S(2)}) %collective-permute-start.3) | collective-permute-done | bytes 16416 | tf_op jit(solution)/shard_map/ppermute | solution.py:420
  14.1 32.7 %all_to_all.20.x_ref = bf16[16,64,896]{2,1,0:T(8,128)(2,1)S(1)} all-to-all(bf16[16,64,896]{2,1,0:T(8,128)(2,1)S(1)} %fill.1), channel_id=1, replica_groups=mesh['z'=4,'y'=4,'xl'=2,'xh'=2,'core'=2] {'z','y'}, dimensions={0} | all-to-all | bytes 3670016 | tf_op jit(solution)/shard_map/all_to_all | solution.py:251
  47.5 0.9 broadcast_select_fusion.2
  48.4 1.7 collective-permute-start.7
  50.8 8.3 %collective-permute-done.5.kv2 = bf16[1024,256]{1,0:T(8,128)(2,1)} collective-permute-done((bf16[1024,256]{1,0:T(8,128)(2,1)S(1)}, bf16[1024,256]{1,0:T(8,128)(2,1)}, u32[]{:S(2)}, u32[]{:S(2)}) %collective-permute-start.5) | collective-permute-done | bytes 524320 | tf_op jit(solution)/shard_map/ppermute | solution.py:242
  59.2 2.4 %collective-permute-start.6 = (bf16[1024,256]{1,0:T(8,128)(2,1)}, bf16[1024,256]{1,0:T(8,128)(2,1)}, u32[]{:S(2)}, u32[]{:S(2)}) collective-permute-start(bf16[1024,256]{1,0:T(8,128)(2,1)} %collective-permute-done.5.kv2), channel_id=1, source_target_pairs={{0,1},{1,0},{2,3},{3,2},{4,5},{5,4},{6,7},{7,6},{8,9},{9,8},{10,11... | collective-permute-start | bytes 1572872 | tf_op jit(solution)/shard_map/ppermute | solution.py:238
  62.0 1.0 broadcast_select_fusion.1
  63.5 1.0 copy-done.13
  64.5 9.6 %forward.1 = (bf16[1024,128]{1,0:T(8,128)(2,1)S(1)}, f32[1,1024]{1,0:T(1,128)S(1)}) custom-call(bf16[1024,128]{1,0:T(8,128)(2,1)S(1)} %get-tuple-element.23.q_ref, bf16[1024,256]{1,0:T(8,128)(2,1)S(1)} %copy-done.13, bf16[1024,256]{1,0:T(8,128)(2,1)} %collective-permute-done.4.kv1, bf16[1024,256]{1,0:T(8,128)(2,1)} %collective-permute-done.5.kv2, ...), custom_call_target="tpu_custom_call" | custom-call | flops 4294967296 | bytes 4194304 | tf_op jit(solution)/shard_map/forward/pallas_call | solution.py:103
  74.2 1.8 %collective-permute-done.8.other_ref = bf16[16,64,512]{2,1,0:T(8,128)(2,1)S(1)} collective-permute-done((bf16[16,64,512]{2,1,0:T(8,128)(2,1)S(1)}, bf16[16,64,512]{2,1,0:T(8,128)(2,1)S(1)}, u32[]{:S(2)}, u32[]{:S(2)}) %collective-permute-start.8) | collective-permute-done | bytes 1048608 | tf_op jit(solution)/shard_map/ppermute | solution.py:279
  75.9 1.0 copy-done.3
  76.9 1.2 copy-done.4
  78.3 0.7 fusion.26
  79.2 1.3 collective-permute-start.9
  80.5 1.5 collective-permute-done.9.peer_ref
  82.0 0.9 cross.1
  82.9 3.6 %all-to-all-start.1 = ((bf16[16,64,256]{2,1,0:T(8,128)(2,1)}), bf16[16,64,256]{2,1,0:T(8,128)(2,1)S(1)}, u32[]{:S(2)}, u32[]{:S(2)}) async-start(bf16[16,64,256]{2,1,0:T(8,128)(2,1)} %cross.1), calls=%async_computation.1 | async-start | bytes 1048576 | tf_op jit(solution)/shard_map/all_to_all | solution.py:251
  86.5 1.7 constant_dynamic-update-slice_fusion.1
  88.2 0.8 constant_dynamic-update-slice_fusion.refs_2_
  89.7 7.8 %all-to-all-done.1.x_ref = bf16[16,64,256]{2,1,0:T(8,128)(2,1)S(1)} async-done(((bf16[16,64,256]{2,1,0:T(8,128)(2,1)}), bf16[16,64,256]{2,1,0:T(8,128)(2,1)S(1)}, u32[]{:S(2)}, u32[]{:S(2)}) %all-to-all-start.1) | async-done | bytes 524320 | tf_op jit(solution)/shard_map/all_to_all | solution.py:251
  98.3 1.5 collective-permute-start.10
  99.8 1.2 collective-permute-done.18
  101.6 2.4 %collective-permute-done.19 = f32[2,1024]{1,0:T(2,128)S(1)} collective-permute-done((f32[2,1024]{1,0:T(2,128)S(1)}, f32[2,1024]{1,0:T(2,128)S(1)}, u32[]{:S(2)}, u32[]{:S(2)}) %collective-permute-start.19) | collective-permute-done | bytes 8224 | tf_op jit(solution)/shard_map/ppermute | solution.py:242
  104.1 1.1 collective-permute-start.14
  105.3 0.7 weight_terms.1
  106.0 1.4 copy-done
  107.4 6.2 %all-to-all-start.3 = ((bf16[16,64,1024]{2,1,0:T(8,128)(2,1)}), bf16[16,64,1024]{2,1,0:T(8,128)(2,1)}, u32[]{:S(2)}, u32[]{:S(2)}) async-start(bf16[16,64,1024]{2,1,0:T(8,128)(2,1)} %bitcast.64), calls=%async_computation.3 | async-start | bytes 4194304 | tf_op jit(solution)/shard_map/all_to_all | solution.py:251
  113.6 1.0 copy-done.14
  114.6 0.9 copy-done.16
  115.6 10.0 %query_grad.1 = bf16[1024,128]{1,0:T(8,128)(2,1)S(1)} custom-call(bf16[1024,128]{1,0:T(8,128)(2,1)S(1)} %copy-done.8, bf16[1024,128]{1,0:T(8,128)(2,1)S(1)} %copy-done.16, bf16[1024,128]{1,0:T(8,128)(2,1)S(1)} %copy-done.6, f32[1,1024]{1,0:T(1,128)S(1)} %get-tuple-element.31.lse_ref, bf16[1024,256]{1,0:T(8,128)(2,1)S(1)} %copy-done.14, ...), custom_call_target="tpu_custom_call" | custom-call | flops 6442450944 | bytes 4194304 | tf_op jit(solution)/shard_map/query_grad/pallas_call | solution.py:152
  126.1 1.0 collective-permute-start.17
  128.5 16.4 %key_grad.1 = (bf16[1024,128]{1,0:T(8,128)(2,1)S(1)}, bf16[1024,128]{1,0:T(8,128)(2,1)S(1)}) custom-call(bf16[1024,256]{1,0:T(8,128)(2,1)S(1)} %copy-done.14, f32[64,128]{1,0:T(8,128)S(1)} %pad.4.bias_ref.refs_1_, bf16[1024,256]{1,0:T(8,128)(2,1)} %constant_dynamic-update-slice_fusion.refs_2_, bf16[1024,256]{1,0:T(8,128)(2,1)} %collective-permute-done.12.refs_3_, ...), custom_call_target="tpu_custom_call" | custom-call | flops 8589934592 | bytes 4194304 | tf_op jit(solution)/shard_map/key_grad/pallas_call | solution.py:208
  144.9 1.0 pad_maximum_fusion
  145.9 6.9 %all-to-all-start.2 = ((bf16[16,64,384]{2,1,0:T(8,128)(2,1)}), bf16[16,64,384]{2,1,0:T(8,128)(2,1)S(1)}, u32[]{:S(2)}, u32[]{:S(2)}) async-start(bf16[16,64,384]{2,1,0:T(8,128)(2,1)} %pad_maximum_fusion), calls=%async_computation.2 | async-start | bytes 1572864 | tf_op jit(solution)/shard_map/all_to_all | solution.py:251
  152.9 2.0 %convert_reduce_fusion = f32[64,1024]{1,0:T(8,128)S(1)} fusion(bf16[16,64,1024]{2,1,0:T(8,128)(2,1)} %all-to-all-done.3), kind=kLoop, calls=%fused_computation | loop fusion | flops 2031616 | bytes 2359296 | tf_op jit(solution)/shard_map/reduce_sum | solution.py:494
  154.9 0.9 collective-permute-start.23
  155.8 0.8 collective-permute-start.22
  156.6 2.3 %collective-permute-start.21 = (f32[16,1024]{1,0:T(8,128)S(1)}, f32[16,1024]{1,0:T(8,128)S(1)}, u32[]{:S(2)}, u32[]{:S(2)}) collective-permute-start(f32[16,1024]{1,0:T(8,128)S(1)} %get-tuple-element.47), channel_id=1, source_target_pairs={{0,2},{2,0},{4,6},{6,4},{1,3},{3,1},{5,7},{7,5},{8,10},{10,8},{12,... | collective-permute-start | bytes 196616 | tf_op jit(solution)/shard_map/ppermute | solution.py:499
  158.9 7.4 %all-to-all-done.2.own_ref = bf16[16,64,384]{2,1,0:T(8,128)(2,1)S(1)} async-done(((bf16[16,64,384]{2,1,0:T(8,128)(2,1)}), bf16[16,64,384]{2,1,0:T(8,128)(2,1)S(1)}, u32[]{:S(2)}, u32[]{:S(2)}) %all-to-all-start.2) | async-done | bytes 786464 | tf_op jit(solution)/shard_map/all_to_all | solution.py:251
  166.3 1.9 %collective-permute-start.20 = (bf16[8,64,384]{2,1,0:T(8,128)(2,1)S(1)}, bf16[8,64,384]{2,1,0:T(8,128)(2,1)S(1)}, u32[]{:S(2)}, u32[]{:S(2)}) collective-permute-start(bf16[8,64,384]{2,1,0:T(8,128)(2,1)S(1)} %constant_dynamic-slice_fusion), channel_id=1, source_target_pairs={{0,1},{1,0},{2,3},{3,2},{4,5},{5,4},{6,7},{7,6},{8,9},{9,8},{10,11... | collective-permute-start | bytes 1179656 | tf_op jit(solution)/shard_map/ppermute | solution.py:238
  168.4 0.8 maximum_bitcast_fusion
  169.5 1.1 final.1
  (92 shorter events, 9.5 us)
Async XLA Ops:
  0.6 1.0 copy-start.9
  1.6 0.9 copy-start.10
  2.5 0.9 copy-start.11
  3.6 10.3 %collective-permute-start = (bf16[8,64,384]{2,1,0:T(8,128)(2,1)S(1)}, bf16[8,64,384]{2,1,0:T(8,128)(2,1)S(1)}, u32[]{:S(2)}, u32[]{:S(2)}) collective-permute-start(bf16[8,64,384]{2,1,0:T(8,128)(2,1)S(1)} %get-tuple-element.22), channel_id=1, source_target_pairs={{0,1},{1,0},{2,3},{3,2},{4,5},{5,4},{6,7},{7,6},{8,9},{9,8},{10,11... | collective-permute-start | bytes 1179656 | tf_op jit(solution)/shard_map/ppermute | solution.py:238
  5.9 3.6 %collective-permute-start.1 = (bf16[8,1024]{1,0:T(8,128)(2,1)S(1)}, bf16[8,1024]{1,0:T(8,128)(2,1)S(1)}, u32[]{:S(2)}, u32[]{:S(2)}) collective-permute-start(bf16[8,1024]{1,0:T(8,128)(2,1)S(1)} %get-tuple-element.56), channel_id=1, source_target_pairs={{0,1},{1,0},{2,3},{3,2},{4,5},{5,4},{6,7},{7,6},{8,9},{9,8},{10,11... | collective-permute-start | bytes 49160 | tf_op jit(solution)/shard_map/ppermute | solution.py:238
  5.9 4.2 %collective-permute-start.2 = (bf16[8,1024]{1,0:T(8,128)(2,1)S(1)}, bf16[8,1024]{1,0:T(8,128)(2,1)S(1)}, u32[]{:S(2)}, u32[]{:S(2)}) collective-permute-start(bf16[8,1024]{1,0:T(8,128)(2,1)S(1)} %get-tuple-element.57.w0), channel_id=1, source_target_pairs={{0,2},{2,0},{1,3},{3,1},{4,6},{6,4},{5,7},{7,5},{8,10},{10,8},{9,1... | collective-permute-start | bytes 49160 | tf_op jit(solution)/shard_map/ppermute | solution.py:419
  8.8 5.1 %collective-permute-start.3 = (bf16[8,1024]{1,0:T(8,128)(2,1)S(1)}, bf16[8,1024]{1,0:T(8,128)(2,1)S(1)}, u32[]{:S(2)}, u32[]{:S(2)}) collective-permute-start(bf16[8,1024]{1,0:T(8,128)(2,1)S(1)} %get-tuple-element.56), channel_id=1, source_target_pairs={{0,3},{1,2},{2,1},{3,0},{4,7},{5,6},{6,5},{7,4},{8,11},{9,10},{10,... | collective-permute-start | bytes 49160 | tf_op jit(solution)/shard_map/ppermute | solution.py:420
  14.1 33.4 %copy-start.18 = (bf16[1,128,2048]{2,1,0:T(8,128)(2,1)S(1)}, bf16[1,128,2048]{2,1,0:T(8,128)(2,1)}, u32[]{:S(2)}) copy-start(bf16[1,128,2048]{2,1,0:T(8,128)(2,1)} %param.13) | copy-start | bytes 1572868
  46.8 3.2 %copy-start.20 = (s32[64]{0:T(128)S(1)}, s32[64]{0:T(128)}, u32[]{:S(2)}) copy-start(s32[64]{0:T(128)} %param.10) | copy-start | bytes 772
  46.8 14.8 %copy-start.19 = (s32[64,64]{1,0:T(8,128)S(1)}, s32[64,64]{1,0:T(8,128)}, u32[]{:S(2)}) copy-start(s32[64,64]{1,0:T(8,128)} %param.11) | copy-start | bytes 49156
  47.1 16.0 %copy-start.1 = (bf16[16,64,512]{2,1,0:T(8,128)(2,1)}, bf16[16,64,512]{2,1,0:T(8,128)(2,1)S(1)}, u32[]{:S(2)}) copy-start(bf16[16,64,512]{2,1,0:T(8,128)(2,1)S(1)} %get-tuple-element.28.own_ref) | copy-start | bytes 3145732
  47.1 16.0 %copy-start.12 = (bf16[1024,256]{1,0:T(8,128)(2,1)}, bf16[1024,256]{1,0:T(8,128)(2,1)S(1)}, u32[]{:S(2)}) copy-start(bf16[1024,256]{1,0:T(8,128)(2,1)S(1)} %get-tuple-element.24.kv0.refs_0_) | copy-start | bytes 1572868
  47.1 27.1 %copy-start.7 = (bf16[1024,128]{1,0:T(8,128)(2,1)}, bf16[1024,128]{1,0:T(8,128)(2,1)S(1)}, u32[]{:S(2)}) copy-start(bf16[1024,128]{1,0:T(8,128)(2,1)S(1)} %get-tuple-element.23.q_ref) | copy-start | bytes 786436
  47.1 12.1 %collective-permute-start.5 = (bf16[1024,256]{1,0:T(8,128)(2,1)S(1)}, bf16[1024,256]{1,0:T(8,128)(2,1)}, u32[]{:S(2)}, u32[]{:S(2)}) collective-permute-start(bf16[1024,256]{1,0:T(8,128)(2,1)S(1)} %get-tuple-element.24.kv0.refs_0_), channel_id=1, source_target_pairs={{0,4},{4,0},{1,5},{5,1},{2,6},{6,2},{3,7},{7,3},{8,12},{12,8},{9,1... | collective-permute-start | bytes 1572872 | tf_op jit(solution)/shard_map/ppermute | solution.py:242
  48.4 13.6 %collective-permute-start.7 = (bf16[128,1024]{1,0:T(8,128)(2,1)}, bf16[128,1024]{1,0:T(8,128)(2,1)}, u32[]{:S(2)}, u32[]{:S(2)}) collective-permute-start(bf16[128,1024]{1,0:T(8,128)(2,1)} %broadcast_select_fusion.2), channel_id=1, source_target_pairs={{0,1},{1,0},{2,3},{3,2},{4,5},{5,4},{6,7},{7,6},{8,9},{9,8},{10,11... | collective-permute-start | bytes 786440 | tf_op jit(solution)/shard_map/ppermute | solution.py:238
  50.2 12.9 %collective-permute-start.4 = (bf16[1024,256]{1,0:T(8,128)(2,1)S(1)}, bf16[1024,256]{1,0:T(8,128)(2,1)}, u32[]{:S(2)}, u32[]{:S(2)}) collective-permute-start(bf16[1024,256]{1,0:T(8,128)(2,1)S(1)} %get-tuple-element.24.kv0.refs_0_), channel_id=1, source_target_pairs={{0,1},{1,0},{2,3},{3,2},{4,5},{5,4},{6,7},{7,6},{8,9},{9,8},{10,11... | collective-permute-start | bytes 1572872 | tf_op jit(solution)/shard_map/ppermute | solution.py:238
  50.3 25.6 %collective-permute-start.8 = (bf16[16,64,512]{2,1,0:T(8,128)(2,1)S(1)}, bf16[16,64,512]{2,1,0:T(8,128)(2,1)S(1)}, u32[]{:S(2)}, u32[]{:S(2)}) collective-permute-start(bf16[16,64,512]{2,1,0:T(8,128)(2,1)S(1)} %get-tuple-element.28.own_ref), channel_id=1, source_target_pairs={{0,6},{2,4},{4,2},{6,0},{1,7},{3,5},{5,3},{7,1},{8,14},{10,12},{12... | collective-permute-start | bytes 3145736 | tf_op jit(solution)/shard_map/ppermute | solution.py:279
  59.2 4.3 %collective-permute-start.6 = (bf16[1024,256]{1,0:T(8,128)(2,1)}, bf16[1024,256]{1,0:T(8,128)(2,1)}, u32[]{:S(2)}, u32[]{:S(2)}) collective-permute-start(bf16[1024,256]{1,0:T(8,128)(2,1)} %collective-permute-done.5.kv2), channel_id=1, source_target_pairs={{0,1},{1,0},{2,3},{3,2},{4,5},{5,4},{6,7},{7,6},{8,9},{9,8},{10,11... | collective-permute-start | bytes 1572872 | tf_op jit(solution)/shard_map/ppermute | solution.py:238
  63.5 1.0 copy-start.13
  64.5 12.4 %copy-start.2 = (bf16[16,64,512]{2,1,0:T(8,128)(2,1)S(1)}, bf16[16,64,512]{2,1,0:T(8,128)(2,1)}, u32[]{:S(2)}) copy-start(bf16[16,64,512]{2,1,0:T(8,128)(2,1)} %copy-done.1) | copy-start | bytes 3145732
  75.9 1.0 copy-start.3
  76.9 1.2 copy-start.4
  79.2 2.9 %collective-permute-start.9 = (f32[128,1024]{1,0:T(8,128)S(1)}, f32[128,1024]{1,0:T(8,128)S(1)}, u32[]{:S(2)}, u32[]{:S(2)}) collective-permute-start(f32[128,1024]{1,0:T(8,128)S(1)} %get-tuple-element.37), channel_id=1, source_target_pairs={{0,1},{1,0},{2,3},{3,2},{4,5},{5,4},{6,7},{7,6},{8,9},{9,8},{10,11... | collective-permute-start | bytes 1572872 | tf_op jit(solution)/shard_map/ppermute | solution.py:238
  82.9 14.5 %all-to-all-start.1 = ((bf16[16,64,256]{2,1,0:T(8,128)(2,1)}), bf16[16,64,256]{2,1,0:T(8,128)(2,1)S(1)}, u32[]{:S(2)}, u32[]{:S(2)}) async-start(bf16[16,64,256]{2,1,0:T(8,128)(2,1)} %cross.1), calls=%async_computation.1 | async-start | bytes 1048576 | tf_op jit(solution)/shard_map/all_to_all | solution.py:251
  89.7 14.3 %collective-permute-start.13 = (bf16[1024,256]{1,0:T(8,128)(2,1)}, bf16[1024,256]{1,0:T(8,128)(2,1)}, u32[]{:S(2)}, u32[]{:S(2)}) collective-permute-start(bf16[1024,256]{1,0:T(8,128)(2,1)} %constant_dynamic-update-slice_fusion.refs_2_), channel_id=1, source_target_pairs={{0,4},{4,0},{1,5},{5,1},{2,6},{6,2},{3,7},{7,3},{8,12},{12,8},{9,1... | collective-permute-start | bytes 1572872 | tf_op jit(solution)/shard_map/ppermute | solution.py:242
  97.6 0.7 copy-start.15
  98.3 7.0 %collective-permute-start.10 = (bf16[128,1024]{1,0:T(8,128)(2,1)S(1)}, bf16[128,1024]{1,0:T(8,128)(2,1)S(1)}, u32[]{:S(2)}, u32[]{:S(2)}) collective-permute-start(bf16[128,1024]{1,0:T(8,128)(2,1)S(1)} %get-tuple-element.29.own_ref), channel_id=1, source_target_pairs={{0,1},{1,0},{2,3},{3,2},{4,5},{5,4},{6,7},{7,6},{8,9},{9,8},{10,11... | collective-permute-start | bytes 786440 | tf_op jit(solution)/shard_map/ppermute | solution.py:238
  99.8 1.2 collective-permute-start.18
  101.0 3.1 %collective-permute-start.19 = (f32[2,1024]{1,0:T(2,128)S(1)}, f32[2,1024]{1,0:T(2,128)S(1)}, u32[]{:S(2)}, u32[]{:S(2)}) collective-permute-start(f32[2,1024]{1,0:T(2,128)S(1)} %pad_maximum_fusion.8), channel_id=1, source_target_pairs={{0,4},{4,0},{1,5},{5,1},{2,6},{6,2},{3,7},{7,3},{8,12},{12,8},{9,1... | collective-permute-start | bytes 24584 | tf_op jit(solution)/shard_map/ppermute | solution.py:242
  101.1 26.7 %collective-permute-start.12 = (bf16[1024,256]{1,0:T(8,128)(2,1)}, bf16[1024,256]{1,0:T(8,128)(2,1)}, u32[]{:S(2)}, u32[]{:S(2)}) collective-permute-start(bf16[1024,256]{1,0:T(8,128)(2,1)} %constant_dynamic-update-slice_fusion.refs_2_), channel_id=1, source_target_pairs={{0,1},{1,0},{2,3},{3,2},{4,5},{5,4},{6,7},{7,6},{8,9},{9,8},{10,11... | collective-permute-start | bytes 1572872 | tf_op jit(solution)/shard_map/ppermute | solution.py:238
  104.1 23.7 %collective-permute-start.14 = (bf16[1024,256]{1,0:T(8,128)(2,1)}, bf16[1024,256]{1,0:T(8,128)(2,1)}, u32[]{:S(2)}, u32[]{:S(2)}) collective-permute-start(bf16[1024,256]{1,0:T(8,128)(2,1)} %collective-permute-done.13.refs_4_), channel_id=1, source_target_pairs={{0,1},{1,0},{2,3},{3,2},{4,5},{5,4},{6,7},{7,6},{8,9},{9,8},{10,11... | collective-permute-start | bytes 1572872 | tf_op jit(solution)/shard_map/ppermute | solution.py:238
  105.2 22.6 %collective-permute-start.15 = (bf16[1024,128]{1,0:T(8,128)(2,1)}, bf16[1024,128]{1,0:T(8,128)(2,1)}, u32[]{:S(2)}, u32[]{:S(2)}) collective-permute-start(bf16[1024,128]{1,0:T(8,128)(2,1)} %copy-done.15), channel_id=1, source_target_pairs={{0,1},{1,0},{2,3},{3,2},{4,5},{5,4},{6,7},{7,6},{8,9},{9,8},{10,11... | collective-permute-start | bytes 786440 | tf_op jit(solution)/shard_map/ppermute | solution.py:238
  105.3 20.8 %collective-permute-start.16 = (bf16[1024,128]{1,0:T(8,128)(2,1)}, bf16[1024,128]{1,0:T(8,128)(2,1)}, u32[]{:S(2)}, u32[]{:S(2)}) collective-permute-start(bf16[1024,128]{1,0:T(8,128)(2,1)} %copy-done.15), channel_id=1, source_target_pairs={{0,4},{4,0},{1,5},{5,1},{2,6},{6,2},{3,7},{7,3},{8,12},{12,8},{9,1... | collective-permute-start | bytes 786440 | tf_op jit(solution)/shard_map/ppermute | solution.py:242
  106.0 1.4 copy-start
  107.4 6.2 %copy-start.6 = (bf16[1024,128]{1,0:T(8,128)(2,1)S(1)}, bf16[1024,128]{1,0:T(8,128)(2,1)}, u32[]{:S(2)}) copy-start(bf16[1024,128]{1,0:T(8,128)(2,1)} %copy-done.5) | copy-start | bytes 786436
  107.4 6.2 %copy-start.8 = (bf16[1024,128]{1,0:T(8,128)(2,1)S(1)}, bf16[1024,128]{1,0:T(8,128)(2,1)}, u32[]{:S(2)}) copy-start(bf16[1024,128]{1,0:T(8,128)(2,1)} %copy-done.7) | copy-start | bytes 786436
  107.4 38.5 %all-to-all-start.3 = ((bf16[16,64,1024]{2,1,0:T(8,128)(2,1)}), bf16[16,64,1024]{2,1,0:T(8,128)(2,1)}, u32[]{:S(2)}, u32[]{:S(2)}) async-start(bf16[16,64,1024]{2,1,0:T(8,128)(2,1)} %bitcast.64), calls=%async_computation.3 | async-start | bytes 4194304 | tf_op jit(solution)/shard_map/all_to_all | solution.py:251
  113.6 1.0 copy-start.14
  114.6 0.9 copy-start.16
  126.0 2.4 %copy-start.17 = (bf16[1024,128]{1,0:T(8,128)(2,1)S(1)}, bf16[1024,128]{1,0:T(8,128)(2,1)}, u32[]{:S(2)}) copy-start(bf16[1024,128]{1,0:T(8,128)(2,1)} %copy-done.15) | copy-start | bytes 786436
  126.1 2.4 %collective-permute-start.17 = (bf16[1024,128]{1,0:T(8,128)(2,1)}, bf16[1024,128]{1,0:T(8,128)(2,1)S(1)}, u32[]{:S(2)}, u32[]{:S(2)}) collective-permute-start(bf16[1024,128]{1,0:T(8,128)(2,1)} %collective-permute-done.16.refs_8_), channel_id=1, source_target_pairs={{0,1},{1,0},{2,3},{3,2},{4,5},{5,4},{6,7},{7,6},{8,9},{9,8},{10,11... | collective-permute-start | bytes 786440 | tf_op jit(solution)/shard_map/ppermute | solution.py:238
  127.6 25.2 %collective-permute-start.11 = (bf16[2,64,1024]{2,1,0:T(8,128)(2,1)S(1)}, bf16[2,64,1024]{2,1,0:T(8,128)(2,1)S(1)}, u32[]{:S(2)}, u32[]{:S(2)}) collective-permute-start(bf16[2,64,1024]{2,1,0:T(8,128)(2,1)S(1)} %pad_maximum_fusion.4), channel_id=1, source_target_pairs={{0,1},{1,0},{2,3},{3,2},{4,5},{5,4},{6,7},{7,6},{8,9},{9,8},{10,11... | collective-permute-start | bytes 786440 | tf_op jit(solution)/shard_map/ppermute | solution.py:238
  145.9 20.4 %all-to-all-start.2 = ((bf16[16,64,384]{2,1,0:T(8,128)(2,1)}), bf16[16,64,384]{2,1,0:T(8,128)(2,1)S(1)}, u32[]{:S(2)}, u32[]{:S(2)}) async-start(bf16[16,64,384]{2,1,0:T(8,128)(2,1)} %pad_maximum_fusion), calls=%async_computation.2 | async-start | bytes 1572864 | tf_op jit(solution)/shard_map/all_to_all | solution.py:251
  154.9 13.3 %collective-permute-start.23 = (f32[16,1024]{1,0:T(8,128)S(1)}, f32[16,1024]{1,0:T(8,128)S(1)}, u32[]{:S(2)}, u32[]{:S(2)}) collective-permute-start(f32[16,1024]{1,0:T(8,128)S(1)} %get-tuple-element.48), channel_id=1, source_target_pairs={{0,6},{2,4},{4,2},{6,0},{1,7},{3,5},{5,3},{7,1},{8,14},{10,12},{12... | collective-permute-start | bytes 196616 | tf_op jit(solution)/shard_map/ppermute | solution.py:499
  155.8 12.4 %collective-permute-start.22 = (f32[16,1024]{1,0:T(8,128)S(1)}, f32[16,1024]{1,0:T(8,128)S(1)}, u32[]{:S(2)}, u32[]{:S(2)}) collective-permute-start(f32[16,1024]{1,0:T(8,128)S(1)} %get-tuple-element.49), channel_id=1, source_target_pairs={{0,4},{2,6},{4,0},{6,2},{1,5},{3,7},{5,1},{7,3},{8,12},{10,14},{12... | collective-permute-start | bytes 196616 | tf_op jit(solution)/shard_map/ppermute | solution.py:499
  156.6 11.6 %collective-permute-start.21 = (f32[16,1024]{1,0:T(8,128)S(1)}, f32[16,1024]{1,0:T(8,128)S(1)}, u32[]{:S(2)}, u32[]{:S(2)}) collective-permute-start(f32[16,1024]{1,0:T(8,128)S(1)} %get-tuple-element.47), channel_id=1, source_target_pairs={{0,2},{2,0},{4,6},{6,4},{1,3},{3,1},{5,7},{7,5},{8,10},{10,8},{12,... | collective-permute-start | bytes 196616 | tf_op jit(solution)/shard_map/ppermute | solution.py:499
  166.3 3.2 %collective-permute-start.20 = (bf16[8,64,384]{2,1,0:T(8,128)(2,1)S(1)}, bf16[8,64,384]{2,1,0:T(8,128)(2,1)S(1)}, u32[]{:S(2)}, u32[]{:S(2)}) collective-permute-start(bf16[8,64,384]{2,1,0:T(8,128)(2,1)S(1)} %constant_dynamic-slice_fusion), channel_id=1, source_target_pairs={{0,1},{1,0},{2,3},{3,2},{4,5},{5,4},{6,7},{7,6},{8,9},{9,8},{10,11... | collective-permute-start | bytes 1179656 | tf_op jit(solution)/shard_map/ppermute | solution.py:238
  168.3 2.4 %collective-permute-start.24 = (f32[8,1024]{1,0:T(8,128)S(1)}, f32[8,1024]{1,0:T(8,128)S(1)}, u32[]{:S(2)}, u32[]{:S(2)}) collective-permute-start(f32[8,1024]{1,0:T(8,128)S(1)} %dynamic-slice_bitcast_fusion.3), channel_id=1, source_target_pairs={{0,1},{1,0},{2,3},{3,2},{4,5},{5,4},{6,7},{7,6},{8,9},{9,8},{10,11... | collective-permute-start | bytes 98312 | tf_op jit(solution)/shard_map/ppermute | solution.py:238
  (1 other events, 0.7 us)

commit v6 on v5

--- a/solution.py
+++ b/solution.py
@@ -11,9 +11,11 @@
 HEAD = 128
 SPAN = 64
 UNITS = 16
+MANY = 12
 ROWS = UNITS * SPAN
 TILE = 256
 LOW = -1e30
+GRANT = 16 << 20
 SCALE = 1.0 / HEAD
 F32 = jnp.float32
 BF16 = jnp.bfloat16
@@ -22,6 +24,10 @@
 TN = (((0,), (0,)), ((), ()))
 
 
+def in_hbm(x):
+    return pltpu.with_memory_space_constraint(x, pltpu.HBM)
+
+
 def dot(a, b, dims):
     return lax.dot_general(a, b, dims, preferred_element_type=F32)
 
@@ -40,11 +46,12 @@
     return jnp.broadcast_to(bias[:, None, :], (UNITS, SPAN, HEAD)).reshape(ROWS, HEAD).astype(BF16)
 
 
-def fill_keys(chunks, bias_ref, ka_ref):
+def fill_keys(chunks, bias_ref, ka_ref, first_chunk=0):
     for c, kv_ref in enumerate(chunks):
         rows = pl.ds(c * ROWS, ROWS)
+        spans = slice((first_chunk + c) * UNITS, (first_chunk + c + 1) * UNITS)
         ka_ref[rows, :HEAD] = kv_ref[:, :HEAD]
-        ka_ref[rows, HEAD:] = spread_bias(bias_ref[c * UNITS : (c + 1) * UNITS, :])
+        ka_ref[rows, HEAD:] = spread_bias(bias_ref[spans, :])
 
 
 def later_in_span():
@@ -53,32 +60,46 @@
     return (key // SPAN == query // SPAN) & (key > query)
 
 
-def forward_body(q_ref, kv0, kv1, kv2, kv3, bias_ref, att_ref, lse_ref, ka_ref, s_ref):
+def forward_body(first, *refs):
+    if first:
+        q_ref, kv0, kv1, bias_ref, o_ref, m_ref, l_ref, ka_ref, s_ref = refs
+    else:
+        q_ref, kv0, kv1, bias_ref, o0_ref, m0_ref, l0_ref, pair_ref, lse_ref, ka_ref, s_ref = refs
     step = pl.program_id(0)
-    chunks = (kv0, kv1, kv2, kv3)
+    chunks = (kv0, kv1)
 
     @pl.when(step == 0)
     def _():
-        fill_keys(chunks, bias_ref, ka_ref)
-
-    qa = query_wide(q_ref[...], step * (TILE // SPAN))
-    top = None
-    for c in range(4):
+        fill_keys(chunks, bias_ref, ka_ref, 0 if first else 2)
+
+    q = q_ref[...]
+    qa = query_wide(q, step * (TILE // SPAN))
+    top = None if first else m0_ref[...]
+    for c in range(2):
         rows = pl.ds(c * ROWS, ROWS)
         s_ref[rows, :] = dot(ka_ref[rows, :], qa, NT)
-        if c == 0:
+        if first and c == 0:
             own = pl.ds(pl.multiple_of(step * TILE, TILE), TILE)
             s_ref[own, :] = jnp.where(later_in_span(), LOW, s_ref[own, :])
         chunk_top = jnp.max(s_ref[rows, :], axis=0, keepdims=True)
-        top = chunk_top if c == 0 else jnp.maximum(top, chunk_top)
+        top = chunk_top if top is None else jnp.maximum(top, chunk_top)
     total = jnp.zeros((1, TILE), F32)
     out = jnp.zeros((HEAD, TILE), F32)
     for c, kv_ref in enumerate(chunks):
         weights = jnp.exp(s_ref[pl.ds(c * ROWS, ROWS), :] - top)
         total += jnp.sum(weights, axis=0, keepdims=True)
         out += dot(kv_ref[:, HEAD:], weights.astype(BF16), TN)
-    att_ref[...] = (out / total).T.astype(BF16)
-    lse_ref[...] = top + jnp.log(total)
+    if first:
+        o_ref[...] = out
+        m_ref[...] = top
+        l_ref[...] = total
+    else:
+        fade = jnp.exp(m0_ref[...] - top)
+        total += l0_ref[...] * fade
+        out = (out + o0_ref[...] * fade) / total
+        pair_ref[:, :HEAD] = q
+        pair_ref[:, HEAD:] = out.T.astype(BF16)
+        lse_ref[...] = top + jnp.log(total)
 
 
 def tile_spec(cols):
@@ -99,31 +120,40 @@
     return pl.BlockSpec(shape, lambda i: (0,) * len(shape), pipeline_mode=pl.Buffered(1))
 
 
-def forward(q, kvs, bias):
+def forward(first, q, kvs, bias, *carry):
+    stat = jax.ShapeDtypeStruct((1, ROWS), F32)
+    if first:
+        outs = [pltpu.HBM((HEAD, ROWS), F32), stat, stat]
+        out_specs = [row_spec(HEAD), row_spec(1), row_spec(1)]
+    else:
+        outs = [pltpu.HBM((ROWS, 2 * HEAD), BF16), stat]
+        out_specs = [tile_spec(2 * HEAD), row_spec(1)]
     return pl.pallas_call(
-        forward_body,
-        out_shape=[
-            jax.ShapeDtypeStruct((ROWS, HEAD), BF16),
-            jax.ShapeDtypeStruct((1, ROWS), F32),
+        functools.partial(forward_body, first),
+        out_shape=outs,
+        grid=(ROWS // TILE,),
+        in_specs=[
+            tile_spec(HEAD),
+            *[once(ROWS, 2 * HEAD)] * 2,
+            once(4 * UNITS, HEAD),
+            *[row_spec(x.shape[0]) for x in carry],
         ],
-        grid=(ROWS // TILE,),
-        in_specs=[tile_spec(HEAD), *[once(ROWS, 2 * HEAD)] * 4, once(4 * UNITS, HEAD)],
-        out_specs=[tile_spec(HEAD), row_spec(1)],
+        out_specs=out_specs,
         scratch_shapes=[
-            pltpu.VMEM((4 * ROWS, 2 * HEAD), BF16),
-            pltpu.VMEM((4 * ROWS, TILE), F32),
+            pltpu.VMEM((2 * ROWS, 2 * HEAD), BF16),
+            pltpu.VMEM((2 * ROWS, TILE), F32),
         ],
-        cost_estimate=cost(2, 4 * ROWS * ROWS),
-        compiler_params=pltpu.CompilerParams(vmem_limit_bytes=24 << 20),
-        name="forward",
-    )(q, *kvs, bias)
+        cost_estimate=cost(2, 2 * ROWS * ROWS),
+        compiler_params=pltpu.CompilerParams(vmem_limit_bytes=GRANT),
+        name="forward_near" if first else "forward_far",
+    )(q, *kvs, bias, *carry)
 
 
 def row_delta(g, att):
     return jnp.sum((g.astype(F32) * att.astype(F32)).T, axis=0, keepdims=True)
 
 
-def query_body(q_ref, g_ref, att_ref, lse_ref, kv0, kv1, kv2, kv3, bias_ref, dq_ref, ka_ref, s_ref):
+def query_body(pair_ref, g_ref, lse_ref, far_ref, kv0, kv1, kv2, kv3, bias_ref, dq_ref, ka_ref, s_ref):
     step = pl.program_id(0)
     chunks = (kv0, kv1, kv2, kv3)
 
@@ -131,10 +161,10 @@
     def _():
         fill_keys(chunks, bias_ref, ka_ref)
 
-    qa = query_wide(q_ref[...], step * (TILE // SPAN))
+    qa = query_wide(pair_ref[:, :HEAD], step * (TILE // SPAN))
     g = g_ref[...]
     lse = lse_ref[...]
-    delta = row_delta(g, att_ref[...])
+    delta = row_delta(g, pair_ref[:, HEAD:])
     total = jnp.zeros((HEAD, TILE), F32)
     for c, kv_ref in enumerate(chunks):
         s_ref[...] = dot(ka_ref[pl.ds(c * ROWS, ROWS), :], qa, NT)
@@ -148,16 +178,16 @@
     dq_ref[...] = (total * SCALE).T.astype(BF16)
 
 
-def query_grad(q, g, att, lse, kvs, bias):
+def query_grad(pair, g, lse, far, kvs, bias):
     return pl.pallas_call(
         query_body,
         out_shape=jax.ShapeDtypeStruct((ROWS, HEAD), BF16),
         grid=(ROWS // TILE,),
         in_specs=[
-            tile_spec(HEAD),
-            tile_spec(HEAD),
+            tile_spec(2 * HEAD),
             tile_spec(HEAD),
             row_spec(1),
+            pl.BlockSpec(memory_space=pl.ANY),
             *[once(ROWS, 2 * HEAD)] * 4,
             once(4 * UNITS, HEAD),
         ],
@@ -167,9 +197,9 @@
             pltpu.VMEM((ROWS, TILE), F32),
         ],
         cost_estimate=cost(3, 4 * ROWS * ROWS),
-        compiler_params=pltpu.CompilerParams(vmem_limit_bytes=16 << 20),
+        compiler_params=pltpu.CompilerParams(vmem_limit_bytes=GRANT),
         name="query_grad",
-    )(q, g, att, lse, *kvs, bias)
+    )(pair, g, lse, far, *kvs, bias)
 
 
 def key_body(*refs):
@@ -224,7 +254,7 @@
             pltpu.VMEM((ROWS, HEAD), F32),
         ],
         cost_estimate=cost(4, 4 * ROWS * ROWS),
-        compiler_params=pltpu.CompilerParams(vmem_limit_bytes=16 << 20),
+        compiler_params=pltpu.CompilerParams(vmem_limit_bytes=GRANT),
         name="key_grad",
     )(kv, bias, *pairs, *gs, lses)
 
@@ -279,24 +309,25 @@
     return lax.ppermute(x, ("xl", "xh"), [(k, k ^ 3) for k in range(4)])
 
 
-def weight_body(xl_ref, own_ref, other_ref, out_ref):
-    for flip, part in enumerate((own_ref, other_ref)):
-        for c in range(2):
-            rows = part[:, c * 32 : (c + 1) * 32, :]
-            out_ref[:, xl_ref[0] ^ flip, :, c * 512 : (c + 1) * 512] = rows
+def weight_body(xl_ref, own0, own1, other0, other1, out_ref):
+    for flip, pieces in enumerate(((own0, own1), (other0, other1))):
+        for units, part in zip((slice(0, MANY), slice(MANY, UNITS)), pieces):
+            for c in range(2):
+                rows = part[:, c * 32 : (c + 1) * 32, :]
+                out_ref[units, xl_ref[0] ^ flip, :, c * 512 : (c + 1) * 512] = rows
 
 
 def weight_whole(xl, own, other):
     return pl.pallas_call(
         weight_body,
-        out_shape=jax.ShapeDtypeStruct((UNITS, 2, 32, 1024), BF16),
+        out_shape=pltpu.HBM((UNITS, 2, 32, 1024), BF16),
         grid=(1,),
-        in_specs=[pl.BlockSpec(memory_space=pltpu.SMEM)] + [once(UNITS, SPAN, 512)] * 2,
+        in_specs=[pl.BlockSpec(memory_space=pltpu.SMEM)] + [once(*x.shape) for x in (*own, *other)],
         out_specs=once(UNITS, 2, 32, 1024),
         cost_estimate=pl.CostEstimate(flops=0, bytes_accessed=4 << 20, transcendentals=0),
-        compiler_params=pltpu.CompilerParams(vmem_limit_bytes=12 << 20),
+        compiler_params=pltpu.CompilerParams(vmem_limit_bytes=GRANT),
         name="weight_whole",
-    )(xl, own, other)
+    )(xl, *own, *other)
 
 
 def term_body(own_ref, peer_ref, up_ref, out_ref):
@@ -309,14 +340,14 @@
 def weight_terms(own, peer, up):
     return pl.pallas_call(
         term_body,
-        out_shape=jax.ShapeDtypeStruct((1024, 1024), BF16),
+        out_shape=pltpu.HBM((1024, 1024), BF16),
         grid=(1,),
         in_specs=[once(128, 1024), once(128, 1024), once(256, 1024)],
         out_specs=once(1024, 1024),
         cost_estimate=pl.CostEstimate(
             flops=2 * 256 * 1024 * 1024, bytes_accessed=4 << 20, transcendentals=0
         ),
-        compiler_params=pltpu.CompilerParams(vmem_limit_bytes=16 << 20),
+        compiler_params=pltpu.CompilerParams(vmem_limit_bytes=GRANT),
         name="weight_terms",
     )(own, peer, up)
 
@@ -324,15 +355,15 @@
 IN_SMEM = pl.BlockSpec(memory_space=pltpu.SMEM)
 
 
-def move(body, name, outs, scalars, *arrays):
+def move(body, name, outs, scalars, *arrays, space=jax.ShapeDtypeStruct):
     return pl.pallas_call(
         body,
-        out_shape=[jax.ShapeDtypeStruct(shape, BF16) for shape in outs],
+        out_shape=[space(shape, BF16) for shape in outs],
         grid=(1,),
         in_specs=[IN_SMEM] * len(scalars) + [once(*x.shape) for x in arrays],
         out_specs=[once(*shape) for shape in outs],
         cost_estimate=pl.CostEstimate(flops=0, bytes_accessed=4 << 20, transcendentals=0),
-        compiler_params=pltpu.CompilerParams(vmem_limit_bytes=12 << 20),
+        compiler_params=pltpu.CompilerParams(vmem_limit_bytes=GRANT),
         name=name,
     )(*scalars, *arrays)
 
@@ -370,18 +401,19 @@
             out_ref[unit, c * 32 : (c + 1) * 32, 3 * HEAD :] = part
 
 
-def split_body(x_ref, q_ref, kv_ref, w_ref):
+def split_body(x_ref, q_ref, kv_ref, w0_ref, w1_ref):
     x = x_ref[...]
     q_ref[...] = x[:, :, :HEAD].reshape(ROWS, HEAD)
     kv_ref[...] = x[:, :, HEAD : 3 * HEAD].reshape(ROWS, 2 * HEAD)
-    w_ref[...] = x[:, :, 3 * HEAD :]
-
-
-def cross_body(att_ref, own_ref, peer_ref, out_ref):
+    w0_ref[...] = x[:MANY, :, 3 * HEAD :]
+    w1_ref[...] = x[MANY:, :, 3 * HEAD :]
+
+
+def cross_body(pair_ref, own_ref, peer_ref, lses_ref, out_ref):
     for s in range(2):
         for h in range(HEADS):
             unit, rows = s * HEADS + h, slice(s * SPAN, (s + 1) * SPAN)
-            out_ref[unit, :, :HEAD] = att_ref[unit * SPAN : (unit + 1) * SPAN, :]
+            out_ref[unit, :, :HEAD] = pair_ref[unit * SPAN : (unit + 1) * SPAN, HEAD:]
             total = own_ref[rows, head_cols(h)] + peer_ref[rows, head_cols(h)]
             out_ref[unit, :, HEAD:] = total.astype(BF16)
 
@@ -425,58 +457,77 @@
         "cut",
         [unit_rows] * 2,
         [half_1],
-        query_states[0],
-        key_states[0],
-        value_states[0],
+        in_hbm(query_states[0]),
+        in_hbm(key_states[0]),
+        in_hbm(value_states[0]),
+        space=pltpu.HBM,
     )
     (blocks,) = move(
         fill_body,
         "fill",
         [(UNITS, SPAN, 3 * HEAD + 512)],
         [core_1, xh_1],
-        own,
+        in_hbm(own),
         other_core(sent),
         *weight_rows,
     )
     blocks = exchange(blocks, ZY)
-    q, own_kv, weight_own = move(
+    q, own_kv, *weight_own = move(
         split_body,
         "split",
-        [(ROWS, HEAD), (ROWS, 2 * HEAD), (UNITS, SPAN, 512)],
+        [(ROWS, HEAD), (ROWS, 2 * HEAD), (MANY, SPAN, 512), (UNITS - MANY, SPAN, 512)],
         [],
         blocks,
+        space=pltpu.HBM,
     )
     far_kv = other_chip(own_kv)
-    weight_other = across(weight_own)
-    kvs = (own_kv, other_core(own_kv), far_kv, other_core(far_kv))
+    weight_other = [across(weight_own[0]), other_chip(weight_own[1])]
+    near_kv = other_core(own_kv)
     bias = span_bias(span_order, block_mask, xl, core)
 
     up_mine, up_theirs = by_core(upstream[0])
     up = in_order(first_core, up_mine, other_core(up_theirs)).reshape(2, 2, SPAN, cols)
     up = in_order(half == 0, up[:, 0], up[:, 1]).reshape(4 * SPAN, cols)
 
-    attended, lse = forward(q, kvs, bias)
+    out, top, total = forward(True, in_hbm(q), (in_hbm(own_kv), near_kv), bias)
+    far_kv, total = lax.optimization_barrier((far_kv, total))
+    kvs = (own_kv, near_kv, far_kv, other_core(far_kv))
+    pair, lse = forward(False, in_hbm(q), kvs[2:], bias, in_hbm(out), top, total)
+    lses = jnp.concatenate([lse, other_core(lse)], axis=0)
+    lses = jnp.concatenate([lses, other_chip(lses)], axis=0)
 
     place, lse = lax.optimization_barrier((xl_1, lse))
-    weight = weight_whole(place, weight_own, weight_other).reshape(HEADS * HEAD, cols)
+    weight = weight_whole(place, [in_hbm(x) for x in weight_own], weight_other).reshape(HEADS * HEAD, cols)
     grad_rows = dot(up, weight, NT)
     grad_own, grad_sent = grad_rows[: 2 * SPAN], grad_rows[2 * SPAN :]
     (crossing,) = move(
-        cross_body, "cross", [(UNITS, SPAN, 2 * HEAD)], [], attended, grad_own, other_core(grad_sent)
+        cross_body,
+        "cross",
+        [(UNITS, SPAN, 2 * HEAD)],
+        [],
+        in_hbm(pair),
+        grad_own,
+        other_core(grad_sent),
+        lses,
     )
     crossed = exchange(crossing, ZY)
-    pairs = everyone(jnp.concatenate([q, attended], axis=1))
-    lses = jnp.concatenate([lse, other_core(lse)], axis=0)
-    lses = jnp.concatenate([lses, other_chip(lses)], axis=0)
-
-    att_own, g = move(land_body, "land", [(2 * SPAN, HEADS * HEAD), (ROWS, HEAD)], [], crossed)
+    pairs = everyone(pair)
+
+    att_own, g = move(
+        land_body,
+        "land",
+        [(2 * SPAN, HEADS * HEAD), (ROWS, HEAD)],
+        [],
+        crossed,
+        space=pltpu.HBM,
+    )
     gs = everyone(g)
     att_peer = other_core(att_own)
     term = weight_terms(att_own, att_peer, up).reshape(UNITS, SPAN, cols)
     term = exchange(term, ZY)
 
-    query_out = query_grad(q, g, attended, lse, kvs, bias)
-    key_out, value_out = key_grad(own_kv, bias, pairs, gs, lses)
+    query_out = query_grad(in_hbm(pair), in_hbm(g), lse, pairs[2], [in_hbm(x) for x in kvs], bias)
+    key_out, value_out = key_grad(in_hbm(own_kv), bias, pairs, gs, lses)
     grads = [x.reshape(UNITS, SPAN, HEAD) for x in (query_out, key_out, value_out)]
     grads = exchange(jnp.concatenate(grads, axis=2), ZY)
 

time: 172 us -> 170 us (0.988)
  Pallas kernels: 39.5 us -> 53.7 us
  local copies, waits for them, and re-layouts: 13.6 us -> 1.17 us
  waiting for transfers between devices: 36.2 us -> 30.9 us
    pallas_call x9 -> x10, Pallas kernels: 13.1 us -> 27.4 us  [the longest x2 14 us: forward(): pl.pallas_call(functools.partial(forward_body, first), out_shape=outs, gr...]
    unnamed x43 -> x26, local copies, waits for them, and re-layouts: 12.6 us -> 1 us
    ppermute x4 -> x5, waiting for transfers between devices: 10.7 us -> 7.31 us  [other_chip(): return lax.ppermute(x, 'xl', SWAP)]
    ppermute x15, starting transfers between devices: 13.5 us -> 11.7 us  [other_core(): return lax.ppermute(x, 'core', SWAP)]
    ppermute x1, waiting for transfers between devices: 1.76 us -> 0.01 us  [across(): return lax.ppermute(x, ('xl', 'xh'), [(k, k ^ 3) for k in range(4)])]
  transfers between devices with their start and end apart: 28 -> 29, of which waited for: 12 -> 11; matrix products, arithmetic and copies ran while one was open for 6% -> 5% of each run, Pallas kernels for 22% -> 26%
where the time goes in v6:
time: 170 us; the launch traced here: 169 us
  Pallas kernels  53.7 us (32%)
  starting transfers between devices  38.7 us (23%)
  blocking collectives  32.7 us (19%)
  waiting for transfers between devices  30.9 us (18%)
  other arithmetic  7.44 us (4%)
  matrix products  3.59 us (2%)
    all_to_all x1, blocking collectives, exchange(): return lax.all_to_all(x, axes, 0, 0, tiled=True)  32.7 us
    all_to_all x3, starting transfers between devices, exchange(): return lax.all_to_all(x, axes, 0, 0, tiled=True)  16.8 us
    all_to_all x3, waiting for transfers between devices, exchange(): return lax.all_to_all(x, axes, 0, 0, tiled=True)  16 us
    pallas_call x1, Pallas kernels, key_grad(): pl.pallas_call(key_body, out_shape=[jax.ShapeDtypeStruct((ROWS, HEAD), BF...  15.8 us
    pallas_call x2, Pallas kernels, forward(): pl.pallas_call(functools.partial(forward_body, first), out_shape=outs, gr...  14 us
    ppermute x15, starting transfers between devices, other_core(): return lax.ppermute(x, 'core', SWAP)  11.7 us
    pallas_call x1, Pallas kernels, query_grad(): pl.pallas_call(query_body, out_shape=jax.ShapeDtypeStruct((ROWS, HEAD), B...  10.5 us
    pallas_call x6, Pallas kernels, move(): pl.pallas_call(body, out_shape=[space(shape, BF16) for shape in outs], gr...  8.57 us
  transfers between devices with their start and end apart: 29, of which 11 were waited for; matrix products, arithmetic and copies ran while one was open for 5% of the time, Pallas kernels for 26%

profile of v6, /device:TPU:1, one launch (start us, length us, event | category | flops | bytes accessed | tf_op | source)
XLA Modules:
  0.0 169.2 jit_solution(4580136501577526403)
XLA Ops:
  0.6 2.1 %cut.1 = (bf16[8,64,384]{2,1,0:T(8,128)(2,1)}, bf16[8,64,384]{2,1,0:T(8,128)(2,1)}) custom-call(s32[1]{0:T(128)} %bitcast.2.half_ref, bf16[128,1024]{1,0:T(8,128)(2,1)} %bitcast.80, bf16[128,1024]{1,0:T(8,128)(2,1)} %bitcast.81, bf16[128,1024]{1,0:T(8,128)(2,1)} %bitcast.82), custom_call_target="tpu_custom_call" | custom-call | bytes 4194304 | tf_op jit(solution)/shard_map/cut/pallas_call | solution.py:359
  2.8 1.4 collective-permute-start
  4.2 0.7 broadcast_select_fusion.10
  5.0 2.9 %collective-permute-start.2 = (bf16[8,1024]{1,0:T(8,128)(2,1)S(1)}, bf16[8,1024]{1,0:T(8,128)(2,1)S(1)}, u32[]{:S(2)}, u32[]{:S(2)}) collective-permute-start(bf16[8,1024]{1,0:T(8,128)(2,1)S(1)} %get-tuple-element.69.w0), channel_id=1, source_target_pairs={{0,2},{2,0},{1,3},{3,1},{4,6},{6,4},{5,7},{7,5},{8,10},{10,8},{9,1... | collective-permute-start | bytes 49160 | tf_op jit(solution)/shard_map/ppermute | solution.py:451
  7.9 0.7 collective-permute-start.3
  8.6 0.5 collective-permute-done.2.w2
  9.1 3.9 %collective-permute-done.3.w3 = bf16[8,1024]{1,0:T(8,128)(2,1)S(1)} collective-permute-done((bf16[8,1024]{1,0:T(8,128)(2,1)S(1)}, bf16[8,1024]{1,0:T(8,128)(2,1)S(1)}, u32[]{:S(2)}, u32[]{:S(2)}) %collective-permute-start.3) | collective-permute-done | bytes 16416 | tf_op jit(solution)/shard_map/ppermute | solution.py:452
  13.0 1.2 fill.1
  14.2 32.7 %all_to_all.20.x_ref = bf16[16,64,896]{2,1,0:T(8,128)(2,1)S(1)} all-to-all(bf16[16,64,896]{2,1,0:T(8,128)(2,1)S(1)} %fill.1), channel_id=1, replica_groups=mesh['z'=4,'y'=4,'xl'=2,'xh'=2,'core'=2] {'z','y'}, dimensions={0} | all-to-all | bytes 3670016 | tf_op jit(solution)/shard_map/all_to_all | solution.py:281
  46.9 1.4 split.1
  48.3 1.5 collective-permute-start.5
  50.9 0.6 collective-permute-start.8
  51.5 6.5 %forward_near.1 = (f32[128,1024]{1,0:T(8,128)}, f32[1,1024]{1,0:T(1,128)S(1)}, f32[1,1024]{1,0:T(1,128)S(1)}) custom-call(bf16[1024,128]{1,0:T(8,128)(2,1)} %get-tuple-element.29.refs_0_, bf16[1024,256]{1,0:T(8,128)(2,1)} %get-tuple-element.30.refs_1_.kv0.refs_0_, bf16[1024,256]{1,0:T(8,128)(2,1)S(1)} %collective-permute-done.5.refs_2_.kv1, ...), custom_call_target="tpu_custom_call" | custom-call | flops 2147483648 | bytes 4194304 | tf_op jit(solution)/shard_map/forward_near/pallas_call | solution.py:131
  58.1 5.2 %collective-permute-done.4.refs_1_.kv2 = bf16[1024,256]{1,0:T(8,128)(2,1)S(1)} collective-permute-done((bf16[1024,256]{1,0:T(8,128)(2,1)}, bf16[1024,256]{1,0:T(8,128)(2,1)S(1)}, u32[]{:S(2)}, u32[]{:S(2)}) %collective-permute-start.4) | collective-permute-done | bytes 524320 | tf_op jit(solution)/shard_map/ppermute | solution.py:272
  63.2 1.3 collective-permute-start.6
  65.2 1.0 collective-permute-done.6.refs_2_.kv3
  66.1 7.4 %forward_far.1 = (bf16[1024,256]{1,0:T(8,128)(2,1)}, f32[1,1024]{1,0:T(1,128)S(1)}) custom-call(bf16[1024,128]{1,0:T(8,128)(2,1)} %get-tuple-element.29.refs_0_, bf16[1024,256]{1,0:T(8,128)(2,1)S(1)} %collective-permute-done.4.refs_1_.kv2, bf16[1024,256]{1,0:T(8,128)(2,1)S(1)} %collective-permute-done.6.refs_2_.kv3, ...), custom_call_target="tpu_custom_call" | custom-call | flops 2147483648 | bytes 4194304 | tf_op jit(solution)/shard_map/forward_far/pallas_call | solution.py:131
  73.6 2.7 %weight_whole.1 = bf16[16,2,32,1024]{3,2,1,0:T(8,128)(2,1)} custom-call(s32[1]{0:T(128)} %bitcast.14.xl_ref, bf16[12,64,512]{2,1,0:T(8,128)(2,1)} %get-tuple-element.39.own0, bf16[4,64,512]{2,1,0:T(8,128)(2,1)} %get-tuple-element.40.own1, bf16[12,64,512]{2,1,0:T(8,128)(2,1)S(1)} %collective-permute-done.8.other0, ...), custom_call_target="tpu_custom_call" | custom-call | bytes 4194304 | tf_op jit(solution)/shard_map/weight_whole/pallas_call | solution.py:321
  76.3 2.4 %fusion.26 = f32[256,1024]{1,0:T(8,128)S(1)} fusion(bf16[256,1024]{1,0:T(8,128)(2,1)S(1)} %bitcast.61, bf16[1024,1024]{1,0:T(8,128)(2,1)} %bitcast.66), kind=kOutput, calls=%fused_computation.76 | convolution fusion | flops 536870912 | bytes 3670016 | tf_op jit(solution)/shard_map/dot_general | solution.py:32
  78.8 0.5 collective-permute-start.10
  79.4 1.4 collective-permute-done.11
  81.2 2.2 %collective-permute-done.12 = f32[2,1024]{1,0:T(2,128)S(1)} collective-permute-done((f32[2,1024]{1,0:T(2,128)S(1)}, f32[2,1024]{1,0:T(2,128)S(1)}, u32[]{:S(2)}, u32[]{:S(2)}) %collective-permute-start.12) | collective-permute-done | bytes 8224 | tf_op jit(solution)/shard_map/ppermute | solution.py:272
  83.4 1.9 %cross.1 = bf16[16,64,256]{2,1,0:T(8,128)(2,1)} custom-call(bf16[1024,256]{1,0:T(8,128)(2,1)} %get-tuple-element.36.pair_ref.refs_2_, f32[128,1024]{1,0:T(8,128)S(1)} %get-tuple-element.50.own_ref, f32[128,1024]{1,0:T(8,128)S(1)} %collective-permute-done.10.peer_ref, f32[4,1024]{1,0:T(4,128)S(1)} %pad_maximum_fusion.7.lses_ref.refs_10_), custom_call_target="tpu_custom_call" | custom-call | bytes 4194304 | tf_op jit(solution)/shard_map/cross/pallas_call | solution.py:359
  85.3 3.6 %all-to-all-start.1 = ((bf16[16,64,256]{2,1,0:T(8,128)(2,1)}), bf16[16,64,256]{2,1,0:T(8,128)(2,1)S(1)}, u32[]{:S(2)}, u32[]{:S(2)}) async-start(bf16[16,64,256]{2,1,0:T(8,128)(2,1)} %cross.1), calls=%async_computation.1 | async-start | bytes 1048576 | tf_op jit(solution)/shard_map/all_to_all | solution.py:281
  89.3 9.6 %all-to-all-done.1.x_ref = bf16[16,64,256]{2,1,0:T(8,128)(2,1)S(1)} async-done(((bf16[16,64,256]{2,1,0:T(8,128)(2,1)}), bf16[16,64,256]{2,1,0:T(8,128)(2,1)S(1)}, u32[]{:S(2)}, u32[]{:S(2)}) %all-to-all-start.1) | async-done | bytes 524320 | tf_op jit(solution)/shard_map/all_to_all | solution.py:281
  99.0 0.9 land.1
  99.9 2.4 %collective-permute-start.13 = (bf16[128,1024]{1,0:T(8,128)(2,1)}, bf16[128,1024]{1,0:T(8,128)(2,1)S(1)}, u32[]{:S(2)}, u32[]{:S(2)}) collective-permute-start(bf16[128,1024]{1,0:T(8,128)(2,1)} %get-tuple-element.41.own_ref), channel_id=1, source_target_pairs={{0,1},{1,0},{2,3},{3,2},{4,5},{5,4},{6,7},{7,6},{8,9},{9,8},{10,11... | collective-permute-start | bytes 786440 | tf_op jit(solution)/shard_map/ppermute | solution.py:268
  102.2 1.1 collective-permute-start.17
  104.0 0.9 copy-done
  104.9 2.1 %weight_terms.1 = bf16[1024,1024]{1,0:T(8,128)(2,1)} custom-call(bf16[128,1024]{1,0:T(8,128)(2,1)S(1)} %copy-done, bf16[128,1024]{1,0:T(8,128)(2,1)S(1)} %collective-permute-done.13.peer_ref, bf16[256,1024]{1,0:T(8,128)(2,1)S(1)} %bitcast.62), custom_call_target="tpu_custom_call" | custom-call | flops 536870912 | bytes 4194304 | tf_op jit(solution)/shard_map/weight_terms/pallas_call | solution.py:341
  107.0 6.4 %all-to-all-start.3 = ((bf16[16,64,1024]{2,1,0:T(8,128)(2,1)}), bf16[16,64,1024]{2,1,0:T(8,128)(2,1)}, u32[]{:S(2)}, u32[]{:S(2)}) async-start(bf16[16,64,1024]{2,1,0:T(8,128)(2,1)} %bitcast.69), calls=%async_computation.3 | async-start | bytes 4194304 | tf_op jit(solution)/shard_map/all_to_all | solution.py:281
  113.4 10.5 %query_grad.1 = bf16[1024,128]{1,0:T(8,128)(2,1)S(1)} custom-call(bf16[1024,256]{1,0:T(8,128)(2,1)} %get-tuple-element.36.pair_ref.refs_2_, bf16[1024,128]{1,0:T(8,128)(2,1)} %get-tuple-element.42.g_ref.refs_6_, f32[1,1024]{1,0:T(1,128)S(1)} %get-tuple-element.43.lse_ref, bf16[1024,256]{1,0:T(8,128)(2,1)S(1)} %collective-permute-done.15.far_ref.refs_4_, ...), custom_call_target="tpu_custom_call" | custom-call | flops 6442450944 | bytes 4194304 | tf_op jit(solution)/shard_map/query_grad/pallas_call | solution.py:182
  124.0 0.5 convolution_convert_fusion.1
  124.5 1.1 collective-permute-start.20
  126.1 0.7 pad_maximum_fusion.4
  127.0 15.8 %key_grad.1 = (bf16[1024,128]{1,0:T(8,128)(2,1)S(1)}, bf16[1024,128]{1,0:T(8,128)(2,1)S(1)}) custom-call(bf16[1024,256]{1,0:T(8,128)(2,1)} %get-tuple-element.30.refs_1_.kv0.refs_0_, f32[64,128]{1,0:T(8,128)S(1)} %pad.4.refs_3_.bias_ref.refs_1_, bf16[1024,256]{1,0:T(8,128)(2,1)S(1)} %copy-done.3, bf16[1024,256]{1,0:T(8,128)(2,1)S(1)} %collective-permute-done.16.refs_3_, ...), custom_call_target="tpu_custom_call" | custom-call | flops 8589934592 | bytes 4194304 | tf_op jit(solution)/shard_map/key_grad/pallas_call | solution.py:238
  142.8 1.0 pad_maximum_fusion
  143.8 6.9 %all-to-all-start.2 = ((bf16[16,64,384]{2,1,0:T(8,128)(2,1)}), bf16[16,64,384]{2,1,0:T(8,128)(2,1)S(1)}, u32[]{:S(2)}, u32[]{:S(2)}) async-start(bf16[16,64,384]{2,1,0:T(8,128)(2,1)} %pad_maximum_fusion), calls=%async_computation.2 | async-start | bytes 1572864 | tf_op jit(solution)/shard_map/all_to_all | solution.py:281
  150.7 1.0 broadcast_select_fusion.7
  151.8 2.0 %convert_reduce_fusion = f32[64,1024]{1,0:T(8,128)S(1)} fusion(bf16[16,64,1024]{2,1,0:T(8,128)(2,1)} %all-to-all-done.3), kind=kLoop, calls=%fused_computation | loop fusion | flops 2031616 | bytes 2359296 | tf_op jit(solution)/shard_map/reduce_sum | solution.py:545
  153.8 0.8 collective-permute-start.24
  154.6 0.6 collective-permute-start.23
  155.3 2.5 %collective-permute-start.22 = (f32[16,1024]{1,0:T(8,128)S(1)}, f32[16,1024]{1,0:T(8,128)S(1)}, u32[]{:S(2)}, u32[]{:S(2)}) collective-permute-start(f32[16,1024]{1,0:T(8,128)S(1)} %get-tuple-element.59), channel_id=1, source_target_pairs={{0,2},{2,0},{4,6},{6,4},{1,3},{3,1},{5,7},{7,5},{8,10},{10,8},{12,... | collective-permute-start | bytes 196616 | tf_op jit(solution)/shard_map/ppermute | solution.py:550
  157.8 6.4 %all-to-all-done.2.own_ref = bf16[16,64,384]{2,1,0:T(8,128)(2,1)S(1)} async-done(((bf16[16,64,384]{2,1,0:T(8,128)(2,1)}), bf16[16,64,384]{2,1,0:T(8,128)(2,1)S(1)}, u32[]{:S(2)}, u32[]{:S(2)}) %all-to-all-start.2) | async-done | bytes 786464 | tf_op jit(solution)/shard_map/all_to_all | solution.py:281
  164.2 1.9 %collective-permute-start.21 = (bf16[8,64,384]{2,1,0:T(8,128)(2,1)S(1)}, bf16[8,64,384]{2,1,0:T(8,128)(2,1)S(1)}, u32[]{:S(2)}, u32[]{:S(2)}) collective-permute-start(bf16[8,64,384]{2,1,0:T(8,128)(2,1)S(1)} %constant_dynamic-slice_fusion), channel_id=1, source_target_pairs={{0,1},{1,0},{2,3},{3,2},{4,5},{5,4},{6,7},{7,6},{8,9},{9,8},{10,11... | collective-permute-start | bytes 1179656 | tf_op jit(solution)/shard_map/ppermute | solution.py:268
  166.3 0.8 maximum_bitcast_fusion
  167.5 1.1 final.1
  168.6 0.6 pad_maximum_fusion.6
  (77 shorter events, 4.6 us)
Async XLA Ops:
  2.8 10.2 %collective-permute-start = (bf16[8,64,384]{2,1,0:T(8,128)(2,1)}, bf16[8,64,384]{2,1,0:T(8,128)(2,1)S(1)}, u32[]{:S(2)}, u32[]{:S(2)}) collective-permute-start(bf16[8,64,384]{2,1,0:T(8,128)(2,1)} %get-tuple-element.28), channel_id=1, source_target_pairs={{0,1},{1,0},{2,3},{3,2},{4,5},{5,4},{6,7},{7,6},{8,9},{9,8},{10,11... | collective-permute-start | bytes 1179656 | tf_op jit(solution)/shard_map/ppermute | solution.py:268
  4.9 3.6 %collective-permute-start.1 = (bf16[8,1024]{1,0:T(8,128)(2,1)S(1)}, bf16[8,1024]{1,0:T(8,128)(2,1)S(1)}, u32[]{:S(2)}, u32[]{:S(2)}) collective-permute-start(bf16[8,1024]{1,0:T(8,128)(2,1)S(1)} %get-tuple-element.68), channel_id=1, source_target_pairs={{0,1},{1,0},{2,3},{3,2},{4,5},{5,4},{6,7},{7,6},{8,9},{9,8},{10,11... | collective-permute-start | bytes 49160 | tf_op jit(solution)/shard_map/ppermute | solution.py:268
  5.0 4.2 %collective-permute-start.2 = (bf16[8,1024]{1,0:T(8,128)(2,1)S(1)}, bf16[8,1024]{1,0:T(8,128)(2,1)S(1)}, u32[]{:S(2)}, u32[]{:S(2)}) collective-permute-start(bf16[8,1024]{1,0:T(8,128)(2,1)S(1)} %get-tuple-element.69.w0), channel_id=1, source_target_pairs={{0,2},{2,0},{1,3},{3,1},{4,6},{6,4},{5,7},{7,5},{8,10},{10,8},{9,1... | collective-permute-start | bytes 49160 | tf_op jit(solution)/shard_map/ppermute | solution.py:451
  7.9 5.1 %collective-permute-start.3 = (bf16[8,1024]{1,0:T(8,128)(2,1)S(1)}, bf16[8,1024]{1,0:T(8,128)(2,1)S(1)}, u32[]{:S(2)}, u32[]{:S(2)}) collective-permute-start(bf16[8,1024]{1,0:T(8,128)(2,1)S(1)} %get-tuple-element.68), channel_id=1, source_target_pairs={{0,3},{1,2},{2,1},{3,0},{4,7},{5,6},{6,5},{7,4},{8,11},{9,10},{10,... | collective-permute-start | bytes 49160 | tf_op jit(solution)/shard_map/ppermute | solution.py:452
  14.2 35.6 %copy-start.9 = (bf16[1,128,2048]{2,1,0:T(8,128)(2,1)S(1)}, bf16[1,128,2048]{2,1,0:T(8,128)(2,1)}, u32[]{:S(2)}) copy-start(bf16[1,128,2048]{2,1,0:T(8,128)(2,1)} %param.13) | copy-start | bytes 1572868
  46.9 3.5 %copy-start.12 = (s32[64]{0:T(128)S(1)}, s32[64]{0:T(128)}, u32[]{:S(2)}) copy-start(s32[64]{0:T(128)} %param.10) | copy-start | bytes 772
  46.9 3.6 %copy-start.11 = (s32[64,64]{1,0:T(8,128)S(1)}, s32[64,64]{1,0:T(8,128)}, u32[]{:S(2)}) copy-start(s32[64,64]{1,0:T(8,128)} %param.11) | copy-start | bytes 49156
  48.3 3.3 %collective-permute-start.5 = (bf16[1024,256]{1,0:T(8,128)(2,1)}, bf16[1024,256]{1,0:T(8,128)(2,1)S(1)}, u32[]{:S(2)}, u32[]{:S(2)}) collective-permute-start(bf16[1024,256]{1,0:T(8,128)(2,1)} %get-tuple-element.30.refs_1_.kv0.refs_0_), channel_id=1, source_target_pairs={{0,1},{1,0},{2,3},{3,2},{4,5},{5,4},{6,7},{7,6},{8,9},{9,8},{10,11... | collective-permute-start | bytes 1572872 | tf_op jit(solution)/shard_map/ppermute | solution.py:268
  49.8 14.8 %collective-permute-start.7 = (bf16[128,1024]{1,0:T(8,128)(2,1)S(1)}, bf16[128,1024]{1,0:T(8,128)(2,1)S(1)}, u32[]{:S(2)}, u32[]{:S(2)}) collective-permute-start(bf16[128,1024]{1,0:T(8,128)(2,1)S(1)} %broadcast_select_fusion.2), channel_id=1, source_target_pairs={{0,1},{1,0},{2,3},{3,2},{4,5},{5,4},{6,7},{7,6},{8,9},{9,8},{10,11... | collective-permute-start | bytes 786440 | tf_op jit(solution)/shard_map/ppermute | solution.py:268
  50.0 13.3 %collective-permute-start.4 = (bf16[1024,256]{1,0:T(8,128)(2,1)}, bf16[1024,256]{1,0:T(8,128)(2,1)S(1)}, u32[]{:S(2)}, u32[]{:S(2)}) collective-permute-start(bf16[1024,256]{1,0:T(8,128)(2,1)} %get-tuple-element.30.refs_1_.kv0.refs_0_), channel_id=1, source_target_pairs={{0,4},{4,0},{1,5},{5,1},{2,6},{6,2},{3,7},{7,3},{8,12},{12,8},{9,1... | collective-permute-start | bytes 1572872 | tf_op jit(solution)/shard_map/ppermute | solution.py:272
  50.9 22.7 %collective-permute-start.8 = (bf16[12,64,512]{2,1,0:T(8,128)(2,1)}, bf16[12,64,512]{2,1,0:T(8,128)(2,1)S(1)}, u32[]{:S(2)}, u32[]{:S(2)}) collective-permute-start(bf16[12,64,512]{2,1,0:T(8,128)(2,1)} %get-tuple-element.39.own0), channel_id=1, source_target_pairs={{0,6},{2,4},{4,2},{6,0},{1,7},{3,5},{5,3},{7,1},{8,14},{10,12},{12... | collective-permute-start | bytes 2359304 | tf_op jit(solution)/shard_map/ppermute | solution.py:309
  51.5 6.5 %copy-start.4 = (bf16[1024,256]{1,0:T(8,128)(2,1)}, bf16[1024,256]{1,0:T(8,128)(2,1)S(1)}, u32[]{:S(2)}) copy-start(bf16[1024,256]{1,0:T(8,128)(2,1)S(1)} %collective-permute-done.5.refs_2_.kv1) | copy-start | bytes 1572868
  58.1 6.6 %copy-start.10 = (bf16[4,64,512]{2,1,0:T(8,128)(2,1)S(1)}, bf16[4,64,512]{2,1,0:T(8,128)(2,1)}, u32[]{:S(2)}) copy-start(bf16[4,64,512]{2,1,0:T(8,128)(2,1)} %get-tuple-element.40.own1) | copy-start | bytes 786436
  63.2 10.3 %copy-start.5 = (bf16[1024,256]{1,0:T(8,128)(2,1)}, bf16[1024,256]{1,0:T(8,128)(2,1)S(1)}, u32[]{:S(2)}) copy-start(bf16[1024,256]{1,0:T(8,128)(2,1)S(1)} %collective-permute-done.4.refs_1_.kv2) | copy-start | bytes 1572868
  63.2 2.9 %collective-permute-start.6 = (bf16[1024,256]{1,0:T(8,128)(2,1)S(1)}, bf16[1024,256]{1,0:T(8,128)(2,1)S(1)}, u32[]{:S(2)}, u32[]{:S(2)}) collective-permute-start(bf16[1024,256]{1,0:T(8,128)(2,1)S(1)} %collective-permute-done.4.refs_1_.kv2), channel_id=1, source_target_pairs={{0,1},{1,0},{2,3},{3,2},{4,5},{5,4},{6,7},{7,6},{8,9},{9,8},{10,11... | collective-permute-start | bytes 1572872 | tf_op jit(solution)/shard_map/ppermute | solution.py:268
  64.7 8.9 %collective-permute-start.9 = (bf16[4,64,512]{2,1,0:T(8,128)(2,1)S(1)}, bf16[4,64,512]{2,1,0:T(8,128)(2,1)S(1)}, u32[]{:S(2)}, u32[]{:S(2)}) collective-permute-start(bf16[4,64,512]{2,1,0:T(8,128)(2,1)S(1)} %copy-done.10), channel_id=1, source_target_pairs={{0,4},{4,0},{1,5},{5,1},{2,6},{6,2},{3,7},{7,3},{8,12},{12,8},{9,1... | collective-permute-start | bytes 786440 | tf_op jit(solution)/shard_map/ppermute | solution.py:272
  66.1 7.4 %copy-start.6 = (bf16[1024,256]{1,0:T(8,128)(2,1)}, bf16[1024,256]{1,0:T(8,128)(2,1)S(1)}, u32[]{:S(2)}) copy-start(bf16[1024,256]{1,0:T(8,128)(2,1)S(1)} %collective-permute-done.6.refs_2_.kv3) | copy-start | bytes 1572868
  78.8 10.2 %copy-start.2 = (bf16[1024,256]{1,0:T(8,128)(2,1)S(1)}, bf16[1024,256]{1,0:T(8,128)(2,1)}, u32[]{:S(2)}) copy-start(bf16[1024,256]{1,0:T(8,128)(2,1)} %get-tuple-element.36.pair_ref.refs_2_) | copy-start | bytes 1572868
  78.8 4.6 %collective-permute-start.10 = (f32[128,1024]{1,0:T(8,128)S(1)}, f32[128,1024]{1,0:T(8,128)S(1)}, u32[]{:S(2)}, u32[]{:S(2)}) collective-permute-start(f32[128,1024]{1,0:T(8,128)S(1)} %get-tuple-element.49), channel_id=1, source_target_pairs={{0,1},{1,0},{2,3},{3,2},{4,5},{5,4},{6,7},{7,6},{8,9},{9,8},{10,11... | collective-permute-start | bytes 1572872 | tf_op jit(solution)/shard_map/ppermute | solution.py:268
  79.2 1.5 collective-permute-start.11
  80.8 2.6 %collective-permute-start.12 = (f32[2,1024]{1,0:T(2,128)S(1)}, f32[2,1024]{1,0:T(2,128)S(1)}, u32[]{:S(2)}, u32[]{:S(2)}) collective-permute-start(f32[2,1024]{1,0:T(2,128)S(1)} %pad_maximum_fusion.8), channel_id=1, source_target_pairs={{0,4},{4,0},{1,5},{5,1},{2,6},{6,2},{3,7},{7,3},{8,12},{12,8},{9,1... | collective-permute-start | bytes 24584 | tf_op jit(solution)/shard_map/ppermute | solution.py:272
  85.3 13.6 %all-to-all-start.1 = ((bf16[16,64,256]{2,1,0:T(8,128)(2,1)}), bf16[16,64,256]{2,1,0:T(8,128)(2,1)S(1)}, u32[]{:S(2)}, u32[]{:S(2)}) async-start(bf16[16,64,256]{2,1,0:T(8,128)(2,1)} %cross.1), calls=%async_computation.1 | async-start | bytes 1048576 | tf_op jit(solution)/shard_map/all_to_all | solution.py:281
  88.9 13.3 %collective-permute-start.15 = (bf16[1024,256]{1,0:T(8,128)(2,1)S(1)}, bf16[1024,256]{1,0:T(8,128)(2,1)S(1)}, u32[]{:S(2)}, u32[]{:S(2)}) collective-permute-start(bf16[1024,256]{1,0:T(8,128)(2,1)S(1)} %copy-done.2), channel_id=1, source_target_pairs={{0,4},{4,0},{1,5},{5,1},{2,6},{6,2},{3,7},{7,3},{8,12},{12,8},{9,1... | collective-permute-start | bytes 1572872 | tf_op jit(solution)/shard_map/ppermute | solution.py:272
  99.9 4.1 %collective-permute-start.13 = (bf16[128,1024]{1,0:T(8,128)(2,1)}, bf16[128,1024]{1,0:T(8,128)(2,1)S(1)}, u32[]{:S(2)}, u32[]{:S(2)}) collective-permute-start(bf16[128,1024]{1,0:T(8,128)(2,1)} %get-tuple-element.41.own_ref), channel_id=1, source_target_pairs={{0,1},{1,0},{2,3},{3,2},{4,5},{5,4},{6,7},{7,6},{8,9},{9,8},{10,11... | collective-permute-start | bytes 786440 | tf_op jit(solution)/shard_map/ppermute | solution.py:268
  102.2 24.6 %collective-permute-start.16 = (bf16[1024,256]{1,0:T(8,128)(2,1)S(1)}, bf16[1024,256]{1,0:T(8,128)(2,1)S(1)}, u32[]{:S(2)}, u32[]{:S(2)}) collective-permute-start(bf16[1024,256]{1,0:T(8,128)(2,1)S(1)} %copy-done.2), channel_id=1, source_target_pairs={{0,1},{1,0},{2,3},{3,2},{4,5},{5,4},{6,7},{7,6},{8,9},{9,8},{10,11... | collective-permute-start | bytes 1572872 | tf_op jit(solution)/shard_map/ppermute | solution.py:268
  102.2 24.6 %collective-permute-start.17 = (bf16[1024,256]{1,0:T(8,128)(2,1)S(1)}, bf16[1024,256]{1,0:T(8,128)(2,1)S(1)}, u32[]{:S(2)}, u32[]{:S(2)}) collective-permute-start(bf16[1024,256]{1,0:T(8,128)(2,1)S(1)} %collective-permute-done.15.far_ref.refs_4_), channel_id=1, source_target_pairs={{0,1},{1,0},{2,3},{3,2},{4,5},{5,4},{6,7},{7,6},{8,9},{9,8},{10,11... | collective-permute-start | bytes 1572872 | tf_op jit(solution)/shard_map/ppermute | solution.py:268
  103.3 23.5 %collective-permute-start.18 = (bf16[1024,128]{1,0:T(8,128)(2,1)}, bf16[1024,128]{1,0:T(8,128)(2,1)S(1)}, u32[]{:S(2)}, u32[]{:S(2)}) collective-permute-start(bf16[1024,128]{1,0:T(8,128)(2,1)} %get-tuple-element.42.g_ref.refs_6_), channel_id=1, source_target_pairs={{0,1},{1,0},{2,3},{3,2},{4,5},{5,4},{6,7},{7,6},{8,9},{9,8},{10,11... | collective-permute-start | bytes 786440 | tf_op jit(solution)/shard_map/ppermute | solution.py:268
  103.3 21.1 %collective-permute-start.19 = (bf16[1024,128]{1,0:T(8,128)(2,1)}, bf16[1024,128]{1,0:T(8,128)(2,1)}, u32[]{:S(2)}, u32[]{:S(2)}) collective-permute-start(bf16[1024,128]{1,0:T(8,128)(2,1)} %get-tuple-element.42.g_ref.refs_6_), channel_id=1, source_target_pairs={{0,4},{4,0},{1,5},{5,1},{2,6},{6,2},{3,7},{7,3},{8,12},{12,8},{9,1... | collective-permute-start | bytes 786440 | tf_op jit(solution)/shard_map/ppermute | solution.py:272
  104.0 0.9 copy-start
  107.0 36.8 %all-to-all-start.3 = ((bf16[16,64,1024]{2,1,0:T(8,128)(2,1)}), bf16[16,64,1024]{2,1,0:T(8,128)(2,1)}, u32[]{:S(2)}, u32[]{:S(2)}) async-start(bf16[16,64,1024]{2,1,0:T(8,128)(2,1)} %bitcast.69), calls=%async_computation.3 | async-start | bytes 4194304 | tf_op jit(solution)/shard_map/all_to_all | solution.py:281
  113.4 10.5 %copy-start.1 = (bf16[128,1024]{1,0:T(8,128)(2,1)S(1)}, bf16[128,1024]{1,0:T(8,128)(2,1)}, u32[]{:S(2)}) copy-start(bf16[128,1024]{1,0:T(8,128)(2,1)} %get-tuple-element.41.own_ref) | copy-start | bytes 786436
  113.4 10.5 %copy-start.8 = (bf16[16,2,32,1024]{3,2,1,0:T(8,128)(2,1)S(1)}, bf16[16,2,32,1024]{3,2,1,0:T(8,128)(2,1)}, u32[]{:S(2)}) copy-start(bf16[16,2,32,1024]{3,2,1,0:T(8,128)(2,1)} %weight_whole.1) | copy-start | bytes 6291460
  124.4 2.6 %copy-start.3 = (bf16[1024,256]{1,0:T(8,128)(2,1)S(1)}, bf16[1024,256]{1,0:T(8,128)(2,1)}, u32[]{:S(2)}) copy-start(bf16[1024,256]{1,0:T(8,128)(2,1)} %get-tuple-element.36.pair_ref.refs_2_) | copy-start | bytes 1572868
  124.4 2.5 %copy-start.7 = (bf16[1024,128]{1,0:T(8,128)(2,1)S(1)}, bf16[1024,128]{1,0:T(8,128)(2,1)}, u32[]{:S(2)}) copy-start(bf16[1024,128]{1,0:T(8,128)(2,1)} %get-tuple-element.42.g_ref.refs_6_) | copy-start | bytes 786436
  124.5 2.5 %collective-permute-start.20 = (bf16[1024,128]{1,0:T(8,128)(2,1)}, bf16[1024,128]{1,0:T(8,128)(2,1)S(1)}, u32[]{:S(2)}, u32[]{:S(2)}) collective-permute-start(bf16[1024,128]{1,0:T(8,128)(2,1)} %collective-permute-done.19.refs_8_), channel_id=1, source_target_pairs={{0,1},{1,0},{2,3},{3,2},{4,5},{5,4},{6,7},{7,6},{8,9},{9,8},{10,11... | collective-permute-start | bytes 786440 | tf_op jit(solution)/shard_map/ppermute | solution.py:268
  126.8 23.9 %collective-permute-start.14 = (bf16[2,64,1024]{2,1,0:T(8,128)(2,1)}, bf16[2,64,1024]{2,1,0:T(8,128)(2,1)}, u32[]{:S(2)}, u32[]{:S(2)}) collective-permute-start(bf16[2,64,1024]{2,1,0:T(8,128)(2,1)} %pad_maximum_fusion.4), channel_id=1, source_target_pairs={{0,1},{1,0},{2,3},{3,2},{4,5},{5,4},{6,7},{7,6},{8,9},{9,8},{10,11... | collective-permute-start | bytes 786440 | tf_op jit(solution)/shard_map/ppermute | solution.py:268
  143.8 20.4 %all-to-all-start.2 = ((bf16[16,64,384]{2,1,0:T(8,128)(2,1)}), bf16[16,64,384]{2,1,0:T(8,128)(2,1)S(1)}, u32[]{:S(2)}, u32[]{:S(2)}) async-start(bf16[16,64,384]{2,1,0:T(8,128)(2,1)} %pad_maximum_fusion), calls=%async_computation.2 | async-start | bytes 1572864 | tf_op jit(solution)/shard_map/all_to_all | solution.py:281
  153.8 12.3 %collective-permute-start.24 = (f32[16,1024]{1,0:T(8,128)S(1)}, f32[16,1024]{1,0:T(8,128)S(1)}, u32[]{:S(2)}, u32[]{:S(2)}) collective-permute-start(f32[16,1024]{1,0:T(8,128)S(1)} %get-tuple-element.60), channel_id=1, source_target_pairs={{0,6},{2,4},{4,2},{6,0},{1,7},{3,5},{5,3},{7,1},{8,14},{10,12},{12... | collective-permute-start | bytes 196616 | tf_op jit(solution)/shard_map/ppermute | solution.py:550
  154.6 11.5 %collective-permute-start.23 = (f32[16,1024]{1,0:T(8,128)S(1)}, f32[16,1024]{1,0:T(8,128)S(1)}, u32[]{:S(2)}, u32[]{:S(2)}) collective-permute-start(f32[16,1024]{1,0:T(8,128)S(1)} %get-tuple-element.61), channel_id=1, source_target_pairs={{0,4},{2,6},{4,0},{6,2},{1,5},{3,7},{5,1},{7,3},{8,12},{10,14},{12... | collective-permute-start | bytes 196616 | tf_op jit(solution)/shard_map/ppermute | solution.py:550
  155.3 10.9 %collective-permute-start.22 = (f32[16,1024]{1,0:T(8,128)S(1)}, f32[16,1024]{1,0:T(8,128)S(1)}, u32[]{:S(2)}, u32[]{:S(2)}) collective-permute-start(f32[16,1024]{1,0:T(8,128)S(1)} %get-tuple-element.59), channel_id=1, source_target_pairs={{0,2},{2,0},{4,6},{6,4},{1,3},{3,1},{5,7},{7,5},{8,10},{10,8},{12,... | collective-permute-start | bytes 196616 | tf_op jit(solution)/shard_map/ppermute | solution.py:550
  164.2 3.3 %collective-permute-start.21 = (bf16[8,64,384]{2,1,0:T(8,128)(2,1)S(1)}, bf16[8,64,384]{2,1,0:T(8,128)(2,1)S(1)}, u32[]{:S(2)}, u32[]{:S(2)}) collective-permute-start(bf16[8,64,384]{2,1,0:T(8,128)(2,1)S(1)} %constant_dynamic-slice_fusion), channel_id=1, source_target_pairs={{0,1},{1,0},{2,3},{3,2},{4,5},{5,4},{6,7},{7,6},{8,9},{9,8},{10,11... | collective-permute-start | bytes 1179656 | tf_op jit(solution)/shard_map/ppermute | solution.py:268
  166.2 2.4 %collective-permute-start.25 = (f32[8,1024]{1,0:T(8,128)S(1)}, f32[8,1024]{1,0:T(8,128)S(1)}, u32[]{:S(2)}, u32[]{:S(2)}) collective-permute-start(f32[8,1024]{1,0:T(8,128)S(1)} %dynamic-slice_bitcast_fusion.3), channel_id=1, source_target_pairs={{0,1},{1,0},{2,3},{3,2},{4,5},{5,4},{6,7},{7,6},{8,9},{9,8},{10,11... | collective-permute-start | bytes 98312 | tf_op jit(solution)/shard_map/ppermute | solution.py:268

commit v7 on v6

--- a/solution.py
+++ b/solution.py
@@ -16,6 +16,7 @@
 TILE = 256
 LOW = -1e30
 GRANT = 16 << 20
+WIDE_GRANT = 32 << 20
 SCALE = 1.0 / HEAD
 F32 = jnp.float32
 BF16 = jnp.bfloat16
@@ -165,13 +166,13 @@
     g = g_ref[...]
     lse = lse_ref[...]
     delta = row_delta(g, pair_ref[:, HEAD:])
+    own = pl.ds(pl.multiple_of(step * TILE, TILE), TILE)
+    s_ref[...] = dot(ka_ref[pl.ds(0, ROWS), :], qa, NT)
+    s_ref[own, :] = jnp.where(later_in_span(), LOW, s_ref[own, :])
     total = jnp.zeros((HEAD, TILE), F32)
     for c, kv_ref in enumerate(chunks):
-        s_ref[...] = dot(ka_ref[pl.ds(c * ROWS, ROWS), :], qa, NT)
-        if c == 0:
-            rows = pl.ds(pl.multiple_of(step * TILE, TILE), TILE)
-            s_ref[rows, :] = jnp.where(later_in_span(), LOW, s_ref[rows, :])
-        prob = jnp.exp(s_ref[...] - lse)
+        scores = dot(ka_ref[pl.ds(c * ROWS, ROWS), :], qa, NT) if c else s_ref[...]
+        prob = jnp.exp(scores - lse)
         dprob = dot(kv_ref[:, HEAD:], g, NT)
         ds = (prob * (dprob - delta)).astype(BF16)
         total += dot(kv_ref[:, :HEAD], ds, TN)
@@ -197,7 +198,7 @@
             pltpu.VMEM((ROWS, TILE), F32),
         ],
         cost_estimate=cost(3, 4 * ROWS * ROWS),
-        compiler_params=pltpu.CompilerParams(vmem_limit_bytes=GRANT),
+        compiler_params=pltpu.CompilerParams(vmem_limit_bytes=WIDE_GRANT),
         name="query_grad",
     )(pair, g, lse, far, *kvs, bias)
 
@@ -210,26 +211,32 @@
     ka_ref[:, HEAD:] = spread_bias(bias_ref[:UNITS, :])
     dk_acc[...] = jnp.zeros_like(dk_acc)
     dv_acc[...] = jnp.zeros_like(dv_acc)
-    for c in range(4):
-
-        def tile(i, _, c=c):
-            rows = pl.ds(pl.multiple_of(i * TILE, TILE), TILE)
+
+    def tile(i, _):
+        rows = pl.ds(pl.multiple_of(i * TILE, TILE), TILE)
+        dk = jnp.zeros((ROWS, HEAD), F32)
+        dv = jnp.zeros((ROWS, HEAD), F32)
+        for c in range(4):
             q = pairs[c][rows, :HEAD]
             g = gs[c][rows, :]
             lse = lses[c : c + 1, rows]
             delta = row_delta(g, pairs[c][rows, HEAD:])
             qa = query_wide(q, i * (TILE // SPAN) + c * UNITS)
-            s_ref[...] = dot(ka_ref[...], qa, NT)
+            scores = dot(ka_ref[...], qa, NT)
             if c == 0:
+                s_ref[...] = scores
                 s_ref[rows, :] = jnp.where(later_in_span(), LOW, s_ref[rows, :])
-            prob = jnp.exp(s_ref[...] - lse)
+                scores = s_ref[...]
+            prob = jnp.exp(scores - lse)
             dprob = dot(kv_ref[:, HEAD:], g, NT)
             ds = (prob * (dprob - delta)).astype(BF16)
-            dv_acc[...] += dot(prob.astype(BF16), g, NN)
-            dk_acc[...] += dot(ds, q, NN)
-            return 0
-
-        lax.fori_loop(0, ROWS // TILE, tile, 0)
+            dv += dot(prob.astype(BF16), g, NN)
+            dk += dot(ds, q, NN)
+        dk_acc[...] += dk
+        dv_acc[...] += dv
+        return 0
+
+    lax.fori_loop(0, ROWS // TILE, tile, 0)
     dk_ref[...] = (dk_acc[...] * SCALE).astype(BF16)
     dv_ref[...] = dv_acc[...].astype(BF16)
 
@@ -254,7 +261,7 @@
             pltpu.VMEM((ROWS, HEAD), F32),
         ],
         cost_estimate=cost(4, 4 * ROWS * ROWS),
-        compiler_params=pltpu.CompilerParams(vmem_limit_bytes=GRANT),
+        compiler_params=pltpu.CompilerParams(vmem_limit_bytes=WIDE_GRANT),
         name="key_grad",
     )(kv, bias, *pairs, *gs, lses)
 
@@ -309,25 +316,37 @@
     return lax.ppermute(x, ("xl", "xh"), [(k, k ^ 3) for k in range(4)])
 
 
-def weight_body(xl_ref, own0, own1, other0, other1, out_ref):
+def weight_body(xl_ref, own0, own1, other0, other1, up_ref, out_ref, keep_ref, send_ref, w_ref):
     for flip, pieces in enumerate(((own0, own1), (other0, other1))):
         for units, part in zip((slice(0, MANY), slice(MANY, UNITS)), pieces):
             for c in range(2):
                 rows = part[:, c * 32 : (c + 1) * 32, :]
-                out_ref[units, xl_ref[0] ^ flip, :, c * 512 : (c + 1) * 512] = rows
-
-
-def weight_whole(xl, own, other):
+                w_ref[units, xl_ref[0] ^ flip, :, c * 512 : (c + 1) * 512] = rows
+    weight = w_ref[...].reshape(1024, 1024)
+    out_ref[...] = weight
+    for rows, out in ((slice(0, 128), keep_ref), (slice(128, 256), send_ref)):
+        out[...] = dot(up_ref[rows, :], weight, NT)
+
+
+def weight_whole(xl, own, other, up):
     return pl.pallas_call(
         weight_body,
-        out_shape=pltpu.HBM((UNITS, 2, 32, 1024), BF16),
+        out_shape=[
+            pltpu.HBM((1024, 1024), BF16),
+            jax.ShapeDtypeStruct((128, 1024), F32),
+            jax.ShapeDtypeStruct((128, 1024), F32),
+        ],
         grid=(1,),
-        in_specs=[pl.BlockSpec(memory_space=pltpu.SMEM)] + [once(*x.shape) for x in (*own, *other)],
-        out_specs=once(UNITS, 2, 32, 1024),
-        cost_estimate=pl.CostEstimate(flops=0, bytes_accessed=4 << 20, transcendentals=0),
+        in_specs=[pl.BlockSpec(memory_space=pltpu.SMEM)]
+        + [once(*x.shape) for x in (*own, *other, up)],
+        out_specs=[once(1024, 1024), once(128, 1024), once(128, 1024)],
+        scratch_shapes=[pltpu.VMEM((UNITS, 2, 32, 1024), BF16)],
+        cost_estimate=pl.CostEstimate(
+            flops=2 * 256 * 1024 * 1024, bytes_accessed=4 << 20, transcendentals=0
+        ),
         compiler_params=pltpu.CompilerParams(vmem_limit_bytes=GRANT),
         name="weight_whole",
-    )(xl, *own, *other)
+    )(xl, *own, *other, up)
 
 
 def term_body(own_ref, peer_ref, up_ref, out_ref):
@@ -356,9 +375,10 @@
 
 
 def move(body, name, outs, scalars, *arrays, space=jax.ShapeDtypeStruct):
+    spaces = space if isinstance(space, list) else [space] * len(outs)
     return pl.pallas_call(
         body,
-        out_shape=[space(shape, BF16) for shape in outs],
+        out_shape=[make(shape, BF16) for make, shape in zip(spaces, outs)],
         grid=(1,),
         in_specs=[IN_SMEM] * len(scalars) + [once(*x.shape) for x in arrays],
         out_specs=[once(*shape) for shape in outs],
@@ -389,7 +409,7 @@
     out_ref[pl.ds(core * HEADS, HEADS), :, : 3 * HEAD] = own_ref[...]
     out_ref[pl.ds((1 - core) * HEADS, HEADS), :, : 3 * HEAD] = peer_ref[...]
     first, mine_first = core == 0, xh == 0
-    w = [x[...].astype(F32) for x in (w0, w1, w2, w3)]
+    w = [jnp.where(first, x[:, :1024], x[:, 1024:]).astype(F32) for x in (w0, w1, w2, w3)]
     near = [jnp.where(first, w[0], w[1]), jnp.where(first, w[1], w[0])]
     far = [jnp.where(first, w[2], w[3]), jnp.where(first, w[3], w[2])]
     front = [jnp.where(mine_first, a, b) for a, b in zip(near, far)]
@@ -409,7 +429,7 @@
     w1_ref[...] = x[MANY:, :, 3 * HEAD :]
 
 
-def cross_body(pair_ref, own_ref, peer_ref, lses_ref, out_ref):
+def cross_body(pair_ref, own_ref, peer_ref, out_ref):
     for s in range(2):
         for h in range(HEADS):
             unit, rows = s * HEADS + h, slice(s * SPAN, (s + 1) * SPAN)
@@ -418,7 +438,7 @@
             out_ref[unit, :, HEAD:] = total.astype(BF16)
 
 
-def land_body(x_ref, att_ref, g_ref):
+def land_body(x_ref, lses_ref, att_ref, g_ref):
     g_ref[...] = x_ref[:, :, HEAD:].reshape(ROWS, HEAD)
     for s in range(2):
         for h in range(HEADS):
@@ -444,13 +464,8 @@
         left, right = x[..., :cols], x[..., cols:]
         return jnp.where(first_core, left, right), jnp.where(first_core, right, left)
 
-    weight_mine, weight_theirs = by_core(output_weight)
-    weight_rows = [
-        weight_mine,
-        other_core(weight_theirs),
-        lax.ppermute(weight_mine, "xh", SWAP),
-        lax.ppermute(weight_theirs, ("xh", "core"), [(k, 3 - k) for k in range(4)]),
-    ]
+    weight_far = lax.ppermute(output_weight, "xh", SWAP)
+    weight_rows = [output_weight, other_core(output_weight), weight_far, other_core(weight_far)]
     unit_rows = (HEADS, SPAN, 3 * HEAD)
     own, sent = move(
         cut_body,
@@ -470,6 +485,7 @@
         in_hbm(own),
         other_core(sent),
         *weight_rows,
+        space=pltpu.HBM,
     )
     blocks = exchange(blocks, ZY)
     q, own_kv, *weight_own = move(
@@ -497,9 +513,9 @@
     lses = jnp.concatenate([lses, other_chip(lses)], axis=0)
 
     place, lse = lax.optimization_barrier((xl_1, lse))
-    weight = weight_whole(place, [in_hbm(x) for x in weight_own], weight_other).reshape(HEADS * HEAD, cols)
-    grad_rows = dot(up, weight, NT)
-    grad_own, grad_sent = grad_rows[: 2 * SPAN], grad_rows[2 * SPAN :]
+    weight, grad_own, grad_sent = weight_whole(
+        place, [in_hbm(x) for x in weight_own], weight_other, up
+    )
     (crossing,) = move(
         cross_body,
         "cross",
@@ -508,7 +524,6 @@
         in_hbm(pair),
         grad_own,
         other_core(grad_sent),
-        lses,
     )
     crossed = exchange(crossing, ZY)
     pairs = everyone(pair)
@@ -519,7 +534,8 @@
         [(2 * SPAN, HEADS * HEAD), (ROWS, HEAD)],
         [],
         crossed,
-        space=pltpu.HBM,
+        lses,
+        space=[jax.ShapeDtypeStruct, pltpu.HBM],
     )
     gs = everyone(g)
     att_peer = other_core(att_own)

time: 170 us -> 167 us (0.982)
  blocking collectives: 32.7 us -> 0 us
  waiting for transfers between devices: 30.9 us -> 56.3 us
  starting transfers between devices: 38.7 us -> 49.1 us
  Pallas kernels: 53.7 us -> 51.3 us
  matrix products: 3.59 us -> 1.21 us
    all_to_all x1 -> x0, blocking collectives: 32.7 us -> none  [exchange(): return lax.all_to_all(x, axes, 0, 0, tiled=True)]
    all_to_all x3 -> x4, waiting for transfers between devices: 16 us -> 37.8 us  [exchange(): return lax.all_to_all(x, axes, 0, 0, tiled=True)]
    ppermute x5, waiting for transfers between devices: 7.31 us -> 13.3 us  [other_chip(): return lax.ppermute(x, 'xl', SWAP)]
    all_to_all x3 -> x4, starting transfers between devices: 16.8 us -> 22.6 us  [exchange(): return lax.all_to_all(x, axes, 0, 0, tiled=True)]
    pallas_call x1, Pallas kernels: 15.8 us -> 12 us  [key_grad(): pl.pallas_call(key_body, out_shape=[jax.ShapeDtypeStruct((ROWS, HEAD), BF...]
    ppermute x5, starting transfers between devices: 1.98 us -> 5.42 us  [other_chip(): return lax.ppermute(x, 'xl', SWAP)]
    ppermute x2 -> x1, waiting for transfers between devices: 4.38 us -> 1.37 us  [local(): weight_far = lax.ppermute(output_weight, 'xh', SWAP)]
    dot_general x3 -> x2, matrix products: 3.28 us -> 0.9 us  [dot(): return lax.dot_general(a, b, dims, preferred_element_type=F32)]
  transfers between devices with their start and end apart: 29 -> 30, of which waited for: 11 -> 12; matrix products, arithmetic and copies ran while one was open for 5% -> 4% of each run, Pallas kernels for 26% -> 24%
where the time goes in v7:
time: 167 us
  waiting for transfers between devices  56.3 us (34%)
  Pallas kernels  51.3 us (31%)
  starting transfers between devices  49.1 us (29%)
  other arithmetic  6.7 us (4%)
    all_to_all x4, waiting for transfers between devices, exchange(): return lax.all_to_all(x, axes, 0, 0, tiled=True)  37.8 us
    all_to_all x4, starting transfers between devices, exchange(): return lax.all_to_all(x, axes, 0, 0, tiled=True)  22.6 us
    pallas_call x2, Pallas kernels, forward(): pl.pallas_call(functools.partial(forward_body, first), out_shape=outs, gr...  14.1 us
    ppermute x5, waiting for transfers between devices, other_chip(): return lax.ppermute(x, 'xl', SWAP)  13.3 us
    ppermute x16, starting transfers between devices, other_core(): return lax.ppermute(x, 'core', SWAP)  12.4 us
    pallas_call x1, Pallas kernels, key_grad(): pl.pallas_call(key_body, out_shape=[jax.ShapeDtypeStruct((ROWS, HEAD), BF...  12 us
    pallas_call x1, Pallas kernels, query_grad(): pl.pallas_call(query_body, out_shape=jax.ShapeDtypeStruct((ROWS, HEAD), B...  10.1 us
    pallas_call x6, Pallas kernels, move(): pl.pallas_call(body, out_shape=[make(shape, BF16) for make, shape in zip(...  9.78 us
  transfers between devices with their start and end apart: 30, of which 12 were waited for; matrix products, arithmetic and copies ran while one was open for 4% of the time, Pallas kernels for 24%

profile of v7, /device:TPU:1, one launch (start us, length us, event | category | flops | bytes accessed | tf_op | source)
XLA Modules:
  0.0 166.6 jit_solution(16748070159762316444)
XLA Ops:
  0.6 2.1 %cut.1 = (bf16[8,64,384]{2,1,0:T(8,128)(2,1)}, bf16[8,64,384]{2,1,0:T(8,128)(2,1)}) custom-call(s32[1]{0:T(128)} %bitcast.2.half_ref, bf16[128,1024]{1,0:T(8,128)(2,1)} %bitcast.74, bf16[128,1024]{1,0:T(8,128)(2,1)} %bitcast.75, bf16[128,1024]{1,0:T(8,128)(2,1)} %bitcast.76), custom_call_target="tpu_custom_call" | custom-call | bytes 4194304 | tf_op jit(solution)/shard_map/cut/pallas_call | solution.py:379
  2.8 1.4 collective-permute-start
  4.2 2.8 %collective-permute-start.2 = (bf16[8,2048]{1,0:T(8,128)(2,1)}, bf16[8,2048]{1,0:T(8,128)(2,1)S(1)}, u32[]{:S(2)}, u32[]{:S(2)}) collective-permute-start(bf16[8,2048]{1,0:T(8,128)(2,1)} %w0.1), channel_id=1, source_target_pairs={{0,2},{2,0},{1,3},{3,1},{4,6},{6,4},{5,7},{7,5},{8,10},{10,8},{9,1... | collective-permute-start | bytes 98312 | tf_op jit(solution)/shard_map/ppermute | solution.py:467
  7.3 1.4 collective-permute-done.2.w2
  8.7 1.2 collective-permute-start.3
  9.8 0.9 collective-permute-done.3.w3
  10.7 0.8 copy-done.2
  11.5 2.5 %fill.1 = bf16[16,64,896]{2,1,0:T(8,128)(2,1)} custom-call(s32[1]{0:T(128)} %bitcast.core_ref, s32[1]{0:T(128)} %bitcast.1.xh_ref, bf16[8,64,384]{2,1,0:T(8,128)(2,1)} %get-tuple-element.30.own_ref, bf16[8,64,384]{2,1,0:T(8,128)(2,1)S(1)} %collective-permute-done.peer_ref, bf16[8,2048]{1,0:T(8,128)(2,1)S(1)} %copy-done.2, ...), custom_call_target="tpu_custom_call" | custom-call | bytes 4194304 | tf_op jit(solution)/shard_map/fill/pallas_call | solution.py:379
  13.9 8.0 %all-to-all-start = ((bf16[16,64,896]{2,1,0:T(8,128)(2,1)}), bf16[16,64,896]{2,1,0:T(8,128)(2,1)S(1)}, u32[]{:S(2)}, u32[]{:S(2)}) async-start(bf16[16,64,896]{2,1,0:T(8,128)(2,1)} %fill.1), calls=%async_computation | async-start | bytes 3670016 | tf_op jit(solution)/shard_map/all_to_all | solution.py:288
  21.9 28.1 %all-to-all-done.x_ref = bf16[16,64,896]{2,1,0:T(8,128)(2,1)S(1)} async-done(((bf16[16,64,896]{2,1,0:T(8,128)(2,1)}), bf16[16,64,896]{2,1,0:T(8,128)(2,1)S(1)}, u32[]{:S(2)}, u32[]{:S(2)}) %all-to-all-start) | async-done | bytes 1835040 | tf_op jit(solution)/shard_map/all_to_all | solution.py:288
  50.0 1.4 split.1
  51.4 1.5 collective-permute-start.5
  53.0 1.3 collective-permute-start.4
  54.8 1.9 %collective-permute-start.7 = (bf16[12,64,512]{2,1,0:T(8,128)(2,1)}, bf16[12,64,512]{2,1,0:T(8,128)(2,1)S(1)}, u32[]{:S(2)}, u32[]{:S(2)}) collective-permute-start(bf16[12,64,512]{2,1,0:T(8,128)(2,1)} %get-tuple-element.42.own0), channel_id=1, source_target_pairs={{0,6},{2,4},{4,2},{6,0},{1,7},{3,5},{5,3},{7,1},{8,14},{10,12},{12... | collective-permute-start | bytes 2359304 | tf_op jit(solution)/shard_map/ppermute | solution.py:316
  56.7 6.5 %forward_near.1 = (f32[128,1024]{1,0:T(8,128)}, f32[1,1024]{1,0:T(1,128)S(1)}, f32[1,1024]{1,0:T(1,128)S(1)}) custom-call(bf16[1024,128]{1,0:T(8,128)(2,1)} %get-tuple-element.32.refs_0_, bf16[1024,256]{1,0:T(8,128)(2,1)} %get-tuple-element.33.refs_1_.kv0.refs_0_, bf16[1024,256]{1,0:T(8,128)(2,1)S(1)} %collective-permute-done.5.refs_2_.kv1, ...), custom_call_target="tpu_custom_call" | custom-call | flops 2147483648 | bytes 4194304 | tf_op jit(solution)/shard_map/forward_near/pallas_call | solution.py:132
  63.3 3.0 %collective-permute-done.4.refs_1_.kv2 = bf16[1024,256]{1,0:T(8,128)(2,1)S(1)} collective-permute-done((bf16[1024,256]{1,0:T(8,128)(2,1)}, bf16[1024,256]{1,0:T(8,128)(2,1)S(1)}, u32[]{:S(2)}, u32[]{:S(2)}) %collective-permute-start.4) | collective-permute-done | bytes 524320 | tf_op jit(solution)/shard_map/ppermute | solution.py:279
  66.3 1.3 collective-permute-start.6
  67.8 1.3 collective-permute-start.8
  69.2 7.5 %forward_far.1 = (bf16[1024,256]{1,0:T(8,128)(2,1)}, f32[1,1024]{1,0:T(1,128)S(1)}) custom-call(bf16[1024,128]{1,0:T(8,128)(2,1)} %get-tuple-element.32.refs_0_, bf16[1024,256]{1,0:T(8,128)(2,1)S(1)} %collective-permute-done.4.refs_1_.kv2, bf16[1024,256]{1,0:T(8,128)(2,1)S(1)} %collective-permute-done.6.refs_2_.kv3, ...), custom_call_target="tpu_custom_call" | custom-call | flops 2147483648 | bytes 4194304 | tf_op jit(solution)/shard_map/forward_far/pallas_call | solution.py:132
  76.7 3.3 %weight_whole.1 = (bf16[1024,1024]{1,0:T(8,128)(2,1)}, f32[128,1024]{1,0:T(8,128)S(1)}, f32[128,1024]{1,0:T(8,128)S(1)}) custom-call(s32[1]{0:T(128)} %bitcast.6.xl_ref, bf16[12,64,512]{2,1,0:T(8,128)(2,1)} %get-tuple-element.42.own0, bf16[4,64,512]{2,1,0:T(8,128)(2,1)} %get-tuple-element.43.own1, bf16[12,64,512]{2,1,0:T(8,128)(2,1)S(1)} %collective-permute-done.7.other0, ...), custom_call_target="tpu_custom_call" | custom-call | flops 536870912 | bytes 4194304 | tf_op jit(solution)/shard_map/weight_whole/pallas_call | solution.py:332
  80.4 1.5 collective-permute-done.10.peer_ref
  82.0 1.9 %cross.1 = bf16[16,64,256]{2,1,0:T(8,128)(2,1)} custom-call(bf16[1024,256]{1,0:T(8,128)(2,1)} %get-tuple-element.39.pair_ref.refs_2_, f32[128,1024]{1,0:T(8,128)S(1)} %get-tuple-element.44.own_ref, f32[128,1024]{1,0:T(8,128)S(1)} %collective-permute-done.10.peer_ref), custom_call_target="tpu_custom_call" | custom-call | bytes 4194304 | tf_op jit(solution)/shard_map/cross/pallas_call | solution.py:379
  83.9 3.6 %all-to-all-start.1 = ((bf16[16,64,256]{2,1,0:T(8,128)(2,1)}), bf16[16,64,256]{2,1,0:T(8,128)(2,1)S(1)}, u32[]{:S(2)}, u32[]{:S(2)}) async-start(bf16[16,64,256]{2,1,0:T(8,128)(2,1)} %cross.1), calls=%async_computation.1 | async-start | bytes 1048576 | tf_op jit(solution)/shard_map/all_to_all | solution.py:288
  87.5 1.3 collective-permute-start.15
  88.8 0.7 collective-permute-start.11
  89.5 0.8 collective-permute-done.11
  90.6 10.3 %collective-permute-done.12 = f32[2,1024]{1,0:T(2,128)S(1)} collective-permute-done((f32[2,1024]{1,0:T(2,128)S(1)}, f32[2,1024]{1,0:T(2,128)S(1)}, u32[]{:S(2)}, u32[]{:S(2)}) %collective-permute-start.12) | collective-permute-done | bytes 8224 | tf_op jit(solution)/shard_map/ppermute | solution.py:279
  100.9 0.8 land.1
  101.7 1.2 collective-permute-start.13
  103.4 1.2 collective-permute-start.19
  104.7 2.1 %weight_terms.1 = bf16[1024,1024]{1,0:T(8,128)(2,1)} custom-call(bf16[128,1024]{1,0:T(8,128)(2,1)S(1)} %get-tuple-element.46.own_ref, bf16[128,1024]{1,0:T(8,128)(2,1)S(1)} %collective-permute-done.13.peer_ref, bf16[256,1024]{1,0:T(8,128)(2,1)S(1)} %bitcast.59), custom_call_target="tpu_custom_call" | custom-call | flops 536870912 | bytes 4194304 | tf_op jit(solution)/shard_map/weight_terms/pallas_call | solution.py:360
  106.8 6.6 %all-to-all-start.3 = ((bf16[16,64,1024]{2,1,0:T(8,128)(2,1)}), bf16[16,64,1024]{2,1,0:T(8,128)(2,1)}, u32[]{:S(2)}, u32[]{:S(2)}) async-start(bf16[16,64,1024]{2,1,0:T(8,128)(2,1)} %bitcast.63), calls=%async_computation.3 | async-start | bytes 4194304 | tf_op jit(solution)/shard_map/all_to_all | solution.py:288
  113.4 10.1 %query_grad.1 = bf16[1024,128]{1,0:T(8,128)(2,1)S(1)} custom-call(bf16[1024,256]{1,0:T(8,128)(2,1)} %get-tuple-element.39.pair_ref.refs_2_, bf16[1024,128]{1,0:T(8,128)(2,1)} %get-tuple-element.48.g_ref.refs_6_, f32[1,1024]{1,0:T(1,128)S(1)} %get-tuple-element.49.lse_ref, bf16[1024,256]{1,0:T(8,128)(2,1)S(1)} %collective-permute-done.15.far_ref.refs_4_, ...), custom_call_target="tpu_custom_call" | custom-call | flops 6442450944 | bytes 4194304 | tf_op jit(solution)/shard_map/query_grad/pallas_call | solution.py:183
  124.0 1.1 collective-permute-start.20
  125.7 0.7 pad_maximum_fusion.4
  126.6 12.0 %key_grad.1 = (bf16[1024,128]{1,0:T(8,128)(2,1)S(1)}, bf16[1024,128]{1,0:T(8,128)(2,1)S(1)}) custom-call(bf16[1024,256]{1,0:T(8,128)(2,1)} %get-tuple-element.33.refs_1_.kv0.refs_0_, f32[64,128]{1,0:T(8,128)S(1)} %pad.4.refs_3_.bias_ref.refs_1_, bf16[1024,256]{1,0:T(8,128)(2,1)S(1)} %copy-done.1, bf16[1024,256]{1,0:T(8,128)(2,1)S(1)} %collective-permute-done.16.refs_3_, ...), custom_call_target="tpu_custom_call" | custom-call | flops 8589934592 | bytes 4194304 | tf_op jit(solution)/shard_map/key_grad/pallas_call | solution.py:245
  138.5 1.0 pad_maximum_fusion
  139.5 4.1 %all-to-all-done.3 = bf16[16,64,1024]{2,1,0:T(8,128)(2,1)} async-done(((bf16[16,64,1024]{2,1,0:T(8,128)(2,1)}), bf16[16,64,1024]{2,1,0:T(8,128)(2,1)}, u32[]{:S(2)}, u32[]{:S(2)}) %all-to-all-start.3) | async-done | bytes 2097184 | tf_op jit(solution)/shard_map/all_to_all | solution.py:288
  143.6 4.4 %all-to-all-start.2 = ((bf16[16,64,384]{2,1,0:T(8,128)(2,1)}), bf16[16,64,384]{2,1,0:T(8,128)(2,1)S(1)}, u32[]{:S(2)}, u32[]{:S(2)}) async-start(bf16[16,64,384]{2,1,0:T(8,128)(2,1)} %pad_maximum_fusion), calls=%async_computation.2 | async-start | bytes 1572864 | tf_op jit(solution)/shard_map/all_to_all | solution.py:288
  148.1 1.0 broadcast_select_fusion.7
  149.1 2.0 %convert_reduce_fusion = f32[64,1024]{1,0:T(8,128)S(1)} fusion(bf16[16,64,1024]{2,1,0:T(8,128)(2,1)} %all-to-all-done.3), kind=kLoop, calls=%fused_computation | loop fusion | flops 2031616 | bytes 2359296 | tf_op jit(solution)/shard_map/reduce_sum | solution.py:561
  151.2 2.1 %collective-permute-start.24 = (f32[16,1024]{1,0:T(8,128)S(1)}, f32[16,1024]{1,0:T(8,128)S(1)}, u32[]{:S(2)}, u32[]{:S(2)}) collective-permute-start(f32[16,1024]{1,0:T(8,128)S(1)} %get-tuple-element.64), channel_id=1, source_target_pairs={{0,6},{2,4},{4,2},{6,0},{1,7},{3,5},{5,3},{7,1},{8,14},{10,12},{12... | collective-permute-start | bytes 196616 | tf_op jit(solution)/shard_map/ppermute | solution.py:566
  153.4 1.7 %collective-permute-start.22 = (f32[16,1024]{1,0:T(8,128)S(1)}, f32[16,1024]{1,0:T(8,128)S(1)}, u32[]{:S(2)}, u32[]{:S(2)}) collective-permute-start(f32[16,1024]{1,0:T(8,128)S(1)} %get-tuple-element.63), channel_id=1, source_target_pairs={{0,2},{2,0},{4,6},{6,4},{1,3},{3,1},{5,7},{7,5},{8,10},{10,8},{12,... | collective-permute-start | bytes 196616 | tf_op jit(solution)/shard_map/ppermute | solution.py:566
  155.1 5.6 %all-to-all-done.2.own_ref = bf16[16,64,384]{2,1,0:T(8,128)(2,1)S(1)} async-done(((bf16[16,64,384]{2,1,0:T(8,128)(2,1)}), bf16[16,64,384]{2,1,0:T(8,128)(2,1)S(1)}, u32[]{:S(2)}, u32[]{:S(2)}) %all-to-all-start.2) | async-done | bytes 786464 | tf_op jit(solution)/shard_map/all_to_all | solution.py:288
  160.8 2.7 %collective-permute-start.21 = (bf16[8,64,384]{2,1,0:T(8,128)(2,1)S(1)}, bf16[8,64,384]{2,1,0:T(8,128)(2,1)S(1)}, u32[]{:S(2)}, u32[]{:S(2)}) collective-permute-start(bf16[8,64,384]{2,1,0:T(8,128)(2,1)S(1)} %constant_dynamic-slice_fusion), channel_id=1, source_target_pairs={{0,1},{1,0},{2,3},{3,2},{4,5},{5,4},{6,7},{7,6},{8,9},{9,8},{10,11... | collective-permute-start | bytes 1179656 | tf_op jit(solution)/shard_map/ppermute | solution.py:275
  163.7 0.8 maximum_bitcast_fusion
  164.8 1.1 final.1
  165.9 0.6 pad_maximum_fusion.6
  (73 shorter events, 4.2 us)
Async XLA Ops:
  2.8 7.9 %collective-permute-start = (bf16[8,64,384]{2,1,0:T(8,128)(2,1)}, bf16[8,64,384]{2,1,0:T(8,128)(2,1)S(1)}, u32[]{:S(2)}, u32[]{:S(2)}) collective-permute-start(bf16[8,64,384]{2,1,0:T(8,128)(2,1)} %get-tuple-element.31), channel_id=1, source_target_pairs={{0,1},{1,0},{2,3},{3,2},{4,5},{5,4},{6,7},{7,6},{8,9},{9,8},{10,11... | collective-permute-start | bytes 1179656 | tf_op jit(solution)/shard_map/ppermute | solution.py:275
  4.2 4.5 %collective-permute-start.2 = (bf16[8,2048]{1,0:T(8,128)(2,1)}, bf16[8,2048]{1,0:T(8,128)(2,1)S(1)}, u32[]{:S(2)}, u32[]{:S(2)}) collective-permute-start(bf16[8,2048]{1,0:T(8,128)(2,1)} %w0.1), channel_id=1, source_target_pairs={{0,2},{2,0},{1,3},{3,1},{4,6},{6,4},{5,7},{7,5},{8,10},{10,8},{9,1... | collective-permute-start | bytes 98312 | tf_op jit(solution)/shard_map/ppermute | solution.py:467
  7.0 2.8 %collective-permute-start.1 = (bf16[8,2048]{1,0:T(8,128)(2,1)}, bf16[8,2048]{1,0:T(8,128)(2,1)S(1)}, u32[]{:S(2)}, u32[]{:S(2)}) collective-permute-start(bf16[8,2048]{1,0:T(8,128)(2,1)} %w0.1), channel_id=1, source_target_pairs={{0,1},{1,0},{2,3},{3,2},{4,5},{5,4},{6,7},{7,6},{8,9},{9,8},{10,11... | collective-permute-start | bytes 98312 | tf_op jit(solution)/shard_map/ppermute | solution.py:275
  8.7 2.0 %collective-permute-start.3 = (bf16[8,2048]{1,0:T(8,128)(2,1)S(1)}, bf16[8,2048]{1,0:T(8,128)(2,1)S(1)}, u32[]{:S(2)}, u32[]{:S(2)}) collective-permute-start(bf16[8,2048]{1,0:T(8,128)(2,1)S(1)} %collective-permute-done.2.w2), channel_id=1, source_target_pairs={{0,1},{1,0},{2,3},{3,2},{4,5},{5,4},{6,7},{7,6},{8,9},{9,8},{10,11... | collective-permute-start | bytes 98312 | tf_op jit(solution)/shard_map/ppermute | solution.py:275
  10.7 0.8 copy-start.2
  13.9 38.9 %copy-start.8 = (bf16[1,128,2048]{2,1,0:T(8,128)(2,1)S(1)}, bf16[1,128,2048]{2,1,0:T(8,128)(2,1)}, u32[]{:S(2)}) copy-start(bf16[1,128,2048]{2,1,0:T(8,128)(2,1)} %param.13) | copy-start | bytes 1572868
  13.9 36.1 %all-to-all-start = ((bf16[16,64,896]{2,1,0:T(8,128)(2,1)}), bf16[16,64,896]{2,1,0:T(8,128)(2,1)S(1)}, u32[]{:S(2)}, u32[]{:S(2)}) async-start(bf16[16,64,896]{2,1,0:T(8,128)(2,1)} %fill.1), calls=%async_computation | async-start | bytes 3670016 | tf_op jit(solution)/shard_map/all_to_all | solution.py:288
  21.9 32.4 %copy-start.11 = (s32[64]{0:T(128)S(1)}, s32[64]{0:T(128)}, u32[]{:S(2)}) copy-start(s32[64]{0:T(128)} %param.10) | copy-start | bytes 772
  21.9 32.6 %copy-start.10 = (s32[64,64]{1,0:T(8,128)S(1)}, s32[64,64]{1,0:T(8,128)}, u32[]{:S(2)}) copy-start(s32[64,64]{1,0:T(8,128)} %param.11) | copy-start | bytes 49156
  51.4 5.3 %collective-permute-start.5 = (bf16[1024,256]{1,0:T(8,128)(2,1)}, bf16[1024,256]{1,0:T(8,128)(2,1)S(1)}, u32[]{:S(2)}, u32[]{:S(2)}) collective-permute-start(bf16[1024,256]{1,0:T(8,128)(2,1)} %get-tuple-element.33.refs_1_.kv0.refs_0_), channel_id=1, source_target_pairs={{0,1},{1,0},{2,3},{3,2},{4,5},{5,4},{6,7},{7,6},{8,9},{9,8},{10,11... | collective-permute-start | bytes 1572872 | tf_op jit(solution)/shard_map/ppermute | solution.py:275
  52.9 14.8 %collective-permute-start.9 = (bf16[128,1024]{1,0:T(8,128)(2,1)S(1)}, bf16[128,1024]{1,0:T(8,128)(2,1)S(1)}, u32[]{:S(2)}, u32[]{:S(2)}) collective-permute-start(bf16[128,1024]{1,0:T(8,128)(2,1)S(1)} %broadcast_select_fusion.2), channel_id=1, source_target_pairs={{0,1},{1,0},{2,3},{3,2},{4,5},{5,4},{6,7},{7,6},{8,9},{9,8},{10,11... | collective-permute-start | bytes 786440 | tf_op jit(solution)/shard_map/ppermute | solution.py:275
  53.0 13.3 %collective-permute-start.4 = (bf16[1024,256]{1,0:T(8,128)(2,1)}, bf16[1024,256]{1,0:T(8,128)(2,1)S(1)}, u32[]{:S(2)}, u32[]{:S(2)}) collective-permute-start(bf16[1024,256]{1,0:T(8,128)(2,1)} %get-tuple-element.33.refs_1_.kv0.refs_0_), channel_id=1, source_target_pairs={{0,4},{4,0},{1,5},{5,1},{2,6},{6,2},{3,7},{7,3},{8,12},{12,8},{9,1... | collective-permute-start | bytes 1572872 | tf_op jit(solution)/shard_map/ppermute | solution.py:279
  54.8 21.9 %collective-permute-start.7 = (bf16[12,64,512]{2,1,0:T(8,128)(2,1)}, bf16[12,64,512]{2,1,0:T(8,128)(2,1)S(1)}, u32[]{:S(2)}, u32[]{:S(2)}) collective-permute-start(bf16[12,64,512]{2,1,0:T(8,128)(2,1)} %get-tuple-element.42.own0), channel_id=1, source_target_pairs={{0,6},{2,4},{4,2},{6,0},{1,7},{3,5},{5,3},{7,1},{8,14},{10,12},{12... | collective-permute-start | bytes 2359304 | tf_op jit(solution)/shard_map/ppermute | solution.py:316
  56.7 6.6 %copy-start.3 = (bf16[1024,256]{1,0:T(8,128)(2,1)}, bf16[1024,256]{1,0:T(8,128)(2,1)S(1)}, u32[]{:S(2)}) copy-start(bf16[1024,256]{1,0:T(8,128)(2,1)S(1)} %collective-permute-done.5.refs_2_.kv1) | copy-start | bytes 1572868
  63.3 4.5 %copy-start.9 = (bf16[4,64,512]{2,1,0:T(8,128)(2,1)S(1)}, bf16[4,64,512]{2,1,0:T(8,128)(2,1)}, u32[]{:S(2)}) copy-start(bf16[4,64,512]{2,1,0:T(8,128)(2,1)} %get-tuple-element.43.own1) | copy-start | bytes 786436
  66.3 10.4 %copy-start.4 = (bf16[1024,256]{1,0:T(8,128)(2,1)}, bf16[1024,256]{1,0:T(8,128)(2,1)S(1)}, u32[]{:S(2)}) copy-start(bf16[1024,256]{1,0:T(8,128)(2,1)S(1)} %collective-permute-done.4.refs_1_.kv2) | copy-start | bytes 1572868
  66.3 2.9 %collective-permute-start.6 = (bf16[1024,256]{1,0:T(8,128)(2,1)S(1)}, bf16[1024,256]{1,0:T(8,128)(2,1)S(1)}, u32[]{:S(2)}, u32[]{:S(2)}) collective-permute-start(bf16[1024,256]{1,0:T(8,128)(2,1)S(1)} %collective-permute-done.4.refs_1_.kv2), channel_id=1, source_target_pairs={{0,1},{1,0},{2,3},{3,2},{4,5},{5,4},{6,7},{7,6},{8,9},{9,8},{10,11... | collective-permute-start | bytes 1572872 | tf_op jit(solution)/shard_map/ppermute | solution.py:275
  67.8 8.9 %collective-permute-start.8 = (bf16[4,64,512]{2,1,0:T(8,128)(2,1)S(1)}, bf16[4,64,512]{2,1,0:T(8,128)(2,1)S(1)}, u32[]{:S(2)}, u32[]{:S(2)}) collective-permute-start(bf16[4,64,512]{2,1,0:T(8,128)(2,1)S(1)} %copy-done.9), channel_id=1, source_target_pairs={{0,4},{4,0},{1,5},{5,1},{2,6},{6,2},{3,7},{7,3},{8,12},{12,8},{9,1... | collective-permute-start | bytes 786440 | tf_op jit(solution)/shard_map/ppermute | solution.py:279
  69.2 7.5 %copy-start.5 = (bf16[1024,256]{1,0:T(8,128)(2,1)}, bf16[1024,256]{1,0:T(8,128)(2,1)S(1)}, u32[]{:S(2)}) copy-start(bf16[1024,256]{1,0:T(8,128)(2,1)S(1)} %collective-permute-done.6.refs_2_.kv3) | copy-start | bytes 1572868
  80.1 7.4 %copy-start = (bf16[1024,256]{1,0:T(8,128)(2,1)S(1)}, bf16[1024,256]{1,0:T(8,128)(2,1)}, u32[]{:S(2)}) copy-start(bf16[1024,256]{1,0:T(8,128)(2,1)} %get-tuple-element.39.pair_ref.refs_2_) | copy-start | bytes 1572868
  80.1 1.9 %collective-permute-start.10 = (f32[128,1024]{1,0:T(8,128)S(1)}, f32[128,1024]{1,0:T(8,128)S(1)}, u32[]{:S(2)}, u32[]{:S(2)}) collective-permute-start(f32[128,1024]{1,0:T(8,128)S(1)} %get-tuple-element.45), channel_id=1, source_target_pairs={{0,1},{1,0},{2,3},{3,2},{4,5},{5,4},{6,7},{7,6},{8,9},{9,8},{10,11... | collective-permute-start | bytes 1572872 | tf_op jit(solution)/shard_map/ppermute | solution.py:275
  83.9 17.0 %all-to-all-start.1 = ((bf16[16,64,256]{2,1,0:T(8,128)(2,1)}), bf16[16,64,256]{2,1,0:T(8,128)(2,1)S(1)}, u32[]{:S(2)}, u32[]{:S(2)}) async-start(bf16[16,64,256]{2,1,0:T(8,128)(2,1)} %cross.1), calls=%async_computation.1 | async-start | bytes 1048576 | tf_op jit(solution)/shard_map/all_to_all | solution.py:288
  87.5 15.4 %collective-permute-start.15 = (bf16[1024,256]{1,0:T(8,128)(2,1)S(1)}, bf16[1024,256]{1,0:T(8,128)(2,1)S(1)}, u32[]{:S(2)}, u32[]{:S(2)}) collective-permute-start(bf16[1024,256]{1,0:T(8,128)(2,1)S(1)} %copy-done), channel_id=1, source_target_pairs={{0,4},{4,0},{1,5},{5,1},{2,6},{6,2},{3,7},{7,3},{8,12},{12,8},{9,1... | collective-permute-start | bytes 1572872 | tf_op jit(solution)/shard_map/ppermute | solution.py:279
  88.8 1.5 collective-permute-start.11
  90.3 10.6 %collective-permute-start.12 = (f32[2,1024]{1,0:T(2,128)S(1)}, f32[2,1024]{1,0:T(2,128)S(1)}, u32[]{:S(2)}, u32[]{:S(2)}) collective-permute-start(f32[2,1024]{1,0:T(2,128)S(1)} %pad_maximum_fusion.8), channel_id=1, source_target_pairs={{0,4},{4,0},{1,5},{5,1},{2,6},{6,2},{3,7},{7,3},{8,12},{12,8},{9,1... | collective-permute-start | bytes 24584 | tf_op jit(solution)/shard_map/ppermute | solution.py:279
  101.7 2.9 %collective-permute-start.13 = (bf16[128,1024]{1,0:T(8,128)(2,1)S(1)}, bf16[128,1024]{1,0:T(8,128)(2,1)S(1)}, u32[]{:S(2)}, u32[]{:S(2)}) collective-permute-start(bf16[128,1024]{1,0:T(8,128)(2,1)S(1)} %get-tuple-element.46.own_ref), channel_id=1, source_target_pairs={{0,1},{1,0},{2,3},{3,2},{4,5},{5,4},{6,7},{7,6},{8,9},{9,8},{10,11... | collective-permute-start | bytes 786440 | tf_op jit(solution)/shard_map/ppermute | solution.py:275
  102.9 23.5 %collective-permute-start.16 = (bf16[1024,256]{1,0:T(8,128)(2,1)S(1)}, bf16[1024,256]{1,0:T(8,128)(2,1)S(1)}, u32[]{:S(2)}, u32[]{:S(2)}) collective-permute-start(bf16[1024,256]{1,0:T(8,128)(2,1)S(1)} %copy-done), channel_id=1, source_target_pairs={{0,1},{1,0},{2,3},{3,2},{4,5},{5,4},{6,7},{7,6},{8,9},{9,8},{10,11... | collective-permute-start | bytes 1572872 | tf_op jit(solution)/shard_map/ppermute | solution.py:275
  102.9 23.5 %collective-permute-start.17 = (bf16[1024,256]{1,0:T(8,128)(2,1)S(1)}, bf16[1024,256]{1,0:T(8,128)(2,1)S(1)}, u32[]{:S(2)}, u32[]{:S(2)}) collective-permute-start(bf16[1024,256]{1,0:T(8,128)(2,1)S(1)} %collective-permute-done.15.far_ref.refs_4_), channel_id=1, source_target_pairs={{0,1},{1,0},{2,3},{3,2},{4,5},{5,4},{6,7},{7,6},{8,9},{9,8},{10,11... | collective-permute-start | bytes 1572872 | tf_op jit(solution)/shard_map/ppermute | solution.py:275
  103.4 23.0 %collective-permute-start.18 = (bf16[1024,128]{1,0:T(8,128)(2,1)}, bf16[1024,128]{1,0:T(8,128)(2,1)S(1)}, u32[]{:S(2)}, u32[]{:S(2)}) collective-permute-start(bf16[1024,128]{1,0:T(8,128)(2,1)} %get-tuple-element.48.g_ref.refs_6_), channel_id=1, source_target_pairs={{0,1},{1,0},{2,3},{3,2},{4,5},{5,4},{6,7},{7,6},{8,9},{9,8},{10,11... | collective-permute-start | bytes 786440 | tf_op jit(solution)/shard_map/ppermute | solution.py:275
  103.4 20.6 %collective-permute-start.19 = (bf16[1024,128]{1,0:T(8,128)(2,1)}, bf16[1024,128]{1,0:T(8,128)(2,1)}, u32[]{:S(2)}, u32[]{:S(2)}) collective-permute-start(bf16[1024,128]{1,0:T(8,128)(2,1)} %get-tuple-element.48.g_ref.refs_6_), channel_id=1, source_target_pairs={{0,4},{4,0},{1,5},{5,1},{2,6},{6,2},{3,7},{7,3},{8,12},{12,8},{9,1... | collective-permute-start | bytes 786440 | tf_op jit(solution)/shard_map/ppermute | solution.py:279
  106.8 36.9 %all-to-all-start.3 = ((bf16[16,64,1024]{2,1,0:T(8,128)(2,1)}), bf16[16,64,1024]{2,1,0:T(8,128)(2,1)}, u32[]{:S(2)}, u32[]{:S(2)}) async-start(bf16[16,64,1024]{2,1,0:T(8,128)(2,1)} %bitcast.63), calls=%async_computation.3 | async-start | bytes 4194304 | tf_op jit(solution)/shard_map/all_to_all | solution.py:288
  113.4 10.1 %copy-start.7 = (bf16[1024,1024]{1,0:T(8,128)(2,1)S(1)}, bf16[1024,1024]{1,0:T(8,128)(2,1)}, u32[]{:S(2)}) copy-start(bf16[1024,1024]{1,0:T(8,128)(2,1)} %get-tuple-element.47) | copy-start | bytes 6291460
  124.0 2.6 %copy-start.1 = (bf16[1024,256]{1,0:T(8,128)(2,1)S(1)}, bf16[1024,256]{1,0:T(8,128)(2,1)}, u32[]{:S(2)}) copy-start(bf16[1024,256]{1,0:T(8,128)(2,1)} %get-tuple-element.39.pair_ref.refs_2_) | copy-start | bytes 1572868
  124.0 2.5 %copy-start.6 = (bf16[1024,128]{1,0:T(8,128)(2,1)S(1)}, bf16[1024,128]{1,0:T(8,128)(2,1)}, u32[]{:S(2)}) copy-start(bf16[1024,128]{1,0:T(8,128)(2,1)} %get-tuple-element.48.g_ref.refs_6_) | copy-start | bytes 786436
  124.0 2.5 %collective-permute-start.20 = (bf16[1024,128]{1,0:T(8,128)(2,1)}, bf16[1024,128]{1,0:T(8,128)(2,1)S(1)}, u32[]{:S(2)}, u32[]{:S(2)}) collective-permute-start(bf16[1024,128]{1,0:T(8,128)(2,1)} %collective-permute-done.19.refs_8_), channel_id=1, source_target_pairs={{0,1},{1,0},{2,3},{3,2},{4,5},{5,4},{6,7},{7,6},{8,9},{9,8},{10,11... | collective-permute-start | bytes 786440 | tf_op jit(solution)/shard_map/ppermute | solution.py:275
  126.4 21.7 %collective-permute-start.14 = (bf16[2,64,1024]{2,1,0:T(8,128)(2,1)}, bf16[2,64,1024]{2,1,0:T(8,128)(2,1)}, u32[]{:S(2)}, u32[]{:S(2)}) collective-permute-start(bf16[2,64,1024]{2,1,0:T(8,128)(2,1)} %pad_maximum_fusion.4), channel_id=1, source_target_pairs={{0,1},{1,0},{2,3},{3,2},{4,5},{5,4},{6,7},{7,6},{8,9},{9,8},{10,11... | collective-permute-start | bytes 786440 | tf_op jit(solution)/shard_map/ppermute | solution.py:275
  143.6 17.1 %all-to-all-start.2 = ((bf16[16,64,384]{2,1,0:T(8,128)(2,1)}), bf16[16,64,384]{2,1,0:T(8,128)(2,1)S(1)}, u32[]{:S(2)}, u32[]{:S(2)}) async-start(bf16[16,64,384]{2,1,0:T(8,128)(2,1)} %pad_maximum_fusion), calls=%async_computation.2 | async-start | bytes 1572864 | tf_op jit(solution)/shard_map/all_to_all | solution.py:288
  151.2 12.3 %collective-permute-start.24 = (f32[16,1024]{1,0:T(8,128)S(1)}, f32[16,1024]{1,0:T(8,128)S(1)}, u32[]{:S(2)}, u32[]{:S(2)}) collective-permute-start(f32[16,1024]{1,0:T(8,128)S(1)} %get-tuple-element.64), channel_id=1, source_target_pairs={{0,6},{2,4},{4,2},{6,0},{1,7},{3,5},{5,3},{7,1},{8,14},{10,12},{12... | collective-permute-start | bytes 196616 | tf_op jit(solution)/shard_map/ppermute | solution.py:566
  153.3 10.2 %collective-permute-start.23 = (f32[16,1024]{1,0:T(8,128)S(1)}, f32[16,1024]{1,0:T(8,128)S(1)}, u32[]{:S(2)}, u32[]{:S(2)}) collective-permute-start(f32[16,1024]{1,0:T(8,128)S(1)} %get-tuple-element.65), channel_id=1, source_target_pairs={{0,4},{2,6},{4,0},{6,2},{1,5},{3,7},{5,1},{7,3},{8,12},{10,14},{12... | collective-permute-start | bytes 196616 | tf_op jit(solution)/shard_map/ppermute | solution.py:566
  153.4 10.1 %collective-permute-start.22 = (f32[16,1024]{1,0:T(8,128)S(1)}, f32[16,1024]{1,0:T(8,128)S(1)}, u32[]{:S(2)}, u32[]{:S(2)}) collective-permute-start(f32[16,1024]{1,0:T(8,128)S(1)} %get-tuple-element.63), channel_id=1, source_target_pairs={{0,2},{2,0},{4,6},{6,4},{1,3},{3,1},{5,7},{7,5},{8,10},{10,8},{12,... | collective-permute-start | bytes 196616 | tf_op jit(solution)/shard_map/ppermute | solution.py:566
  160.8 4.0 %collective-permute-start.21 = (bf16[8,64,384]{2,1,0:T(8,128)(2,1)S(1)}, bf16[8,64,384]{2,1,0:T(8,128)(2,1)S(1)}, u32[]{:S(2)}, u32[]{:S(2)}) collective-permute-start(bf16[8,64,384]{2,1,0:T(8,128)(2,1)S(1)} %constant_dynamic-slice_fusion), channel_id=1, source_target_pairs={{0,1},{1,0},{2,3},{3,2},{4,5},{5,4},{6,7},{7,6},{8,9},{9,8},{10,11... | collective-permute-start | bytes 1179656 | tf_op jit(solution)/shard_map/ppermute | solution.py:275
  163.5 2.4 %collective-permute-start.25 = (f32[8,1024]{1,0:T(8,128)S(1)}, f32[8,1024]{1,0:T(8,128)S(1)}, u32[]{:S(2)}, u32[]{:S(2)}) collective-permute-start(f32[8,1024]{1,0:T(8,128)S(1)} %dynamic-slice_bitcast_fusion.3), channel_id=1, source_target_pairs={{0,1},{1,0},{2,3},{3,2},{4,5},{5,4},{6,7},{7,6},{8,9},{9,8},{10,11... | collective-permute-start | bytes 98312 | tf_op jit(solution)/shard_map/ppermute | solution.py:275

commit v8 on v7

--- a/solution.py
+++ b/solution.py
@@ -374,18 +374,25 @@
 IN_SMEM = pl.BlockSpec(memory_space=pltpu.SMEM)
 
 
-def move(body, name, outs, scalars, *arrays, space=jax.ShapeDtypeStruct):
+def move(body, name, outs, scalars, *arrays, space=jax.ShapeDtypeStruct, after=()):
     spaces = space if isinstance(space, list) else [space] * len(outs)
+    read = len(scalars) + len(arrays)
+
+    def run(*refs):
+        body(*refs[:read], *refs[read + len(after) :])
+
     return pl.pallas_call(
-        body,
+        run,
         out_shape=[make(shape, BF16) for make, shape in zip(spaces, outs)],
         grid=(1,),
-        in_specs=[IN_SMEM] * len(scalars) + [once(*x.shape) for x in arrays],
+        in_specs=[IN_SMEM] * len(scalars)
+        + [once(*x.shape) for x in arrays]
+        + [pl.BlockSpec(memory_space=pl.ANY)] * len(after),
         out_specs=[once(*shape) for shape in outs],
         cost_estimate=pl.CostEstimate(flops=0, bytes_accessed=4 << 20, transcendentals=0),
         compiler_params=pltpu.CompilerParams(vmem_limit_bytes=GRANT),
         name=name,
-    )(*scalars, *arrays)
+    )(*scalars, *arrays, *after)
 
 
 def head_cols(h):
@@ -421,6 +428,16 @@
             out_ref[unit, c * 32 : (c + 1) * 32, 3 * HEAD :] = part
 
 
+def up_body(core_ref, half_ref, own_ref, peer_ref, out_ref):
+    core, half = core_ref[0], half_ref[0]
+    for side in range(2):
+        rows = span_rows(half ^ side)
+        wide = own_ref[rows, :]
+        mine = jnp.where(core == 0, wide[:, :1024], wide[:, 1024:])
+        out_ref[span_rows(2 * side + core), :] = mine
+        out_ref[span_rows(2 * side + 1 - core), :] = peer_ref[rows, :]
+
+
 def split_body(x_ref, q_ref, kv_ref, w0_ref, w1_ref):
     x = x_ref[...]
     q_ref[...] = x[:, :, :HEAD].reshape(ROWS, HEAD)
@@ -438,7 +455,7 @@
             out_ref[unit, :, HEAD:] = total.astype(BF16)
 
 
-def land_body(x_ref, lses_ref, att_ref, g_ref):
+def land_body(x_ref, att_ref, g_ref):
     g_ref[...] = x_ref[:, :, HEAD:].reshape(ROWS, HEAD)
     for s in range(2):
         for h in range(HEADS):
@@ -460,9 +477,18 @@
     core_1, xl_1, xh_1, half_1 = (x.reshape(1) for x in (core, xl, xh, half))
     cols = output_weight.shape[1] // 2
 
-    def by_core(x):
-        left, right = x[..., :cols], x[..., cols:]
-        return jnp.where(first_core, left, right), jnp.where(first_core, right, left)
+    bias = span_bias(span_order, block_mask, xl, core)
+    wide = upstream[0]
+    up_sent = jnp.where(first_core, wide[:, cols:], wide[:, :cols])
+    (up,) = move(
+        up_body,
+        "up",
+        [(4 * SPAN, cols)],
+        [core_1, half_1],
+        in_hbm(wide),
+        other_core(up_sent),
+        space=pltpu.HBM,
+    )
 
     weight_far = lax.ppermute(output_weight, "xh", SWAP)
     weight_rows = [output_weight, other_core(output_weight), weight_far, other_core(weight_far)]
@@ -485,7 +511,7 @@
         in_hbm(own),
         other_core(sent),
         *weight_rows,
-        space=pltpu.HBM,
+        after=(in_hbm(up), bias),
     )
     blocks = exchange(blocks, ZY)
     q, own_kv, *weight_own = move(
@@ -499,12 +525,6 @@
     far_kv = other_chip(own_kv)
     weight_other = [across(weight_own[0]), other_chip(weight_own[1])]
     near_kv = other_core(own_kv)
-    bias = span_bias(span_order, block_mask, xl, core)
-
-    up_mine, up_theirs = by_core(upstream[0])
-    up = in_order(first_core, up_mine, other_core(up_theirs)).reshape(2, 2, SPAN, cols)
-    up = in_order(half == 0, up[:, 0], up[:, 1]).reshape(4 * SPAN, cols)
-
     out, top, total = forward(True, in_hbm(q), (in_hbm(own_kv), near_kv), bias)
     far_kv, total = lax.optimization_barrier((far_kv, total))
     kvs = (own_kv, near_kv, far_kv, other_core(far_kv))
@@ -514,7 +534,7 @@
 
     place, lse = lax.optimization_barrier((xl_1, lse))
     weight, grad_own, grad_sent = weight_whole(
-        place, [in_hbm(x) for x in weight_own], weight_other, up
+        place, [in_hbm(x) for x in weight_own], weight_other, in_hbm(up)
     )
     (crossing,) = move(
         cross_body,
@@ -526,7 +546,8 @@
         other_core(grad_sent),
     )
     crossed = exchange(crossing, ZY)
-    pairs = everyone(pair)
+    pair_sent, lses = lax.optimization_barrier((pair, lses))
+    pairs = everyone(pair_sent)
 
     att_own, g = move(
         land_body,
@@ -534,12 +555,12 @@
         [(2 * SPAN, HEADS * HEAD), (ROWS, HEAD)],
         [],
         crossed,
-        lses,
+        after=(lses,),
         space=[jax.ShapeDtypeStruct, pltpu.HBM],
     )
     gs = everyone(g)
     att_peer = other_core(att_own)
-    term = weight_terms(att_own, att_peer, up).reshape(UNITS, SPAN, cols)
+    term = weight_terms(att_own, att_peer, in_hbm(up)).reshape(UNITS, SPAN, cols)
     term = exchange(term, ZY)
 
     query_out = query_grad(in_hbm(pair), in_hbm(g), lse, pairs[2], [in_hbm(x) for x in kvs], bias)

time: 167 us -> 166 us (level)
  blocking collectives: 0 us -> 32.8 us
  waiting for transfers between devices: 56.3 us -> 30.6 us
  starting transfers between devices: 49.1 us -> 37.1 us
  Pallas kernels: 51.3 us -> 53.1 us
    all_to_all x0 -> x1, blocking collectives: none -> 32.8 us  [exchange(): return lax.all_to_all(x, axes, 0, 0, tiled=True)]
    all_to_all x4 -> x3, waiting for transfers between devices: 37.8 us -> 17.8 us  [exchange(): return lax.all_to_all(x, axes, 0, 0, tiled=True)]
    all_to_all x4 -> x3, starting transfers between devices: 22.6 us -> 14.9 us  [exchange(): return lax.all_to_all(x, axes, 0, 0, tiled=True)]
    ppermute x5, waiting for transfers between devices: 13.3 us -> 8.99 us  [other_chip(): return lax.ppermute(x, 'xl', SWAP)]
    ppermute x5, starting transfers between devices: 5.42 us -> 1.71 us  [other_chip(): return lax.ppermute(x, 'xl', SWAP)]
    pallas_call x6 -> x7, Pallas kernels: 9.78 us -> 10.4 us  [move(): pl.pallas_call(run, out_shape=[make(shape, BF16) for make, shape in zip(s...]
  transfers between devices with their start and end apart: 30 -> 29, of which waited for: 12 -> 10; matrix products, arithmetic and copies ran while one was open for 4% -> 6% of each run, Pallas kernels for 24% -> 29%
where the time goes in v8:
time: 166 us; the launch traced here: 165 us
  Pallas kernels  53.1 us (32%)
  starting transfers between devices  37.1 us (22%)
  blocking collectives  32.8 us (20%)
  waiting for transfers between devices  30.6 us (18%)
  other arithmetic  8.26 us (5%)
  matrix products  1.97 us (1%)
    all_to_all x1, blocking collectives, exchange(): return lax.all_to_all(x, axes, 0, 0, tiled=True)  32.8 us
    all_to_all x3, waiting for transfers between devices, exchange(): return lax.all_to_all(x, axes, 0, 0, tiled=True)  17.8 us
    all_to_all x3, starting transfers between devices, exchange(): return lax.all_to_all(x, axes, 0, 0, tiled=True)  14.9 us
    pallas_call x2, Pallas kernels, forward(): pl.pallas_call(functools.partial(forward_body, first), out_shape=outs, gr...  14.1 us
    ppermute x16, starting transfers between devices, other_core(): return lax.ppermute(x, 'core', SWAP)  13 us
    pallas_call x1, Pallas kernels, key_grad(): pl.pallas_call(key_body, out_shape=[jax.ShapeDtypeStruct((ROWS, HEAD), BF...  11.9 us
    pallas_call x7, Pallas kernels, move(): pl.pallas_call(run, out_shape=[make(shape, BF16) for make, shape in zip(s...  10.4 us
    pallas_call x1, Pallas kernels, query_grad(): pl.pallas_call(query_body, out_shape=jax.ShapeDtypeStruct((ROWS, HEAD), B...  10.1 us
  transfers between devices with their start and end apart: 29, of which 10 were waited for; matrix products, arithmetic and copies ran while one was open for 6% of the time, Pallas kernels for 29%

profile of v8, /device:TPU:1, one launch (start us, length us, event | category | flops | bytes accessed | tf_op | source)
XLA Modules:
  0.0 164.9 jit_solution(653646006296976200)
XLA Ops:
  0.6 1.5 collective-permute-start.1
  2.1 2.8 %collective-permute-start.2 = (bf16[8,2048]{1,0:T(8,128)(2,1)}, bf16[8,2048]{1,0:T(8,128)(2,1)S(1)}, u32[]{:S(2)}, u32[]{:S(2)}) collective-permute-start(bf16[8,2048]{1,0:T(8,128)(2,1)} %refs_4_.1), channel_id=1, source_target_pairs={{0,2},{2,0},{1,3},{3,1},{4,6},{6,4},{5,7},{7,5},{8,10},{10,8},{9,1... | collective-permute-start | bytes 98312 | tf_op jit(solution)/shard_map/ppermute | solution.py:493
  5.0 2.1 %cut.1 = (bf16[8,64,384]{2,1,0:T(8,128)(2,1)}, bf16[8,64,384]{2,1,0:T(8,128)(2,1)}) custom-call(s32[1]{0:T(128)} %bitcast.2.refs_0_.refs_1_, bf16[128,1024]{1,0:T(8,128)(2,1)} %bitcast.59, bf16[128,1024]{1,0:T(8,128)(2,1)} %bitcast.60, bf16[128,1024]{1,0:T(8,128)(2,1)} %bitcast.61), custom_call_target="tpu_custom_call" | custom-call | bytes 4194304 | tf_op jit(solution)/shard_map/cut/pallas_call | solution.py:384
  7.5 1.1 slice_select_fusion
  8.8 0.8 select_reduce_fusion
  10.1 1.1 fusion.9
  11.2 1.9 %up.1.refs_8_.up_ref = bf16[256,1024]{1,0:T(8,128)(2,1)} custom-call(s32[1]{0:T(128)} %bitcast.refs_0_, s32[1]{0:T(128)} %bitcast.2.refs_0_.refs_1_, bf16[128,2048]{1,0:T(8,128)(2,1)} %bitcast.52, bf16[128,1024]{1,0:T(8,128)(2,1)S(1)} %collective-permute-done.4.refs_3_), custom_call_target="tpu_custom_call" | custom-call | bytes 4194304 | tf_op jit(solution)/shard_map/up/pallas_call | solution.py:384
  13.1 1.2 fill.1
  14.3 32.8 %all_to_all.20.refs_0_ = bf16[16,64,896]{2,1,0:T(8,128)(2,1)S(1)} all-to-all(bf16[16,64,896]{2,1,0:T(8,128)(2,1)S(1)} %fill.1), channel_id=1, replica_groups=mesh['z'=4,'y'=4,'xl'=2,'xh'=2,'core'=2] {'z','y'}, dimensions={0} | all-to-all | bytes 3670016 | tf_op jit(solution)/shard_map/all_to_all | solution.py:288
  47.1 1.4 split.1
  48.5 1.3 collective-permute-start.6
  50.1 0.7 collective-permute-start.8
  50.7 0.8 collective-permute-done.6.refs_2_.kv1
  51.5 6.6 %forward_near.1 = (f32[128,1024]{1,0:T(8,128)}, f32[1,1024]{1,0:T(1,128)S(1)}, f32[1,1024]{1,0:T(1,128)S(1)}) custom-call(bf16[1024,128]{1,0:T(8,128)(2,1)} %get-tuple-element.34.refs_0_, bf16[1024,256]{1,0:T(8,128)(2,1)} %get-tuple-element.35.refs_1_.kv0.refs_0_, bf16[1024,256]{1,0:T(8,128)(2,1)S(1)} %collective-permute-done.6.refs_2_.kv1, ...), custom_call_target="tpu_custom_call" | custom-call | flops 2147483648 | bytes 4194304 | tf_op jit(solution)/shard_map/forward_near/pallas_call | solution.py:132
  58.1 5.4 %collective-permute-done.5.refs_1_.kv2 = bf16[1024,256]{1,0:T(8,128)(2,1)S(1)} collective-permute-done((bf16[1024,256]{1,0:T(8,128)(2,1)}, bf16[1024,256]{1,0:T(8,128)(2,1)S(1)}, u32[]{:S(2)}, u32[]{:S(2)}) %collective-permute-start.5) | collective-permute-done | bytes 524320 | tf_op jit(solution)/shard_map/ppermute | solution.py:279
  63.5 0.8 collective-permute-start.7
  64.6 1.2 collective-permute-done.7.refs_2_.kv3
  65.9 7.5 %forward_far.1 = (bf16[1024,256]{1,0:T(8,128)(2,1)}, f32[1,1024]{1,0:T(1,128)S(1)}) custom-call(bf16[1024,128]{1,0:T(8,128)(2,1)} %get-tuple-element.34.refs_0_, bf16[1024,256]{1,0:T(8,128)(2,1)S(1)} %collective-permute-done.5.refs_1_.kv2, bf16[1024,256]{1,0:T(8,128)(2,1)S(1)} %collective-permute-done.7.refs_2_.kv3, ...), custom_call_target="tpu_custom_call" | custom-call | flops 2147483648 | bytes 4194304 | tf_op jit(solution)/shard_map/forward_far/pallas_call | solution.py:132
  73.4 3.5 %weight_whole.1 = (bf16[1024,1024]{1,0:T(8,128)(2,1)}, f32[128,1024]{1,0:T(8,128)S(1)}, f32[128,1024]{1,0:T(8,128)S(1)}) custom-call(s32[1]{0:T(128)} %bitcast.7.xl_ref, bf16[12,64,512]{2,1,0:T(8,128)(2,1)} %get-tuple-element.44.own0, bf16[4,64,512]{2,1,0:T(8,128)(2,1)} %get-tuple-element.45.own1, bf16[12,64,512]{2,1,0:T(8,128)(2,1)S(1)} %collective-permute-done.8.other0, ...), custom_call_target="tpu_custom_call" | custom-call | flops 536870912 | bytes 4194304 | tf_op jit(solution)/shard_map/weight_whole/pallas_call | solution.py:332
  77.4 1.4 collective-permute-done.10.refs_2_
  78.8 1.9 %cross.1 = bf16[16,64,256]{2,1,0:T(8,128)(2,1)} custom-call(bf16[1024,256]{1,0:T(8,128)(2,1)} %get-tuple-element.53.refs_0_.pair_ref.refs_2_, f32[128,1024]{1,0:T(8,128)S(1)} %get-tuple-element.46.refs_1_, f32[128,1024]{1,0:T(8,128)S(1)} %collective-permute-done.10.refs_2_), custom_call_target="tpu_custom_call" | custom-call | bytes 4194304 | tf_op jit(solution)/shard_map/cross/pallas_call | solution.py:384
  80.7 3.6 %all-to-all-start.1 = ((bf16[16,64,256]{2,1,0:T(8,128)(2,1)}), bf16[16,64,256]{2,1,0:T(8,128)(2,1)S(1)}, u32[]{:S(2)}, u32[]{:S(2)}) async-start(bf16[16,64,256]{2,1,0:T(8,128)(2,1)} %cross.1), calls=%async_computation.1 | async-start | bytes 1048576 | tf_op jit(solution)/shard_map/all_to_all | solution.py:288
  84.7 2.2 %collective-permute-done.12 = f32[2,1024]{1,0:T(2,128)S(1)} collective-permute-done((f32[2,1024]{1,0:T(2,128)S(1)}, f32[2,1024]{1,0:T(2,128)S(1)}, u32[]{:S(2)}, u32[]{:S(2)}) %collective-permute-start.12) | collective-permute-done | bytes 8224 | tf_op jit(solution)/shard_map/ppermute | solution.py:279
  87.4 7.9 %all-to-all-done.1.refs_0_ = bf16[16,64,256]{2,1,0:T(8,128)(2,1)S(1)} async-done(((bf16[16,64,256]{2,1,0:T(8,128)(2,1)}), bf16[16,64,256]{2,1,0:T(8,128)(2,1)S(1)}, u32[]{:S(2)}, u32[]{:S(2)}) %all-to-all-start.1) | async-done | bytes 524320 | tf_op jit(solution)/shard_map/all_to_all | solution.py:288
  95.3 0.8 land.1
  96.1 1.5 collective-permute-start.13
  97.6 1.4 collective-permute-done.15.far_ref.refs_4_
  98.9 2.4 %collective-permute-start.17 = (bf16[1024,256]{1,0:T(8,128)(2,1)S(1)}, bf16[1024,256]{1,0:T(8,128)(2,1)S(1)}, u32[]{:S(2)}, u32[]{:S(2)}) collective-permute-start(bf16[1024,256]{1,0:T(8,128)(2,1)S(1)} %collective-permute-done.15.far_ref.refs_4_), channel_id=1, source_target_pairs={{0,1},{1,0},{2,3},{3,2},{4,5},{5,4},{6,7},{7,6},{8,9},{9,8},{10,11... | collective-permute-start | bytes 1572872 | tf_op jit(solution)/shard_map/ppermute | solution.py:275
  101.7 3.1 %weight_terms.1 = bf16[1024,1024]{1,0:T(8,128)(2,1)} custom-call(bf16[128,1024]{1,0:T(8,128)(2,1)S(1)} %get-tuple-element.49.own_ref, bf16[128,1024]{1,0:T(8,128)(2,1)S(1)} %collective-permute-done.13.peer_ref, bf16[256,1024]{1,0:T(8,128)(2,1)} %up.1.refs_8_.up_ref), custom_call_target="tpu_custom_call" | custom-call | flops 536870912 | bytes 4194304 | tf_op jit(solution)/shard_map/weight_terms/pallas_call | solution.py:360
  104.8 7.0 %all-to-all-start.3 = ((bf16[16,64,1024]{2,1,0:T(8,128)(2,1)}), bf16[16,64,1024]{2,1,0:T(8,128)(2,1)}, u32[]{:S(2)}, u32[]{:S(2)}) async-start(bf16[16,64,1024]{2,1,0:T(8,128)(2,1)} %bitcast.50), calls=%async_computation.3 | async-start | bytes 4194304 | tf_op jit(solution)/shard_map/all_to_all | solution.py:288
  111.8 10.1 %query_grad.1 = bf16[1024,128]{1,0:T(8,128)(2,1)S(1)} custom-call(bf16[1024,256]{1,0:T(8,128)(2,1)} %get-tuple-element.53.refs_0_.pair_ref.refs_2_, bf16[1024,128]{1,0:T(8,128)(2,1)} %get-tuple-element.51.g_ref.refs_6_, f32[1,1024]{1,0:T(1,128)S(1)} %get-tuple-element.52.lse_ref, bf16[1024,256]{1,0:T(8,128)(2,1)S(1)} %collective-permute-done.15.far_ref.refs_4_, ...), custom_call_target="tpu_custom_call" | custom-call | flops 6442450944 | bytes 4194304 | tf_op jit(solution)/shard_map/query_grad/pallas_call | solution.py:183
  121.9 0.5 convolution_convert_fusion.1
  122.4 1.1 collective-permute-start.20
  124.0 0.7 pad_maximum_fusion.2
  124.8 11.9 %key_grad.1 = (bf16[1024,128]{1,0:T(8,128)(2,1)S(1)}, bf16[1024,128]{1,0:T(8,128)(2,1)S(1)}) custom-call(bf16[1024,256]{1,0:T(8,128)(2,1)} %get-tuple-element.35.refs_1_.kv0.refs_0_, f32[64,128]{1,0:T(8,128)S(1)} %pad.4.refs_9_.refs_3_.bias_ref.refs_1_, bf16[1024,256]{1,0:T(8,128)(2,1)S(1)} %copy-done.1, ...), custom_call_target="tpu_custom_call" | custom-call | flops 8589934592 | bytes 4194304 | tf_op jit(solution)/shard_map/key_grad/pallas_call | solution.py:245
  136.8 1.0 pad_maximum_fusion
  137.8 4.2 %all-to-all-done.3 = bf16[16,64,1024]{2,1,0:T(8,128)(2,1)} async-done(((bf16[16,64,1024]{2,1,0:T(8,128)(2,1)}), bf16[16,64,1024]{2,1,0:T(8,128)(2,1)}, u32[]{:S(2)}, u32[]{:S(2)}) %all-to-all-start.3) | async-done | bytes 2097184 | tf_op jit(solution)/shard_map/all_to_all | solution.py:288
  142.0 4.4 %all-to-all-start.2 = ((bf16[16,64,384]{2,1,0:T(8,128)(2,1)}), bf16[16,64,384]{2,1,0:T(8,128)(2,1)S(1)}, u32[]{:S(2)}, u32[]{:S(2)}) async-start(bf16[16,64,384]{2,1,0:T(8,128)(2,1)} %pad_maximum_fusion), calls=%async_computation.2 | async-start | bytes 1572864 | tf_op jit(solution)/shard_map/all_to_all | solution.py:288
  146.4 1.0 broadcast_select_fusion.3
  147.5 2.0 %convert_reduce_fusion = f32[64,1024]{1,0:T(8,128)S(1)} fusion(bf16[16,64,1024]{2,1,0:T(8,128)(2,1)} %all-to-all-done.3), kind=kLoop, calls=%fused_computation | loop fusion | flops 2031616 | bytes 2359296 | tf_op jit(solution)/shard_map/reduce_sum | solution.py:582
  149.5 0.8 collective-permute-start.24
  150.3 0.7 collective-permute-start.23
  151.0 2.5 %collective-permute-start.22 = (f32[16,1024]{1,0:T(8,128)S(1)}, f32[16,1024]{1,0:T(8,128)S(1)}, u32[]{:S(2)}, u32[]{:S(2)}) collective-permute-start(f32[16,1024]{1,0:T(8,128)S(1)} %get-tuple-element.63), channel_id=1, source_target_pairs={{0,2},{2,0},{4,6},{6,4},{1,3},{3,1},{5,7},{7,5},{8,10},{10,8},{12,... | collective-permute-start | bytes 196616 | tf_op jit(solution)/shard_map/ppermute | solution.py:587
  153.5 5.6 %all-to-all-done.2.refs_2_ = bf16[16,64,384]{2,1,0:T(8,128)(2,1)S(1)} async-done(((bf16[16,64,384]{2,1,0:T(8,128)(2,1)}), bf16[16,64,384]{2,1,0:T(8,128)(2,1)S(1)}, u32[]{:S(2)}, u32[]{:S(2)}) %all-to-all-start.2) | async-done | bytes 786464 | tf_op jit(solution)/shard_map/all_to_all | solution.py:288
  159.2 2.7 %collective-permute-start.21 = (bf16[8,64,384]{2,1,0:T(8,128)(2,1)S(1)}, bf16[8,64,384]{2,1,0:T(8,128)(2,1)S(1)}, u32[]{:S(2)}, u32[]{:S(2)}) collective-permute-start(bf16[8,64,384]{2,1,0:T(8,128)(2,1)S(1)} %constant_dynamic-slice_fusion), channel_id=1, source_target_pairs={{0,1},{1,0},{2,3},{3,2},{4,5},{5,4},{6,7},{7,6},{8,9},{9,8},{10,11... | collective-permute-start | bytes 1179656 | tf_op jit(solution)/shard_map/ppermute | solution.py:275
  162.0 0.8 maximum_bitcast_fusion
  163.2 1.1 final.1
  164.3 0.6 pad_maximum_fusion.4
  (64 shorter events, 4.5 us)
Async XLA Ops:
  0.6 12.5 %copy-start.2 = (bf16[8,2048]{1,0:T(8,128)(2,1)S(1)}, bf16[8,2048]{1,0:T(8,128)(2,1)}, u32[]{:S(2)}) copy-start(bf16[8,2048]{1,0:T(8,128)(2,1)} %refs_4_.1) | copy-start | bytes 98308
  0.6 12.4 %collective-permute-start.1 = (bf16[8,2048]{1,0:T(8,128)(2,1)}, bf16[8,2048]{1,0:T(8,128)(2,1)S(1)}, u32[]{:S(2)}, u32[]{:S(2)}) collective-permute-start(bf16[8,2048]{1,0:T(8,128)(2,1)} %refs_4_.1), channel_id=1, source_target_pairs={{0,1},{1,0},{2,3},{3,2},{4,5},{5,4},{6,7},{7,6},{8,9},{9,8},{10,11... | collective-permute-start | bytes 98312 | tf_op jit(solution)/shard_map/ppermute | solution.py:275
  2.1 7.5 %collective-permute-start.2 = (bf16[8,2048]{1,0:T(8,128)(2,1)}, bf16[8,2048]{1,0:T(8,128)(2,1)S(1)}, u32[]{:S(2)}, u32[]{:S(2)}) collective-permute-start(bf16[8,2048]{1,0:T(8,128)(2,1)} %refs_4_.1), channel_id=1, source_target_pairs={{0,2},{2,0},{1,3},{3,1},{4,6},{6,4},{5,7},{7,5},{8,10},{10,8},{9,1... | collective-permute-start | bytes 98312 | tf_op jit(solution)/shard_map/ppermute | solution.py:493
  7.1 5.9 %collective-permute-start = (bf16[8,64,384]{2,1,0:T(8,128)(2,1)}, bf16[8,64,384]{2,1,0:T(8,128)(2,1)S(1)}, u32[]{:S(2)}, u32[]{:S(2)}) collective-permute-start(bf16[8,64,384]{2,1,0:T(8,128)(2,1)} %get-tuple-element.33), channel_id=1, source_target_pairs={{0,1},{1,0},{2,3},{3,2},{4,5},{5,4},{6,7},{7,6},{8,9},{9,8},{10,11... | collective-permute-start | bytes 1179656 | tf_op jit(solution)/shard_map/ppermute | solution.py:275
  8.6 2.6 %collective-permute-start.4 = (bf16[128,1024]{1,0:T(8,128)(2,1)S(1)}, bf16[128,1024]{1,0:T(8,128)(2,1)S(1)}, u32[]{:S(2)}, u32[]{:S(2)}) collective-permute-start(bf16[128,1024]{1,0:T(8,128)(2,1)S(1)} %slice_select_fusion), channel_id=1, source_target_pairs={{0,1},{1,0},{2,3},{3,2},{4,5},{5,4},{6,7},{7,6},{8,9},{9,8},{10,11... | collective-permute-start | bytes 786440 | tf_op jit(solution)/shard_map/ppermute | solution.py:275
  9.6 3.4 %collective-permute-start.3 = (bf16[8,2048]{1,0:T(8,128)(2,1)S(1)}, bf16[8,2048]{1,0:T(8,128)(2,1)S(1)}, u32[]{:S(2)}, u32[]{:S(2)}) collective-permute-start(bf16[8,2048]{1,0:T(8,128)(2,1)S(1)} %collective-permute-done.2.refs_6_), channel_id=1, source_target_pairs={{0,1},{1,0},{2,3},{3,2},{4,5},{5,4},{6,7},{7,6},{8,9},{9,8},{10,11... | collective-permute-start | bytes 98312 | tf_op jit(solution)/shard_map/ppermute | solution.py:275
  48.5 3.0 %collective-permute-start.6 = (bf16[1024,256]{1,0:T(8,128)(2,1)}, bf16[1024,256]{1,0:T(8,128)(2,1)S(1)}, u32[]{:S(2)}, u32[]{:S(2)}) collective-permute-start(bf16[1024,256]{1,0:T(8,128)(2,1)} %get-tuple-element.35.refs_1_.kv0.refs_0_), channel_id=1, source_target_pairs={{0,1},{1,0},{2,3},{3,2},{4,5},{5,4},{6,7},{7,6},{8,9},{9,8},{10,11... | collective-permute-start | bytes 1572872 | tf_op jit(solution)/shard_map/ppermute | solution.py:275
  49.8 13.8 %collective-permute-start.5 = (bf16[1024,256]{1,0:T(8,128)(2,1)}, bf16[1024,256]{1,0:T(8,128)(2,1)S(1)}, u32[]{:S(2)}, u32[]{:S(2)}) collective-permute-start(bf16[1024,256]{1,0:T(8,128)(2,1)} %get-tuple-element.35.refs_1_.kv0.refs_0_), channel_id=1, source_target_pairs={{0,4},{4,0},{1,5},{5,1},{2,6},{6,2},{3,7},{7,3},{8,12},{12,8},{9,1... | collective-permute-start | bytes 1572872 | tf_op jit(solution)/shard_map/ppermute | solution.py:279
  50.1 23.3 %collective-permute-start.8 = (bf16[12,64,512]{2,1,0:T(8,128)(2,1)}, bf16[12,64,512]{2,1,0:T(8,128)(2,1)S(1)}, u32[]{:S(2)}, u32[]{:S(2)}) collective-permute-start(bf16[12,64,512]{2,1,0:T(8,128)(2,1)} %get-tuple-element.44.own0), channel_id=1, source_target_pairs={{0,6},{2,4},{4,2},{6,0},{1,7},{3,5},{5,3},{7,1},{8,14},{10,12},{12... | collective-permute-start | bytes 2359304 | tf_op jit(solution)/shard_map/ppermute | solution.py:316
  51.5 6.6 %copy-start.3 = (bf16[1024,256]{1,0:T(8,128)(2,1)}, bf16[1024,256]{1,0:T(8,128)(2,1)S(1)}, u32[]{:S(2)}) copy-start(bf16[1024,256]{1,0:T(8,128)(2,1)S(1)} %collective-permute-done.6.refs_2_.kv1) | copy-start | bytes 1572868
  51.5 12.8 %copy-start.8 = (bf16[4,64,512]{2,1,0:T(8,128)(2,1)S(1)}, bf16[4,64,512]{2,1,0:T(8,128)(2,1)}, u32[]{:S(2)}) copy-start(bf16[4,64,512]{2,1,0:T(8,128)(2,1)} %get-tuple-element.45.own1) | copy-start | bytes 786436
  63.5 9.8 %copy-start.4 = (bf16[1024,256]{1,0:T(8,128)(2,1)}, bf16[1024,256]{1,0:T(8,128)(2,1)S(1)}, u32[]{:S(2)}) copy-start(bf16[1024,256]{1,0:T(8,128)(2,1)S(1)} %collective-permute-done.5.refs_1_.kv2) | copy-start | bytes 1572868
  63.5 2.3 %collective-permute-start.7 = (bf16[1024,256]{1,0:T(8,128)(2,1)S(1)}, bf16[1024,256]{1,0:T(8,128)(2,1)S(1)}, u32[]{:S(2)}, u32[]{:S(2)}) collective-permute-start(bf16[1024,256]{1,0:T(8,128)(2,1)S(1)} %collective-permute-done.5.refs_1_.kv2), channel_id=1, source_target_pairs={{0,1},{1,0},{2,3},{3,2},{4,5},{5,4},{6,7},{7,6},{8,9},{9,8},{10,11... | collective-permute-start | bytes 1572872 | tf_op jit(solution)/shard_map/ppermute | solution.py:275
  64.3 9.0 %collective-permute-start.9 = (bf16[4,64,512]{2,1,0:T(8,128)(2,1)S(1)}, bf16[4,64,512]{2,1,0:T(8,128)(2,1)S(1)}, u32[]{:S(2)}, u32[]{:S(2)}) collective-permute-start(bf16[4,64,512]{2,1,0:T(8,128)(2,1)S(1)} %copy-done.8), channel_id=1, source_target_pairs={{0,4},{4,0},{1,5},{5,1},{2,6},{6,2},{3,7},{7,3},{8,12},{12,8},{9,1... | collective-permute-start | bytes 786440 | tf_op jit(solution)/shard_map/ppermute | solution.py:279
  65.9 7.5 %copy-start.5 = (bf16[1024,256]{1,0:T(8,128)(2,1)}, bf16[1024,256]{1,0:T(8,128)(2,1)S(1)}, u32[]{:S(2)}) copy-start(bf16[1024,256]{1,0:T(8,128)(2,1)S(1)} %collective-permute-done.7.refs_2_.kv3) | copy-start | bytes 1572868
  76.9 10.1 %copy-start = (bf16[1024,256]{1,0:T(8,128)(2,1)S(1)}, bf16[1024,256]{1,0:T(8,128)(2,1)}, u32[]{:S(2)}) copy-start(bf16[1024,256]{1,0:T(8,128)(2,1)} %get-tuple-element.53.refs_0_.pair_ref.refs_2_) | copy-start | bytes 1572868
  76.9 1.9 %collective-permute-start.10 = (f32[128,1024]{1,0:T(8,128)S(1)}, f32[128,1024]{1,0:T(8,128)S(1)}, u32[]{:S(2)}, u32[]{:S(2)}) collective-permute-start(f32[128,1024]{1,0:T(8,128)S(1)} %get-tuple-element.47), channel_id=1, source_target_pairs={{0,1},{1,0},{2,3},{3,2},{4,5},{5,4},{6,7},{7,6},{8,9},{9,8},{10,11... | collective-permute-start | bytes 1572872 | tf_op jit(solution)/shard_map/ppermute | solution.py:275
  77.3 7.1 %collective-permute-start.11 = (f32[1,1024]{1,0:T(1,128)S(1)}, f32[1,1024]{1,0:T(1,128)S(1)}, u32[]{:S(2)}, u32[]{:S(2)}) collective-permute-start(f32[1,1024]{1,0:T(1,128)S(1)} %get-tuple-element.52.lse_ref), channel_id=1, source_target_pairs={{0,1},{1,0},{2,3},{3,2},{4,5},{5,4},{6,7},{7,6},{8,9},{9,8},{10,11... | collective-permute-start | bytes 12296 | tf_op jit(solution)/shard_map/ppermute | solution.py:275
  80.7 14.5 %all-to-all-start.1 = ((bf16[16,64,256]{2,1,0:T(8,128)(2,1)}), bf16[16,64,256]{2,1,0:T(8,128)(2,1)S(1)}, u32[]{:S(2)}, u32[]{:S(2)}) async-start(bf16[16,64,256]{2,1,0:T(8,128)(2,1)} %cross.1), calls=%async_computation.1 | async-start | bytes 1048576 | tf_op jit(solution)/shard_map/all_to_all | solution.py:288
  84.4 2.6 %collective-permute-start.12 = (f32[2,1024]{1,0:T(2,128)S(1)}, f32[2,1024]{1,0:T(2,128)S(1)}, u32[]{:S(2)}, u32[]{:S(2)}) collective-permute-start(f32[2,1024]{1,0:T(2,128)S(1)} %pad_maximum_fusion.6), channel_id=1, source_target_pairs={{0,4},{4,0},{1,5},{5,1},{2,6},{6,2},{3,7},{7,3},{8,12},{12,8},{9,1... | collective-permute-start | bytes 24584 | tf_op jit(solution)/shard_map/ppermute | solution.py:279
  87.0 12.0 %collective-permute-start.15 = (bf16[1024,256]{1,0:T(8,128)(2,1)S(1)}, bf16[1024,256]{1,0:T(8,128)(2,1)S(1)}, u32[]{:S(2)}, u32[]{:S(2)}) collective-permute-start(bf16[1024,256]{1,0:T(8,128)(2,1)S(1)} %copy-done), channel_id=1, source_target_pairs={{0,4},{4,0},{1,5},{5,1},{2,6},{6,2},{3,7},{7,3},{8,12},{12,8},{9,1... | collective-permute-start | bytes 1572872 | tf_op jit(solution)/shard_map/ppermute | solution.py:279
  96.1 5.6 %collective-permute-start.13 = (bf16[128,1024]{1,0:T(8,128)(2,1)S(1)}, bf16[128,1024]{1,0:T(8,128)(2,1)S(1)}, u32[]{:S(2)}, u32[]{:S(2)}) collective-permute-start(bf16[128,1024]{1,0:T(8,128)(2,1)S(1)} %get-tuple-element.49.own_ref), channel_id=1, source_target_pairs={{0,1},{1,0},{2,3},{3,2},{4,5},{5,4},{6,7},{7,6},{8,9},{9,8},{10,11... | collective-permute-start | bytes 786440 | tf_op jit(solution)/shard_map/ppermute | solution.py:275
  97.6 27.2 %collective-permute-start.16 = (bf16[1024,256]{1,0:T(8,128)(2,1)S(1)}, bf16[1024,256]{1,0:T(8,128)(2,1)S(1)}, u32[]{:S(2)}, u32[]{:S(2)}) collective-permute-start(bf16[1024,256]{1,0:T(8,128)(2,1)S(1)} %copy-done), channel_id=1, source_target_pairs={{0,1},{1,0},{2,3},{3,2},{4,5},{5,4},{6,7},{7,6},{8,9},{9,8},{10,11... | collective-permute-start | bytes 1572872 | tf_op jit(solution)/shard_map/ppermute | solution.py:275
  98.9 25.9 %collective-permute-start.17 = (bf16[1024,256]{1,0:T(8,128)(2,1)S(1)}, bf16[1024,256]{1,0:T(8,128)(2,1)S(1)}, u32[]{:S(2)}, u32[]{:S(2)}) collective-permute-start(bf16[1024,256]{1,0:T(8,128)(2,1)S(1)} %collective-permute-done.15.far_ref.refs_4_), channel_id=1, source_target_pairs={{0,1},{1,0},{2,3},{3,2},{4,5},{5,4},{6,7},{7,6},{8,9},{9,8},{10,11... | collective-permute-start | bytes 1572872 | tf_op jit(solution)/shard_map/ppermute | solution.py:275
  101.4 23.4 %collective-permute-start.18 = (bf16[1024,128]{1,0:T(8,128)(2,1)}, bf16[1024,128]{1,0:T(8,128)(2,1)S(1)}, u32[]{:S(2)}, u32[]{:S(2)}) collective-permute-start(bf16[1024,128]{1,0:T(8,128)(2,1)} %get-tuple-element.51.g_ref.refs_6_), channel_id=1, source_target_pairs={{0,1},{1,0},{2,3},{3,2},{4,5},{5,4},{6,7},{7,6},{8,9},{9,8},{10,11... | collective-permute-start | bytes 786440 | tf_op jit(solution)/shard_map/ppermute | solution.py:275
  101.4 21.0 %collective-permute-start.19 = (bf16[1024,128]{1,0:T(8,128)(2,1)}, bf16[1024,128]{1,0:T(8,128)(2,1)S(1)}, u32[]{:S(2)}, u32[]{:S(2)}) collective-permute-start(bf16[1024,128]{1,0:T(8,128)(2,1)} %get-tuple-element.51.g_ref.refs_6_), channel_id=1, source_target_pairs={{0,4},{4,0},{1,5},{5,1},{2,6},{6,2},{3,7},{7,3},{8,12},{12,8},{9,1... | collective-permute-start | bytes 786440 | tf_op jit(solution)/shard_map/ppermute | solution.py:279
  104.8 37.2 %all-to-all-start.3 = ((bf16[16,64,1024]{2,1,0:T(8,128)(2,1)}), bf16[16,64,1024]{2,1,0:T(8,128)(2,1)}, u32[]{:S(2)}, u32[]{:S(2)}) async-start(bf16[16,64,1024]{2,1,0:T(8,128)(2,1)} %bitcast.50), calls=%async_computation.3 | async-start | bytes 4194304 | tf_op jit(solution)/shard_map/all_to_all | solution.py:288
  111.8 10.1 %copy-start.7 = (bf16[1024,1024]{1,0:T(8,128)(2,1)S(1)}, bf16[1024,1024]{1,0:T(8,128)(2,1)}, u32[]{:S(2)}) copy-start(bf16[1024,1024]{1,0:T(8,128)(2,1)} %get-tuple-element.50) | copy-start | bytes 6291460
  122.4 2.5 %copy-start.1 = (bf16[1024,256]{1,0:T(8,128)(2,1)S(1)}, bf16[1024,256]{1,0:T(8,128)(2,1)}, u32[]{:S(2)}) copy-start(bf16[1024,256]{1,0:T(8,128)(2,1)} %get-tuple-element.53.refs_0_.pair_ref.refs_2_) | copy-start | bytes 1572868
  122.4 2.5 %copy-start.6 = (bf16[1024,128]{1,0:T(8,128)(2,1)S(1)}, bf16[1024,128]{1,0:T(8,128)(2,1)}, u32[]{:S(2)}) copy-start(bf16[1024,128]{1,0:T(8,128)(2,1)} %get-tuple-element.51.g_ref.refs_6_) | copy-start | bytes 786436
  122.4 2.4 %collective-permute-start.20 = (bf16[1024,128]{1,0:T(8,128)(2,1)S(1)}, bf16[1024,128]{1,0:T(8,128)(2,1)S(1)}, u32[]{:S(2)}, u32[]{:S(2)}) collective-permute-start(bf16[1024,128]{1,0:T(8,128)(2,1)S(1)} %collective-permute-done.19.refs_8_), channel_id=1, source_target_pairs={{0,1},{1,0},{2,3},{3,2},{4,5},{5,4},{6,7},{7,6},{8,9},{9,8},{10,11... | collective-permute-start | bytes 786440 | tf_op jit(solution)/shard_map/ppermute | solution.py:275
  124.8 21.7 %collective-permute-start.14 = (bf16[2,64,1024]{2,1,0:T(8,128)(2,1)}, bf16[2,64,1024]{2,1,0:T(8,128)(2,1)}, u32[]{:S(2)}, u32[]{:S(2)}) collective-permute-start(bf16[2,64,1024]{2,1,0:T(8,128)(2,1)} %pad_maximum_fusion.2), channel_id=1, source_target_pairs={{0,1},{1,0},{2,3},{3,2},{4,5},{5,4},{6,7},{7,6},{8,9},{9,8},{10,11... | collective-permute-start | bytes 786440 | tf_op jit(solution)/shard_map/ppermute | solution.py:275
  142.0 17.1 %all-to-all-start.2 = ((bf16[16,64,384]{2,1,0:T(8,128)(2,1)}), bf16[16,64,384]{2,1,0:T(8,128)(2,1)S(1)}, u32[]{:S(2)}, u32[]{:S(2)}) async-start(bf16[16,64,384]{2,1,0:T(8,128)(2,1)} %pad_maximum_fusion), calls=%async_computation.2 | async-start | bytes 1572864 | tf_op jit(solution)/shard_map/all_to_all | solution.py:288
  149.5 12.3 %collective-permute-start.24 = (f32[16,1024]{1,0:T(8,128)S(1)}, f32[16,1024]{1,0:T(8,128)S(1)}, u32[]{:S(2)}, u32[]{:S(2)}) collective-permute-start(f32[16,1024]{1,0:T(8,128)S(1)} %get-tuple-element.64), channel_id=1, source_target_pairs={{0,6},{2,4},{4,2},{6,0},{1,7},{3,5},{5,3},{7,1},{8,14},{10,12},{12... | collective-permute-start | bytes 196616 | tf_op jit(solution)/shard_map/ppermute | solution.py:587
  150.3 11.5 %collective-permute-start.23 = (f32[16,1024]{1,0:T(8,128)S(1)}, f32[16,1024]{1,0:T(8,128)S(1)}, u32[]{:S(2)}, u32[]{:S(2)}) collective-permute-start(f32[16,1024]{1,0:T(8,128)S(1)} %get-tuple-element.65), channel_id=1, source_target_pairs={{0,4},{2,6},{4,0},{6,2},{1,5},{3,7},{5,1},{7,3},{8,12},{10,14},{12... | collective-permute-start | bytes 196616 | tf_op jit(solution)/shard_map/ppermute | solution.py:587
  151.0 10.8 %collective-permute-start.22 = (f32[16,1024]{1,0:T(8,128)S(1)}, f32[16,1024]{1,0:T(8,128)S(1)}, u32[]{:S(2)}, u32[]{:S(2)}) collective-permute-start(f32[16,1024]{1,0:T(8,128)S(1)} %get-tuple-element.63), channel_id=1, source_target_pairs={{0,2},{2,0},{4,6},{6,4},{1,3},{3,1},{5,7},{7,5},{8,10},{10,8},{12,... | collective-permute-start | bytes 196616 | tf_op jit(solution)/shard_map/ppermute | solution.py:587
  159.2 4.0 %collective-permute-start.21 = (bf16[8,64,384]{2,1,0:T(8,128)(2,1)S(1)}, bf16[8,64,384]{2,1,0:T(8,128)(2,1)S(1)}, u32[]{:S(2)}, u32[]{:S(2)}) collective-permute-start(bf16[8,64,384]{2,1,0:T(8,128)(2,1)S(1)} %constant_dynamic-slice_fusion), channel_id=1, source_target_pairs={{0,1},{1,0},{2,3},{3,2},{4,5},{5,4},{6,7},{7,6},{8,9},{9,8},{10,11... | collective-permute-start | bytes 1179656 | tf_op jit(solution)/shard_map/ppermute | solution.py:275
  161.9 2.4 %collective-permute-start.25 = (f32[8,1024]{1,0:T(8,128)S(1)}, f32[8,1024]{1,0:T(8,128)S(1)}, u32[]{:S(2)}, u32[]{:S(2)}) collective-permute-start(f32[8,1024]{1,0:T(8,128)S(1)} %dynamic-slice_bitcast_fusion.3), channel_id=1, source_target_pairs={{0,1},{1,0},{2,3},{3,2},{4,5},{5,4},{6,7},{7,6},{8,9},{9,8},{10,11... | collective-permute-start | bytes 98312 | tf_op jit(solution)/shard_map/ppermute | solution.py:275

commit v9 on v8

--- a/solution.py
+++ b/solution.py
@@ -477,19 +477,6 @@
     core_1, xl_1, xh_1, half_1 = (x.reshape(1) for x in (core, xl, xh, half))
     cols = output_weight.shape[1] // 2
 
-    bias = span_bias(span_order, block_mask, xl, core)
-    wide = upstream[0]
-    up_sent = jnp.where(first_core, wide[:, cols:], wide[:, :cols])
-    (up,) = move(
-        up_body,
-        "up",
-        [(4 * SPAN, cols)],
-        [core_1, half_1],
-        in_hbm(wide),
-        other_core(up_sent),
-        space=pltpu.HBM,
-    )
-
     weight_far = lax.ppermute(output_weight, "xh", SWAP)
     weight_rows = [output_weight, other_core(output_weight), weight_far, other_core(weight_far)]
     unit_rows = (HEADS, SPAN, 3 * HEAD)
@@ -511,7 +498,6 @@
         in_hbm(own),
         other_core(sent),
         *weight_rows,
-        after=(in_hbm(up), bias),
     )
     blocks = exchange(blocks, ZY)
     q, own_kv, *weight_own = move(
@@ -525,6 +511,20 @@
     far_kv = other_chip(own_kv)
     weight_other = [across(weight_own[0]), other_chip(weight_own[1])]
     near_kv = other_core(own_kv)
+    own_kv, span_order, wide = lax.optimization_barrier((own_kv, span_order, upstream[0]))
+    bias = span_bias(span_order, block_mask, xl, core)
+
+    up_sent = jnp.where(first_core, wide[:, cols:], wide[:, :cols])
+    (up,) = move(
+        up_body,
+        "up",
+        [(4 * SPAN, cols)],
+        [core_1, half_1],
+        in_hbm(wide),
+        other_core(up_sent),
+        space=pltpu.HBM,
+    )
+
     out, top, total = forward(True, in_hbm(q), (in_hbm(own_kv), near_kv), bias)
     far_kv, total = lax.optimization_barrier((far_kv, total))
     kvs = (own_kv, near_kv, far_kv, other_core(far_kv))
@@ -547,7 +547,7 @@
     )
     crossed = exchange(crossing, ZY)
     pair_sent, lses = lax.optimization_barrier((pair, lses))
-    pairs = everyone(pair_sent)
+    pair_far = other_chip(pair_sent)
 
     att_own, g = move(
         land_body,
@@ -562,6 +562,8 @@
     att_peer = other_core(att_own)
     term = weight_terms(att_own, att_peer, in_hbm(up)).reshape(UNITS, SPAN, cols)
     term = exchange(term, ZY)
+    att_peer, pair_far = lax.optimization_barrier((att_peer, pair_far))
+    pairs = (pair_sent, other_core(pair_sent), pair_far, other_core(pair_far))
 
     query_out = query_grad(in_hbm(pair), in_hbm(g), lse, pairs[2], [in_hbm(x) for x in kvs], bias)
     key_out, value_out = key_grad(in_hbm(own_kv), bias, pairs, gs, lses)

time: 166 us -> 168 us (1.012)
  starting transfers between devices: 37.1 us -> 47.8 us
  waiting for transfers between devices: 30.6 us -> 22.3 us
  other arithmetic: 8.26 us -> 4.93 us
  matrix products: 1.97 us -> 4.39 us
    all_to_all x3, waiting for transfers between devices: 17.8 us -> 11.7 us  [exchange(): return lax.all_to_all(x, axes, 0, 0, tiled=True)]
    ppermute x5, starting transfers between devices: 1.71 us -> 6.36 us  [other_chip(): return lax.ppermute(x, 'xl', SWAP)]
    ppermute x5, waiting for transfers between devices: 8.99 us -> 5.17 us  [other_chip(): return lax.ppermute(x, 'xl', SWAP)]
    dot_general x2, matrix products: 0.9 us -> 4.07 us  [dot(): return lax.dot_general(a, b, dims, preferred_element_type=F32)]
    ppermute x16, starting transfers between devices: 13 us -> 15.9 us  [other_core(): return lax.ppermute(x, 'core', SWAP)]
    all_to_all x3, starting transfers between devices: 14.9 us -> 17 us  [exchange(): return lax.all_to_all(x, axes, 0, 0, tiled=True)]
  transfers between devices with their start and end apart: 29 -> 29, of which waited for: 10 -> 10; matrix products, arithmetic and copies ran while one was open for 6% -> 5% of each run, Pallas kernels for 29% -> 26%
where the time goes in v9:
time: 168 us; the launch traced here: 167 us
  Pallas kernels  52.9 us (31%)
  starting transfers between devices  47.8 us (28%)
  blocking collectives  32.7 us (19%)
  waiting for transfers between devices  22.3 us (13%)
  other arithmetic  4.93 us (3%)
  matrix products  4.39 us (3%)
    all_to_all x1, blocking collectives, exchange(): return lax.all_to_all(x, axes, 0, 0, tiled=True)  32.7 us
    all_to_all x3, starting transfers between devices, exchange(): return lax.all_to_all(x, axes, 0, 0, tiled=True)  17 us
    ppermute x16, starting transfers between devices, other_core(): return lax.ppermute(x, 'core', SWAP)  15.9 us
    pallas_call x2, Pallas kernels, forward(): pl.pallas_call(functools.partial(forward_body, first), out_shape=outs, gr...  14.1 us
    pallas_call x1, Pallas kernels, key_grad(): pl.pallas_call(key_body, out_shape=[jax.ShapeDtypeStruct((ROWS, HEAD), BF...  11.9 us
    all_to_all x3, waiting for transfers between devices, exchange(): return lax.all_to_all(x, axes, 0, 0, tiled=True)  11.7 us
    pallas_call x7, Pallas kernels, move(): pl.pallas_call(run, out_shape=[make(shape, BF16) for make, shape in zip(s...  10.4 us
    pallas_call x1, Pallas kernels, query_grad(): pl.pallas_call(query_body, out_shape=jax.ShapeDtypeStruct((ROWS, HEAD), B...  9.92 us
  transfers between devices with their start and end apart: 29, of which 10 were waited for; matrix products, arithmetic and copies ran while one was open for 5% of the time, Pallas kernels for 26%

profile of v9, /device:TPU:1, one launch (start us, length us, event | category | flops | bytes accessed | tf_op | source)
XLA Modules:
  0.0 167.0 jit_solution(3146321097106528659)
XLA Ops:
  0.6 2.1 %cut.1 = (bf16[8,64,384]{2,1,0:T(8,128)(2,1)}, bf16[8,64,384]{2,1,0:T(8,128)(2,1)}) custom-call(s32[1]{0:T(128)} %bitcast.2.refs_0_.refs_1_, bf16[128,1024]{1,0:T(8,128)(2,1)} %bitcast.59, bf16[128,1024]{1,0:T(8,128)(2,1)} %bitcast.60, bf16[128,1024]{1,0:T(8,128)(2,1)} %bitcast.61), custom_call_target="tpu_custom_call" | custom-call | bytes 4194304 | tf_op jit(solution)/shard_map/cut/pallas_call | solution.py:384
  2.8 1.4 collective-permute-start
  4.2 2.8 %collective-permute-start.2 = (bf16[8,2048]{1,0:T(8,128)(2,1)}, bf16[8,2048]{1,0:T(8,128)(2,1)S(1)}, u32[]{:S(2)}, u32[]{:S(2)}) collective-permute-start(bf16[8,2048]{1,0:T(8,128)(2,1)} %refs_4_.1), channel_id=1, source_target_pairs={{0,2},{2,0},{1,3},{3,1},{4,6},{6,4},{5,7},{7,5},{8,10},{10,8},{9,1... | collective-permute-start | bytes 98312 | tf_op jit(solution)/shard_map/ppermute | solution.py:480
  7.3 1.4 collective-permute-done.2.refs_6_
  8.7 1.2 collective-permute-start.3
  9.8 0.9 collective-permute-done.3.refs_7_
  10.7 0.8 copy-done.2
  11.4 1.2 fill.1
  12.6 32.7 %all_to_all.20.refs_0_ = bf16[16,64,896]{2,1,0:T(8,128)(2,1)S(1)} all-to-all(bf16[16,64,896]{2,1,0:T(8,128)(2,1)S(1)} %fill.1), channel_id=1, replica_groups=mesh['z'=4,'y'=4,'xl'=2,'xh'=2,'core'=2] {'z','y'}, dimensions={0} | all-to-all | bytes 3670016 | tf_op jit(solution)/shard_map/all_to_all | solution.py:288
  45.4 1.4 split.1
  46.8 1.5 collective-permute-start.5
  48.2 1.3 collective-permute-start.4
  49.5 1.8 %collective-permute-start.7 = (bf16[12,64,512]{2,1,0:T(8,128)(2,1)}, bf16[12,64,512]{2,1,0:T(8,128)(2,1)S(1)}, u32[]{:S(2)}, u32[]{:S(2)}) collective-permute-start(bf16[12,64,512]{2,1,0:T(8,128)(2,1)} %get-tuple-element.51.own0), channel_id=1, source_target_pairs={{0,6},{2,4},{4,2},{6,0},{1,7},{3,5},{5,3},{7,1},{8,14},{10,12},{12... | collective-permute-start | bytes 2359304 | tf_op jit(solution)/shard_map/ppermute | solution.py:316
  51.9 6.6 %forward_near.1 = (f32[128,1024]{1,0:T(8,128)}, f32[1,1024]{1,0:T(1,128)S(1)}, f32[1,1024]{1,0:T(1,128)S(1)}) custom-call(bf16[1024,128]{1,0:T(8,128)(2,1)} %get-tuple-element.39.refs_0_, bf16[1024,256]{1,0:T(8,128)(2,1)} %get-tuple-element.41.refs_1_.kv0.refs_0_, bf16[1024,256]{1,0:T(8,128)(2,1)S(1)} %collective-permute-done.5.refs_2_.kv1, ...), custom_call_target="tpu_custom_call" | custom-call | flops 2147483648 | bytes 4194304 | tf_op jit(solution)/shard_map/forward_near/pallas_call | solution.py:132
  58.5 3.6 %collective-permute-done.4.refs_1_.kv2 = bf16[1024,256]{1,0:T(8,128)(2,1)S(1)} collective-permute-done((bf16[1024,256]{1,0:T(8,128)(2,1)}, bf16[1024,256]{1,0:T(8,128)(2,1)S(1)}, u32[]{:S(2)}, u32[]{:S(2)}) %collective-permute-start.4) | collective-permute-done | bytes 524320 | tf_op jit(solution)/shard_map/ppermute | solution.py:279
  62.1 0.8 collective-permute-start.6
  63.0 1.3 collective-permute-start.8
  64.8 1.9 %up.1.up_ref = bf16[256,1024]{1,0:T(8,128)(2,1)} custom-call(s32[1]{0:T(128)} %bitcast.refs_0_, s32[1]{0:T(128)} %bitcast.2.refs_0_.refs_1_, bf16[128,2048]{1,0:T(8,128)(2,1)} %bitcast.51, bf16[128,1024]{1,0:T(8,128)(2,1)S(1)} %collective-permute-done.9.refs_3_), custom_call_target="tpu_custom_call" | custom-call | bytes 4194304 | tf_op jit(solution)/shard_map/up/pallas_call | solution.py:384
  66.7 7.5 %forward_far.1 = (bf16[1024,256]{1,0:T(8,128)(2,1)}, f32[1,1024]{1,0:T(1,128)S(1)}) custom-call(bf16[1024,128]{1,0:T(8,128)(2,1)} %get-tuple-element.39.refs_0_, bf16[1024,256]{1,0:T(8,128)(2,1)S(1)} %collective-permute-done.4.refs_1_.kv2, bf16[1024,256]{1,0:T(8,128)(2,1)S(1)} %collective-permute-done.6.refs_2_.kv3, ...), custom_call_target="tpu_custom_call" | custom-call | flops 2147483648 | bytes 4194304 | tf_op jit(solution)/shard_map/forward_far/pallas_call | solution.py:132
  74.2 3.5 %weight_whole.1 = (bf16[1024,1024]{1,0:T(8,128)(2,1)}, f32[128,1024]{1,0:T(8,128)S(1)}, f32[128,1024]{1,0:T(8,128)S(1)}) custom-call(s32[1]{0:T(128)} %bitcast.7.xl_ref, bf16[12,64,512]{2,1,0:T(8,128)(2,1)} %get-tuple-element.51.own0, bf16[4,64,512]{2,1,0:T(8,128)(2,1)} %get-tuple-element.52.own1, bf16[12,64,512]{2,1,0:T(8,128)(2,1)S(1)} %collective-permute-done.7.other0, ...), custom_call_target="tpu_custom_call" | custom-call | flops 536870912 | bytes 4194304 | tf_op jit(solution)/shard_map/weight_whole/pallas_call | solution.py:332
  78.1 1.5 collective-permute-done.10.refs_2_
  79.6 1.9 %cross.1 = bf16[16,64,256]{2,1,0:T(8,128)(2,1)} custom-call(bf16[1024,256]{1,0:T(8,128)(2,1)} %get-tuple-element.59.refs_0_.pair_ref.refs_2_, f32[128,1024]{1,0:T(8,128)S(1)} %get-tuple-element.54.refs_1_, f32[128,1024]{1,0:T(8,128)S(1)} %collective-permute-done.10.refs_2_), custom_call_target="tpu_custom_call" | custom-call | bytes 4194304 | tf_op jit(solution)/shard_map/cross/pallas_call | solution.py:384
  81.6 3.6 %all-to-all-start.1 = ((bf16[16,64,256]{2,1,0:T(8,128)(2,1)}), bf16[16,64,256]{2,1,0:T(8,128)(2,1)S(1)}, u32[]{:S(2)}, u32[]{:S(2)}) async-start(bf16[16,64,256]{2,1,0:T(8,128)(2,1)} %cross.1), calls=%async_computation.1 | async-start | bytes 1048576 | tf_op jit(solution)/shard_map/all_to_all | solution.py:288
  85.6 0.8 collective-permute-done.11
  86.4 1.3 collective-permute-start.12
  87.7 1.6 collective-permute-done.12
  89.3 1.3 collective-permute-start.14
  90.6 1.5 collective-permute-start.16
  92.1 4.0 %all-to-all-done.1.refs_0_ = bf16[16,64,256]{2,1,0:T(8,128)(2,1)S(1)} async-done(((bf16[16,64,256]{2,1,0:T(8,128)(2,1)}), bf16[16,64,256]{2,1,0:T(8,128)(2,1)S(1)}, u32[]{:S(2)}, u32[]{:S(2)}) %all-to-all-start.1) | async-done | bytes 524320 | tf_op jit(solution)/shard_map/all_to_all | solution.py:288
  96.1 0.8 land.1
  96.9 1.5 collective-permute-start.18
  98.4 1.2 collective-permute-start.19
  99.9 2.0 %convolution_convert_fusion.1 = bf16[128,1024]{1,0:T(8,128)(2,1)S(1)} fusion(bf16[128,1024]{1,0:T(8,128)(2,1)S(1)} %get-tuple-element.57.own_ref, bf16[1024,1024]{1,0:T(8,128)(2,1)} %get-tuple-element.58), kind=kOutput, calls=%fused_computation.2 | convolution fusion | flops 268566528 | bytes 2621440 | tf_op jit(solution)/shard_map/dot_general | solution.py:33
  101.9 3.1 %weight_terms.1 = bf16[1024,1024]{1,0:T(8,128)(2,1)} custom-call(bf16[128,1024]{1,0:T(8,128)(2,1)S(1)} %get-tuple-element.57.own_ref, bf16[128,1024]{1,0:T(8,128)(2,1)S(1)} %collective-permute-done.13.peer_ref, bf16[256,1024]{1,0:T(8,128)(2,1)} %up.1.up_ref), custom_call_target="tpu_custom_call" | custom-call | flops 536870912 | bytes 4194304 | tf_op jit(solution)/shard_map/weight_terms/pallas_call | solution.py:360
  105.1 6.5 %all-to-all-start.3 = ((bf16[16,64,1024]{2,1,0:T(8,128)(2,1)}), bf16[16,64,1024]{2,1,0:T(8,128)(2,1)}, u32[]{:S(2)}, u32[]{:S(2)}) async-start(bf16[16,64,1024]{2,1,0:T(8,128)(2,1)} %bitcast.50), calls=%async_computation.3 | async-start | bytes 4194304 | tf_op jit(solution)/shard_map/all_to_all | solution.py:288
  111.6 2.0 %convolution_convert_fusion = bf16[128,1024]{1,0:T(8,128)(2,1)S(1)} fusion(bf16[128,1024]{1,0:T(8,128)(2,1)S(1)} %collective-permute-done.13.peer_ref, bf16[1024,1024]{1,0:T(8,128)(2,1)} %get-tuple-element.58), kind=kOutput, calls=%fused_computation.1 | convolution fusion | flops 268566528 | bytes 2621440 | tf_op jit(solution)/shard_map/dot_general | solution.py:33
  113.8 4.4 %collective-permute-start.15 = (bf16[2,64,1024]{2,1,0:T(8,128)(2,1)S(1)}, bf16[2,64,1024]{2,1,0:T(8,128)(2,1)S(1)}, u32[]{:S(2)}, u32[]{:S(2)}) collective-permute-start(bf16[2,64,1024]{2,1,0:T(8,128)(2,1)S(1)} %pad_maximum_fusion.2), channel_id=1, source_target_pairs={{0,1},{1,0},{2,3},{3,2},{4,5},{5,4},{6,7},{7,6},{8,9},{9,8},{10,11... | collective-permute-start | bytes 786440 | tf_op jit(solution)/shard_map/ppermute | solution.py:275
  118.7 9.9 %query_grad.1 = bf16[1024,128]{1,0:T(8,128)(2,1)S(1)} custom-call(bf16[1024,256]{1,0:T(8,128)(2,1)} %get-tuple-element.59.refs_0_.pair_ref.refs_2_, bf16[1024,128]{1,0:T(8,128)(2,1)} %get-tuple-element.61.g_ref.refs_6_, f32[1,1024]{1,0:T(1,128)S(1)} %get-tuple-element.62.lse_ref, bf16[1024,256]{1,0:T(8,128)(2,1)S(1)} %collective-permute-done.14.far_ref.refs_4_, ...), custom_call_target="tpu_custom_call" | custom-call | flops 6442450944 | bytes 4194304 | tf_op jit(solution)/shard_map/query_grad/pallas_call | solution.py:183
  128.7 11.9 %key_grad.1 = (bf16[1024,128]{1,0:T(8,128)(2,1)S(1)}, bf16[1024,128]{1,0:T(8,128)(2,1)S(1)}) custom-call(bf16[1024,256]{1,0:T(8,128)(2,1)} %get-tuple-element.41.refs_1_.kv0.refs_0_, f32[64,128]{1,0:T(8,128)S(1)} %pad.4.refs_3_.bias_ref.refs_1_, bf16[1024,256]{1,0:T(8,128)(2,1)S(1)} %copy-done.1, bf16[1024,256]{1,0:T(8,128)(2,1)S(1)} %collective-permute-done.16.refs_3_, ...), custom_call_target="tpu_custom_call" | custom-call | flops 8589934592 | bytes 4194304 | tf_op jit(solution)/shard_map/key_grad/pallas_call | solution.py:245
  140.6 1.0 pad_maximum_fusion
  141.7 6.9 %all-to-all-start.2 = ((bf16[16,64,384]{2,1,0:T(8,128)(2,1)}), bf16[16,64,384]{2,1,0:T(8,128)(2,1)S(1)}, u32[]{:S(2)}, u32[]{:S(2)}) async-start(bf16[16,64,384]{2,1,0:T(8,128)(2,1)} %pad_maximum_fusion), calls=%async_computation.2 | async-start | bytes 1572864 | tf_op jit(solution)/shard_map/all_to_all | solution.py:288
  148.7 2.0 %convert_reduce_fusion = f32[64,1024]{1,0:T(8,128)S(1)} fusion(bf16[16,64,1024]{2,1,0:T(8,128)(2,1)} %all-to-all-done.3), kind=kLoop, calls=%fused_computation | loop fusion | flops 2031616 | bytes 2359296 | tf_op jit(solution)/shard_map/reduce_sum | solution.py:584
  150.7 2.5 %collective-permute-start.24 = (f32[16,1024]{1,0:T(8,128)S(1)}, f32[16,1024]{1,0:T(8,128)S(1)}, u32[]{:S(2)}, u32[]{:S(2)}) collective-permute-start(f32[16,1024]{1,0:T(8,128)S(1)} %get-tuple-element.74), channel_id=1, source_target_pairs={{0,6},{2,4},{4,2},{6,0},{1,7},{3,5},{5,3},{7,1},{8,14},{10,12},{12... | collective-permute-start | bytes 196616 | tf_op jit(solution)/shard_map/ppermute | solution.py:589
  153.3 1.4 collective-permute-start.22
  154.7 7.7 %all-to-all-done.2.refs_2_ = bf16[16,64,384]{2,1,0:T(8,128)(2,1)S(1)} async-done(((bf16[16,64,384]{2,1,0:T(8,128)(2,1)}), bf16[16,64,384]{2,1,0:T(8,128)(2,1)S(1)}, u32[]{:S(2)}, u32[]{:S(2)}) %all-to-all-start.2) | async-done | bytes 786464 | tf_op jit(solution)/shard_map/all_to_all | solution.py:288
  162.4 1.6 collective-permute-start.21
  164.1 0.8 maximum_bitcast_fusion
  165.3 1.1 final.1
  (68 shorter events, 4.5 us)
Async XLA Ops:
  2.8 7.9 %collective-permute-start = (bf16[8,64,384]{2,1,0:T(8,128)(2,1)}, bf16[8,64,384]{2,1,0:T(8,128)(2,1)S(1)}, u32[]{:S(2)}, u32[]{:S(2)}) collective-permute-start(bf16[8,64,384]{2,1,0:T(8,128)(2,1)} %get-tuple-element.38), channel_id=1, source_target_pairs={{0,1},{1,0},{2,3},{3,2},{4,5},{5,4},{6,7},{7,6},{8,9},{9,8},{10,11... | collective-permute-start | bytes 1179656 | tf_op jit(solution)/shard_map/ppermute | solution.py:275
  4.2 4.5 %collective-permute-start.2 = (bf16[8,2048]{1,0:T(8,128)(2,1)}, bf16[8,2048]{1,0:T(8,128)(2,1)S(1)}, u32[]{:S(2)}, u32[]{:S(2)}) collective-permute-start(bf16[8,2048]{1,0:T(8,128)(2,1)} %refs_4_.1), channel_id=1, source_target_pairs={{0,2},{2,0},{1,3},{3,1},{4,6},{6,4},{5,7},{7,5},{8,10},{10,8},{9,1... | collective-permute-start | bytes 98312 | tf_op jit(solution)/shard_map/ppermute | solution.py:480
  7.0 2.8 %collective-permute-start.1 = (bf16[8,2048]{1,0:T(8,128)(2,1)}, bf16[8,2048]{1,0:T(8,128)(2,1)S(1)}, u32[]{:S(2)}, u32[]{:S(2)}) collective-permute-start(bf16[8,2048]{1,0:T(8,128)(2,1)} %refs_4_.1), channel_id=1, source_target_pairs={{0,1},{1,0},{2,3},{3,2},{4,5},{5,4},{6,7},{7,6},{8,9},{9,8},{10,11... | collective-permute-start | bytes 98312 | tf_op jit(solution)/shard_map/ppermute | solution.py:275
  8.7 2.0 %collective-permute-start.3 = (bf16[8,2048]{1,0:T(8,128)(2,1)S(1)}, bf16[8,2048]{1,0:T(8,128)(2,1)S(1)}, u32[]{:S(2)}, u32[]{:S(2)}) collective-permute-start(bf16[8,2048]{1,0:T(8,128)(2,1)S(1)} %collective-permute-done.2.refs_6_), channel_id=1, source_target_pairs={{0,1},{1,0},{2,3},{3,2},{4,5},{5,4},{6,7},{7,6},{8,9},{9,8},{10,11... | collective-permute-start | bytes 98312 | tf_op jit(solution)/shard_map/ppermute | solution.py:275
  10.7 0.8 copy-start.2
  12.6 38.7 %copy-start.10 = (s32[64]{0:T(128)S(1)}, s32[64]{0:T(128)}, u32[]{:S(2)}) copy-start(s32[64]{0:T(128)} %param.10) | copy-start | bytes 772
  12.6 38.9 %copy-start.9 = (s32[64,64]{1,0:T(8,128)S(1)}, s32[64,64]{1,0:T(8,128)}, u32[]{:S(2)}) copy-start(s32[64,64]{1,0:T(8,128)} %param.11) | copy-start | bytes 49156
  46.8 5.1 %collective-permute-start.5 = (bf16[1024,256]{1,0:T(8,128)(2,1)}, bf16[1024,256]{1,0:T(8,128)(2,1)S(1)}, u32[]{:S(2)}, u32[]{:S(2)}) collective-permute-start(bf16[1024,256]{1,0:T(8,128)(2,1)} %get-tuple-element.41.refs_1_.kv0.refs_0_), channel_id=1, source_target_pairs={{0,1},{1,0},{2,3},{3,2},{4,5},{5,4},{6,7},{7,6},{8,9},{9,8},{10,11... | collective-permute-start | bytes 1572872 | tf_op jit(solution)/shard_map/ppermute | solution.py:275
  48.2 13.8 %collective-permute-start.4 = (bf16[1024,256]{1,0:T(8,128)(2,1)}, bf16[1024,256]{1,0:T(8,128)(2,1)S(1)}, u32[]{:S(2)}, u32[]{:S(2)}) collective-permute-start(bf16[1024,256]{1,0:T(8,128)(2,1)} %get-tuple-element.41.refs_1_.kv0.refs_0_), channel_id=1, source_target_pairs={{0,4},{4,0},{1,5},{5,1},{2,6},{6,2},{3,7},{7,3},{8,12},{12,8},{9,1... | collective-permute-start | bytes 1572872 | tf_op jit(solution)/shard_map/ppermute | solution.py:279
  49.5 24.7 %collective-permute-start.7 = (bf16[12,64,512]{2,1,0:T(8,128)(2,1)}, bf16[12,64,512]{2,1,0:T(8,128)(2,1)S(1)}, u32[]{:S(2)}, u32[]{:S(2)}) collective-permute-start(bf16[12,64,512]{2,1,0:T(8,128)(2,1)} %get-tuple-element.51.own0), channel_id=1, source_target_pairs={{0,6},{2,4},{4,2},{6,0},{1,7},{3,5},{5,3},{7,1},{8,14},{10,12},{12... | collective-permute-start | bytes 2359304 | tf_op jit(solution)/shard_map/ppermute | solution.py:316
  51.9 6.6 %copy-start.3 = (bf16[1024,256]{1,0:T(8,128)(2,1)}, bf16[1024,256]{1,0:T(8,128)(2,1)S(1)}, u32[]{:S(2)}) copy-start(bf16[1024,256]{1,0:T(8,128)(2,1)S(1)} %collective-permute-done.5.refs_2_.kv1) | copy-start | bytes 1572868
  51.9 11.0 %copy-start.7 = (bf16[1,128,2048]{2,1,0:T(8,128)(2,1)S(1)}, bf16[1,128,2048]{2,1,0:T(8,128)(2,1)}, u32[]{:S(2)}) copy-start(bf16[1,128,2048]{2,1,0:T(8,128)(2,1)} %param.13) | copy-start | bytes 1572868
  51.9 11.1 %copy-start.8 = (bf16[4,64,512]{2,1,0:T(8,128)(2,1)S(1)}, bf16[4,64,512]{2,1,0:T(8,128)(2,1)}, u32[]{:S(2)}) copy-start(bf16[4,64,512]{2,1,0:T(8,128)(2,1)} %get-tuple-element.52.own1) | copy-start | bytes 786436
  62.1 12.1 %copy-start.4 = (bf16[1024,256]{1,0:T(8,128)(2,1)}, bf16[1024,256]{1,0:T(8,128)(2,1)S(1)}, u32[]{:S(2)}) copy-start(bf16[1024,256]{1,0:T(8,128)(2,1)S(1)} %collective-permute-done.4.refs_1_.kv2) | copy-start | bytes 1572868
  62.1 4.6 %collective-permute-start.6 = (bf16[1024,256]{1,0:T(8,128)(2,1)S(1)}, bf16[1024,256]{1,0:T(8,128)(2,1)S(1)}, u32[]{:S(2)}, u32[]{:S(2)}) collective-permute-start(bf16[1024,256]{1,0:T(8,128)(2,1)S(1)} %collective-permute-done.4.refs_1_.kv2), channel_id=1, source_target_pairs={{0,1},{1,0},{2,3},{3,2},{4,5},{5,4},{6,7},{7,6},{8,9},{9,8},{10,11... | collective-permute-start | bytes 1572872 | tf_op jit(solution)/shard_map/ppermute | solution.py:275
  62.9 1.9 %collective-permute-start.9 = (bf16[128,1024]{1,0:T(8,128)(2,1)S(1)}, bf16[128,1024]{1,0:T(8,128)(2,1)S(1)}, u32[]{:S(2)}, u32[]{:S(2)}) collective-permute-start(bf16[128,1024]{1,0:T(8,128)(2,1)S(1)} %slice_select_fusion), channel_id=1, source_target_pairs={{0,1},{1,0},{2,3},{3,2},{4,5},{5,4},{6,7},{7,6},{8,9},{9,8},{10,11... | collective-permute-start | bytes 786440 | tf_op jit(solution)/shard_map/ppermute | solution.py:275
  63.0 11.2 %collective-permute-start.8 = (bf16[4,64,512]{2,1,0:T(8,128)(2,1)S(1)}, bf16[4,64,512]{2,1,0:T(8,128)(2,1)S(1)}, u32[]{:S(2)}, u32[]{:S(2)}) collective-permute-start(bf16[4,64,512]{2,1,0:T(8,128)(2,1)S(1)} %copy-done.8), channel_id=1, source_target_pairs={{0,4},{4,0},{1,5},{5,1},{2,6},{6,2},{3,7},{7,3},{8,12},{12,8},{9,1... | collective-permute-start | bytes 786440 | tf_op jit(solution)/shard_map/ppermute | solution.py:279
  66.7 7.5 %copy-start.5 = (bf16[1024,256]{1,0:T(8,128)(2,1)}, bf16[1024,256]{1,0:T(8,128)(2,1)S(1)}, u32[]{:S(2)}) copy-start(bf16[1024,256]{1,0:T(8,128)(2,1)S(1)} %collective-permute-done.6.refs_2_.kv3) | copy-start | bytes 1572868
  77.7 11.6 %copy-start = (bf16[1024,256]{1,0:T(8,128)(2,1)S(1)}, bf16[1024,256]{1,0:T(8,128)(2,1)}, u32[]{:S(2)}) copy-start(bf16[1024,256]{1,0:T(8,128)(2,1)} %get-tuple-element.59.refs_0_.pair_ref.refs_2_) | copy-start | bytes 1572868
  77.7 1.9 %collective-permute-start.10 = (f32[128,1024]{1,0:T(8,128)S(1)}, f32[128,1024]{1,0:T(8,128)S(1)}, u32[]{:S(2)}, u32[]{:S(2)}) collective-permute-start(f32[128,1024]{1,0:T(8,128)S(1)} %get-tuple-element.55), channel_id=1, source_target_pairs={{0,1},{1,0},{2,3},{3,2},{4,5},{5,4},{6,7},{7,6},{8,9},{9,8},{10,11... | collective-permute-start | bytes 1572872 | tf_op jit(solution)/shard_map/ppermute | solution.py:275
  81.6 14.5 %all-to-all-start.1 = ((bf16[16,64,256]{2,1,0:T(8,128)(2,1)}), bf16[16,64,256]{2,1,0:T(8,128)(2,1)S(1)}, u32[]{:S(2)}, u32[]{:S(2)}) async-start(bf16[16,64,256]{2,1,0:T(8,128)(2,1)} %cross.1), calls=%async_computation.1 | async-start | bytes 1048576 | tf_op jit(solution)/shard_map/all_to_all | solution.py:288
  85.1 1.3 collective-permute-start.11
  86.4 2.9 %collective-permute-start.12 = (f32[2,1024]{1,0:T(2,128)S(1)}, f32[2,1024]{1,0:T(2,128)S(1)}, u32[]{:S(2)}, u32[]{:S(2)}) collective-permute-start(f32[2,1024]{1,0:T(2,128)S(1)} %pad_maximum_fusion.6), channel_id=1, source_target_pairs={{0,4},{4,0},{1,5},{5,1},{2,6},{6,2},{3,7},{7,3},{8,12},{12,8},{9,1... | collective-permute-start | bytes 24584 | tf_op jit(solution)/shard_map/ppermute | solution.py:279
  89.3 12.6 %collective-permute-start.14 = (bf16[1024,256]{1,0:T(8,128)(2,1)S(1)}, bf16[1024,256]{1,0:T(8,128)(2,1)S(1)}, u32[]{:S(2)}, u32[]{:S(2)}) collective-permute-start(bf16[1024,256]{1,0:T(8,128)(2,1)S(1)} %copy-done), channel_id=1, source_target_pairs={{0,4},{4,0},{1,5},{5,1},{2,6},{6,2},{3,7},{7,3},{8,12},{12,8},{9,1... | collective-permute-start | bytes 1572872 | tf_op jit(solution)/shard_map/ppermute | solution.py:279
  90.6 38.0 %collective-permute-start.16 = (bf16[1024,256]{1,0:T(8,128)(2,1)S(1)}, bf16[1024,256]{1,0:T(8,128)(2,1)S(1)}, u32[]{:S(2)}, u32[]{:S(2)}) collective-permute-start(bf16[1024,256]{1,0:T(8,128)(2,1)S(1)} %copy-done), channel_id=1, source_target_pairs={{0,1},{1,0},{2,3},{3,2},{4,5},{5,4},{6,7},{7,6},{8,9},{9,8},{10,11... | collective-permute-start | bytes 1572872 | tf_op jit(solution)/shard_map/ppermute | solution.py:275
  96.9 31.7 %collective-permute-start.18 = (bf16[1024,128]{1,0:T(8,128)(2,1)}, bf16[1024,128]{1,0:T(8,128)(2,1)S(1)}, u32[]{:S(2)}, u32[]{:S(2)}) collective-permute-start(bf16[1024,128]{1,0:T(8,128)(2,1)} %get-tuple-element.61.g_ref.refs_6_), channel_id=1, source_target_pairs={{0,1},{1,0},{2,3},{3,2},{4,5},{5,4},{6,7},{7,6},{8,9},{9,8},{10,11... | collective-permute-start | bytes 786440 | tf_op jit(solution)/shard_map/ppermute | solution.py:275
  98.4 19.9 %collective-permute-start.19 = (bf16[1024,128]{1,0:T(8,128)(2,1)}, bf16[1024,128]{1,0:T(8,128)(2,1)S(1)}, u32[]{:S(2)}, u32[]{:S(2)}) collective-permute-start(bf16[1024,128]{1,0:T(8,128)(2,1)} %get-tuple-element.61.g_ref.refs_6_), channel_id=1, source_target_pairs={{0,4},{4,0},{1,5},{5,1},{2,6},{6,2},{3,7},{7,3},{8,12},{12,8},{9,1... | collective-permute-start | bytes 786440 | tf_op jit(solution)/shard_map/ppermute | solution.py:279
  99.6 2.3 %collective-permute-start.13 = (bf16[128,1024]{1,0:T(8,128)(2,1)S(1)}, bf16[128,1024]{1,0:T(8,128)(2,1)S(1)}, u32[]{:S(2)}, u32[]{:S(2)}) collective-permute-start(bf16[128,1024]{1,0:T(8,128)(2,1)S(1)} %get-tuple-element.57.own_ref), channel_id=1, source_target_pairs={{0,1},{1,0},{2,3},{3,2},{4,5},{5,4},{6,7},{7,6},{8,9},{9,8},{10,11... | collective-permute-start | bytes 786440 | tf_op jit(solution)/shard_map/ppermute | solution.py:275
  105.1 36.6 %all-to-all-start.3 = ((bf16[16,64,1024]{2,1,0:T(8,128)(2,1)}), bf16[16,64,1024]{2,1,0:T(8,128)(2,1)}, u32[]{:S(2)}, u32[]{:S(2)}) async-start(bf16[16,64,1024]{2,1,0:T(8,128)(2,1)} %bitcast.50), calls=%async_computation.3 | async-start | bytes 4194304 | tf_op jit(solution)/shard_map/all_to_all | solution.py:288
  113.8 14.9 %copy-start.1 = (bf16[1024,256]{1,0:T(8,128)(2,1)S(1)}, bf16[1024,256]{1,0:T(8,128)(2,1)}, u32[]{:S(2)}) copy-start(bf16[1024,256]{1,0:T(8,128)(2,1)} %get-tuple-element.59.refs_0_.pair_ref.refs_2_) | copy-start | bytes 1572868
  113.8 14.9 %copy-start.6 = (bf16[1024,128]{1,0:T(8,128)(2,1)S(1)}, bf16[1024,128]{1,0:T(8,128)(2,1)}, u32[]{:S(2)}) copy-start(bf16[1024,128]{1,0:T(8,128)(2,1)} %get-tuple-element.61.g_ref.refs_6_) | copy-start | bytes 786436
  113.8 34.8 %collective-permute-start.15 = (bf16[2,64,1024]{2,1,0:T(8,128)(2,1)S(1)}, bf16[2,64,1024]{2,1,0:T(8,128)(2,1)S(1)}, u32[]{:S(2)}, u32[]{:S(2)}) collective-permute-start(bf16[2,64,1024]{2,1,0:T(8,128)(2,1)S(1)} %pad_maximum_fusion.2), channel_id=1, source_target_pairs={{0,1},{1,0},{2,3},{3,2},{4,5},{5,4},{6,7},{7,6},{8,9},{9,8},{10,11... | collective-permute-start | bytes 786440 | tf_op jit(solution)/shard_map/ppermute | solution.py:275
  118.2 10.5 %collective-permute-start.17 = (bf16[1024,256]{1,0:T(8,128)(2,1)S(1)}, bf16[1024,256]{1,0:T(8,128)(2,1)S(1)}, u32[]{:S(2)}, u32[]{:S(2)}) collective-permute-start(bf16[1024,256]{1,0:T(8,128)(2,1)S(1)} %collective-permute-done.14.far_ref.refs_4_), channel_id=1, source_target_pairs={{0,1},{1,0},{2,3},{3,2},{4,5},{5,4},{6,7},{7,6},{8,9},{9,8},{10,11... | collective-permute-start | bytes 1572872 | tf_op jit(solution)/shard_map/ppermute | solution.py:275
  118.3 10.4 %collective-permute-start.20 = (bf16[1024,128]{1,0:T(8,128)(2,1)S(1)}, bf16[1024,128]{1,0:T(8,128)(2,1)S(1)}, u32[]{:S(2)}, u32[]{:S(2)}) collective-permute-start(bf16[1024,128]{1,0:T(8,128)(2,1)S(1)} %collective-permute-done.19.refs_8_), channel_id=1, source_target_pairs={{0,1},{1,0},{2,3},{3,2},{4,5},{5,4},{6,7},{7,6},{8,9},{9,8},{10,11... | collective-permute-start | bytes 786440 | tf_op jit(solution)/shard_map/ppermute | solution.py:275
  141.7 20.7 %all-to-all-start.2 = ((bf16[16,64,384]{2,1,0:T(8,128)(2,1)}), bf16[16,64,384]{2,1,0:T(8,128)(2,1)S(1)}, u32[]{:S(2)}, u32[]{:S(2)}) async-start(bf16[16,64,384]{2,1,0:T(8,128)(2,1)} %pad_maximum_fusion), calls=%async_computation.2 | async-start | bytes 1572864 | tf_op jit(solution)/shard_map/all_to_all | solution.py:288
  150.7 13.3 %collective-permute-start.24 = (f32[16,1024]{1,0:T(8,128)S(1)}, f32[16,1024]{1,0:T(8,128)S(1)}, u32[]{:S(2)}, u32[]{:S(2)}) collective-permute-start(f32[16,1024]{1,0:T(8,128)S(1)} %get-tuple-element.74), channel_id=1, source_target_pairs={{0,6},{2,4},{4,2},{6,0},{1,7},{3,5},{5,3},{7,1},{8,14},{10,12},{12... | collective-permute-start | bytes 196616 | tf_op jit(solution)/shard_map/ppermute | solution.py:589
  153.3 10.7 %collective-permute-start.23 = (f32[16,1024]{1,0:T(8,128)S(1)}, f32[16,1024]{1,0:T(8,128)S(1)}, u32[]{:S(2)}, u32[]{:S(2)}) collective-permute-start(f32[16,1024]{1,0:T(8,128)S(1)} %get-tuple-element.75), channel_id=1, source_target_pairs={{0,4},{2,6},{4,0},{6,2},{1,5},{3,7},{5,1},{7,3},{8,12},{10,14},{12... | collective-permute-start | bytes 196616 | tf_op jit(solution)/shard_map/ppermute | solution.py:589
  153.3 10.7 %collective-permute-start.22 = (f32[16,1024]{1,0:T(8,128)S(1)}, f32[16,1024]{1,0:T(8,128)S(1)}, u32[]{:S(2)}, u32[]{:S(2)}) collective-permute-start(f32[16,1024]{1,0:T(8,128)S(1)} %get-tuple-element.73), channel_id=1, source_target_pairs={{0,2},{2,0},{4,6},{6,4},{1,3},{3,1},{5,7},{7,5},{8,10},{10,8},{12,... | collective-permute-start | bytes 196616 | tf_op jit(solution)/shard_map/ppermute | solution.py:589
  162.4 2.9 %collective-permute-start.21 = (bf16[8,64,384]{2,1,0:T(8,128)(2,1)S(1)}, bf16[8,64,384]{2,1,0:T(8,128)(2,1)S(1)}, u32[]{:S(2)}, u32[]{:S(2)}) collective-permute-start(bf16[8,64,384]{2,1,0:T(8,128)(2,1)S(1)} %constant_dynamic-slice_fusion), channel_id=1, source_target_pairs={{0,1},{1,0},{2,3},{3,2},{4,5},{5,4},{6,7},{7,6},{8,9},{9,8},{10,11... | collective-permute-start | bytes 1179656 | tf_op jit(solution)/shard_map/ppermute | solution.py:275
  164.0 2.4 %collective-permute-start.25 = (f32[8,1024]{1,0:T(8,128)S(1)}, f32[8,1024]{1,0:T(8,128)S(1)}, u32[]{:S(2)}, u32[]{:S(2)}) collective-permute-start(f32[8,1024]{1,0:T(8,128)S(1)} %dynamic-slice_bitcast_fusion.3), channel_id=1, source_target_pairs={{0,1},{1,0},{2,3},{3,2},{4,5},{5,4},{6,7},{7,6},{8,9},{9,8},{10,11... | collective-permute-start | bytes 98312 | tf_op jit(solution)/shard_map/ppermute | solution.py:275

commit v10 on v9

--- a/solution.py
+++ b/solution.py
@@ -154,7 +154,7 @@
     return jnp.sum((g.astype(F32) * att.astype(F32)).T, axis=0, keepdims=True)
 
 
-def query_body(pair_ref, g_ref, lse_ref, far_ref, kv0, kv1, kv2, kv3, bias_ref, dq_ref, ka_ref, s_ref):
+def query_body(pair_ref, g_ref, lse_ref, kv0, kv1, kv2, kv3, bias_ref, dq_ref, ka_ref, s_ref):
     step = pl.program_id(0)
     chunks = (kv0, kv1, kv2, kv3)
 
@@ -179,7 +179,7 @@
     dq_ref[...] = (total * SCALE).T.astype(BF16)
 
 
-def query_grad(pair, g, lse, far, kvs, bias):
+def query_grad(pair, g, lse, kvs, bias):
     return pl.pallas_call(
         query_body,
         out_shape=jax.ShapeDtypeStruct((ROWS, HEAD), BF16),
@@ -188,7 +188,6 @@
             tile_spec(2 * HEAD),
             tile_spec(HEAD),
             row_spec(1),
-            pl.BlockSpec(memory_space=pl.ANY),
             *[once(ROWS, 2 * HEAD)] * 4,
             once(4 * UNITS, HEAD),
         ],
@@ -200,7 +199,7 @@
         cost_estimate=cost(3, 4 * ROWS * ROWS),
         compiler_params=pltpu.CompilerParams(vmem_limit_bytes=WIDE_GRANT),
         name="query_grad",
-    )(pair, g, lse, far, *kvs, bias)
+    )(pair, g, lse, *kvs, bias)
 
 
 def key_body(*refs):
@@ -349,7 +348,8 @@
     )(xl, *own, *other, up)
 
 
-def term_body(own_ref, peer_ref, up_ref, out_ref):
+def term_body(own_ref, peer_ref, up_ref, out_ref, token_ref):
+    token_ref[...] = jnp.zeros_like(token_ref)
     att = jnp.concatenate([own_ref[...], peer_ref[...]], axis=0)
     for c in range(2):
         cols = slice(c * 512, (c + 1) * 512)
@@ -359,10 +359,10 @@
 def weight_terms(own, peer, up):
     return pl.pallas_call(
         term_body,
-        out_shape=pltpu.HBM((1024, 1024), BF16),
+        out_shape=[pltpu.HBM((1024, 1024), BF16), jax.ShapeDtypeStruct((8, HEAD), F32)],
         grid=(1,),
         in_specs=[once(128, 1024), once(128, 1024), once(256, 1024)],
-        out_specs=once(1024, 1024),
+        out_specs=[once(1024, 1024), once(8, HEAD)],
         cost_estimate=pl.CostEstimate(
             flops=2 * 256 * 1024 * 1024, bytes_accessed=4 << 20, transcendentals=0
         ),
@@ -511,8 +511,10 @@
     far_kv = other_chip(own_kv)
     weight_other = [across(weight_own[0]), other_chip(weight_own[1])]
     near_kv = other_core(own_kv)
-    own_kv, span_order, wide = lax.optimization_barrier((own_kv, span_order, upstream[0]))
-    bias = span_bias(span_order, block_mask, xl, core)
+    own_kv, span_order, wide, side, which = lax.optimization_barrier(
+        (own_kv, span_order, upstream[0], xl, core)
+    )
+    bias = span_bias(span_order, block_mask, side, which)
 
     up_sent = jnp.where(first_core, wide[:, cols:], wide[:, :cols])
     (up,) = move(
@@ -526,7 +528,7 @@
     )
 
     out, top, total = forward(True, in_hbm(q), (in_hbm(own_kv), near_kv), bias)
-    far_kv, total = lax.optimization_barrier((far_kv, total))
+    far_kv, total, up = lax.optimization_barrier((far_kv, total, up))
     kvs = (own_kv, near_kv, far_kv, other_core(far_kv))
     pair, lse = forward(False, in_hbm(q), kvs[2:], bias, in_hbm(out), top, total)
     lses = jnp.concatenate([lse, other_core(lse)], axis=0)
@@ -560,12 +562,12 @@
     )
     gs = everyone(g)
     att_peer = other_core(att_own)
-    term = weight_terms(att_own, att_peer, in_hbm(up)).reshape(UNITS, SPAN, cols)
-    term = exchange(term, ZY)
-    att_peer, pair_far = lax.optimization_barrier((att_peer, pair_far))
+    term, token = weight_terms(att_own, att_peer, in_hbm(up))
+    term = exchange(term.reshape(UNITS, SPAN, cols), ZY)
+    weight, pair_far, token = lax.optimization_barrier((weight, pair_far, token))
     pairs = (pair_sent, other_core(pair_sent), pair_far, other_core(pair_far))
 
-    query_out = query_grad(in_hbm(pair), in_hbm(g), lse, pairs[2], [in_hbm(x) for x in kvs], bias)
+    query_out = query_grad(in_hbm(pair), in_hbm(g), lse, [in_hbm(x) for x in kvs], bias)
     key_out, value_out = key_grad(in_hbm(own_kv), bias, pairs, gs, lses)
     grads = [x.reshape(UNITS, SPAN, HEAD) for x in (query_out, key_out, value_out)]
     grads = exchange(jnp.concatenate(grads, axis=2), ZY)
@@ -595,7 +597,7 @@
     peer = other_core(lax.dynamic_slice_in_dim(grads, (1 - core) * HEADS, HEADS, 0))
     own_rows = (2 * SPAN, HEADS * HEAD)
     query_gradient, key_gradient, value_gradient = move(
-        final_body, "final", [own_rows] * 3, [core_1, half_1], grads, peer
+        final_body, "final", [own_rows] * 3, [core_1, half_1], grads, peer, after=(token,)
     )
     return (
         projected[None],

time: 168 us -> 165 us (0.982)
  waiting for transfers between devices: 22.3 us -> 56 us
  blocking collectives: 32.7 us -> 0 us
  matrix products: 4.39 us -> 1.22 us
  starting transfers between devices: 47.8 us -> 45.7 us
    all_to_all x3 -> x4, waiting for transfers between devices: 11.7 us -> 48.2 us  [exchange(): return lax.all_to_all(x, axes, 0, 0, tiled=True)]
    all_to_all x1 -> x0, blocking collectives: 32.7 us -> none  [exchange(): return lax.all_to_all(x, axes, 0, 0, tiled=True)]
    ppermute x16, starting transfers between devices: 15.9 us -> 12.6 us  [other_core(): return lax.ppermute(x, 'core', SWAP)]
    ppermute x5, waiting for transfers between devices: 5.17 us -> 1.95 us  [other_chip(): return lax.ppermute(x, 'xl', SWAP)]
    dot_general x2, matrix products: 4.07 us -> 0.91 us  [dot(): return lax.dot_general(a, b, dims, preferred_element_type=F32)]
    all_to_all x3 -> x4, starting transfers between devices: 17 us -> 19.8 us  [exchange(): return lax.all_to_all(x, axes, 0, 0, tiled=True)]
    ppermute x5, starting transfers between devices: 6.36 us -> 4.6 us  [other_chip(): return lax.ppermute(x, 'xl', SWAP)]
  transfers between devices with their start and end apart: 29 -> 30, of which waited for: 10 -> 12; matrix products, arithmetic and copies ran while one was open for 5% -> 3% of each run, Pallas kernels for 26% -> 26%
where the time goes in v10:
time: 165 us; the launch traced here: 164 us
  waiting for transfers between devices  56 us (34%)
  Pallas kernels  53 us (32%)
  starting transfers between devices  45.7 us (28%)
  other arithmetic  4.91 us (3%)
  local copies, waits for them, and re-layouts  2.18 us (1%)
    all_to_all x4, waiting for transfers between devices, exchange(): return lax.all_to_all(x, axes, 0, 0, tiled=True)  48.2 us
    all_to_all x4, starting transfers between devices, exchange(): return lax.all_to_all(x, axes, 0, 0, tiled=True)  19.8 us
    pallas_call x2, Pallas kernels, forward(): pl.pallas_call(functools.partial(forward_body, first), out_shape=outs, gr...  14 us
    ppermute x16, starting transfers between devices, other_core(): return lax.ppermute(x, 'core', SWAP)  12.6 us
    pallas_call x1, Pallas kernels, key_grad(): pl.pallas_call(key_body, out_shape=[jax.ShapeDtypeStruct((ROWS, HEAD), BF...  11.9 us
    pallas_call x7, Pallas kernels, move(): pl.pallas_call(run, out_shape=[make(shape, BF16) for make, shape in zip(s...  10.4 us
    pallas_call x1, Pallas kernels, query_grad(): pl.pallas_call(query_body, out_shape=jax.ShapeDtypeStruct((ROWS, HEAD), B...  10.1 us
    ppermute x5, starting transfers between devices, other_chip(): return lax.ppermute(x, 'xl', SWAP)  4.6 us
  transfers between devices with their start and end apart: 30, of which 12 were waited for; matrix products, arithmetic and copies ran while one was open for 3% of the time, Pallas kernels for 26%

profile of v10, /device:TPU:1, one launch (start us, length us, event | category | flops | bytes accessed | tf_op | source)
XLA Modules:
  0.0 163.9 jit_solution(9425828695242467188)
XLA Ops:
  0.6 2.1 %cut.1 = (bf16[8,64,384]{2,1,0:T(8,128)(2,1)}, bf16[8,64,384]{2,1,0:T(8,128)(2,1)}) custom-call(s32[1]{0:T(128)} %bitcast.2.refs_0_.refs_1_, bf16[128,1024]{1,0:T(8,128)(2,1)} %bitcast.59, bf16[128,1024]{1,0:T(8,128)(2,1)} %bitcast.60, bf16[128,1024]{1,0:T(8,128)(2,1)} %bitcast.61), custom_call_target="tpu_custom_call" | custom-call | bytes 4194304 | tf_op jit(solution)/shard_map/cut/pallas_call | solution.py:384
  2.8 1.4 collective-permute-start
  4.2 2.8 %collective-permute-start.2 = (bf16[8,2048]{1,0:T(8,128)(2,1)}, bf16[8,2048]{1,0:T(8,128)(2,1)S(1)}, u32[]{:S(2)}, u32[]{:S(2)}) collective-permute-start(bf16[8,2048]{1,0:T(8,128)(2,1)} %refs_4_.1), channel_id=1, source_target_pairs={{0,2},{2,0},{1,3},{3,1},{4,6},{6,4},{5,7},{7,5},{8,10},{10,8},{9,1... | collective-permute-start | bytes 98312 | tf_op jit(solution)/shard_map/ppermute | solution.py:480
  7.3 1.4 collective-permute-done.2.refs_6_
  8.7 1.2 collective-permute-start.3
  9.8 0.9 collective-permute-done.3.refs_7_
  10.7 0.8 copy-done.3
  11.5 1.2 fill.1
  12.7 1.3 copy-done
  13.9 8.0 %all-to-all-start = ((bf16[16,64,896]{2,1,0:T(8,128)(2,1)}), bf16[16,64,896]{2,1,0:T(8,128)(2,1)S(1)}, u32[]{:S(2)}, u32[]{:S(2)}) async-start(bf16[16,64,896]{2,1,0:T(8,128)(2,1)} %copy-done), calls=%async_computation | async-start | bytes 3670016 | tf_op jit(solution)/shard_map/all_to_all | solution.py:287
  22.0 28.1 %all-to-all-done.refs_0_ = bf16[16,64,896]{2,1,0:T(8,128)(2,1)S(1)} async-done(((bf16[16,64,896]{2,1,0:T(8,128)(2,1)}), bf16[16,64,896]{2,1,0:T(8,128)(2,1)S(1)}, u32[]{:S(2)}, u32[]{:S(2)}) %all-to-all-start) | async-done | bytes 1835040 | tf_op jit(solution)/shard_map/all_to_all | solution.py:287
  50.0 1.4 split.1
  51.4 1.2 collective-permute-start.4
  52.6 1.7 %collective-permute-start.5 = (bf16[1024,256]{1,0:T(8,128)(2,1)}, bf16[1024,256]{1,0:T(8,128)(2,1)S(1)}, u32[]{:S(2)}, u32[]{:S(2)}) collective-permute-start(bf16[1024,256]{1,0:T(8,128)(2,1)} %get-tuple-element.47.refs_1_.kv0.refs_0_), channel_id=1, source_target_pairs={{0,1},{1,0},{2,3},{3,2},{4,5},{5,4},{6,7},{7,6},{8,9},{9,8},{10,11... | collective-permute-start | bytes 1572872 | tf_op jit(solution)/shard_map/ppermute | solution.py:274
  54.5 1.9 %collective-permute-start.8 = (bf16[12,64,512]{2,1,0:T(8,128)(2,1)}, bf16[12,64,512]{2,1,0:T(8,128)(2,1)S(1)}, u32[]{:S(2)}, u32[]{:S(2)}) collective-permute-start(bf16[12,64,512]{2,1,0:T(8,128)(2,1)} %get-tuple-element.60.own0), channel_id=1, source_target_pairs={{0,6},{2,4},{4,2},{6,0},{1,7},{3,5},{5,3},{7,1},{8,14},{10,12},{12... | collective-permute-start | bytes 2359304 | tf_op jit(solution)/shard_map/ppermute | solution.py:315
  56.9 1.9 %up.1.up_ref = bf16[256,1024]{1,0:T(8,128)(2,1)} custom-call(s32[1]{0:T(128)} %bitcast.refs_0_, s32[1]{0:T(128)} %bitcast.2.refs_0_.refs_1_, bf16[128,2048]{1,0:T(8,128)(2,1)} %bitcast.51, bf16[128,1024]{1,0:T(8,128)(2,1)S(1)} %collective-permute-done.6.refs_3_), custom_call_target="tpu_custom_call" | custom-call | bytes 4194304 | tf_op jit(solution)/shard_map/up/pallas_call | solution.py:384
  58.8 6.6 %forward_near.1 = (f32[128,1024]{1,0:T(8,128)}, f32[1,1024]{1,0:T(1,128)S(1)}, f32[1,1024]{1,0:T(1,128)S(1)}) custom-call(bf16[1024,128]{1,0:T(8,128)(2,1)} %get-tuple-element.45.refs_0_, bf16[1024,256]{1,0:T(8,128)(2,1)} %get-tuple-element.47.refs_1_.kv0.refs_0_, bf16[1024,256]{1,0:T(8,128)(2,1)S(1)} %collective-permute-done.5.refs_2_.kv1, ...), custom_call_target="tpu_custom_call" | custom-call | flops 2147483648 | bytes 4194304 | tf_op jit(solution)/shard_map/forward_near/pallas_call | solution.py:132
  65.4 0.8 collective-permute-start.7
  66.2 1.0 collective-permute-start.9
  67.7 7.4 %forward_far.1 = (bf16[1024,256]{1,0:T(8,128)(2,1)}, f32[1,1024]{1,0:T(1,128)S(1)}) custom-call(bf16[1024,128]{1,0:T(8,128)(2,1)} %get-tuple-element.45.refs_0_, bf16[1024,256]{1,0:T(8,128)(2,1)S(1)} %collective-permute-done.4.refs_1_.kv2, bf16[1024,256]{1,0:T(8,128)(2,1)S(1)} %collective-permute-done.7.refs_2_.kv3, ...), custom_call_target="tpu_custom_call" | custom-call | flops 2147483648 | bytes 4194304 | tf_op jit(solution)/shard_map/forward_far/pallas_call | solution.py:132
  75.2 3.5 %weight_whole.1 = (bf16[1024,1024]{1,0:T(8,128)(2,1)}, f32[128,1024]{1,0:T(8,128)S(1)}, f32[128,1024]{1,0:T(8,128)S(1)}) custom-call(s32[1]{0:T(128)} %bitcast.7.xl_ref, bf16[12,64,512]{2,1,0:T(8,128)(2,1)} %get-tuple-element.60.own0, bf16[4,64,512]{2,1,0:T(8,128)(2,1)} %get-tuple-element.61.own1, bf16[12,64,512]{2,1,0:T(8,128)(2,1)S(1)} %collective-permute-done.8.other0, ...), custom_call_target="tpu_custom_call" | custom-call | flops 536870912 | bytes 4194304 | tf_op jit(solution)/shard_map/weight_whole/pallas_call | solution.py:331
  78.7 0.7 collective-permute-start.10
  79.4 1.5 collective-permute-done.10.refs_2_
  81.0 1.9 %cross.1 = bf16[16,64,256]{2,1,0:T(8,128)(2,1)} custom-call(bf16[1024,256]{1,0:T(8,128)(2,1)} %get-tuple-element.68.refs_0_.pair_ref.refs_2_, f32[128,1024]{1,0:T(8,128)S(1)} %get-tuple-element.63.refs_1_, f32[128,1024]{1,0:T(8,128)S(1)} %collective-permute-done.10.refs_2_), custom_call_target="tpu_custom_call" | custom-call | bytes 4194304 | tf_op jit(solution)/shard_map/cross/pallas_call | solution.py:384
  82.9 3.6 %all-to-all-start.1 = ((bf16[16,64,256]{2,1,0:T(8,128)(2,1)}), bf16[16,64,256]{2,1,0:T(8,128)(2,1)S(1)}, u32[]{:S(2)}, u32[]{:S(2)}) async-start(bf16[16,64,256]{2,1,0:T(8,128)(2,1)} %cross.1), calls=%async_computation.1 | async-start | bytes 1048576 | tf_op jit(solution)/shard_map/all_to_all | solution.py:287
  86.9 0.8 collective-permute-done.11
  87.8 0.9 collective-permute-start.12
  88.7 1.9 %collective-permute-done.12 = f32[2,1024]{1,0:T(2,128)S(1)} collective-permute-done((f32[2,1024]{1,0:T(2,128)S(1)}, f32[2,1024]{1,0:T(2,128)S(1)}, u32[]{:S(2)}, u32[]{:S(2)}) %collective-permute-start.12) | collective-permute-done | bytes 8224 | tf_op jit(solution)/shard_map/ppermute | solution.py:278
  90.7 6.8 %all-to-all-done.1.refs_0_ = bf16[16,64,256]{2,1,0:T(8,128)(2,1)S(1)} async-done(((bf16[16,64,256]{2,1,0:T(8,128)(2,1)}), bf16[16,64,256]{2,1,0:T(8,128)(2,1)S(1)}, u32[]{:S(2)}, u32[]{:S(2)}) %all-to-all-start.1) | async-done | bytes 524320 | tf_op jit(solution)/shard_map/all_to_all | solution.py:287
  97.4 0.8 land.1
  98.2 1.5 collective-permute-start.14
  100.9 0.8 collective-permute-start.19
  101.7 3.2 %weight_terms.1 = (bf16[1024,1024]{1,0:T(8,128)(2,1)}, f32[8,128]{1,0:T(8,128)S(1)}) custom-call(bf16[128,1024]{1,0:T(8,128)(2,1)S(1)} %get-tuple-element.66.own_ref, bf16[128,1024]{1,0:T(8,128)(2,1)S(1)} %collective-permute-done.14.peer_ref, bf16[256,1024]{1,0:T(8,128)(2,1)} %up.1.up_ref), custom_call_target="tpu_custom_call" | custom-call | flops 536870912 | bytes 4194304 | tf_op jit(solution)/shard_map/weight_terms/pallas_call | solution.py:360
  104.9 4.6 %all-to-all-start.3 = ((bf16[16,64,1024]{2,1,0:T(8,128)(2,1)}), bf16[16,64,1024]{2,1,0:T(8,128)(2,1)}, u32[]{:S(2)}, u32[]{:S(2)}) async-start(bf16[16,64,1024]{2,1,0:T(8,128)(2,1)} %bitcast.50), calls=%async_computation.3 | async-start | bytes 4194304 | tf_op jit(solution)/shard_map/all_to_all | solution.py:287
  109.5 10.1 %query_grad.1 = bf16[1024,128]{1,0:T(8,128)(2,1)S(1)} custom-call(bf16[1024,256]{1,0:T(8,128)(2,1)} %get-tuple-element.68.refs_0_.pair_ref.refs_2_, bf16[1024,128]{1,0:T(8,128)(2,1)} %get-tuple-element.71.g_ref.refs_6_, f32[1,1024]{1,0:T(1,128)S(1)} %get-tuple-element.72.lse_ref, bf16[1024,256]{1,0:T(8,128)(2,1)} %get-tuple-element.47.refs_1_.kv0.refs_0_, ...), custom_call_target="tpu_custom_call" | custom-call | flops 6442450944 | bytes 4194304 | tf_op jit(solution)/shard_map/query_grad/pallas_call | solution.py:183
  119.6 0.6 collective-permute-start.17
  122.2 11.9 %key_grad.1 = (bf16[1024,128]{1,0:T(8,128)(2,1)S(1)}, bf16[1024,128]{1,0:T(8,128)(2,1)S(1)}) custom-call(bf16[1024,256]{1,0:T(8,128)(2,1)} %get-tuple-element.47.refs_1_.kv0.refs_0_, f32[64,128]{1,0:T(8,128)S(1)} %pad.4.refs_3_.bias_ref.refs_1_, bf16[1024,256]{1,0:T(8,128)(2,1)S(1)} %copy-done.2, bf16[1024,256]{1,0:T(8,128)(2,1)S(1)} %collective-permute-done.16.refs_3_, ...), custom_call_target="tpu_custom_call" | custom-call | flops 8589934592 | bytes 4194304 | tf_op jit(solution)/shard_map/key_grad/pallas_call | solution.py:244
  134.1 1.0 pad_maximum_fusion
  135.1 6.8 %all-to-all-done.3 = bf16[16,64,1024]{2,1,0:T(8,128)(2,1)} async-done(((bf16[16,64,1024]{2,1,0:T(8,128)(2,1)}), bf16[16,64,1024]{2,1,0:T(8,128)(2,1)}, u32[]{:S(2)}, u32[]{:S(2)}) %all-to-all-start.3) | async-done | bytes 2097184 | tf_op jit(solution)/shard_map/all_to_all | solution.py:287
  141.9 3.6 %all-to-all-start.2 = ((bf16[16,64,384]{2,1,0:T(8,128)(2,1)}), bf16[16,64,384]{2,1,0:T(8,128)(2,1)S(1)}, u32[]{:S(2)}, u32[]{:S(2)}) async-start(bf16[16,64,384]{2,1,0:T(8,128)(2,1)} %pad_maximum_fusion), calls=%async_computation.2 | async-start | bytes 1572864 | tf_op jit(solution)/shard_map/all_to_all | solution.py:287
  145.6 2.0 %convert_reduce_fusion = f32[64,1024]{1,0:T(8,128)S(1)} fusion(bf16[16,64,1024]{2,1,0:T(8,128)(2,1)} %all-to-all-done.3), kind=kLoop, calls=%fused_computation | loop fusion | flops 2031616 | bytes 2359296 | tf_op jit(solution)/shard_map/reduce_sum | solution.py:586
  147.7 2.0 %collective-permute-start.24 = (f32[16,1024]{1,0:T(8,128)S(1)}, f32[16,1024]{1,0:T(8,128)S(1)}, u32[]{:S(2)}, u32[]{:S(2)}) collective-permute-start(f32[16,1024]{1,0:T(8,128)S(1)} %get-tuple-element.86), channel_id=1, source_target_pairs={{0,6},{2,4},{4,2},{6,0},{1,7},{3,5},{5,3},{7,1},{8,14},{10,12},{12... | collective-permute-start | bytes 196616 | tf_op jit(solution)/shard_map/ppermute | solution.py:591
  149.6 2.0 %collective-permute-start.22 = (f32[16,1024]{1,0:T(8,128)S(1)}, f32[16,1024]{1,0:T(8,128)S(1)}, u32[]{:S(2)}, u32[]{:S(2)}) collective-permute-start(f32[16,1024]{1,0:T(8,128)S(1)} %get-tuple-element.85), channel_id=1, source_target_pairs={{0,2},{2,0},{4,6},{6,4},{1,3},{3,1},{5,7},{7,5},{8,10},{10,8},{12,... | collective-permute-start | bytes 196616 | tf_op jit(solution)/shard_map/ppermute | solution.py:591
  151.6 6.6 %all-to-all-done.2.refs_2_ = bf16[16,64,384]{2,1,0:T(8,128)(2,1)S(1)} async-done(((bf16[16,64,384]{2,1,0:T(8,128)(2,1)}), bf16[16,64,384]{2,1,0:T(8,128)(2,1)S(1)}, u32[]{:S(2)}, u32[]{:S(2)}) %all-to-all-start.2) | async-done | bytes 786464 | tf_op jit(solution)/shard_map/all_to_all | solution.py:287
  158.2 2.6 %collective-permute-start.21 = (bf16[8,64,384]{2,1,0:T(8,128)(2,1)S(1)}, bf16[8,64,384]{2,1,0:T(8,128)(2,1)S(1)}, u32[]{:S(2)}, u32[]{:S(2)}) collective-permute-start(bf16[8,64,384]{2,1,0:T(8,128)(2,1)S(1)} %constant_dynamic-slice_fusion), channel_id=1, source_target_pairs={{0,1},{1,0},{2,3},{3,2},{4,5},{5,4},{6,7},{7,6},{8,9},{9,8},{10,11... | collective-permute-start | bytes 1179656 | tf_op jit(solution)/shard_map/ppermute | solution.py:274
  161.0 0.8 maximum_bitcast_fusion
  162.2 1.1 final.1
  163.3 0.6 pad_maximum_fusion.4
  (73 shorter events, 5.7 us)
Async XLA Ops:
  2.8 7.9 %collective-permute-start = (bf16[8,64,384]{2,1,0:T(8,128)(2,1)}, bf16[8,64,384]{2,1,0:T(8,128)(2,1)S(1)}, u32[]{:S(2)}, u32[]{:S(2)}) collective-permute-start(bf16[8,64,384]{2,1,0:T(8,128)(2,1)} %get-tuple-element.44), channel_id=1, source_target_pairs={{0,1},{1,0},{2,3},{3,2},{4,5},{5,4},{6,7},{7,6},{8,9},{9,8},{10,11... | collective-permute-start | bytes 1179656 | tf_op jit(solution)/shard_map/ppermute | solution.py:274
  4.2 4.5 %collective-permute-start.2 = (bf16[8,2048]{1,0:T(8,128)(2,1)}, bf16[8,2048]{1,0:T(8,128)(2,1)S(1)}, u32[]{:S(2)}, u32[]{:S(2)}) collective-permute-start(bf16[8,2048]{1,0:T(8,128)(2,1)} %refs_4_.1), channel_id=1, source_target_pairs={{0,2},{2,0},{1,3},{3,1},{4,6},{6,4},{5,7},{7,5},{8,10},{10,8},{9,1... | collective-permute-start | bytes 98312 | tf_op jit(solution)/shard_map/ppermute | solution.py:480
  7.0 2.8 %collective-permute-start.1 = (bf16[8,2048]{1,0:T(8,128)(2,1)}, bf16[8,2048]{1,0:T(8,128)(2,1)S(1)}, u32[]{:S(2)}, u32[]{:S(2)}) collective-permute-start(bf16[8,2048]{1,0:T(8,128)(2,1)} %refs_4_.1), channel_id=1, source_target_pairs={{0,1},{1,0},{2,3},{3,2},{4,5},{5,4},{6,7},{7,6},{8,9},{9,8},{10,11... | collective-permute-start | bytes 98312 | tf_op jit(solution)/shard_map/ppermute | solution.py:274
  8.7 2.0 %collective-permute-start.3 = (bf16[8,2048]{1,0:T(8,128)(2,1)S(1)}, bf16[8,2048]{1,0:T(8,128)(2,1)S(1)}, u32[]{:S(2)}, u32[]{:S(2)}) collective-permute-start(bf16[8,2048]{1,0:T(8,128)(2,1)S(1)} %collective-permute-done.2.refs_6_), channel_id=1, source_target_pairs={{0,1},{1,0},{2,3},{3,2},{4,5},{5,4},{6,7},{7,6},{8,9},{9,8},{10,11... | collective-permute-start | bytes 98312 | tf_op jit(solution)/shard_map/ppermute | solution.py:274
  10.7 0.8 copy-start.3
  12.6 1.3 copy-start
  13.9 40.4 %copy-start.9 = (bf16[1,128,2048]{2,1,0:T(8,128)(2,1)S(1)}, bf16[1,128,2048]{2,1,0:T(8,128)(2,1)}, u32[]{:S(2)}) copy-start(bf16[1,128,2048]{2,1,0:T(8,128)(2,1)} %param.13) | copy-start | bytes 1572868
  13.9 36.1 %all-to-all-start = ((bf16[16,64,896]{2,1,0:T(8,128)(2,1)}), bf16[16,64,896]{2,1,0:T(8,128)(2,1)S(1)}, u32[]{:S(2)}, u32[]{:S(2)}) async-start(bf16[16,64,896]{2,1,0:T(8,128)(2,1)} %copy-done), calls=%async_computation | async-start | bytes 3670016 | tf_op jit(solution)/shard_map/all_to_all | solution.py:287
  21.9 34.5 %copy-start.12 = (s32[64]{0:T(128)S(1)}, s32[64]{0:T(128)}, u32[]{:S(2)}) copy-start(s32[64]{0:T(128)} %param.10) | copy-start | bytes 772
  21.9 34.7 %copy-start.11 = (s32[64,64]{1,0:T(8,128)S(1)}, s32[64,64]{1,0:T(8,128)}, u32[]{:S(2)}) copy-start(s32[64,64]{1,0:T(8,128)} %param.11) | copy-start | bytes 49156
  51.4 14.0 %collective-permute-start.4 = (bf16[1024,256]{1,0:T(8,128)(2,1)}, bf16[1024,256]{1,0:T(8,128)(2,1)S(1)}, u32[]{:S(2)}, u32[]{:S(2)}) collective-permute-start(bf16[1024,256]{1,0:T(8,128)(2,1)} %get-tuple-element.47.refs_1_.kv0.refs_0_), channel_id=1, source_target_pairs={{0,4},{4,0},{1,5},{5,1},{2,6},{6,2},{3,7},{7,3},{8,12},{12,8},{9,1... | collective-permute-start | bytes 1572872 | tf_op jit(solution)/shard_map/ppermute | solution.py:278
  52.6 6.2 %collective-permute-start.5 = (bf16[1024,256]{1,0:T(8,128)(2,1)}, bf16[1024,256]{1,0:T(8,128)(2,1)S(1)}, u32[]{:S(2)}, u32[]{:S(2)}) collective-permute-start(bf16[1024,256]{1,0:T(8,128)(2,1)} %get-tuple-element.47.refs_1_.kv0.refs_0_), channel_id=1, source_target_pairs={{0,1},{1,0},{2,3},{3,2},{4,5},{5,4},{6,7},{7,6},{8,9},{9,8},{10,11... | collective-permute-start | bytes 1572872 | tf_op jit(solution)/shard_map/ppermute | solution.py:274
  54.4 2.5 %collective-permute-start.6 = (bf16[128,1024]{1,0:T(8,128)(2,1)S(1)}, bf16[128,1024]{1,0:T(8,128)(2,1)S(1)}, u32[]{:S(2)}, u32[]{:S(2)}) collective-permute-start(bf16[128,1024]{1,0:T(8,128)(2,1)S(1)} %slice_select_fusion), channel_id=1, source_target_pairs={{0,1},{1,0},{2,3},{3,2},{4,5},{5,4},{6,7},{7,6},{8,9},{9,8},{10,11... | collective-permute-start | bytes 786440 | tf_op jit(solution)/shard_map/ppermute | solution.py:274
  54.5 20.7 %collective-permute-start.8 = (bf16[12,64,512]{2,1,0:T(8,128)(2,1)}, bf16[12,64,512]{2,1,0:T(8,128)(2,1)S(1)}, u32[]{:S(2)}, u32[]{:S(2)}) collective-permute-start(bf16[12,64,512]{2,1,0:T(8,128)(2,1)} %get-tuple-element.60.own0), channel_id=1, source_target_pairs={{0,6},{2,4},{4,2},{6,0},{1,7},{3,5},{5,3},{7,1},{8,14},{10,12},{12... | collective-permute-start | bytes 2359304 | tf_op jit(solution)/shard_map/ppermute | solution.py:315
  58.8 6.6 %copy-start.5 = (bf16[1024,256]{1,0:T(8,128)(2,1)}, bf16[1024,256]{1,0:T(8,128)(2,1)S(1)}, u32[]{:S(2)}) copy-start(bf16[1024,256]{1,0:T(8,128)(2,1)S(1)} %collective-permute-done.5.refs_2_.kv1) | copy-start | bytes 1572868
  58.8 7.4 %copy-start.10 = (bf16[4,64,512]{2,1,0:T(8,128)(2,1)S(1)}, bf16[4,64,512]{2,1,0:T(8,128)(2,1)}, u32[]{:S(2)}) copy-start(bf16[4,64,512]{2,1,0:T(8,128)(2,1)} %get-tuple-element.61.own1) | copy-start | bytes 786436
  65.4 9.8 %copy-start.4 = (bf16[1024,256]{1,0:T(8,128)(2,1)}, bf16[1024,256]{1,0:T(8,128)(2,1)S(1)}, u32[]{:S(2)}) copy-start(bf16[1024,256]{1,0:T(8,128)(2,1)S(1)} %collective-permute-done.4.refs_1_.kv2) | copy-start | bytes 1572868
  65.4 2.3 %collective-permute-start.7 = (bf16[1024,256]{1,0:T(8,128)(2,1)S(1)}, bf16[1024,256]{1,0:T(8,128)(2,1)S(1)}, u32[]{:S(2)}, u32[]{:S(2)}) collective-permute-start(bf16[1024,256]{1,0:T(8,128)(2,1)S(1)} %collective-permute-done.4.refs_1_.kv2), channel_id=1, source_target_pairs={{0,1},{1,0},{2,3},{3,2},{4,5},{5,4},{6,7},{7,6},{8,9},{9,8},{10,11... | collective-permute-start | bytes 1572872 | tf_op jit(solution)/shard_map/ppermute | solution.py:274
  66.2 9.0 %collective-permute-start.9 = (bf16[4,64,512]{2,1,0:T(8,128)(2,1)S(1)}, bf16[4,64,512]{2,1,0:T(8,128)(2,1)S(1)}, u32[]{:S(2)}, u32[]{:S(2)}) collective-permute-start(bf16[4,64,512]{2,1,0:T(8,128)(2,1)S(1)} %copy-done.10), channel_id=1, source_target_pairs={{0,4},{4,0},{1,5},{5,1},{2,6},{6,2},{3,7},{7,3},{8,12},{12,8},{9,1... | collective-permute-start | bytes 786440 | tf_op jit(solution)/shard_map/ppermute | solution.py:278
  67.7 7.5 %copy-start.6 = (bf16[1024,256]{1,0:T(8,128)(2,1)}, bf16[1024,256]{1,0:T(8,128)(2,1)S(1)}, u32[]{:S(2)}) copy-start(bf16[1024,256]{1,0:T(8,128)(2,1)S(1)} %collective-permute-done.7.refs_2_.kv3) | copy-start | bytes 1572868
  78.7 21.0 %copy-start.1 = (bf16[1024,256]{1,0:T(8,128)(2,1)S(1)}, bf16[1024,256]{1,0:T(8,128)(2,1)}, u32[]{:S(2)}) copy-start(bf16[1024,256]{1,0:T(8,128)(2,1)} %get-tuple-element.68.refs_0_.pair_ref.refs_2_) | copy-start | bytes 1572868
  78.7 2.3 %collective-permute-start.10 = (f32[128,1024]{1,0:T(8,128)S(1)}, f32[128,1024]{1,0:T(8,128)S(1)}, u32[]{:S(2)}, u32[]{:S(2)}) collective-permute-start(f32[128,1024]{1,0:T(8,128)S(1)} %get-tuple-element.64), channel_id=1, source_target_pairs={{0,1},{1,0},{2,3},{3,2},{4,5},{5,4},{6,7},{7,6},{8,9},{9,8},{10,11... | collective-permute-start | bytes 1572872 | tf_op jit(solution)/shard_map/ppermute | solution.py:274
  82.9 14.5 %all-to-all-start.1 = ((bf16[16,64,256]{2,1,0:T(8,128)(2,1)}), bf16[16,64,256]{2,1,0:T(8,128)(2,1)S(1)}, u32[]{:S(2)}, u32[]{:S(2)}) async-start(bf16[16,64,256]{2,1,0:T(8,128)(2,1)} %cross.1), calls=%async_computation.1 | async-start | bytes 1048576 | tf_op jit(solution)/shard_map/all_to_all | solution.py:287
  86.5 1.3 collective-permute-start.11
  87.8 2.9 %collective-permute-start.12 = (f32[2,1024]{1,0:T(2,128)S(1)}, f32[2,1024]{1,0:T(2,128)S(1)}, u32[]{:S(2)}, u32[]{:S(2)}) collective-permute-start(f32[2,1024]{1,0:T(2,128)S(1)} %pad_maximum_fusion.6), channel_id=1, source_target_pairs={{0,4},{4,0},{1,5},{5,1},{2,6},{6,2},{3,7},{7,3},{8,12},{12,8},{9,1... | collective-permute-start | bytes 24584 | tf_op jit(solution)/shard_map/ppermute | solution.py:278
  98.2 3.5 %collective-permute-start.14 = (bf16[128,1024]{1,0:T(8,128)(2,1)S(1)}, bf16[128,1024]{1,0:T(8,128)(2,1)S(1)}, u32[]{:S(2)}, u32[]{:S(2)}) collective-permute-start(bf16[128,1024]{1,0:T(8,128)(2,1)S(1)} %get-tuple-element.66.own_ref), channel_id=1, source_target_pairs={{0,1},{1,0},{2,3},{3,2},{4,5},{5,4},{6,7},{7,6},{8,9},{9,8},{10,11... | collective-permute-start | bytes 786440 | tf_op jit(solution)/shard_map/ppermute | solution.py:274
  99.7 19.9 %collective-permute-start.13 = (bf16[1024,256]{1,0:T(8,128)(2,1)S(1)}, bf16[1024,256]{1,0:T(8,128)(2,1)S(1)}, u32[]{:S(2)}, u32[]{:S(2)}) collective-permute-start(bf16[1024,256]{1,0:T(8,128)(2,1)S(1)} %copy-done.1), channel_id=1, source_target_pairs={{0,4},{4,0},{1,5},{5,1},{2,6},{6,2},{3,7},{7,3},{8,12},{12,8},{9,1... | collective-permute-start | bytes 1572872 | tf_op jit(solution)/shard_map/ppermute | solution.py:278
  100.3 21.5 %collective-permute-start.16 = (bf16[1024,256]{1,0:T(8,128)(2,1)S(1)}, bf16[1024,256]{1,0:T(8,128)(2,1)S(1)}, u32[]{:S(2)}, u32[]{:S(2)}) collective-permute-start(bf16[1024,256]{1,0:T(8,128)(2,1)S(1)} %copy-done.1), channel_id=1, source_target_pairs={{0,1},{1,0},{2,3},{3,2},{4,5},{5,4},{6,7},{7,6},{8,9},{9,8},{10,11... | collective-permute-start | bytes 1572872 | tf_op jit(solution)/shard_map/ppermute | solution.py:274
  100.6 21.2 %collective-permute-start.18 = (bf16[1024,128]{1,0:T(8,128)(2,1)}, bf16[1024,128]{1,0:T(8,128)(2,1)S(1)}, u32[]{:S(2)}, u32[]{:S(2)}) collective-permute-start(bf16[1024,128]{1,0:T(8,128)(2,1)} %get-tuple-element.71.g_ref.refs_6_), channel_id=1, source_target_pairs={{0,1},{1,0},{2,3},{3,2},{4,5},{5,4},{6,7},{7,6},{8,9},{9,8},{10,11... | collective-permute-start | bytes 786440 | tf_op jit(solution)/shard_map/ppermute | solution.py:274
  100.9 19.4 %collective-permute-start.19 = (bf16[1024,128]{1,0:T(8,128)(2,1)}, bf16[1024,128]{1,0:T(8,128)(2,1)S(1)}, u32[]{:S(2)}, u32[]{:S(2)}) collective-permute-start(bf16[1024,128]{1,0:T(8,128)(2,1)} %get-tuple-element.71.g_ref.refs_6_), channel_id=1, source_target_pairs={{0,4},{4,0},{1,5},{5,1},{2,6},{6,2},{3,7},{7,3},{8,12},{12,8},{9,1... | collective-permute-start | bytes 786440 | tf_op jit(solution)/shard_map/ppermute | solution.py:278
  104.9 37.0 %all-to-all-start.3 = ((bf16[16,64,1024]{2,1,0:T(8,128)(2,1)}), bf16[16,64,1024]{2,1,0:T(8,128)(2,1)}, u32[]{:S(2)}, u32[]{:S(2)}) async-start(bf16[16,64,1024]{2,1,0:T(8,128)(2,1)} %bitcast.50), calls=%async_computation.3 | async-start | bytes 4194304 | tf_op jit(solution)/shard_map/all_to_all | solution.py:287
  109.5 10.9 %copy-start.8 = (bf16[1024,1024]{1,0:T(8,128)(2,1)S(1)}, bf16[1024,1024]{1,0:T(8,128)(2,1)}, u32[]{:S(2)}) copy-start(bf16[1024,1024]{1,0:T(8,128)(2,1)} %get-tuple-element.70) | copy-start | bytes 6291460
  119.6 2.6 %collective-permute-start.17 = (bf16[1024,256]{1,0:T(8,128)(2,1)S(1)}, bf16[1024,256]{1,0:T(8,128)(2,1)S(1)}, u32[]{:S(2)}, u32[]{:S(2)}) collective-permute-start(bf16[1024,256]{1,0:T(8,128)(2,1)S(1)} %collective-permute-done.13.refs_4_), channel_id=1, source_target_pairs={{0,1},{1,0},{2,3},{3,2},{4,5},{5,4},{6,7},{7,6},{8,9},{9,8},{10,11... | collective-permute-start | bytes 1572872 | tf_op jit(solution)/shard_map/ppermute | solution.py:274
  120.2 1.9 %collective-permute-start.20 = (bf16[1024,128]{1,0:T(8,128)(2,1)S(1)}, bf16[1024,128]{1,0:T(8,128)(2,1)S(1)}, u32[]{:S(2)}, u32[]{:S(2)}) collective-permute-start(bf16[1024,128]{1,0:T(8,128)(2,1)S(1)} %collective-permute-done.19.refs_8_), channel_id=1, source_target_pairs={{0,1},{1,0},{2,3},{3,2},{4,5},{5,4},{6,7},{7,6},{8,9},{9,8},{10,11... | collective-permute-start | bytes 786440 | tf_op jit(solution)/shard_map/ppermute | solution.py:274
  120.8 1.4 copy-start.2
  120.8 1.3 copy-start.7
  121.4 24.1 %collective-permute-start.15 = (bf16[2,64,1024]{2,1,0:T(8,128)(2,1)S(1)}, bf16[2,64,1024]{2,1,0:T(8,128)(2,1)S(1)}, u32[]{:S(2)}, u32[]{:S(2)}) collective-permute-start(bf16[2,64,1024]{2,1,0:T(8,128)(2,1)S(1)} %pad_maximum_fusion.2), channel_id=1, source_target_pairs={{0,1},{1,0},{2,3},{3,2},{4,5},{5,4},{6,7},{7,6},{8,9},{9,8},{10,11... | collective-permute-start | bytes 786440 | tf_op jit(solution)/shard_map/ppermute | solution.py:274
  141.9 16.3 %all-to-all-start.2 = ((bf16[16,64,384]{2,1,0:T(8,128)(2,1)}), bf16[16,64,384]{2,1,0:T(8,128)(2,1)S(1)}, u32[]{:S(2)}, u32[]{:S(2)}) async-start(bf16[16,64,384]{2,1,0:T(8,128)(2,1)} %pad_maximum_fusion), calls=%async_computation.2 | async-start | bytes 1572864 | tf_op jit(solution)/shard_map/all_to_all | solution.py:287
  147.7 13.2 %collective-permute-start.24 = (f32[16,1024]{1,0:T(8,128)S(1)}, f32[16,1024]{1,0:T(8,128)S(1)}, u32[]{:S(2)}, u32[]{:S(2)}) collective-permute-start(f32[16,1024]{1,0:T(8,128)S(1)} %get-tuple-element.86), channel_id=1, source_target_pairs={{0,6},{2,4},{4,2},{6,0},{1,7},{3,5},{5,3},{7,1},{8,14},{10,12},{12... | collective-permute-start | bytes 196616 | tf_op jit(solution)/shard_map/ppermute | solution.py:591
  149.6 11.3 %collective-permute-start.23 = (f32[16,1024]{1,0:T(8,128)S(1)}, f32[16,1024]{1,0:T(8,128)S(1)}, u32[]{:S(2)}, u32[]{:S(2)}) collective-permute-start(f32[16,1024]{1,0:T(8,128)S(1)} %get-tuple-element.87), channel_id=1, source_target_pairs={{0,4},{2,6},{4,0},{6,2},{1,5},{3,7},{5,1},{7,3},{8,12},{10,14},{12... | collective-permute-start | bytes 196616 | tf_op jit(solution)/shard_map/ppermute | solution.py:591
  149.6 11.3 %collective-permute-start.22 = (f32[16,1024]{1,0:T(8,128)S(1)}, f32[16,1024]{1,0:T(8,128)S(1)}, u32[]{:S(2)}, u32[]{:S(2)}) collective-permute-start(f32[16,1024]{1,0:T(8,128)S(1)} %get-tuple-element.85), channel_id=1, source_target_pairs={{0,2},{2,0},{4,6},{6,4},{1,3},{3,1},{5,7},{7,5},{8,10},{10,8},{12,... | collective-permute-start | bytes 196616 | tf_op jit(solution)/shard_map/ppermute | solution.py:591
  158.2 4.0 %collective-permute-start.21 = (bf16[8,64,384]{2,1,0:T(8,128)(2,1)S(1)}, bf16[8,64,384]{2,1,0:T(8,128)(2,1)S(1)}, u32[]{:S(2)}, u32[]{:S(2)}) collective-permute-start(bf16[8,64,384]{2,1,0:T(8,128)(2,1)S(1)} %constant_dynamic-slice_fusion), channel_id=1, source_target_pairs={{0,1},{1,0},{2,3},{3,2},{4,5},{5,4},{6,7},{7,6},{8,9},{9,8},{10,11... | collective-permute-start | bytes 1179656 | tf_op jit(solution)/shard_map/ppermute | solution.py:274
  160.9 2.4 %collective-permute-start.25 = (f32[8,1024]{1,0:T(8,128)S(1)}, f32[8,1024]{1,0:T(8,128)S(1)}, u32[]{:S(2)}, u32[]{:S(2)}) collective-permute-start(f32[8,1024]{1,0:T(8,128)S(1)} %dynamic-slice_bitcast_fusion.3), channel_id=1, source_target_pairs={{0,1},{1,0},{2,3},{3,2},{4,5},{5,4},{6,7},{7,6},{8,9},{9,8},{10,11... | collective-permute-start | bytes 98312 | tf_op jit(solution)/shard_map/ppermute | solution.py:274

commit v11 on v10

--- a/solution.py
+++ b/solution.py
@@ -411,7 +411,7 @@
                 out[h, :, head_cols(t)] = x[rows, head_cols(h)]
 
 
-def fill_body(core_ref, xh_ref, own_ref, peer_ref, w0, w1, w2, w3, out_ref):
+def fill_body(core_ref, xh_ref, xl_ref, own_ref, peer_ref, w0, w1, w2, w3, out_ref):
     core, xh = core_ref[0], xh_ref[0]
     out_ref[pl.ds(core * HEADS, HEADS), :, : 3 * HEAD] = own_ref[...]
     out_ref[pl.ds((1 - core) * HEADS, HEADS), :, : 3 * HEAD] = peer_ref[...]
@@ -472,13 +472,12 @@
 
 def local(query_states, key_states, value_states, span_order, block_mask, output_weight, upstream):
     z, y, xl, xh, core = (lax.axis_index(a) for a in ("z", "y", "xl", "xh", "core"))
-    first_core = core == 0
     half = core ^ ((z + y) % 2)
     core_1, xl_1, xh_1, half_1 = (x.reshape(1) for x in (core, xl, xh, half))
     cols = output_weight.shape[1] // 2
 
     weight_far = lax.ppermute(output_weight, "xh", SWAP)
-    weight_rows = [output_weight, other_core(output_weight), weight_far, other_core(weight_far)]
+    weight_rows = [in_hbm(output_weight), other_core(output_weight), weight_far, other_core(weight_far)]
     unit_rows = (HEADS, SPAN, 3 * HEAD)
     own, sent = move(
         cut_body,
@@ -494,7 +493,7 @@
         fill_body,
         "fill",
         [(UNITS, SPAN, 3 * HEAD + 512)],
-        [core_1, xh_1],
+        [core_1, xh_1, xl_1],
         in_hbm(own),
         other_core(sent),
         *weight_rows,
@@ -514,6 +513,7 @@
     own_kv, span_order, wide, side, which = lax.optimization_barrier(
         (own_kv, span_order, upstream[0], xl, core)
     )
+    first_core = which == 0
     bias = span_bias(span_order, block_mask, side, which)
 
     up_sent = jnp.where(first_core, wide[:, cols:], wide[:, :cols])

time: 165 us -> 159 us (0.964)
  blocking collectives: 0 us -> 32.9 us
  waiting for transfers between devices: 56 us -> 28.1 us
  starting transfers between devices: 45.7 us -> 37.4 us
  local copies, waits for them, and re-layouts: 2.18 us -> 0.14 us
    all_to_all x0 -> x1, blocking collectives: none -> 32.9 us  [exchange(): return lax.all_to_all(x, axes, 0, 0, tiled=True)]
    all_to_all x4 -> x3, waiting for transfers between devices: 48.2 us -> 20.1 us  [exchange(): return lax.all_to_all(x, axes, 0, 0, tiled=True)]
    all_to_all x4 -> x3, starting transfers between devices: 19.8 us -> 11.8 us  [exchange(): return lax.all_to_all(x, axes, 0, 0, tiled=True)]
    unnamed x26 -> x22, local copies, waits for them, and re-layouts: 2.09 us -> 0.05 us
  transfers between devices with their start and end apart: 30 -> 29, of which waited for: 12 -> 11; matrix products, arithmetic and copies ran while one was open for 3% -> 4% of each run, Pallas kernels for 26% -> 27%
where the time goes in v11:
time: 159 us
  Pallas kernels  53 us (33%)
  starting transfers between devices  37.4 us (24%)
  blocking collectives  32.9 us (21%)
  waiting for transfers between devices  28.1 us (18%)
  other arithmetic  4.89 us (3%)
    all_to_all x1, blocking collectives, exchange(): return lax.all_to_all(x, axes, 0, 0, tiled=True)  32.9 us
    all_to_all x3, waiting for transfers between devices, exchange(): return lax.all_to_all(x, axes, 0, 0, tiled=True)  20.1 us
    pallas_call x2, Pallas kernels, forward(): pl.pallas_call(functools.partial(forward_body, first), out_shape=outs, gr...  14 us
    ppermute x16, starting transfers between devices, other_core(): return lax.ppermute(x, 'core', SWAP)  12.6 us
    pallas_call x1, Pallas kernels, key_grad(): pl.pallas_call(key_body, out_shape=[jax.ShapeDtypeStruct((ROWS, HEAD), BF...  11.9 us
    all_to_all x3, starting transfers between devices, exchange(): return lax.all_to_all(x, axes, 0, 0, tiled=True)  11.8 us
    pallas_call x7, Pallas kernels, move(): pl.pallas_call(run, out_shape=[make(shape, BF16) for make, shape in zip(s...  10.4 us
    pallas_call x1, Pallas kernels, query_grad(): pl.pallas_call(query_body, out_shape=jax.ShapeDtypeStruct((ROWS, HEAD), B...  10.1 us
  transfers between devices with their start and end apart: 29, of which 11 were waited for; matrix products, arithmetic and copies ran while one was open for 4% of the time, Pallas kernels for 27%

profile of v11, /device:TPU:1, one launch (start us, length us, event | category | flops | bytes accessed | tf_op | source)
XLA Modules:
  0.0 158.7 jit_solution(5345640042308461140)
XLA Ops:
  0.6 2.1 %cut.1 = (bf16[8,64,384]{2,1,0:T(8,128)(2,1)}, bf16[8,64,384]{2,1,0:T(8,128)(2,1)}) custom-call(s32[1]{0:T(128)} %bitcast.3.refs_0_.refs_1_, bf16[128,1024]{1,0:T(8,128)(2,1)} %bitcast.59, bf16[128,1024]{1,0:T(8,128)(2,1)} %bitcast.60, bf16[128,1024]{1,0:T(8,128)(2,1)} %bitcast.61), custom_call_target="tpu_custom_call" | custom-call | bytes 4194304 | tf_op jit(solution)/shard_map/cut/pallas_call | solution.py:384
  2.8 1.4 collective-permute-start
  4.2 2.8 %collective-permute-start.2 = (bf16[8,2048]{1,0:T(8,128)(2,1)}, bf16[8,2048]{1,0:T(8,128)(2,1)S(1)}, u32[]{:S(2)}, u32[]{:S(2)}) collective-permute-start(bf16[8,2048]{1,0:T(8,128)(2,1)} %refs_5_.1), channel_id=1, source_target_pairs={{0,2},{2,0},{1,3},{3,1},{4,6},{6,4},{5,7},{7,5},{8,10},{10,8},{9,1... | collective-permute-start | bytes 98312 | tf_op jit(solution)/shard_map/ppermute | solution.py:479
  7.3 1.4 collective-permute-done.2.refs_7_
  8.7 1.2 collective-permute-start.3
  9.8 0.9 collective-permute-done.3.refs_8_
  10.7 1.2 fill.1
  11.9 32.9 %all_to_all.20.refs_0_ = bf16[16,64,896]{2,1,0:T(8,128)(2,1)S(1)} all-to-all(bf16[16,64,896]{2,1,0:T(8,128)(2,1)S(1)} %fill.1), channel_id=1, replica_groups=mesh['z'=4,'y'=4,'xl'=2,'xh'=2,'core'=2] {'z','y'}, dimensions={0} | all-to-all | bytes 3670016 | tf_op jit(solution)/shard_map/all_to_all | solution.py:287
  44.7 1.4 split.1
  46.1 1.2 collective-permute-start.4
  47.3 1.7 %collective-permute-start.5 = (bf16[1024,256]{1,0:T(8,128)(2,1)}, bf16[1024,256]{1,0:T(8,128)(2,1)S(1)}, u32[]{:S(2)}, u32[]{:S(2)}) collective-permute-start(bf16[1024,256]{1,0:T(8,128)(2,1)} %get-tuple-element.48.refs_1_.kv0.refs_0_), channel_id=1, source_target_pairs={{0,1},{1,0},{2,3},{3,2},{4,5},{5,4},{6,7},{7,6},{8,9},{9,8},{10,11... | collective-permute-start | bytes 1572872 | tf_op jit(solution)/shard_map/ppermute | solution.py:274
  49.2 1.9 %collective-permute-start.8 = (bf16[12,64,512]{2,1,0:T(8,128)(2,1)}, bf16[12,64,512]{2,1,0:T(8,128)(2,1)S(1)}, u32[]{:S(2)}, u32[]{:S(2)}) collective-permute-start(bf16[12,64,512]{2,1,0:T(8,128)(2,1)} %get-tuple-element.60.own0), channel_id=1, source_target_pairs={{0,6},{2,4},{4,2},{6,0},{1,7},{3,5},{5,3},{7,1},{8,14},{10,12},{12... | collective-permute-start | bytes 2359304 | tf_op jit(solution)/shard_map/ppermute | solution.py:315
  51.7 1.9 %up.1.up_ref = bf16[256,1024]{1,0:T(8,128)(2,1)} custom-call(s32[1]{0:T(128)} %bitcast.refs_0_, s32[1]{0:T(128)} %bitcast.3.refs_0_.refs_1_, bf16[128,2048]{1,0:T(8,128)(2,1)} %bitcast.51, bf16[128,1024]{1,0:T(8,128)(2,1)S(1)} %collective-permute-done.6.refs_3_), custom_call_target="tpu_custom_call" | custom-call | bytes 4194304 | tf_op jit(solution)/shard_map/up/pallas_call | solution.py:384
  53.5 6.6 %forward_near.1 = (f32[128,1024]{1,0:T(8,128)}, f32[1,1024]{1,0:T(1,128)S(1)}, f32[1,1024]{1,0:T(1,128)S(1)}) custom-call(bf16[1024,128]{1,0:T(8,128)(2,1)} %get-tuple-element.47.refs_0_, bf16[1024,256]{1,0:T(8,128)(2,1)} %get-tuple-element.48.refs_1_.kv0.refs_0_, bf16[1024,256]{1,0:T(8,128)(2,1)S(1)} %collective-permute-done.5.refs_2_.kv1, ...), custom_call_target="tpu_custom_call" | custom-call | flops 2147483648 | bytes 4194304 | tf_op jit(solution)/shard_map/forward_near/pallas_call | solution.py:132
  60.1 0.8 collective-permute-start.7
  60.9 1.0 collective-permute-start.9
  61.9 0.6 collective-permute-done.7.refs_2_.kv3
  62.5 7.4 %forward_far.1 = (bf16[1024,256]{1,0:T(8,128)(2,1)}, f32[1,1024]{1,0:T(1,128)S(1)}) custom-call(bf16[1024,128]{1,0:T(8,128)(2,1)} %get-tuple-element.47.refs_0_, bf16[1024,256]{1,0:T(8,128)(2,1)S(1)} %collective-permute-done.4.refs_1_.kv2, bf16[1024,256]{1,0:T(8,128)(2,1)S(1)} %collective-permute-done.7.refs_2_.kv3, ...), custom_call_target="tpu_custom_call" | custom-call | flops 2147483648 | bytes 4194304 | tf_op jit(solution)/shard_map/forward_far/pallas_call | solution.py:132
  69.9 3.5 %weight_whole.1 = (bf16[1024,1024]{1,0:T(8,128)(2,1)}, f32[128,1024]{1,0:T(8,128)S(1)}, f32[128,1024]{1,0:T(8,128)S(1)}) custom-call(s32[1]{0:T(128)} %bitcast.2.refs_2_.xl_ref, bf16[12,64,512]{2,1,0:T(8,128)(2,1)} %get-tuple-element.60.own0, bf16[4,64,512]{2,1,0:T(8,128)(2,1)} %get-tuple-element.61.own1, ...), custom_call_target="tpu_custom_call" | custom-call | flops 536870912 | bytes 4194304 | tf_op jit(solution)/shard_map/weight_whole/pallas_call | solution.py:331
  73.4 0.7 collective-permute-start.10
  74.2 1.5 collective-permute-done.10.refs_2_
  75.7 1.9 %cross.1 = bf16[16,64,256]{2,1,0:T(8,128)(2,1)} custom-call(bf16[1024,256]{1,0:T(8,128)(2,1)} %get-tuple-element.68.refs_0_.pair_ref.refs_2_, f32[128,1024]{1,0:T(8,128)S(1)} %get-tuple-element.63.refs_1_, f32[128,1024]{1,0:T(8,128)S(1)} %collective-permute-done.10.refs_2_), custom_call_target="tpu_custom_call" | custom-call | bytes 4194304 | tf_op jit(solution)/shard_map/cross/pallas_call | solution.py:384
  77.6 3.6 %all-to-all-start.1 = ((bf16[16,64,256]{2,1,0:T(8,128)(2,1)}), bf16[16,64,256]{2,1,0:T(8,128)(2,1)S(1)}, u32[]{:S(2)}, u32[]{:S(2)}) async-start(bf16[16,64,256]{2,1,0:T(8,128)(2,1)} %cross.1), calls=%async_computation.1 | async-start | bytes 1048576 | tf_op jit(solution)/shard_map/all_to_all | solution.py:287
  81.7 0.8 collective-permute-done.11
  82.5 0.7 collective-permute-start.12
  83.2 2.2 %collective-permute-done.12 = f32[2,1024]{1,0:T(2,128)S(1)} collective-permute-done((f32[2,1024]{1,0:T(2,128)S(1)}, f32[2,1024]{1,0:T(2,128)S(1)}, u32[]{:S(2)}, u32[]{:S(2)}) %collective-permute-start.12) | collective-permute-done | bytes 8224 | tf_op jit(solution)/shard_map/ppermute | solution.py:278
  85.4 6.8 %all-to-all-done.1.refs_0_ = bf16[16,64,256]{2,1,0:T(8,128)(2,1)S(1)} async-done(((bf16[16,64,256]{2,1,0:T(8,128)(2,1)}), bf16[16,64,256]{2,1,0:T(8,128)(2,1)S(1)}, u32[]{:S(2)}, u32[]{:S(2)}) %all-to-all-start.1) | async-done | bytes 524320 | tf_op jit(solution)/shard_map/all_to_all | solution.py:287
  92.2 0.8 land.1
  93.0 1.5 collective-permute-start.14
  94.5 0.6 collective-permute-start.13
  95.6 0.8 collective-permute-start.19
  96.4 3.2 %weight_terms.1 = (bf16[1024,1024]{1,0:T(8,128)(2,1)}, f32[8,128]{1,0:T(8,128)S(1)}) custom-call(bf16[128,1024]{1,0:T(8,128)(2,1)S(1)} %get-tuple-element.66.own_ref, bf16[128,1024]{1,0:T(8,128)(2,1)S(1)} %collective-permute-done.14.peer_ref, bf16[256,1024]{1,0:T(8,128)(2,1)} %up.1.up_ref), custom_call_target="tpu_custom_call" | custom-call | flops 536870912 | bytes 4194304 | tf_op jit(solution)/shard_map/weight_terms/pallas_call | solution.py:360
  99.6 4.6 %all-to-all-start.3 = ((bf16[16,64,1024]{2,1,0:T(8,128)(2,1)}), bf16[16,64,1024]{2,1,0:T(8,128)(2,1)}, u32[]{:S(2)}, u32[]{:S(2)}) async-start(bf16[16,64,1024]{2,1,0:T(8,128)(2,1)} %bitcast.50), calls=%async_computation.3 | async-start | bytes 4194304 | tf_op jit(solution)/shard_map/all_to_all | solution.py:287
  104.2 10.1 %query_grad.1 = bf16[1024,128]{1,0:T(8,128)(2,1)S(1)} custom-call(bf16[1024,256]{1,0:T(8,128)(2,1)} %get-tuple-element.68.refs_0_.pair_ref.refs_2_, bf16[1024,128]{1,0:T(8,128)(2,1)} %get-tuple-element.71.g_ref.refs_6_, f32[1,1024]{1,0:T(1,128)S(1)} %get-tuple-element.72.lse_ref, bf16[1024,256]{1,0:T(8,128)(2,1)} %get-tuple-element.48.refs_1_.kv0.refs_0_, ...), custom_call_target="tpu_custom_call" | custom-call | flops 6442450944 | bytes 4194304 | tf_op jit(solution)/shard_map/query_grad/pallas_call | solution.py:183
  114.3 0.6 collective-permute-start.17
  116.1 0.5 collective-permute-start.15
  116.9 11.9 %key_grad.1 = (bf16[1024,128]{1,0:T(8,128)(2,1)S(1)}, bf16[1024,128]{1,0:T(8,128)(2,1)S(1)}) custom-call(bf16[1024,256]{1,0:T(8,128)(2,1)} %get-tuple-element.48.refs_1_.kv0.refs_0_, f32[64,128]{1,0:T(8,128)S(1)} %pad.4.refs_3_.bias_ref.refs_1_, bf16[1024,256]{1,0:T(8,128)(2,1)S(1)} %copy-done.1, bf16[1024,256]{1,0:T(8,128)(2,1)S(1)} %collective-permute-done.16.refs_3_, ...), custom_call_target="tpu_custom_call" | custom-call | flops 8589934592 | bytes 4194304 | tf_op jit(solution)/shard_map/key_grad/pallas_call | solution.py:244
  128.8 1.0 pad_maximum_fusion
  129.8 6.8 %all-to-all-done.3 = bf16[16,64,1024]{2,1,0:T(8,128)(2,1)} async-done(((bf16[16,64,1024]{2,1,0:T(8,128)(2,1)}), bf16[16,64,1024]{2,1,0:T(8,128)(2,1)}, u32[]{:S(2)}, u32[]{:S(2)}) %all-to-all-start.3) | async-done | bytes 2097184 | tf_op jit(solution)/shard_map/all_to_all | solution.py:287
  136.6 3.6 %all-to-all-start.2 = ((bf16[16,64,384]{2,1,0:T(8,128)(2,1)}), bf16[16,64,384]{2,1,0:T(8,128)(2,1)S(1)}, u32[]{:S(2)}, u32[]{:S(2)}) async-start(bf16[16,64,384]{2,1,0:T(8,128)(2,1)} %pad_maximum_fusion), calls=%async_computation.2 | async-start | bytes 1572864 | tf_op jit(solution)/shard_map/all_to_all | solution.py:287
  140.3 2.0 %convert_reduce_fusion = f32[64,1024]{1,0:T(8,128)S(1)} fusion(bf16[16,64,1024]{2,1,0:T(8,128)(2,1)} %all-to-all-done.3), kind=kLoop, calls=%fused_computation | loop fusion | flops 2031616 | bytes 2359296 | tf_op jit(solution)/shard_map/reduce_sum | solution.py:586
  142.4 2.0 %collective-permute-start.24 = (f32[16,1024]{1,0:T(8,128)S(1)}, f32[16,1024]{1,0:T(8,128)S(1)}, u32[]{:S(2)}, u32[]{:S(2)}) collective-permute-start(f32[16,1024]{1,0:T(8,128)S(1)} %get-tuple-element.86), channel_id=1, source_target_pairs={{0,6},{2,4},{4,2},{6,0},{1,7},{3,5},{5,3},{7,1},{8,14},{10,12},{12... | collective-permute-start | bytes 196616 | tf_op jit(solution)/shard_map/ppermute | solution.py:591
  144.3 2.0 %collective-permute-start.22 = (f32[16,1024]{1,0:T(8,128)S(1)}, f32[16,1024]{1,0:T(8,128)S(1)}, u32[]{:S(2)}, u32[]{:S(2)}) collective-permute-start(f32[16,1024]{1,0:T(8,128)S(1)} %get-tuple-element.85), channel_id=1, source_target_pairs={{0,2},{2,0},{4,6},{6,4},{1,3},{3,1},{5,7},{7,5},{8,10},{10,8},{12,... | collective-permute-start | bytes 196616 | tf_op jit(solution)/shard_map/ppermute | solution.py:591
  146.3 6.6 %all-to-all-done.2.refs_2_ = bf16[16,64,384]{2,1,0:T(8,128)(2,1)S(1)} async-done(((bf16[16,64,384]{2,1,0:T(8,128)(2,1)}), bf16[16,64,384]{2,1,0:T(8,128)(2,1)S(1)}, u32[]{:S(2)}, u32[]{:S(2)}) %all-to-all-start.2) | async-done | bytes 786464 | tf_op jit(solution)/shard_map/all_to_all | solution.py:287
  153.0 2.6 %collective-permute-start.21 = (bf16[8,64,384]{2,1,0:T(8,128)(2,1)S(1)}, bf16[8,64,384]{2,1,0:T(8,128)(2,1)S(1)}, u32[]{:S(2)}, u32[]{:S(2)}) collective-permute-start(bf16[8,64,384]{2,1,0:T(8,128)(2,1)S(1)} %constant_dynamic-slice_fusion), channel_id=1, source_target_pairs={{0,1},{1,0},{2,3},{3,2},{4,5},{5,4},{6,7},{7,6},{8,9},{9,8},{10,11... | collective-permute-start | bytes 1179656 | tf_op jit(solution)/shard_map/ppermute | solution.py:274
  155.8 0.8 maximum_bitcast_fusion
  156.9 1.1 final.1
  158.0 0.6 pad_maximum_fusion.4
  (68 shorter events, 4.0 us)
Async XLA Ops:
  2.8 7.9 %collective-permute-start = (bf16[8,64,384]{2,1,0:T(8,128)(2,1)}, bf16[8,64,384]{2,1,0:T(8,128)(2,1)S(1)}, u32[]{:S(2)}, u32[]{:S(2)}) collective-permute-start(bf16[8,64,384]{2,1,0:T(8,128)(2,1)} %get-tuple-element.44), channel_id=1, source_target_pairs={{0,1},{1,0},{2,3},{3,2},{4,5},{5,4},{6,7},{7,6},{8,9},{9,8},{10,11... | collective-permute-start | bytes 1179656 | tf_op jit(solution)/shard_map/ppermute | solution.py:274
  4.2 4.5 %collective-permute-start.2 = (bf16[8,2048]{1,0:T(8,128)(2,1)}, bf16[8,2048]{1,0:T(8,128)(2,1)S(1)}, u32[]{:S(2)}, u32[]{:S(2)}) collective-permute-start(bf16[8,2048]{1,0:T(8,128)(2,1)} %refs_5_.1), channel_id=1, source_target_pairs={{0,2},{2,0},{1,3},{3,1},{4,6},{6,4},{5,7},{7,5},{8,10},{10,8},{9,1... | collective-permute-start | bytes 98312 | tf_op jit(solution)/shard_map/ppermute | solution.py:479
  7.0 2.8 %collective-permute-start.1 = (bf16[8,2048]{1,0:T(8,128)(2,1)}, bf16[8,2048]{1,0:T(8,128)(2,1)S(1)}, u32[]{:S(2)}, u32[]{:S(2)}) collective-permute-start(bf16[8,2048]{1,0:T(8,128)(2,1)} %refs_5_.1), channel_id=1, source_target_pairs={{0,1},{1,0},{2,3},{3,2},{4,5},{5,4},{6,7},{7,6},{8,9},{9,8},{10,11... | collective-permute-start | bytes 98312 | tf_op jit(solution)/shard_map/ppermute | solution.py:274
  8.7 2.0 %collective-permute-start.3 = (bf16[8,2048]{1,0:T(8,128)(2,1)S(1)}, bf16[8,2048]{1,0:T(8,128)(2,1)S(1)}, u32[]{:S(2)}, u32[]{:S(2)}) collective-permute-start(bf16[8,2048]{1,0:T(8,128)(2,1)S(1)} %collective-permute-done.2.refs_7_), channel_id=1, source_target_pairs={{0,1},{1,0},{2,3},{3,2},{4,5},{5,4},{6,7},{7,6},{8,9},{9,8},{10,11... | collective-permute-start | bytes 98312 | tf_op jit(solution)/shard_map/ppermute | solution.py:274
  11.9 37.2 %copy-start.7 = (bf16[1,128,2048]{2,1,0:T(8,128)(2,1)S(1)}, bf16[1,128,2048]{2,1,0:T(8,128)(2,1)}, u32[]{:S(2)}) copy-start(bf16[1,128,2048]{2,1,0:T(8,128)(2,1)} %param.13) | copy-start | bytes 1572868
  44.7 6.4 %copy-start.10 = (s32[64]{0:T(128)S(1)}, s32[64]{0:T(128)}, u32[]{:S(2)}) copy-start(s32[64]{0:T(128)} %param.10) | copy-start | bytes 772
  44.7 6.6 %copy-start.9 = (s32[64,64]{1,0:T(8,128)S(1)}, s32[64,64]{1,0:T(8,128)}, u32[]{:S(2)}) copy-start(s32[64,64]{1,0:T(8,128)} %param.11) | copy-start | bytes 49156
  46.1 14.0 %collective-permute-start.4 = (bf16[1024,256]{1,0:T(8,128)(2,1)}, bf16[1024,256]{1,0:T(8,128)(2,1)S(1)}, u32[]{:S(2)}, u32[]{:S(2)}) collective-permute-start(bf16[1024,256]{1,0:T(8,128)(2,1)} %get-tuple-element.48.refs_1_.kv0.refs_0_), channel_id=1, source_target_pairs={{0,4},{4,0},{1,5},{5,1},{2,6},{6,2},{3,7},{7,3},{8,12},{12,8},{9,1... | collective-permute-start | bytes 1572872 | tf_op jit(solution)/shard_map/ppermute | solution.py:278
  47.3 6.2 %collective-permute-start.5 = (bf16[1024,256]{1,0:T(8,128)(2,1)}, bf16[1024,256]{1,0:T(8,128)(2,1)S(1)}, u32[]{:S(2)}, u32[]{:S(2)}) collective-permute-start(bf16[1024,256]{1,0:T(8,128)(2,1)} %get-tuple-element.48.refs_1_.kv0.refs_0_), channel_id=1, source_target_pairs={{0,1},{1,0},{2,3},{3,2},{4,5},{5,4},{6,7},{7,6},{8,9},{9,8},{10,11... | collective-permute-start | bytes 1572872 | tf_op jit(solution)/shard_map/ppermute | solution.py:274
  49.1 2.5 %collective-permute-start.6 = (bf16[128,1024]{1,0:T(8,128)(2,1)S(1)}, bf16[128,1024]{1,0:T(8,128)(2,1)S(1)}, u32[]{:S(2)}, u32[]{:S(2)}) collective-permute-start(bf16[128,1024]{1,0:T(8,128)(2,1)S(1)} %slice_select_fusion), channel_id=1, source_target_pairs={{0,1},{1,0},{2,3},{3,2},{4,5},{5,4},{6,7},{7,6},{8,9},{9,8},{10,11... | collective-permute-start | bytes 786440 | tf_op jit(solution)/shard_map/ppermute | solution.py:274
  49.2 20.7 %collective-permute-start.8 = (bf16[12,64,512]{2,1,0:T(8,128)(2,1)}, bf16[12,64,512]{2,1,0:T(8,128)(2,1)S(1)}, u32[]{:S(2)}, u32[]{:S(2)}) collective-permute-start(bf16[12,64,512]{2,1,0:T(8,128)(2,1)} %get-tuple-element.60.own0), channel_id=1, source_target_pairs={{0,6},{2,4},{4,2},{6,0},{1,7},{3,5},{5,3},{7,1},{8,14},{10,12},{12... | collective-permute-start | bytes 2359304 | tf_op jit(solution)/shard_map/ppermute | solution.py:315
  53.5 6.6 %copy-start.3 = (bf16[1024,256]{1,0:T(8,128)(2,1)}, bf16[1024,256]{1,0:T(8,128)(2,1)S(1)}, u32[]{:S(2)}) copy-start(bf16[1024,256]{1,0:T(8,128)(2,1)S(1)} %collective-permute-done.5.refs_2_.kv1) | copy-start | bytes 1572868
  53.5 7.4 %copy-start.8 = (bf16[4,64,512]{2,1,0:T(8,128)(2,1)S(1)}, bf16[4,64,512]{2,1,0:T(8,128)(2,1)}, u32[]{:S(2)}) copy-start(bf16[4,64,512]{2,1,0:T(8,128)(2,1)} %get-tuple-element.61.own1) | copy-start | bytes 786436
  60.1 9.8 %copy-start.2 = (bf16[1024,256]{1,0:T(8,128)(2,1)}, bf16[1024,256]{1,0:T(8,128)(2,1)S(1)}, u32[]{:S(2)}) copy-start(bf16[1024,256]{1,0:T(8,128)(2,1)S(1)} %collective-permute-done.4.refs_1_.kv2) | copy-start | bytes 1572868
  60.1 2.3 %collective-permute-start.7 = (bf16[1024,256]{1,0:T(8,128)(2,1)S(1)}, bf16[1024,256]{1,0:T(8,128)(2,1)S(1)}, u32[]{:S(2)}, u32[]{:S(2)}) collective-permute-start(bf16[1024,256]{1,0:T(8,128)(2,1)S(1)} %collective-permute-done.4.refs_1_.kv2), channel_id=1, source_target_pairs={{0,1},{1,0},{2,3},{3,2},{4,5},{5,4},{6,7},{7,6},{8,9},{9,8},{10,11... | collective-permute-start | bytes 1572872 | tf_op jit(solution)/shard_map/ppermute | solution.py:274
  60.9 9.0 %collective-permute-start.9 = (bf16[4,64,512]{2,1,0:T(8,128)(2,1)S(1)}, bf16[4,64,512]{2,1,0:T(8,128)(2,1)S(1)}, u32[]{:S(2)}, u32[]{:S(2)}) collective-permute-start(bf16[4,64,512]{2,1,0:T(8,128)(2,1)S(1)} %copy-done.8), channel_id=1, source_target_pairs={{0,4},{4,0},{1,5},{5,1},{2,6},{6,2},{3,7},{7,3},{8,12},{12,8},{9,1... | collective-permute-start | bytes 786440 | tf_op jit(solution)/shard_map/ppermute | solution.py:278
  62.5 7.5 %copy-start.4 = (bf16[1024,256]{1,0:T(8,128)(2,1)}, bf16[1024,256]{1,0:T(8,128)(2,1)S(1)}, u32[]{:S(2)}) copy-start(bf16[1024,256]{1,0:T(8,128)(2,1)S(1)} %collective-permute-done.7.refs_2_.kv3) | copy-start | bytes 1572868
  73.4 21.0 %copy-start = (bf16[1024,256]{1,0:T(8,128)(2,1)S(1)}, bf16[1024,256]{1,0:T(8,128)(2,1)}, u32[]{:S(2)}) copy-start(bf16[1024,256]{1,0:T(8,128)(2,1)} %get-tuple-element.68.refs_0_.pair_ref.refs_2_) | copy-start | bytes 1572868
  73.4 2.3 %collective-permute-start.10 = (f32[128,1024]{1,0:T(8,128)S(1)}, f32[128,1024]{1,0:T(8,128)S(1)}, u32[]{:S(2)}, u32[]{:S(2)}) collective-permute-start(f32[128,1024]{1,0:T(8,128)S(1)} %get-tuple-element.64), channel_id=1, source_target_pairs={{0,1},{1,0},{2,3},{3,2},{4,5},{5,4},{6,7},{7,6},{8,9},{9,8},{10,11... | collective-permute-start | bytes 1572872 | tf_op jit(solution)/shard_map/ppermute | solution.py:274
  77.6 14.5 %all-to-all-start.1 = ((bf16[16,64,256]{2,1,0:T(8,128)(2,1)}), bf16[16,64,256]{2,1,0:T(8,128)(2,1)S(1)}, u32[]{:S(2)}, u32[]{:S(2)}) async-start(bf16[16,64,256]{2,1,0:T(8,128)(2,1)} %cross.1), calls=%async_computation.1 | async-start | bytes 1048576 | tf_op jit(solution)/shard_map/all_to_all | solution.py:287
  81.2 1.3 collective-permute-start.11
  82.5 2.9 %collective-permute-start.12 = (f32[2,1024]{1,0:T(2,128)S(1)}, f32[2,1024]{1,0:T(2,128)S(1)}, u32[]{:S(2)}, u32[]{:S(2)}) collective-permute-start(f32[2,1024]{1,0:T(2,128)S(1)} %pad_maximum_fusion.6), channel_id=1, source_target_pairs={{0,4},{4,0},{1,5},{5,1},{2,6},{6,2},{3,7},{7,3},{8,12},{12,8},{9,1... | collective-permute-start | bytes 24584 | tf_op jit(solution)/shard_map/ppermute | solution.py:278
  93.0 3.5 %collective-permute-start.14 = (bf16[128,1024]{1,0:T(8,128)(2,1)S(1)}, bf16[128,1024]{1,0:T(8,128)(2,1)S(1)}, u32[]{:S(2)}, u32[]{:S(2)}) collective-permute-start(bf16[128,1024]{1,0:T(8,128)(2,1)S(1)} %get-tuple-element.66.own_ref), channel_id=1, source_target_pairs={{0,1},{1,0},{2,3},{3,2},{4,5},{5,4},{6,7},{7,6},{8,9},{9,8},{10,11... | collective-permute-start | bytes 786440 | tf_op jit(solution)/shard_map/ppermute | solution.py:274
  94.5 19.9 %collective-permute-start.13 = (bf16[1024,256]{1,0:T(8,128)(2,1)S(1)}, bf16[1024,256]{1,0:T(8,128)(2,1)S(1)}, u32[]{:S(2)}, u32[]{:S(2)}) collective-permute-start(bf16[1024,256]{1,0:T(8,128)(2,1)S(1)} %copy-done), channel_id=1, source_target_pairs={{0,4},{4,0},{1,5},{5,1},{2,6},{6,2},{3,7},{7,3},{8,12},{12,8},{9,1... | collective-permute-start | bytes 1572872 | tf_op jit(solution)/shard_map/ppermute | solution.py:278
  95.1 21.5 %collective-permute-start.16 = (bf16[1024,256]{1,0:T(8,128)(2,1)S(1)}, bf16[1024,256]{1,0:T(8,128)(2,1)S(1)}, u32[]{:S(2)}, u32[]{:S(2)}) collective-permute-start(bf16[1024,256]{1,0:T(8,128)(2,1)S(1)} %copy-done), channel_id=1, source_target_pairs={{0,1},{1,0},{2,3},{3,2},{4,5},{5,4},{6,7},{7,6},{8,9},{9,8},{10,11... | collective-permute-start | bytes 1572872 | tf_op jit(solution)/shard_map/ppermute | solution.py:274
  95.4 21.3 %collective-permute-start.18 = (bf16[1024,128]{1,0:T(8,128)(2,1)}, bf16[1024,128]{1,0:T(8,128)(2,1)S(1)}, u32[]{:S(2)}, u32[]{:S(2)}) collective-permute-start(bf16[1024,128]{1,0:T(8,128)(2,1)} %get-tuple-element.71.g_ref.refs_6_), channel_id=1, source_target_pairs={{0,1},{1,0},{2,3},{3,2},{4,5},{5,4},{6,7},{7,6},{8,9},{9,8},{10,11... | collective-permute-start | bytes 786440 | tf_op jit(solution)/shard_map/ppermute | solution.py:274
  95.6 19.4 %collective-permute-start.19 = (bf16[1024,128]{1,0:T(8,128)(2,1)}, bf16[1024,128]{1,0:T(8,128)(2,1)S(1)}, u32[]{:S(2)}, u32[]{:S(2)}) collective-permute-start(bf16[1024,128]{1,0:T(8,128)(2,1)} %get-tuple-element.71.g_ref.refs_6_), channel_id=1, source_target_pairs={{0,4},{4,0},{1,5},{5,1},{2,6},{6,2},{3,7},{7,3},{8,12},{12,8},{9,1... | collective-permute-start | bytes 786440 | tf_op jit(solution)/shard_map/ppermute | solution.py:278
  99.6 37.0 %all-to-all-start.3 = ((bf16[16,64,1024]{2,1,0:T(8,128)(2,1)}), bf16[16,64,1024]{2,1,0:T(8,128)(2,1)}, u32[]{:S(2)}, u32[]{:S(2)}) async-start(bf16[16,64,1024]{2,1,0:T(8,128)(2,1)} %bitcast.50), calls=%async_computation.3 | async-start | bytes 4194304 | tf_op jit(solution)/shard_map/all_to_all | solution.py:287
  104.2 10.9 %copy-start.6 = (bf16[1024,1024]{1,0:T(8,128)(2,1)S(1)}, bf16[1024,1024]{1,0:T(8,128)(2,1)}, u32[]{:S(2)}) copy-start(bf16[1024,1024]{1,0:T(8,128)(2,1)} %get-tuple-element.70) | copy-start | bytes 6291460
  114.3 2.6 %collective-permute-start.17 = (bf16[1024,256]{1,0:T(8,128)(2,1)S(1)}, bf16[1024,256]{1,0:T(8,128)(2,1)S(1)}, u32[]{:S(2)}, u32[]{:S(2)}) collective-permute-start(bf16[1024,256]{1,0:T(8,128)(2,1)S(1)} %collective-permute-done.13.refs_4_), channel_id=1, source_target_pairs={{0,1},{1,0},{2,3},{3,2},{4,5},{5,4},{6,7},{7,6},{8,9},{9,8},{10,11... | collective-permute-start | bytes 1572872 | tf_op jit(solution)/shard_map/ppermute | solution.py:274
  115.0 1.9 %collective-permute-start.20 = (bf16[1024,128]{1,0:T(8,128)(2,1)S(1)}, bf16[1024,128]{1,0:T(8,128)(2,1)S(1)}, u32[]{:S(2)}, u32[]{:S(2)}) collective-permute-start(bf16[1024,128]{1,0:T(8,128)(2,1)S(1)} %collective-permute-done.19.refs_8_), channel_id=1, source_target_pairs={{0,1},{1,0},{2,3},{3,2},{4,5},{5,4},{6,7},{7,6},{8,9},{9,8},{10,11... | collective-permute-start | bytes 786440 | tf_op jit(solution)/shard_map/ppermute | solution.py:274
  115.5 1.4 copy-start.1
  115.6 1.3 copy-start.5
  116.1 24.1 %collective-permute-start.15 = (bf16[2,64,1024]{2,1,0:T(8,128)(2,1)S(1)}, bf16[2,64,1024]{2,1,0:T(8,128)(2,1)S(1)}, u32[]{:S(2)}, u32[]{:S(2)}) collective-permute-start(bf16[2,64,1024]{2,1,0:T(8,128)(2,1)S(1)} %pad_maximum_fusion.2), channel_id=1, source_target_pairs={{0,1},{1,0},{2,3},{3,2},{4,5},{5,4},{6,7},{7,6},{8,9},{9,8},{10,11... | collective-permute-start | bytes 786440 | tf_op jit(solution)/shard_map/ppermute | solution.py:274
  136.6 16.3 %all-to-all-start.2 = ((bf16[16,64,384]{2,1,0:T(8,128)(2,1)}), bf16[16,64,384]{2,1,0:T(8,128)(2,1)S(1)}, u32[]{:S(2)}, u32[]{:S(2)}) async-start(bf16[16,64,384]{2,1,0:T(8,128)(2,1)} %pad_maximum_fusion), calls=%async_computation.2 | async-start | bytes 1572864 | tf_op jit(solution)/shard_map/all_to_all | solution.py:287
  142.4 13.2 %collective-permute-start.24 = (f32[16,1024]{1,0:T(8,128)S(1)}, f32[16,1024]{1,0:T(8,128)S(1)}, u32[]{:S(2)}, u32[]{:S(2)}) collective-permute-start(f32[16,1024]{1,0:T(8,128)S(1)} %get-tuple-element.86), channel_id=1, source_target_pairs={{0,6},{2,4},{4,2},{6,0},{1,7},{3,5},{5,3},{7,1},{8,14},{10,12},{12... | collective-permute-start | bytes 196616 | tf_op jit(solution)/shard_map/ppermute | solution.py:591
  144.3 11.3 %collective-permute-start.23 = (f32[16,1024]{1,0:T(8,128)S(1)}, f32[16,1024]{1,0:T(8,128)S(1)}, u32[]{:S(2)}, u32[]{:S(2)}) collective-permute-start(f32[16,1024]{1,0:T(8,128)S(1)} %get-tuple-element.87), channel_id=1, source_target_pairs={{0,4},{2,6},{4,0},{6,2},{1,5},{3,7},{5,1},{7,3},{8,12},{10,14},{12... | collective-permute-start | bytes 196616 | tf_op jit(solution)/shard_map/ppermute | solution.py:591
  144.3 11.3 %collective-permute-start.22 = (f32[16,1024]{1,0:T(8,128)S(1)}, f32[16,1024]{1,0:T(8,128)S(1)}, u32[]{:S(2)}, u32[]{:S(2)}) collective-permute-start(f32[16,1024]{1,0:T(8,128)S(1)} %get-tuple-element.85), channel_id=1, source_target_pairs={{0,2},{2,0},{4,6},{6,4},{1,3},{3,1},{5,7},{7,5},{8,10},{10,8},{12,... | collective-permute-start | bytes 196616 | tf_op jit(solution)/shard_map/ppermute | solution.py:591
  153.0 4.0 %collective-permute-start.21 = (bf16[8,64,384]{2,1,0:T(8,128)(2,1)S(1)}, bf16[8,64,384]{2,1,0:T(8,128)(2,1)S(1)}, u32[]{:S(2)}, u32[]{:S(2)}) collective-permute-start(bf16[8,64,384]{2,1,0:T(8,128)(2,1)S(1)} %constant_dynamic-slice_fusion), channel_id=1, source_target_pairs={{0,1},{1,0},{2,3},{3,2},{4,5},{5,4},{6,7},{7,6},{8,9},{9,8},{10,11... | collective-permute-start | bytes 1179656 | tf_op jit(solution)/shard_map/ppermute | solution.py:274
  155.7 2.4 %collective-permute-start.25 = (f32[8,1024]{1,0:T(8,128)S(1)}, f32[8,1024]{1,0:T(8,128)S(1)}, u32[]{:S(2)}, u32[]{:S(2)}) collective-permute-start(f32[8,1024]{1,0:T(8,128)S(1)} %dynamic-slice_bitcast_fusion.3), channel_id=1, source_target_pairs={{0,1},{1,0},{2,3},{3,2},{4,5},{5,4},{6,7},{7,6},{8,9},{9,8},{10,11... | collective-permute-start | bytes 98312 | tf_op jit(solution)/shard_map/ppermute | solution.py:274

commit v12 on v11

--- a/solution.py
+++ b/solution.py
@@ -476,6 +476,18 @@
     core_1, xl_1, xh_1, half_1 = (x.reshape(1) for x in (core, xl, xh, half))
     cols = output_weight.shape[1] // 2
 
+    wide = upstream[0]
+    up_sent = jnp.where(core == 0, wide[:, cols:], wide[:, :cols])
+    (up,) = move(
+        up_body,
+        "up",
+        [(4 * SPAN, cols)],
+        [core_1, half_1],
+        in_hbm(wide),
+        other_core(up_sent),
+        space=pltpu.HBM,
+    )
+
     weight_far = lax.ppermute(output_weight, "xh", SWAP)
     weight_rows = [in_hbm(output_weight), other_core(output_weight), weight_far, other_core(weight_far)]
     unit_rows = (HEADS, SPAN, 3 * HEAD)
@@ -497,6 +509,7 @@
         in_hbm(own),
         other_core(sent),
         *weight_rows,
+        after=(in_hbm(up),),
     )
     blocks = exchange(blocks, ZY)
     q, own_kv, *weight_own = move(
@@ -510,25 +523,13 @@
     far_kv = other_chip(own_kv)
     weight_other = [across(weight_own[0]), other_chip(weight_own[1])]
     near_kv = other_core(own_kv)
-    own_kv, span_order, wide, side, which = lax.optimization_barrier(
-        (own_kv, span_order, upstream[0], xl, core)
-    )
+    own_kv, span_order, side, which = lax.optimization_barrier((own_kv, span_order, xl, core))
     first_core = which == 0
     bias = span_bias(span_order, block_mask, side, which)
 
-    up_sent = jnp.where(first_core, wide[:, cols:], wide[:, :cols])
-    (up,) = move(
-        up_body,
-        "up",
-        [(4 * SPAN, cols)],
-        [core_1, half_1],
-        in_hbm(wide),
-        other_core(up_sent),
-        space=pltpu.HBM,
-    )
 
     out, top, total = forward(True, in_hbm(q), (in_hbm(own_kv), near_kv), bias)
-    far_kv, total, up = lax.optimization_barrier((far_kv, total, up))
+    far_kv, total = lax.optimization_barrier((far_kv, total))
     kvs = (own_kv, near_kv, far_kv, other_core(far_kv))
     pair, lse = forward(False, in_hbm(q), kvs[2:], bias, in_hbm(out), top, total)
     lses = jnp.concatenate([lse, other_core(lse)], axis=0)

time: 159 us -> 163 us (1.025)
    ppermute x5, waiting for transfers between devices: 2.17 us -> 5.16 us  [other_chip(): return lax.ppermute(x, 'xl', SWAP)]
  transfers between devices with their start and end apart: 29 -> 29, of which waited for: 11 -> 11; matrix products, arithmetic and copies ran while one was open for 4% -> 4% of each run, Pallas kernels for 27% -> 26%
where the time goes in v12:
time: 163 us; the launch traced here: 162 us
  Pallas kernels  53.1 us (33%)
  starting transfers between devices  38.3 us (23%)
  blocking collectives  33 us (20%)
  waiting for transfers between devices  29.6 us (18%)
  other arithmetic  5.92 us (4%)
    all_to_all x1, blocking collectives, exchange(): return lax.all_to_all(x, axes, 0, 0, tiled=True)  33 us
    all_to_all x3, waiting for transfers between devices, exchange(): return lax.all_to_all(x, axes, 0, 0, tiled=True)  20.2 us
    pallas_call x2, Pallas kernels, forward(): pl.pallas_call(functools.partial(forward_body, first), out_shape=outs, gr...  14 us
    ppermute x16, starting transfers between devices, other_core(): return lax.ppermute(x, 'core', SWAP)  12.7 us
    pallas_call x1, Pallas kernels, key_grad(): pl.pallas_call(key_body, out_shape=[jax.ShapeDtypeStruct((ROWS, HEAD), BF...  11.9 us
    all_to_all x3, starting transfers between devices, exchange(): return lax.all_to_all(x, axes, 0, 0, tiled=True)  11.8 us
    pallas_call x7, Pallas kernels, move(): pl.pallas_call(run, out_shape=[make(shape, BF16) for make, shape in zip(s...  10.4 us
    pallas_call x1, Pallas kernels, query_grad(): pl.pallas_call(query_body, out_shape=jax.ShapeDtypeStruct((ROWS, HEAD), B...  10.1 us
  transfers between devices with their start and end apart: 29, of which 11 were waited for; matrix products, arithmetic and copies ran while one was open for 4% of the time, Pallas kernels for 26%

profile of v12, /device:TPU:1, one launch (start us, length us, event | category | flops | bytes accessed | tf_op | source)
XLA Modules:
  0.0 162.2 jit_solution(6058526932815772544)
XLA Ops:
  0.6 2.1 %cut.1 = (bf16[8,64,384]{2,1,0:T(8,128)(2,1)}, bf16[8,64,384]{2,1,0:T(8,128)(2,1)}) custom-call(s32[1]{0:T(128)} %bitcast.3.refs_0_.refs_1_, bf16[128,1024]{1,0:T(8,128)(2,1)} %bitcast.59, bf16[128,1024]{1,0:T(8,128)(2,1)} %bitcast.60, bf16[128,1024]{1,0:T(8,128)(2,1)} %bitcast.61), custom_call_target="tpu_custom_call" | custom-call | bytes 4194304 | tf_op jit(solution)/shard_map/cut/pallas_call | solution.py:384
  2.8 1.4 collective-permute-start
  4.2 1.1 slice_select_fusion
  5.4 2.9 %collective-permute-start.2 = (bf16[8,2048]{1,0:T(8,128)(2,1)}, bf16[8,2048]{1,0:T(8,128)(2,1)S(1)}, u32[]{:S(2)}, u32[]{:S(2)}) collective-permute-start(bf16[8,2048]{1,0:T(8,128)(2,1)} %refs_5_.1), channel_id=1, source_target_pairs={{0,2},{2,0},{1,3},{3,1},{4,6},{6,4},{5,7},{7,5},{8,10},{10,8},{9,1... | collective-permute-start | bytes 98312 | tf_op jit(solution)/shard_map/ppermute | solution.py:491
  8.3 0.7 collective-permute-start.1
  9.0 1.0 collective-permute-done.2.refs_7_
  9.9 1.6 collective-permute-start.3
  11.5 1.9 %up.1.refs_9_.up_ref = bf16[256,1024]{1,0:T(8,128)(2,1)} custom-call(s32[1]{0:T(128)} %bitcast.refs_0_, s32[1]{0:T(128)} %bitcast.3.refs_0_.refs_1_, bf16[128,2048]{1,0:T(8,128)(2,1)} %bitcast.52, bf16[128,1024]{1,0:T(8,128)(2,1)S(1)} %collective-permute-done.4.refs_3_), custom_call_target="tpu_custom_call" | custom-call | bytes 4194304 | tf_op jit(solution)/shard_map/up/pallas_call | solution.py:384
  13.4 1.2 fill.1
  14.6 33.0 %all_to_all.20.refs_0_ = bf16[16,64,896]{2,1,0:T(8,128)(2,1)S(1)} all-to-all(bf16[16,64,896]{2,1,0:T(8,128)(2,1)S(1)} %fill.1), channel_id=1, replica_groups=mesh['z'=4,'y'=4,'xl'=2,'xh'=2,'core'=2] {'z','y'}, dimensions={0} | all-to-all | bytes 3670016 | tf_op jit(solution)/shard_map/all_to_all | solution.py:287
  47.6 1.4 split.1
  48.9 1.3 collective-permute-start.6
  50.3 1.2 collective-permute-start.5
  51.5 1.8 %collective-permute-start.8 = (bf16[12,64,512]{2,1,0:T(8,128)(2,1)}, bf16[12,64,512]{2,1,0:T(8,128)(2,1)S(1)}, u32[]{:S(2)}, u32[]{:S(2)}) collective-permute-start(bf16[12,64,512]{2,1,0:T(8,128)(2,1)} %get-tuple-element.57.own0), channel_id=1, source_target_pairs={{0,6},{2,4},{4,2},{6,0},{1,7},{3,5},{5,3},{7,1},{8,14},{10,12},{12... | collective-permute-start | bytes 2359304 | tf_op jit(solution)/shard_map/ppermute | solution.py:315
  53.9 6.6 %forward_near.1 = (f32[128,1024]{1,0:T(8,128)}, f32[1,1024]{1,0:T(1,128)S(1)}, f32[1,1024]{1,0:T(1,128)S(1)}) custom-call(bf16[1024,128]{1,0:T(8,128)(2,1)} %get-tuple-element.45.refs_0_, bf16[1024,256]{1,0:T(8,128)(2,1)} %get-tuple-element.46.refs_1_.kv0.refs_0_, bf16[1024,256]{1,0:T(8,128)(2,1)S(1)} %collective-permute-done.6.refs_2_.kv1, ...), custom_call_target="tpu_custom_call" | custom-call | flops 2147483648 | bytes 4194304 | tf_op jit(solution)/shard_map/forward_near/pallas_call | solution.py:132
  60.5 3.6 %collective-permute-done.5.refs_1_.kv2 = bf16[1024,256]{1,0:T(8,128)(2,1)S(1)} collective-permute-done((bf16[1024,256]{1,0:T(8,128)(2,1)}, bf16[1024,256]{1,0:T(8,128)(2,1)S(1)}, u32[]{:S(2)}, u32[]{:S(2)}) %collective-permute-start.5) | collective-permute-done | bytes 524320 | tf_op jit(solution)/shard_map/ppermute | solution.py:278
  64.0 0.8 collective-permute-start.7
  64.8 1.2 collective-permute-start.9
  66.4 7.5 %forward_far.1 = (bf16[1024,256]{1,0:T(8,128)(2,1)}, f32[1,1024]{1,0:T(1,128)S(1)}) custom-call(bf16[1024,128]{1,0:T(8,128)(2,1)} %get-tuple-element.45.refs_0_, bf16[1024,256]{1,0:T(8,128)(2,1)S(1)} %collective-permute-done.5.refs_1_.kv2, bf16[1024,256]{1,0:T(8,128)(2,1)S(1)} %collective-permute-done.7.refs_2_.kv3, ...), custom_call_target="tpu_custom_call" | custom-call | flops 2147483648 | bytes 4194304 | tf_op jit(solution)/shard_map/forward_far/pallas_call | solution.py:132
  73.8 3.5 %weight_whole.1 = (bf16[1024,1024]{1,0:T(8,128)(2,1)}, f32[128,1024]{1,0:T(8,128)S(1)}, f32[128,1024]{1,0:T(8,128)S(1)}) custom-call(s32[1]{0:T(128)} %bitcast.2.refs_2_.xl_ref, bf16[12,64,512]{2,1,0:T(8,128)(2,1)} %get-tuple-element.57.own0, bf16[4,64,512]{2,1,0:T(8,128)(2,1)} %get-tuple-element.58.own1, ...), custom_call_target="tpu_custom_call" | custom-call | flops 536870912 | bytes 4194304 | tf_op jit(solution)/shard_map/weight_whole/pallas_call | solution.py:331
  77.7 1.5 collective-permute-done.10.refs_2_
  79.2 1.9 %cross.1 = bf16[16,64,256]{2,1,0:T(8,128)(2,1)} custom-call(bf16[1024,256]{1,0:T(8,128)(2,1)} %get-tuple-element.64.refs_0_.pair_ref.refs_2_, f32[128,1024]{1,0:T(8,128)S(1)} %get-tuple-element.59.refs_1_, f32[128,1024]{1,0:T(8,128)S(1)} %collective-permute-done.10.refs_2_), custom_call_target="tpu_custom_call" | custom-call | bytes 4194304 | tf_op jit(solution)/shard_map/cross/pallas_call | solution.py:384
  81.2 3.6 %all-to-all-start.1 = ((bf16[16,64,256]{2,1,0:T(8,128)(2,1)}), bf16[16,64,256]{2,1,0:T(8,128)(2,1)S(1)}, u32[]{:S(2)}, u32[]{:S(2)}) async-start(bf16[16,64,256]{2,1,0:T(8,128)(2,1)} %cross.1), calls=%async_computation.1 | async-start | bytes 1048576 | tf_op jit(solution)/shard_map/all_to_all | solution.py:287
  85.2 0.8 collective-permute-done.11
  86.0 1.3 collective-permute-start.12
  87.3 1.6 collective-permute-done.12
  88.9 6.8 %all-to-all-done.1.refs_0_ = bf16[16,64,256]{2,1,0:T(8,128)(2,1)S(1)} async-done(((bf16[16,64,256]{2,1,0:T(8,128)(2,1)}), bf16[16,64,256]{2,1,0:T(8,128)(2,1)S(1)}, u32[]{:S(2)}, u32[]{:S(2)}) %all-to-all-start.1) | async-done | bytes 524320 | tf_op jit(solution)/shard_map/all_to_all | solution.py:287
  95.7 0.8 land.1
  96.5 1.5 collective-permute-start.14
  98.0 1.2 collective-permute-start.13
  100.0 3.1 %weight_terms.1 = (bf16[1024,1024]{1,0:T(8,128)(2,1)}, f32[8,128]{1,0:T(8,128)S(1)}) custom-call(bf16[128,1024]{1,0:T(8,128)(2,1)S(1)} %get-tuple-element.62.own_ref, bf16[128,1024]{1,0:T(8,128)(2,1)S(1)} %collective-permute-done.14.peer_ref, bf16[256,1024]{1,0:T(8,128)(2,1)} %up.1.refs_9_.up_ref), custom_call_target="tpu_custom_call" | custom-call | flops 536870912 | bytes 4194304 | tf_op jit(solution)/shard_map/weight_terms/pallas_call | solution.py:360
  103.1 4.6 %all-to-all-start.3 = ((bf16[16,64,1024]{2,1,0:T(8,128)(2,1)}), bf16[16,64,1024]{2,1,0:T(8,128)(2,1)}, u32[]{:S(2)}, u32[]{:S(2)}) async-start(bf16[16,64,1024]{2,1,0:T(8,128)(2,1)} %bitcast.50), calls=%async_computation.3 | async-start | bytes 4194304 | tf_op jit(solution)/shard_map/all_to_all | solution.py:287
  107.8 10.1 %query_grad.1 = bf16[1024,128]{1,0:T(8,128)(2,1)S(1)} custom-call(bf16[1024,256]{1,0:T(8,128)(2,1)} %get-tuple-element.64.refs_0_.pair_ref.refs_2_, bf16[1024,128]{1,0:T(8,128)(2,1)} %get-tuple-element.67.g_ref.refs_6_, f32[1,1024]{1,0:T(1,128)S(1)} %get-tuple-element.68.lse_ref, bf16[1024,256]{1,0:T(8,128)(2,1)} %get-tuple-element.46.refs_1_.kv0.refs_0_, ...), custom_call_target="tpu_custom_call" | custom-call | flops 6442450944 | bytes 4194304 | tf_op jit(solution)/shard_map/query_grad/pallas_call | solution.py:183
  117.9 0.6 collective-permute-start.17
  118.6 0.5 convolution_convert_fusion.1
  119.6 0.5 collective-permute-start.15
  120.4 11.9 %key_grad.1 = (bf16[1024,128]{1,0:T(8,128)(2,1)S(1)}, bf16[1024,128]{1,0:T(8,128)(2,1)S(1)}) custom-call(bf16[1024,256]{1,0:T(8,128)(2,1)} %get-tuple-element.46.refs_1_.kv0.refs_0_, f32[64,128]{1,0:T(8,128)S(1)} %pad.4.refs_3_.bias_ref.refs_1_, bf16[1024,256]{1,0:T(8,128)(2,1)S(1)} %copy-done.1, bf16[1024,256]{1,0:T(8,128)(2,1)S(1)} %collective-permute-done.16.refs_3_, ...), custom_call_target="tpu_custom_call" | custom-call | flops 8589934592 | bytes 4194304 | tf_op jit(solution)/shard_map/key_grad/pallas_call | solution.py:244
  132.3 1.0 pad_maximum_fusion
  133.3 6.8 %all-to-all-done.3 = bf16[16,64,1024]{2,1,0:T(8,128)(2,1)} async-done(((bf16[16,64,1024]{2,1,0:T(8,128)(2,1)}), bf16[16,64,1024]{2,1,0:T(8,128)(2,1)}, u32[]{:S(2)}, u32[]{:S(2)}) %all-to-all-start.3) | async-done | bytes 2097184 | tf_op jit(solution)/shard_map/all_to_all | solution.py:287
  140.1 3.6 %all-to-all-start.2 = ((bf16[16,64,384]{2,1,0:T(8,128)(2,1)}), bf16[16,64,384]{2,1,0:T(8,128)(2,1)S(1)}, u32[]{:S(2)}, u32[]{:S(2)}) async-start(bf16[16,64,384]{2,1,0:T(8,128)(2,1)} %pad_maximum_fusion), calls=%async_computation.2 | async-start | bytes 1572864 | tf_op jit(solution)/shard_map/all_to_all | solution.py:287
  143.9 2.0 %convert_reduce_fusion = f32[64,1024]{1,0:T(8,128)S(1)} fusion(bf16[16,64,1024]{2,1,0:T(8,128)(2,1)} %all-to-all-done.3), kind=kLoop, calls=%fused_computation | loop fusion | flops 2031616 | bytes 2359296 | tf_op jit(solution)/shard_map/reduce_sum | solution.py:587
  145.9 2.6 %collective-permute-start.24 = (f32[16,1024]{1,0:T(8,128)S(1)}, f32[16,1024]{1,0:T(8,128)S(1)}, u32[]{:S(2)}, u32[]{:S(2)}) collective-permute-start(f32[16,1024]{1,0:T(8,128)S(1)} %get-tuple-element.82), channel_id=1, source_target_pairs={{0,6},{2,4},{4,2},{6,0},{1,7},{3,5},{5,3},{7,1},{8,14},{10,12},{12... | collective-permute-start | bytes 196616 | tf_op jit(solution)/shard_map/ppermute | solution.py:592
  148.5 1.4 collective-permute-start.22
  149.9 6.6 %all-to-all-done.2.refs_2_ = bf16[16,64,384]{2,1,0:T(8,128)(2,1)S(1)} async-done(((bf16[16,64,384]{2,1,0:T(8,128)(2,1)}), bf16[16,64,384]{2,1,0:T(8,128)(2,1)S(1)}, u32[]{:S(2)}, u32[]{:S(2)}) %all-to-all-start.2) | async-done | bytes 786464 | tf_op jit(solution)/shard_map/all_to_all | solution.py:287
  156.5 2.6 %collective-permute-start.21 = (bf16[8,64,384]{2,1,0:T(8,128)(2,1)S(1)}, bf16[8,64,384]{2,1,0:T(8,128)(2,1)S(1)}, u32[]{:S(2)}, u32[]{:S(2)}) collective-permute-start(bf16[8,64,384]{2,1,0:T(8,128)(2,1)S(1)} %constant_dynamic-slice_fusion), channel_id=1, source_target_pairs={{0,1},{1,0},{2,3},{3,2},{4,5},{5,4},{6,7},{7,6},{8,9},{9,8},{10,11... | collective-permute-start | bytes 1179656 | tf_op jit(solution)/shard_map/ppermute | solution.py:274
  159.3 0.8 maximum_bitcast_fusion
  160.5 1.1 final.1
  161.6 0.6 pad_maximum_fusion.4
  (66 shorter events, 4.2 us)
Async XLA Ops:
  2.8 10.6 %collective-permute-start = (bf16[8,64,384]{2,1,0:T(8,128)(2,1)}, bf16[8,64,384]{2,1,0:T(8,128)(2,1)S(1)}, u32[]{:S(2)}, u32[]{:S(2)}) collective-permute-start(bf16[8,64,384]{2,1,0:T(8,128)(2,1)} %get-tuple-element.42), channel_id=1, source_target_pairs={{0,1},{1,0},{2,3},{3,2},{4,5},{5,4},{6,7},{7,6},{8,9},{9,8},{10,11... | collective-permute-start | bytes 1179656 | tf_op jit(solution)/shard_map/ppermute | solution.py:274
  5.3 6.2 %collective-permute-start.4 = (bf16[128,1024]{1,0:T(8,128)(2,1)S(1)}, bf16[128,1024]{1,0:T(8,128)(2,1)S(1)}, u32[]{:S(2)}, u32[]{:S(2)}) collective-permute-start(bf16[128,1024]{1,0:T(8,128)(2,1)S(1)} %slice_select_fusion), channel_id=1, source_target_pairs={{0,1},{1,0},{2,3},{3,2},{4,5},{5,4},{6,7},{7,6},{8,9},{9,8},{10,11... | collective-permute-start | bytes 786440 | tf_op jit(solution)/shard_map/ppermute | solution.py:274
  5.4 4.6 %collective-permute-start.2 = (bf16[8,2048]{1,0:T(8,128)(2,1)}, bf16[8,2048]{1,0:T(8,128)(2,1)S(1)}, u32[]{:S(2)}, u32[]{:S(2)}) collective-permute-start(bf16[8,2048]{1,0:T(8,128)(2,1)} %refs_5_.1), channel_id=1, source_target_pairs={{0,2},{2,0},{1,3},{3,1},{4,6},{6,4},{5,7},{7,5},{8,10},{10,8},{9,1... | collective-permute-start | bytes 98312 | tf_op jit(solution)/shard_map/ppermute | solution.py:491
  8.3 5.1 %collective-permute-start.1 = (bf16[8,2048]{1,0:T(8,128)(2,1)}, bf16[8,2048]{1,0:T(8,128)(2,1)S(1)}, u32[]{:S(2)}, u32[]{:S(2)}) collective-permute-start(bf16[8,2048]{1,0:T(8,128)(2,1)} %refs_5_.1), channel_id=1, source_target_pairs={{0,1},{1,0},{2,3},{3,2},{4,5},{5,4},{6,7},{7,6},{8,9},{9,8},{10,11... | collective-permute-start | bytes 98312 | tf_op jit(solution)/shard_map/ppermute | solution.py:274
  9.9 3.5 %collective-permute-start.3 = (bf16[8,2048]{1,0:T(8,128)(2,1)S(1)}, bf16[8,2048]{1,0:T(8,128)(2,1)S(1)}, u32[]{:S(2)}, u32[]{:S(2)}) collective-permute-start(bf16[8,2048]{1,0:T(8,128)(2,1)S(1)} %collective-permute-done.2.refs_7_), channel_id=1, source_target_pairs={{0,1},{1,0},{2,3},{3,2},{4,5},{5,4},{6,7},{7,6},{8,9},{9,8},{10,11... | collective-permute-start | bytes 98312 | tf_op jit(solution)/shard_map/ppermute | solution.py:274
  14.6 38.7 %copy-start.9 = (s32[64]{0:T(128)S(1)}, s32[64]{0:T(128)}, u32[]{:S(2)}) copy-start(s32[64]{0:T(128)} %param.10) | copy-start | bytes 772
  14.6 38.9 %copy-start.8 = (s32[64,64]{1,0:T(8,128)S(1)}, s32[64,64]{1,0:T(8,128)}, u32[]{:S(2)}) copy-start(s32[64,64]{1,0:T(8,128)} %param.11) | copy-start | bytes 49156
  48.9 4.9 %collective-permute-start.6 = (bf16[1024,256]{1,0:T(8,128)(2,1)}, bf16[1024,256]{1,0:T(8,128)(2,1)S(1)}, u32[]{:S(2)}, u32[]{:S(2)}) collective-permute-start(bf16[1024,256]{1,0:T(8,128)(2,1)} %get-tuple-element.46.refs_1_.kv0.refs_0_), channel_id=1, source_target_pairs={{0,1},{1,0},{2,3},{3,2},{4,5},{5,4},{6,7},{7,6},{8,9},{9,8},{10,11... | collective-permute-start | bytes 1572872 | tf_op jit(solution)/shard_map/ppermute | solution.py:274
  50.3 13.8 %collective-permute-start.5 = (bf16[1024,256]{1,0:T(8,128)(2,1)}, bf16[1024,256]{1,0:T(8,128)(2,1)S(1)}, u32[]{:S(2)}, u32[]{:S(2)}) collective-permute-start(bf16[1024,256]{1,0:T(8,128)(2,1)} %get-tuple-element.46.refs_1_.kv0.refs_0_), channel_id=1, source_target_pairs={{0,4},{4,0},{1,5},{5,1},{2,6},{6,2},{3,7},{7,3},{8,12},{12,8},{9,1... | collective-permute-start | bytes 1572872 | tf_op jit(solution)/shard_map/ppermute | solution.py:278
  51.5 22.4 %collective-permute-start.8 = (bf16[12,64,512]{2,1,0:T(8,128)(2,1)}, bf16[12,64,512]{2,1,0:T(8,128)(2,1)S(1)}, u32[]{:S(2)}, u32[]{:S(2)}) collective-permute-start(bf16[12,64,512]{2,1,0:T(8,128)(2,1)} %get-tuple-element.57.own0), channel_id=1, source_target_pairs={{0,6},{2,4},{4,2},{6,0},{1,7},{3,5},{5,3},{7,1},{8,14},{10,12},{12... | collective-permute-start | bytes 2359304 | tf_op jit(solution)/shard_map/ppermute | solution.py:315
  53.9 6.6 %copy-start.2 = (bf16[1024,256]{1,0:T(8,128)(2,1)}, bf16[1024,256]{1,0:T(8,128)(2,1)S(1)}, u32[]{:S(2)}) copy-start(bf16[1024,256]{1,0:T(8,128)(2,1)S(1)} %collective-permute-done.6.refs_2_.kv1) | copy-start | bytes 1572868
  53.9 11.0 %copy-start.7 = (bf16[4,64,512]{2,1,0:T(8,128)(2,1)S(1)}, bf16[4,64,512]{2,1,0:T(8,128)(2,1)}, u32[]{:S(2)}) copy-start(bf16[4,64,512]{2,1,0:T(8,128)(2,1)} %get-tuple-element.58.own1) | copy-start | bytes 786436
  64.0 9.8 %copy-start.3 = (bf16[1024,256]{1,0:T(8,128)(2,1)}, bf16[1024,256]{1,0:T(8,128)(2,1)S(1)}, u32[]{:S(2)}) copy-start(bf16[1024,256]{1,0:T(8,128)(2,1)S(1)} %collective-permute-done.5.refs_1_.kv2) | copy-start | bytes 1572868
  64.0 2.3 %collective-permute-start.7 = (bf16[1024,256]{1,0:T(8,128)(2,1)S(1)}, bf16[1024,256]{1,0:T(8,128)(2,1)S(1)}, u32[]{:S(2)}, u32[]{:S(2)}) collective-permute-start(bf16[1024,256]{1,0:T(8,128)(2,1)S(1)} %collective-permute-done.5.refs_1_.kv2), channel_id=1, source_target_pairs={{0,1},{1,0},{2,3},{3,2},{4,5},{5,4},{6,7},{7,6},{8,9},{9,8},{10,11... | collective-permute-start | bytes 1572872 | tf_op jit(solution)/shard_map/ppermute | solution.py:274
  64.8 9.0 %collective-permute-start.9 = (bf16[4,64,512]{2,1,0:T(8,128)(2,1)S(1)}, bf16[4,64,512]{2,1,0:T(8,128)(2,1)S(1)}, u32[]{:S(2)}, u32[]{:S(2)}) collective-permute-start(bf16[4,64,512]{2,1,0:T(8,128)(2,1)S(1)} %copy-done.7), channel_id=1, source_target_pairs={{0,4},{4,0},{1,5},{5,1},{2,6},{6,2},{3,7},{7,3},{8,12},{12,8},{9,1... | collective-permute-start | bytes 786440 | tf_op jit(solution)/shard_map/ppermute | solution.py:278
  66.4 7.5 %copy-start.4 = (bf16[1024,256]{1,0:T(8,128)(2,1)}, bf16[1024,256]{1,0:T(8,128)(2,1)S(1)}, u32[]{:S(2)}) copy-start(bf16[1024,256]{1,0:T(8,128)(2,1)S(1)} %collective-permute-done.7.refs_2_.kv3) | copy-start | bytes 1572868
  77.3 20.7 %copy-start = (bf16[1024,256]{1,0:T(8,128)(2,1)S(1)}, bf16[1024,256]{1,0:T(8,128)(2,1)}, u32[]{:S(2)}) copy-start(bf16[1024,256]{1,0:T(8,128)(2,1)} %get-tuple-element.64.refs_0_.pair_ref.refs_2_) | copy-start | bytes 1572868
  77.3 1.9 %collective-permute-start.10 = (f32[128,1024]{1,0:T(8,128)S(1)}, f32[128,1024]{1,0:T(8,128)S(1)}, u32[]{:S(2)}, u32[]{:S(2)}) collective-permute-start(f32[128,1024]{1,0:T(8,128)S(1)} %get-tuple-element.60), channel_id=1, source_target_pairs={{0,1},{1,0},{2,3},{3,2},{4,5},{5,4},{6,7},{7,6},{8,9},{9,8},{10,11... | collective-permute-start | bytes 1572872 | tf_op jit(solution)/shard_map/ppermute | solution.py:274
  81.2 14.5 %all-to-all-start.1 = ((bf16[16,64,256]{2,1,0:T(8,128)(2,1)}), bf16[16,64,256]{2,1,0:T(8,128)(2,1)S(1)}, u32[]{:S(2)}, u32[]{:S(2)}) async-start(bf16[16,64,256]{2,1,0:T(8,128)(2,1)} %cross.1), calls=%async_computation.1 | async-start | bytes 1048576 | tf_op jit(solution)/shard_map/all_to_all | solution.py:287
  84.8 1.3 collective-permute-start.11
  86.0 2.9 %collective-permute-start.12 = (f32[2,1024]{1,0:T(2,128)S(1)}, f32[2,1024]{1,0:T(2,128)S(1)}, u32[]{:S(2)}, u32[]{:S(2)}) collective-permute-start(f32[2,1024]{1,0:T(2,128)S(1)} %pad_maximum_fusion.6), channel_id=1, source_target_pairs={{0,4},{4,0},{1,5},{5,1},{2,6},{6,2},{3,7},{7,3},{8,12},{12,8},{9,1... | collective-permute-start | bytes 24584 | tf_op jit(solution)/shard_map/ppermute | solution.py:278
  96.5 3.5 %collective-permute-start.14 = (bf16[128,1024]{1,0:T(8,128)(2,1)S(1)}, bf16[128,1024]{1,0:T(8,128)(2,1)S(1)}, u32[]{:S(2)}, u32[]{:S(2)}) collective-permute-start(bf16[128,1024]{1,0:T(8,128)(2,1)S(1)} %get-tuple-element.62.own_ref), channel_id=1, source_target_pairs={{0,1},{1,0},{2,3},{3,2},{4,5},{5,4},{6,7},{7,6},{8,9},{9,8},{10,11... | collective-permute-start | bytes 786440 | tf_op jit(solution)/shard_map/ppermute | solution.py:274
  98.0 19.8 %collective-permute-start.13 = (bf16[1024,256]{1,0:T(8,128)(2,1)S(1)}, bf16[1024,256]{1,0:T(8,128)(2,1)S(1)}, u32[]{:S(2)}, u32[]{:S(2)}) collective-permute-start(bf16[1024,256]{1,0:T(8,128)(2,1)S(1)} %copy-done), channel_id=1, source_target_pairs={{0,4},{4,0},{1,5},{5,1},{2,6},{6,2},{3,7},{7,3},{8,12},{12,8},{9,1... | collective-permute-start | bytes 1572872 | tf_op jit(solution)/shard_map/ppermute | solution.py:278
  99.2 20.9 %collective-permute-start.16 = (bf16[1024,256]{1,0:T(8,128)(2,1)S(1)}, bf16[1024,256]{1,0:T(8,128)(2,1)S(1)}, u32[]{:S(2)}, u32[]{:S(2)}) collective-permute-start(bf16[1024,256]{1,0:T(8,128)(2,1)S(1)} %copy-done), channel_id=1, source_target_pairs={{0,1},{1,0},{2,3},{3,2},{4,5},{5,4},{6,7},{7,6},{8,9},{9,8},{10,11... | collective-permute-start | bytes 1572872 | tf_op jit(solution)/shard_map/ppermute | solution.py:274
  99.5 20.6 %collective-permute-start.18 = (bf16[1024,128]{1,0:T(8,128)(2,1)}, bf16[1024,128]{1,0:T(8,128)(2,1)S(1)}, u32[]{:S(2)}, u32[]{:S(2)}) collective-permute-start(bf16[1024,128]{1,0:T(8,128)(2,1)} %get-tuple-element.67.g_ref.refs_6_), channel_id=1, source_target_pairs={{0,1},{1,0},{2,3},{3,2},{4,5},{5,4},{6,7},{7,6},{8,9},{9,8},{10,11... | collective-permute-start | bytes 786440 | tf_op jit(solution)/shard_map/ppermute | solution.py:274
  99.7 18.8 %collective-permute-start.19 = (bf16[1024,128]{1,0:T(8,128)(2,1)}, bf16[1024,128]{1,0:T(8,128)(2,1)S(1)}, u32[]{:S(2)}, u32[]{:S(2)}) collective-permute-start(bf16[1024,128]{1,0:T(8,128)(2,1)} %get-tuple-element.67.g_ref.refs_6_), channel_id=1, source_target_pairs={{0,4},{4,0},{1,5},{5,1},{2,6},{6,2},{3,7},{7,3},{8,12},{12,8},{9,1... | collective-permute-start | bytes 786440 | tf_op jit(solution)/shard_map/ppermute | solution.py:278
  103.1 37.0 %all-to-all-start.3 = ((bf16[16,64,1024]{2,1,0:T(8,128)(2,1)}), bf16[16,64,1024]{2,1,0:T(8,128)(2,1)}, u32[]{:S(2)}, u32[]{:S(2)}) async-start(bf16[16,64,1024]{2,1,0:T(8,128)(2,1)} %bitcast.50), calls=%async_computation.3 | async-start | bytes 4194304 | tf_op jit(solution)/shard_map/all_to_all | solution.py:287
  107.7 10.9 %copy-start.6 = (bf16[1024,1024]{1,0:T(8,128)(2,1)S(1)}, bf16[1024,1024]{1,0:T(8,128)(2,1)}, u32[]{:S(2)}) copy-start(bf16[1024,1024]{1,0:T(8,128)(2,1)} %get-tuple-element.66) | copy-start | bytes 6291460
  117.9 2.6 %collective-permute-start.17 = (bf16[1024,256]{1,0:T(8,128)(2,1)S(1)}, bf16[1024,256]{1,0:T(8,128)(2,1)S(1)}, u32[]{:S(2)}, u32[]{:S(2)}) collective-permute-start(bf16[1024,256]{1,0:T(8,128)(2,1)S(1)} %collective-permute-done.13.refs_4_), channel_id=1, source_target_pairs={{0,1},{1,0},{2,3},{3,2},{4,5},{5,4},{6,7},{7,6},{8,9},{9,8},{10,11... | collective-permute-start | bytes 1572872 | tf_op jit(solution)/shard_map/ppermute | solution.py:274
  118.5 1.9 %collective-permute-start.20 = (bf16[1024,128]{1,0:T(8,128)(2,1)S(1)}, bf16[1024,128]{1,0:T(8,128)(2,1)S(1)}, u32[]{:S(2)}, u32[]{:S(2)}) collective-permute-start(bf16[1024,128]{1,0:T(8,128)(2,1)S(1)} %collective-permute-done.19.refs_8_), channel_id=1, source_target_pairs={{0,1},{1,0},{2,3},{3,2},{4,5},{5,4},{6,7},{7,6},{8,9},{9,8},{10,11... | collective-permute-start | bytes 786440 | tf_op jit(solution)/shard_map/ppermute | solution.py:274
  119.1 1.4 copy-start.1
  119.1 1.3 copy-start.5
  119.6 24.1 %collective-permute-start.15 = (bf16[2,64,1024]{2,1,0:T(8,128)(2,1)S(1)}, bf16[2,64,1024]{2,1,0:T(8,128)(2,1)S(1)}, u32[]{:S(2)}, u32[]{:S(2)}) collective-permute-start(bf16[2,64,1024]{2,1,0:T(8,128)(2,1)S(1)} %pad_maximum_fusion.2), channel_id=1, source_target_pairs={{0,1},{1,0},{2,3},{3,2},{4,5},{5,4},{6,7},{7,6},{8,9},{9,8},{10,11... | collective-permute-start | bytes 786440 | tf_op jit(solution)/shard_map/ppermute | solution.py:274
  140.1 16.3 %all-to-all-start.2 = ((bf16[16,64,384]{2,1,0:T(8,128)(2,1)}), bf16[16,64,384]{2,1,0:T(8,128)(2,1)S(1)}, u32[]{:S(2)}, u32[]{:S(2)}) async-start(bf16[16,64,384]{2,1,0:T(8,128)(2,1)} %pad_maximum_fusion), calls=%async_computation.2 | async-start | bytes 1572864 | tf_op jit(solution)/shard_map/all_to_all | solution.py:287
  145.9 13.2 %collective-permute-start.24 = (f32[16,1024]{1,0:T(8,128)S(1)}, f32[16,1024]{1,0:T(8,128)S(1)}, u32[]{:S(2)}, u32[]{:S(2)}) collective-permute-start(f32[16,1024]{1,0:T(8,128)S(1)} %get-tuple-element.82), channel_id=1, source_target_pairs={{0,6},{2,4},{4,2},{6,0},{1,7},{3,5},{5,3},{7,1},{8,14},{10,12},{12... | collective-permute-start | bytes 196616 | tf_op jit(solution)/shard_map/ppermute | solution.py:592
  148.5 10.7 %collective-permute-start.23 = (f32[16,1024]{1,0:T(8,128)S(1)}, f32[16,1024]{1,0:T(8,128)S(1)}, u32[]{:S(2)}, u32[]{:S(2)}) collective-permute-start(f32[16,1024]{1,0:T(8,128)S(1)} %get-tuple-element.83), channel_id=1, source_target_pairs={{0,4},{2,6},{4,0},{6,2},{1,5},{3,7},{5,1},{7,3},{8,12},{10,14},{12... | collective-permute-start | bytes 196616 | tf_op jit(solution)/shard_map/ppermute | solution.py:592
  148.5 10.7 %collective-permute-start.22 = (f32[16,1024]{1,0:T(8,128)S(1)}, f32[16,1024]{1,0:T(8,128)S(1)}, u32[]{:S(2)}, u32[]{:S(2)}) collective-permute-start(f32[16,1024]{1,0:T(8,128)S(1)} %get-tuple-element.81), channel_id=1, source_target_pairs={{0,2},{2,0},{4,6},{6,4},{1,3},{3,1},{5,7},{7,5},{8,10},{10,8},{12,... | collective-permute-start | bytes 196616 | tf_op jit(solution)/shard_map/ppermute | solution.py:592
  156.5 4.0 %collective-permute-start.21 = (bf16[8,64,384]{2,1,0:T(8,128)(2,1)S(1)}, bf16[8,64,384]{2,1,0:T(8,128)(2,1)S(1)}, u32[]{:S(2)}, u32[]{:S(2)}) collective-permute-start(bf16[8,64,384]{2,1,0:T(8,128)(2,1)S(1)} %constant_dynamic-slice_fusion), channel_id=1, source_target_pairs={{0,1},{1,0},{2,3},{3,2},{4,5},{5,4},{6,7},{7,6},{8,9},{9,8},{10,11... | collective-permute-start | bytes 1179656 | tf_op jit(solution)/shard_map/ppermute | solution.py:274
  159.2 2.4 %collective-permute-start.25 = (f32[8,1024]{1,0:T(8,128)S(1)}, f32[8,1024]{1,0:T(8,128)S(1)}, u32[]{:S(2)}, u32[]{:S(2)}) collective-permute-start(f32[8,1024]{1,0:T(8,128)S(1)} %dynamic-slice_bitcast_fusion.3), channel_id=1, source_target_pairs={{0,1},{1,0},{2,3},{3,2},{4,5},{5,4},{6,7},{7,6},{8,9},{9,8},{10,11... | collective-permute-start | bytes 98312 | tf_op jit(solution)/shard_map/ppermute | solution.py:274

commit v13 on v11

--- a/solution.py
+++ b/solution.py
@@ -517,6 +517,8 @@
     bias = span_bias(span_order, block_mask, side, which)
 
     up_sent = jnp.where(first_core, wide[:, cols:], wide[:, :cols])
+
+    out, top, total = forward(True, in_hbm(q), (in_hbm(own_kv), near_kv), bias)
     (up,) = move(
         up_body,
         "up",
@@ -525,9 +527,8 @@
         in_hbm(wide),
         other_core(up_sent),
         space=pltpu.HBM,
-    )
-
-    out, top, total = forward(True, in_hbm(q), (in_hbm(own_kv), near_kv), bias)
+        after=(total,),
+    )
     far_kv, total, up = lax.optimization_barrier((far_kv, total, up))
     kvs = (own_kv, near_kv, far_kv, other_core(far_kv))
     pair, lse = forward(False, in_hbm(q), kvs[2:], bias, in_hbm(out), top, total)

time: 159 us -> 159 us (level)
  no operation moved by 1% of the time
where the time goes in v13:
time: 159 us
  Pallas kernels  53 us (33%)
  starting transfers between devices  37.5 us (24%)
  blocking collectives  32.9 us (21%)
  waiting for transfers between devices  28.1 us (18%)
  other arithmetic  4.89 us (3%)
    all_to_all x1, blocking collectives, exchange(): return lax.all_to_all(x, axes, 0, 0, tiled=True)  32.9 us
    all_to_all x3, waiting for transfers between devices, exchange(): return lax.all_to_all(x, axes, 0, 0, tiled=True)  20.1 us
    pallas_call x2, Pallas kernels, forward(): pl.pallas_call(functools.partial(forward_body, first), out_shape=outs, gr...  14 us
    ppermute x16, starting transfers between devices, other_core(): return lax.ppermute(x, 'core', SWAP)  12.6 us
    pallas_call x1, Pallas kernels, key_grad(): pl.pallas_call(key_body, out_shape=[jax.ShapeDtypeStruct((ROWS, HEAD), BF...  11.9 us
    all_to_all x3, starting transfers between devices, exchange(): return lax.all_to_all(x, axes, 0, 0, tiled=True)  11.8 us
    pallas_call x7, Pallas kernels, move(): pl.pallas_call(run, out_shape=[make(shape, BF16) for make, shape in zip(s...  10.4 us
    pallas_call x1, Pallas kernels, query_grad(): pl.pallas_call(query_body, out_shape=jax.ShapeDtypeStruct((ROWS, HEAD), B...  10.1 us
  transfers between devices with their start and end apart: 29, of which 11 were waited for; matrix products, arithmetic and copies ran while one was open for 4% of the time, Pallas kernels for 27%

profile of v13, /device:TPU:1, one launch (start us, length us, event | category | flops | bytes accessed | tf_op | source)
XLA Modules:
  0.0 158.7 jit_solution(12971557592698768898)
XLA Ops:
  0.6 2.1 %cut.1 = (bf16[8,64,384]{2,1,0:T(8,128)(2,1)}, bf16[8,64,384]{2,1,0:T(8,128)(2,1)}) custom-call(s32[1]{0:T(128)} %bitcast.3.refs_0_.refs_1_, bf16[128,1024]{1,0:T(8,128)(2,1)} %bitcast.59, bf16[128,1024]{1,0:T(8,128)(2,1)} %bitcast.60, bf16[128,1024]{1,0:T(8,128)(2,1)} %bitcast.61), custom_call_target="tpu_custom_call" | custom-call | bytes 4194304 | tf_op jit(solution)/shard_map/cut/pallas_call | solution.py:384
  2.8 1.4 collective-permute-start
  4.2 2.8 %collective-permute-start.2 = (bf16[8,2048]{1,0:T(8,128)(2,1)}, bf16[8,2048]{1,0:T(8,128)(2,1)S(1)}, u32[]{:S(2)}, u32[]{:S(2)}) collective-permute-start(bf16[8,2048]{1,0:T(8,128)(2,1)} %refs_5_.1), channel_id=1, source_target_pairs={{0,2},{2,0},{1,3},{3,1},{4,6},{6,4},{5,7},{7,5},{8,10},{10,8},{9,1... | collective-permute-start | bytes 98312 | tf_op jit(solution)/shard_map/ppermute | solution.py:479
  7.3 1.4 collective-permute-done.2.refs_7_
  8.7 1.2 collective-permute-start.3
  9.8 0.9 collective-permute-done.3.refs_8_
  10.7 1.2 fill.1
  11.9 32.9 %all_to_all.20.refs_0_ = bf16[16,64,896]{2,1,0:T(8,128)(2,1)S(1)} all-to-all(bf16[16,64,896]{2,1,0:T(8,128)(2,1)S(1)} %fill.1), channel_id=1, replica_groups=mesh['z'=4,'y'=4,'xl'=2,'xh'=2,'core'=2] {'z','y'}, dimensions={0} | all-to-all | bytes 3670016 | tf_op jit(solution)/shard_map/all_to_all | solution.py:287
  44.7 1.4 split.1
  46.1 1.2 collective-permute-start.4
  47.3 1.7 %collective-permute-start.5 = (bf16[1024,256]{1,0:T(8,128)(2,1)}, bf16[1024,256]{1,0:T(8,128)(2,1)S(1)}, u32[]{:S(2)}, u32[]{:S(2)}) collective-permute-start(bf16[1024,256]{1,0:T(8,128)(2,1)} %get-tuple-element.48.refs_1_.kv0.refs_0_), channel_id=1, source_target_pairs={{0,1},{1,0},{2,3},{3,2},{4,5},{5,4},{6,7},{7,6},{8,9},{9,8},{10,11... | collective-permute-start | bytes 1572872 | tf_op jit(solution)/shard_map/ppermute | solution.py:274
  49.2 1.9 %collective-permute-start.8 = (bf16[12,64,512]{2,1,0:T(8,128)(2,1)}, bf16[12,64,512]{2,1,0:T(8,128)(2,1)S(1)}, u32[]{:S(2)}, u32[]{:S(2)}) collective-permute-start(bf16[12,64,512]{2,1,0:T(8,128)(2,1)} %get-tuple-element.60.own0), channel_id=1, source_target_pairs={{0,6},{2,4},{4,2},{6,0},{1,7},{3,5},{5,3},{7,1},{8,14},{10,12},{12... | collective-permute-start | bytes 2359304 | tf_op jit(solution)/shard_map/ppermute | solution.py:315
  51.7 6.6 %forward_near.1 = (f32[128,1024]{1,0:T(8,128)}, f32[1,1024]{1,0:T(1,128)S(1)}, f32[1,1024]{1,0:T(1,128)S(1)}) custom-call(bf16[1024,128]{1,0:T(8,128)(2,1)} %get-tuple-element.47.refs_0_, bf16[1024,256]{1,0:T(8,128)(2,1)} %get-tuple-element.48.refs_1_.kv0.refs_0_, bf16[1024,256]{1,0:T(8,128)(2,1)S(1)} %collective-permute-done.5.refs_2_.kv1, ...), custom_call_target="tpu_custom_call" | custom-call | flops 2147483648 | bytes 4194304 | tf_op jit(solution)/shard_map/forward_near/pallas_call | solution.py:132
  58.3 1.9 %up.1.up_ref = bf16[256,1024]{1,0:T(8,128)(2,1)} custom-call(s32[1]{0:T(128)} %bitcast.refs_0_, s32[1]{0:T(128)} %bitcast.3.refs_0_.refs_1_, bf16[128,2048]{1,0:T(8,128)(2,1)} %bitcast.51, bf16[128,1024]{1,0:T(8,128)(2,1)S(1)} %collective-permute-done.6.refs_3_, f32[1,1024]{1,0:T(1,128)S(1)} %get-tuple-element.56.refs_4_.refs_6_), custom_call_target="tpu_custom_call" | custom-call | bytes 4194304 | tf_op jit(solution)/shard_map/up/pallas_call | solution.py:384
  60.2 0.7 collective-permute-start.7
  60.9 1.0 collective-permute-start.9
  61.9 0.5 collective-permute-done.7.refs_2_.kv3
  62.4 7.4 %forward_far.1 = (bf16[1024,256]{1,0:T(8,128)(2,1)}, f32[1,1024]{1,0:T(1,128)S(1)}) custom-call(bf16[1024,128]{1,0:T(8,128)(2,1)} %get-tuple-element.47.refs_0_, bf16[1024,256]{1,0:T(8,128)(2,1)S(1)} %collective-permute-done.4.refs_1_.kv2, bf16[1024,256]{1,0:T(8,128)(2,1)S(1)} %collective-permute-done.7.refs_2_.kv3, ...), custom_call_target="tpu_custom_call" | custom-call | flops 2147483648 | bytes 4194304 | tf_op jit(solution)/shard_map/forward_far/pallas_call | solution.py:132
  69.9 3.5 %weight_whole.1 = (bf16[1024,1024]{1,0:T(8,128)(2,1)}, f32[128,1024]{1,0:T(8,128)S(1)}, f32[128,1024]{1,0:T(8,128)S(1)}) custom-call(s32[1]{0:T(128)} %bitcast.2.refs_2_.xl_ref, bf16[12,64,512]{2,1,0:T(8,128)(2,1)} %get-tuple-element.60.own0, bf16[4,64,512]{2,1,0:T(8,128)(2,1)} %get-tuple-element.61.own1, ...), custom_call_target="tpu_custom_call" | custom-call | flops 536870912 | bytes 4194304 | tf_op jit(solution)/shard_map/weight_whole/pallas_call | solution.py:331
  73.4 0.8 collective-permute-start.10
  74.2 1.5 collective-permute-done.10.refs_2_
  75.7 1.9 %cross.1 = bf16[16,64,256]{2,1,0:T(8,128)(2,1)} custom-call(bf16[1024,256]{1,0:T(8,128)(2,1)} %get-tuple-element.68.refs_0_.pair_ref.refs_2_, f32[128,1024]{1,0:T(8,128)S(1)} %get-tuple-element.63.refs_1_, f32[128,1024]{1,0:T(8,128)S(1)} %collective-permute-done.10.refs_2_), custom_call_target="tpu_custom_call" | custom-call | bytes 4194304 | tf_op jit(solution)/shard_map/cross/pallas_call | solution.py:384
  77.6 3.6 %all-to-all-start.1 = ((bf16[16,64,256]{2,1,0:T(8,128)(2,1)}), bf16[16,64,256]{2,1,0:T(8,128)(2,1)S(1)}, u32[]{:S(2)}, u32[]{:S(2)}) async-start(bf16[16,64,256]{2,1,0:T(8,128)(2,1)} %cross.1), calls=%async_computation.1 | async-start | bytes 1048576 | tf_op jit(solution)/shard_map/all_to_all | solution.py:287
  81.7 0.8 collective-permute-done.11
  82.5 0.7 collective-permute-start.12
  83.2 2.2 %collective-permute-done.12 = f32[2,1024]{1,0:T(2,128)S(1)} collective-permute-done((f32[2,1024]{1,0:T(2,128)S(1)}, f32[2,1024]{1,0:T(2,128)S(1)}, u32[]{:S(2)}, u32[]{:S(2)}) %collective-permute-start.12) | collective-permute-done | bytes 8224 | tf_op jit(solution)/shard_map/ppermute | solution.py:278
  85.4 6.8 %all-to-all-done.1.refs_0_ = bf16[16,64,256]{2,1,0:T(8,128)(2,1)S(1)} async-done(((bf16[16,64,256]{2,1,0:T(8,128)(2,1)}), bf16[16,64,256]{2,1,0:T(8,128)(2,1)S(1)}, u32[]{:S(2)}, u32[]{:S(2)}) %all-to-all-start.1) | async-done | bytes 524320 | tf_op jit(solution)/shard_map/all_to_all | solution.py:287
  92.2 0.8 land.1
  93.0 1.5 collective-permute-start.14
  94.5 0.6 collective-permute-start.13
  95.6 0.8 collective-permute-start.19
  96.4 3.2 %weight_terms.1 = (bf16[1024,1024]{1,0:T(8,128)(2,1)}, f32[8,128]{1,0:T(8,128)S(1)}) custom-call(bf16[128,1024]{1,0:T(8,128)(2,1)S(1)} %get-tuple-element.66.own_ref, bf16[128,1024]{1,0:T(8,128)(2,1)S(1)} %collective-permute-done.14.peer_ref, bf16[256,1024]{1,0:T(8,128)(2,1)} %up.1.up_ref), custom_call_target="tpu_custom_call" | custom-call | flops 536870912 | bytes 4194304 | tf_op jit(solution)/shard_map/weight_terms/pallas_call | solution.py:360
  99.6 4.6 %all-to-all-start.3 = ((bf16[16,64,1024]{2,1,0:T(8,128)(2,1)}), bf16[16,64,1024]{2,1,0:T(8,128)(2,1)}, u32[]{:S(2)}, u32[]{:S(2)}) async-start(bf16[16,64,1024]{2,1,0:T(8,128)(2,1)} %bitcast.50), calls=%async_computation.3 | async-start | bytes 4194304 | tf_op jit(solution)/shard_map/all_to_all | solution.py:287
  104.2 10.1 %query_grad.1 = bf16[1024,128]{1,0:T(8,128)(2,1)S(1)} custom-call(bf16[1024,256]{1,0:T(8,128)(2,1)} %get-tuple-element.68.refs_0_.pair_ref.refs_2_, bf16[1024,128]{1,0:T(8,128)(2,1)} %get-tuple-element.71.g_ref.refs_6_, f32[1,1024]{1,0:T(1,128)S(1)} %get-tuple-element.72.lse_ref, bf16[1024,256]{1,0:T(8,128)(2,1)} %get-tuple-element.48.refs_1_.kv0.refs_0_, ...), custom_call_target="tpu_custom_call" | custom-call | flops 6442450944 | bytes 4194304 | tf_op jit(solution)/shard_map/query_grad/pallas_call | solution.py:183
  114.3 0.6 collective-permute-start.17
  116.1 0.5 collective-permute-start.15
  116.9 11.9 %key_grad.1 = (bf16[1024,128]{1,0:T(8,128)(2,1)S(1)}, bf16[1024,128]{1,0:T(8,128)(2,1)S(1)}) custom-call(bf16[1024,256]{1,0:T(8,128)(2,1)} %get-tuple-element.48.refs_1_.kv0.refs_0_, f32[64,128]{1,0:T(8,128)S(1)} %pad.4.refs_3_.bias_ref.refs_1_, bf16[1024,256]{1,0:T(8,128)(2,1)S(1)} %copy-done.1, bf16[1024,256]{1,0:T(8,128)(2,1)S(1)} %collective-permute-done.16.refs_3_, ...), custom_call_target="tpu_custom_call" | custom-call | flops 8589934592 | bytes 4194304 | tf_op jit(solution)/shard_map/key_grad/pallas_call | solution.py:244
  128.8 1.0 pad_maximum_fusion
  129.8 6.8 %all-to-all-done.3 = bf16[16,64,1024]{2,1,0:T(8,128)(2,1)} async-done(((bf16[16,64,1024]{2,1,0:T(8,128)(2,1)}), bf16[16,64,1024]{2,1,0:T(8,128)(2,1)}, u32[]{:S(2)}, u32[]{:S(2)}) %all-to-all-start.3) | async-done | bytes 2097184 | tf_op jit(solution)/shard_map/all_to_all | solution.py:287
  136.6 3.6 %all-to-all-start.2 = ((bf16[16,64,384]{2,1,0:T(8,128)(2,1)}), bf16[16,64,384]{2,1,0:T(8,128)(2,1)S(1)}, u32[]{:S(2)}, u32[]{:S(2)}) async-start(bf16[16,64,384]{2,1,0:T(8,128)(2,1)} %pad_maximum_fusion), calls=%async_computation.2 | async-start | bytes 1572864 | tf_op jit(solution)/shard_map/all_to_all | solution.py:287
  140.3 2.0 %convert_reduce_fusion = f32[64,1024]{1,0:T(8,128)S(1)} fusion(bf16[16,64,1024]{2,1,0:T(8,128)(2,1)} %all-to-all-done.3), kind=kLoop, calls=%fused_computation | loop fusion | flops 2031616 | bytes 2359296 | tf_op jit(solution)/shard_map/reduce_sum | solution.py:587
  142.4 1.9 %collective-permute-start.24 = (f32[16,1024]{1,0:T(8,128)S(1)}, f32[16,1024]{1,0:T(8,128)S(1)}, u32[]{:S(2)}, u32[]{:S(2)}) collective-permute-start(f32[16,1024]{1,0:T(8,128)S(1)} %get-tuple-element.86), channel_id=1, source_target_pairs={{0,6},{2,4},{4,2},{6,0},{1,7},{3,5},{5,3},{7,1},{8,14},{10,12},{12... | collective-permute-start | bytes 196616 | tf_op jit(solution)/shard_map/ppermute | solution.py:592
  144.3 2.0 %collective-permute-start.22 = (f32[16,1024]{1,0:T(8,128)S(1)}, f32[16,1024]{1,0:T(8,128)S(1)}, u32[]{:S(2)}, u32[]{:S(2)}) collective-permute-start(f32[16,1024]{1,0:T(8,128)S(1)} %get-tuple-element.85), channel_id=1, source_target_pairs={{0,2},{2,0},{4,6},{6,4},{1,3},{3,1},{5,7},{7,5},{8,10},{10,8},{12,... | collective-permute-start | bytes 196616 | tf_op jit(solution)/shard_map/ppermute | solution.py:592
  146.3 6.6 %all-to-all-done.2.refs_2_ = bf16[16,64,384]{2,1,0:T(8,128)(2,1)S(1)} async-done(((bf16[16,64,384]{2,1,0:T(8,128)(2,1)}), bf16[16,64,384]{2,1,0:T(8,128)(2,1)S(1)}, u32[]{:S(2)}, u32[]{:S(2)}) %all-to-all-start.2) | async-done | bytes 786464 | tf_op jit(solution)/shard_map/all_to_all | solution.py:287
  153.0 2.6 %collective-permute-start.21 = (bf16[8,64,384]{2,1,0:T(8,128)(2,1)S(1)}, bf16[8,64,384]{2,1,0:T(8,128)(2,1)S(1)}, u32[]{:S(2)}, u32[]{:S(2)}) collective-permute-start(bf16[8,64,384]{2,1,0:T(8,128)(2,1)S(1)} %constant_dynamic-slice_fusion), channel_id=1, source_target_pairs={{0,1},{1,0},{2,3},{3,2},{4,5},{5,4},{6,7},{7,6},{8,9},{9,8},{10,11... | collective-permute-start | bytes 1179656 | tf_op jit(solution)/shard_map/ppermute | solution.py:274
  155.8 0.8 maximum_bitcast_fusion
  156.9 1.1 final.1
  158.0 0.6 pad_maximum_fusion.4
  (68 shorter events, 4.0 us)
Async XLA Ops:
  2.8 7.9 %collective-permute-start = (bf16[8,64,384]{2,1,0:T(8,128)(2,1)}, bf16[8,64,384]{2,1,0:T(8,128)(2,1)S(1)}, u32[]{:S(2)}, u32[]{:S(2)}) collective-permute-start(bf16[8,64,384]{2,1,0:T(8,128)(2,1)} %get-tuple-element.44), channel_id=1, source_target_pairs={{0,1},{1,0},{2,3},{3,2},{4,5},{5,4},{6,7},{7,6},{8,9},{9,8},{10,11... | collective-permute-start | bytes 1179656 | tf_op jit(solution)/shard_map/ppermute | solution.py:274
  4.2 4.5 %collective-permute-start.2 = (bf16[8,2048]{1,0:T(8,128)(2,1)}, bf16[8,2048]{1,0:T(8,128)(2,1)S(1)}, u32[]{:S(2)}, u32[]{:S(2)}) collective-permute-start(bf16[8,2048]{1,0:T(8,128)(2,1)} %refs_5_.1), channel_id=1, source_target_pairs={{0,2},{2,0},{1,3},{3,1},{4,6},{6,4},{5,7},{7,5},{8,10},{10,8},{9,1... | collective-permute-start | bytes 98312 | tf_op jit(solution)/shard_map/ppermute | solution.py:479
  7.0 2.8 %collective-permute-start.1 = (bf16[8,2048]{1,0:T(8,128)(2,1)}, bf16[8,2048]{1,0:T(8,128)(2,1)S(1)}, u32[]{:S(2)}, u32[]{:S(2)}) collective-permute-start(bf16[8,2048]{1,0:T(8,128)(2,1)} %refs_5_.1), channel_id=1, source_target_pairs={{0,1},{1,0},{2,3},{3,2},{4,5},{5,4},{6,7},{7,6},{8,9},{9,8},{10,11... | collective-permute-start | bytes 98312 | tf_op jit(solution)/shard_map/ppermute | solution.py:274
  8.7 2.0 %collective-permute-start.3 = (bf16[8,2048]{1,0:T(8,128)(2,1)S(1)}, bf16[8,2048]{1,0:T(8,128)(2,1)S(1)}, u32[]{:S(2)}, u32[]{:S(2)}) collective-permute-start(bf16[8,2048]{1,0:T(8,128)(2,1)S(1)} %collective-permute-done.2.refs_7_), channel_id=1, source_target_pairs={{0,1},{1,0},{2,3},{3,2},{4,5},{5,4},{6,7},{7,6},{8,9},{9,8},{10,11... | collective-permute-start | bytes 98312 | tf_op jit(solution)/shard_map/ppermute | solution.py:274
  11.9 37.2 %copy-start.7 = (bf16[1,128,2048]{2,1,0:T(8,128)(2,1)S(1)}, bf16[1,128,2048]{2,1,0:T(8,128)(2,1)}, u32[]{:S(2)}) copy-start(bf16[1,128,2048]{2,1,0:T(8,128)(2,1)} %param.13) | copy-start | bytes 1572868
  44.7 6.4 %copy-start.10 = (s32[64]{0:T(128)S(1)}, s32[64]{0:T(128)}, u32[]{:S(2)}) copy-start(s32[64]{0:T(128)} %param.10) | copy-start | bytes 772
  44.7 6.6 %copy-start.9 = (s32[64,64]{1,0:T(8,128)S(1)}, s32[64,64]{1,0:T(8,128)}, u32[]{:S(2)}) copy-start(s32[64,64]{1,0:T(8,128)} %param.11) | copy-start | bytes 49156
  46.1 14.0 %collective-permute-start.4 = (bf16[1024,256]{1,0:T(8,128)(2,1)}, bf16[1024,256]{1,0:T(8,128)(2,1)S(1)}, u32[]{:S(2)}, u32[]{:S(2)}) collective-permute-start(bf16[1024,256]{1,0:T(8,128)(2,1)} %get-tuple-element.48.refs_1_.kv0.refs_0_), channel_id=1, source_target_pairs={{0,4},{4,0},{1,5},{5,1},{2,6},{6,2},{3,7},{7,3},{8,12},{12,8},{9,1... | collective-permute-start | bytes 1572872 | tf_op jit(solution)/shard_map/ppermute | solution.py:278
  47.3 4.3 %collective-permute-start.5 = (bf16[1024,256]{1,0:T(8,128)(2,1)}, bf16[1024,256]{1,0:T(8,128)(2,1)S(1)}, u32[]{:S(2)}, u32[]{:S(2)}) collective-permute-start(bf16[1024,256]{1,0:T(8,128)(2,1)} %get-tuple-element.48.refs_1_.kv0.refs_0_), channel_id=1, source_target_pairs={{0,1},{1,0},{2,3},{3,2},{4,5},{5,4},{6,7},{7,6},{8,9},{9,8},{10,11... | collective-permute-start | bytes 1572872 | tf_op jit(solution)/shard_map/ppermute | solution.py:274
  49.1 9.2 %collective-permute-start.6 = (bf16[128,1024]{1,0:T(8,128)(2,1)S(1)}, bf16[128,1024]{1,0:T(8,128)(2,1)S(1)}, u32[]{:S(2)}, u32[]{:S(2)}) collective-permute-start(bf16[128,1024]{1,0:T(8,128)(2,1)S(1)} %slice_select_fusion), channel_id=1, source_target_pairs={{0,1},{1,0},{2,3},{3,2},{4,5},{5,4},{6,7},{7,6},{8,9},{9,8},{10,11... | collective-permute-start | bytes 786440 | tf_op jit(solution)/shard_map/ppermute | solution.py:274
  49.2 20.7 %collective-permute-start.8 = (bf16[12,64,512]{2,1,0:T(8,128)(2,1)}, bf16[12,64,512]{2,1,0:T(8,128)(2,1)S(1)}, u32[]{:S(2)}, u32[]{:S(2)}) collective-permute-start(bf16[12,64,512]{2,1,0:T(8,128)(2,1)} %get-tuple-element.60.own0), channel_id=1, source_target_pairs={{0,6},{2,4},{4,2},{6,0},{1,7},{3,5},{5,3},{7,1},{8,14},{10,12},{12... | collective-permute-start | bytes 2359304 | tf_op jit(solution)/shard_map/ppermute | solution.py:315
  51.7 6.6 %copy-start.3 = (bf16[1024,256]{1,0:T(8,128)(2,1)}, bf16[1024,256]{1,0:T(8,128)(2,1)S(1)}, u32[]{:S(2)}) copy-start(bf16[1024,256]{1,0:T(8,128)(2,1)S(1)} %collective-permute-done.5.refs_2_.kv1) | copy-start | bytes 1572868
  51.7 9.2 %copy-start.8 = (bf16[4,64,512]{2,1,0:T(8,128)(2,1)S(1)}, bf16[4,64,512]{2,1,0:T(8,128)(2,1)}, u32[]{:S(2)}) copy-start(bf16[4,64,512]{2,1,0:T(8,128)(2,1)} %get-tuple-element.61.own1) | copy-start | bytes 786436
  60.2 9.7 %copy-start.2 = (bf16[1024,256]{1,0:T(8,128)(2,1)}, bf16[1024,256]{1,0:T(8,128)(2,1)S(1)}, u32[]{:S(2)}) copy-start(bf16[1024,256]{1,0:T(8,128)(2,1)S(1)} %collective-permute-done.4.refs_1_.kv2) | copy-start | bytes 1572868
  60.2 2.2 %collective-permute-start.7 = (bf16[1024,256]{1,0:T(8,128)(2,1)S(1)}, bf16[1024,256]{1,0:T(8,128)(2,1)S(1)}, u32[]{:S(2)}, u32[]{:S(2)}) collective-permute-start(bf16[1024,256]{1,0:T(8,128)(2,1)S(1)} %collective-permute-done.4.refs_1_.kv2), channel_id=1, source_target_pairs={{0,1},{1,0},{2,3},{3,2},{4,5},{5,4},{6,7},{7,6},{8,9},{9,8},{10,11... | collective-permute-start | bytes 1572872 | tf_op jit(solution)/shard_map/ppermute | solution.py:274
  60.9 9.0 %collective-permute-start.9 = (bf16[4,64,512]{2,1,0:T(8,128)(2,1)S(1)}, bf16[4,64,512]{2,1,0:T(8,128)(2,1)S(1)}, u32[]{:S(2)}, u32[]{:S(2)}) collective-permute-start(bf16[4,64,512]{2,1,0:T(8,128)(2,1)S(1)} %copy-done.8), channel_id=1, source_target_pairs={{0,4},{4,0},{1,5},{5,1},{2,6},{6,2},{3,7},{7,3},{8,12},{12,8},{9,1... | collective-permute-start | bytes 786440 | tf_op jit(solution)/shard_map/ppermute | solution.py:278
  62.4 7.5 %copy-start.4 = (bf16[1024,256]{1,0:T(8,128)(2,1)}, bf16[1024,256]{1,0:T(8,128)(2,1)S(1)}, u32[]{:S(2)}) copy-start(bf16[1024,256]{1,0:T(8,128)(2,1)S(1)} %collective-permute-done.7.refs_2_.kv3) | copy-start | bytes 1572868
  73.4 21.1 %copy-start = (bf16[1024,256]{1,0:T(8,128)(2,1)S(1)}, bf16[1024,256]{1,0:T(8,128)(2,1)}, u32[]{:S(2)}) copy-start(bf16[1024,256]{1,0:T(8,128)(2,1)} %get-tuple-element.68.refs_0_.pair_ref.refs_2_) | copy-start | bytes 1572868
  73.4 2.3 %collective-permute-start.10 = (f32[128,1024]{1,0:T(8,128)S(1)}, f32[128,1024]{1,0:T(8,128)S(1)}, u32[]{:S(2)}, u32[]{:S(2)}) collective-permute-start(f32[128,1024]{1,0:T(8,128)S(1)} %get-tuple-element.64), channel_id=1, source_target_pairs={{0,1},{1,0},{2,3},{3,2},{4,5},{5,4},{6,7},{7,6},{8,9},{9,8},{10,11... | collective-permute-start | bytes 1572872 | tf_op jit(solution)/shard_map/ppermute | solution.py:274
  77.6 14.5 %all-to-all-start.1 = ((bf16[16,64,256]{2,1,0:T(8,128)(2,1)}), bf16[16,64,256]{2,1,0:T(8,128)(2,1)S(1)}, u32[]{:S(2)}, u32[]{:S(2)}) async-start(bf16[16,64,256]{2,1,0:T(8,128)(2,1)} %cross.1), calls=%async_computation.1 | async-start | bytes 1048576 | tf_op jit(solution)/shard_map/all_to_all | solution.py:287
  81.2 1.3 collective-permute-start.11
  82.5 2.9 %collective-permute-start.12 = (f32[2,1024]{1,0:T(2,128)S(1)}, f32[2,1024]{1,0:T(2,128)S(1)}, u32[]{:S(2)}, u32[]{:S(2)}) collective-permute-start(f32[2,1024]{1,0:T(2,128)S(1)} %pad_maximum_fusion.6), channel_id=1, source_target_pairs={{0,4},{4,0},{1,5},{5,1},{2,6},{6,2},{3,7},{7,3},{8,12},{12,8},{9,1... | collective-permute-start | bytes 24584 | tf_op jit(solution)/shard_map/ppermute | solution.py:278
  93.0 3.5 %collective-permute-start.14 = (bf16[128,1024]{1,0:T(8,128)(2,1)S(1)}, bf16[128,1024]{1,0:T(8,128)(2,1)S(1)}, u32[]{:S(2)}, u32[]{:S(2)}) collective-permute-start(bf16[128,1024]{1,0:T(8,128)(2,1)S(1)} %get-tuple-element.66.own_ref), channel_id=1, source_target_pairs={{0,1},{1,0},{2,3},{3,2},{4,5},{5,4},{6,7},{7,6},{8,9},{9,8},{10,11... | collective-permute-start | bytes 786440 | tf_op jit(solution)/shard_map/ppermute | solution.py:274
  94.5 19.9 %collective-permute-start.13 = (bf16[1024,256]{1,0:T(8,128)(2,1)S(1)}, bf16[1024,256]{1,0:T(8,128)(2,1)S(1)}, u32[]{:S(2)}, u32[]{:S(2)}) collective-permute-start(bf16[1024,256]{1,0:T(8,128)(2,1)S(1)} %copy-done), channel_id=1, source_target_pairs={{0,4},{4,0},{1,5},{5,1},{2,6},{6,2},{3,7},{7,3},{8,12},{12,8},{9,1... | collective-permute-start | bytes 1572872 | tf_op jit(solution)/shard_map/ppermute | solution.py:278
  95.1 21.5 %collective-permute-start.16 = (bf16[1024,256]{1,0:T(8,128)(2,1)S(1)}, bf16[1024,256]{1,0:T(8,128)(2,1)S(1)}, u32[]{:S(2)}, u32[]{:S(2)}) collective-permute-start(bf16[1024,256]{1,0:T(8,128)(2,1)S(1)} %copy-done), channel_id=1, source_target_pairs={{0,1},{1,0},{2,3},{3,2},{4,5},{5,4},{6,7},{7,6},{8,9},{9,8},{10,11... | collective-permute-start | bytes 1572872 | tf_op jit(solution)/shard_map/ppermute | solution.py:274
  95.4 21.2 %collective-permute-start.18 = (bf16[1024,128]{1,0:T(8,128)(2,1)}, bf16[1024,128]{1,0:T(8,128)(2,1)S(1)}, u32[]{:S(2)}, u32[]{:S(2)}) collective-permute-start(bf16[1024,128]{1,0:T(8,128)(2,1)} %get-tuple-element.71.g_ref.refs_6_), channel_id=1, source_target_pairs={{0,1},{1,0},{2,3},{3,2},{4,5},{5,4},{6,7},{7,6},{8,9},{9,8},{10,11... | collective-permute-start | bytes 786440 | tf_op jit(solution)/shard_map/ppermute | solution.py:274
  95.6 19.4 %collective-permute-start.19 = (bf16[1024,128]{1,0:T(8,128)(2,1)}, bf16[1024,128]{1,0:T(8,128)(2,1)S(1)}, u32[]{:S(2)}, u32[]{:S(2)}) collective-permute-start(bf16[1024,128]{1,0:T(8,128)(2,1)} %get-tuple-element.71.g_ref.refs_6_), channel_id=1, source_target_pairs={{0,4},{4,0},{1,5},{5,1},{2,6},{6,2},{3,7},{7,3},{8,12},{12,8},{9,1... | collective-permute-start | bytes 786440 | tf_op jit(solution)/shard_map/ppermute | solution.py:278
  99.6 37.0 %all-to-all-start.3 = ((bf16[16,64,1024]{2,1,0:T(8,128)(2,1)}), bf16[16,64,1024]{2,1,0:T(8,128)(2,1)}, u32[]{:S(2)}, u32[]{:S(2)}) async-start(bf16[16,64,1024]{2,1,0:T(8,128)(2,1)} %bitcast.50), calls=%async_computation.3 | async-start | bytes 4194304 | tf_op jit(solution)/shard_map/all_to_all | solution.py:287
  104.2 10.9 %copy-start.6 = (bf16[1024,1024]{1,0:T(8,128)(2,1)S(1)}, bf16[1024,1024]{1,0:T(8,128)(2,1)}, u32[]{:S(2)}) copy-start(bf16[1024,1024]{1,0:T(8,128)(2,1)} %get-tuple-element.70) | copy-start | bytes 6291460
  114.3 2.6 %collective-permute-start.17 = (bf16[1024,256]{1,0:T(8,128)(2,1)S(1)}, bf16[1024,256]{1,0:T(8,128)(2,1)S(1)}, u32[]{:S(2)}, u32[]{:S(2)}) collective-permute-start(bf16[1024,256]{1,0:T(8,128)(2,1)S(1)} %collective-permute-done.13.refs_4_), channel_id=1, source_target_pairs={{0,1},{1,0},{2,3},{3,2},{4,5},{5,4},{6,7},{7,6},{8,9},{9,8},{10,11... | collective-permute-start | bytes 1572872 | tf_op jit(solution)/shard_map/ppermute | solution.py:274
  115.0 1.9 %collective-permute-start.20 = (bf16[1024,128]{1,0:T(8,128)(2,1)S(1)}, bf16[1024,128]{1,0:T(8,128)(2,1)S(1)}, u32[]{:S(2)}, u32[]{:S(2)}) collective-permute-start(bf16[1024,128]{1,0:T(8,128)(2,1)S(1)} %collective-permute-done.19.refs_8_), channel_id=1, source_target_pairs={{0,1},{1,0},{2,3},{3,2},{4,5},{5,4},{6,7},{7,6},{8,9},{9,8},{10,11... | collective-permute-start | bytes 786440 | tf_op jit(solution)/shard_map/ppermute | solution.py:274
  115.5 1.4 copy-start.1
  115.6 1.3 copy-start.5
  116.1 24.1 %collective-permute-start.15 = (bf16[2,64,1024]{2,1,0:T(8,128)(2,1)S(1)}, bf16[2,64,1024]{2,1,0:T(8,128)(2,1)S(1)}, u32[]{:S(2)}, u32[]{:S(2)}) collective-permute-start(bf16[2,64,1024]{2,1,0:T(8,128)(2,1)S(1)} %pad_maximum_fusion.2), channel_id=1, source_target_pairs={{0,1},{1,0},{2,3},{3,2},{4,5},{5,4},{6,7},{7,6},{8,9},{9,8},{10,11... | collective-permute-start | bytes 786440 | tf_op jit(solution)/shard_map/ppermute | solution.py:274
  136.6 16.3 %all-to-all-start.2 = ((bf16[16,64,384]{2,1,0:T(8,128)(2,1)}), bf16[16,64,384]{2,1,0:T(8,128)(2,1)S(1)}, u32[]{:S(2)}, u32[]{:S(2)}) async-start(bf16[16,64,384]{2,1,0:T(8,128)(2,1)} %pad_maximum_fusion), calls=%async_computation.2 | async-start | bytes 1572864 | tf_op jit(solution)/shard_map/all_to_all | solution.py:287
  142.4 13.2 %collective-permute-start.24 = (f32[16,1024]{1,0:T(8,128)S(1)}, f32[16,1024]{1,0:T(8,128)S(1)}, u32[]{:S(2)}, u32[]{:S(2)}) collective-permute-start(f32[16,1024]{1,0:T(8,128)S(1)} %get-tuple-element.86), channel_id=1, source_target_pairs={{0,6},{2,4},{4,2},{6,0},{1,7},{3,5},{5,3},{7,1},{8,14},{10,12},{12... | collective-permute-start | bytes 196616 | tf_op jit(solution)/shard_map/ppermute | solution.py:592
  144.3 11.3 %collective-permute-start.23 = (f32[16,1024]{1,0:T(8,128)S(1)}, f32[16,1024]{1,0:T(8,128)S(1)}, u32[]{:S(2)}, u32[]{:S(2)}) collective-permute-start(f32[16,1024]{1,0:T(8,128)S(1)} %get-tuple-element.87), channel_id=1, source_target_pairs={{0,4},{2,6},{4,0},{6,2},{1,5},{3,7},{5,1},{7,3},{8,12},{10,14},{12... | collective-permute-start | bytes 196616 | tf_op jit(solution)/shard_map/ppermute | solution.py:592
  144.3 11.3 %collective-permute-start.22 = (f32[16,1024]{1,0:T(8,128)S(1)}, f32[16,1024]{1,0:T(8,128)S(1)}, u32[]{:S(2)}, u32[]{:S(2)}) collective-permute-start(f32[16,1024]{1,0:T(8,128)S(1)} %get-tuple-element.85), channel_id=1, source_target_pairs={{0,2},{2,0},{4,6},{6,4},{1,3},{3,1},{5,7},{7,5},{8,10},{10,8},{12,... | collective-permute-start | bytes 196616 | tf_op jit(solution)/shard_map/ppermute | solution.py:592
  153.0 4.0 %collective-permute-start.21 = (bf16[8,64,384]{2,1,0:T(8,128)(2,1)S(1)}, bf16[8,64,384]{2,1,0:T(8,128)(2,1)S(1)}, u32[]{:S(2)}, u32[]{:S(2)}) collective-permute-start(bf16[8,64,384]{2,1,0:T(8,128)(2,1)S(1)} %constant_dynamic-slice_fusion), channel_id=1, source_target_pairs={{0,1},{1,0},{2,3},{3,2},{4,5},{5,4},{6,7},{7,6},{8,9},{9,8},{10,11... | collective-permute-start | bytes 1179656 | tf_op jit(solution)/shard_map/ppermute | solution.py:274
  155.7 2.4 %collective-permute-start.25 = (f32[8,1024]{1,0:T(8,128)S(1)}, f32[8,1024]{1,0:T(8,128)S(1)}, u32[]{:S(2)}, u32[]{:S(2)}) collective-permute-start(f32[8,1024]{1,0:T(8,128)S(1)} %dynamic-slice_bitcast_fusion.3), channel_id=1, source_target_pairs={{0,1},{1,0},{2,3},{3,2},{4,5},{5,4},{6,7},{7,6},{8,9},{9,8},{10,11... | collective-permute-start | bytes 98312 | tf_op jit(solution)/shard_map/ppermute | solution.py:274
